TPU v7x, 32 devices: a whole 2x2x4 slice. The times are simulated.
32 devices in a mesh: dp: 4 (over y, core), ctx: 2 (over x), exp: 4 (over z).
Axes of the slice: x: 2, y: 2, z: 4, core: 2. Of those that a mesh axis runs over, the one named last changes fastest.
Arguments:
- tokens: bfloat16 [16, 256, 2048], P(('dp', 'exp'), 'ctx'), may hold values from -6 to 6
- teacher: float32 [16, 256, 2048], P(('dp', 'exp'), 'ctx'), may hold values from -6 to 6
- lengths: int32 [16], replicated, may hold values from 64 to 256, as said below
- routes: int32 [16, 256, 4], P(('dp', 'exp'), 'ctx'), may hold values from 0 to 7, all different within a row; in each aligned block of 128 rows (0 to 127, 128 to 255, ..., all dimensions but the last counted through in order) at most 89 rows name the same one
- attn_gain: bfloat16 [2048], P(('dp', 'ctx', 'exp')), may hold values from 0.5 to 1.5
- ffn_gain: bfloat16 [2048], P(('dp', 'ctx', 'exp')), may hold values from 0.5 to 1.5
- router_weight: bfloat16 [2048, 8], P(('dp', 'ctx', 'exp')), may hold values from -0.0625 to 0.0625
- shared_gate: bfloat16 [2048], P(('dp', 'ctx', 'exp')), may hold values from -0.125 to 0.125
- qkv_weight: bfloat16 [2048, 3, 2048], P(('dp', 'ctx'), None, 'exp'), may hold values from -0.125 to 0.125
- qkv_bias: bfloat16 [3, 2048], P(None, 'exp'), may hold values from -1.1953125 to 1.1953125
- out_weight: bfloat16 [2048, 2048], P(('dp', 'ctx'), 'exp'), may hold values from -1 to 1
- shared_up: bfloat16 [2048, 2, 5632], P(('dp', 'ctx'), None, 'exp'), may hold values from -0.125 to 0.125
- shared_down: bfloat16 [2048, 5632], P(('dp', 'ctx'), 'exp'), may hold values from -0.21875 to 0.21875
- expert_up: bfloat16 [2048, 8, 2816], P(('dp', 'ctx'), 'exp'), may hold values from -0.125 to 0.125
- expert_down: bfloat16 [2048, 8, 1408], P(('dp', 'ctx'), 'exp'), may hold values from -0.875 to 0.875
Outputs:
- layer_out: bfloat16 [16, 256, 2048], P(('dp', 'exp'), 'ctx')
- grad_tokens: float32 [16, 256, 2048], P(('dp', 'exp'), 'ctx')
- grad_attn_gain: float32 [2048], P(('dp', 'ctx', 'exp'))
- grad_ffn_gain: float32 [2048], P(('dp', 'ctx', 'exp'))
- grad_router: float32 [2048, 8], P(('dp', 'ctx', 'exp'))
- grad_shared_gate: float32 [2048], P(('dp', 'ctx', 'exp'))
- grad_qkv: float32 [2048, 3, 2048], P(('dp', 'ctx'), None, 'exp')
- grad_qkv_bias: float32 [2, 2048], P(None, ('dp', 'ctx', 'exp'))
- grad_key_bias: float32 [2048], P(('dp', 'ctx', 'exp'))
- grad_out: float32 [2048, 2048], P(('dp', 'ctx'), 'exp')
- grad_shared_up: float32 [2048, 2, 5632], P(('dp', 'ctx'), None, 'exp')
- grad_shared_down: float32 [2048, 5632], P(('dp', 'ctx'), 'exp')
- grad_expert_up: float32 [2048, 8, 2816], P(('dp', 'ctx'), 'exp')
- grad_expert_down: float32 [2048, 8, 1408], P(('dp', 'ctx'), 'exp')
Inputs may be any that keep to these rules, and one draw needn't show every extreme that they name: A sequence's valid positions are its first lengths[s]; one sequence is full and another has a quarter of 256. `routes`: the 4 experts of a token differ. In the rows of one device (aligned blocks of 128 positions of one sequence) no expert is named more than 89 times, a bound that some block reaches.
All inputs are finite; a program needn't handle non-finite values.
Results may differ from a plain program's by a relative error of at most 0.015.
Values may be sent and summed in bfloat16 or wider, within the bound.
No kernel may reach another device: no remote copies, remote signals or barrier semaphores. Data moves between devices by JAX's collectives and lax.ppermute only.
A program may use at most 320 MiB of HBM per device.

v0:
```python
import jax
import jax.numpy as jnp
from jax import lax
from jax.sharding import PartitionSpec as P

HD = 128


EPSILON = 1e-06
ROPE_BASE = 1000000.0
NEGATIVE = -1e30
HIGHEST = lax.Precision.HIGHEST


def rope_tables(positions, head_width):
    frequency = ROPE_BASE ** (-jnp.arange(0, head_width, 2, dtype=jnp.float32) / head_width)
    angles = positions[:, None] * frequency[None, :]
    cosine_table = jnp.concatenate([jnp.cos(angles), jnp.cos(angles)], axis=1)
    sine_table = jnp.concatenate([jnp.sin(angles), jnp.sin(angles)], axis=1)
    return (cosine_table, sine_table)


def rotate(values, cosine_table, sine_table):
    halfway = values.shape[-1] // 2
    turned = jnp.concatenate([-values[..., halfway:], values[..., :halfway]], axis=-1)
    return values * cosine_table[:, None, :] + turned * sine_table[:, None, :]


def rotate_back(grads, cosine_table, sine_table):
    halfway = grads.shape[-1] // 2
    scaled = grads * sine_table[:, None, :]
    turned = jnp.concatenate([scaled[..., halfway:], -scaled[..., :halfway]], axis=-1)
    return grads * cosine_table[:, None, :] + turned


def norm_back(values, scale, gain, grads):
    weighted = grads * gain
    grad_values = scale * weighted - values * scale**3 * jnp.mean(
        weighted * values, axis=1, keepdims=True
    )
    grad_gain = jnp.sum(grads * values * scale, axis=0)
    return (grad_values, grad_gain)


def silu_back(gate_in, up_in, grads):
    sigmoid_gate = jax.nn.sigmoid(gate_in)
    activated = gate_in * sigmoid_gate
    grad_gate = grads * up_in * sigmoid_gate * (1.0 + gate_in * (1.0 - sigmoid_gate))
    return (grad_gate, grads * activated)


def gather_rows(values):
    return lax.all_gather(values, "exp", axis=0, tiled=True)


def sum_rows(partial_value):
    return lax.psum_scatter(partial_value, "exp", scatter_dimension=0, tiled=True)


def send_out(buffer):
    return lax.all_to_all(buffer, "exp", split_axis=0, concat_axis=1, tiled=True)


def send_home(buffer):
    return lax.all_to_all(buffer, "exp", split_axis=1, concat_axis=0, tiled=True)


def project_in(activity, weight):

    def accumulate(portion):
        if activity.ndim == 2:
            sliced = activity
            return jnp.einsum("rd,dbc->brc", sliced, portion, preferred_element_type=jnp.float32)
        sliced = activity
        return jnp.einsum("brd,dbc->brc", sliced, portion, preferred_element_type=jnp.float32)

    return accumulate(lax.all_gather(weight, ("dp", "ctx"), axis=0, tiled=True))


def project_out(activity, weight, merged):

    def produce(portion):
        if merged:
            return jnp.einsum("brc,nbc->rn", activity, portion, preferred_element_type=jnp.float32)[
                None
            ]
        return jnp.einsum("brc,nbc->brn", activity, portion, preferred_element_type=jnp.float32)

    return produce(lax.all_gather(weight, ("dp", "ctx"), axis=0, tiled=True))


def weight_grads(activity, partner):
    row_count = activity.shape[-1] // lax.axis_size(("dp", "ctx"))

    def partial_value(offset, amount):
        if activity.ndim == 2:
            sliced = activity
            return jnp.einsum("rd,brc->dbc", sliced, partner, preferred_element_type=jnp.float32)
        sliced = activity
        return jnp.einsum("brd,brc->dbc", sliced, partner, preferred_element_type=jnp.float32)

    return lax.psum_scatter(
        partial_value(jnp.int32(0), row_count * lax.axis_size(("dp", "ctx"))).astype(jnp.bfloat16),
        ("dp", "ctx"),
        scatter_dimension=0,
        tiled=True,
    ).astype(jnp.float32)


def key_mask(key_places, positions, group_lengths):
    causal = (key_places[None, :] <= positions[:, None])[None, None]
    inside = (key_places[None, :] < group_lengths[:, None])[:, None, None, :]
    return causal & inside


def attend_block(running, portion, query_heads, positions, group_lengths, score_scale):
    key_block, value_block = portion
    running_max, denominator, weighted_sum = running
    groups, tok_rows, heads_local, head_width = query_heads.shape
    key_count = key_block.shape[1]
    key_heads = key_block.reshape(groups, key_count, heads_local, head_width)
    value_heads = value_block.reshape(groups, key_count, heads_local, head_width).astype(
        jnp.float32
    )
    scores = (
        jnp.einsum("gihd,gjhd->ghij", query_heads, key_heads, preferred_element_type=jnp.float32)
        * score_scale
    )
    allowed = key_mask(jnp.arange(key_count, dtype=jnp.int32), positions, group_lengths)
    masked = jnp.where(allowed, scores, NEGATIVE)
    new_max = jnp.maximum(running_max, jnp.max(masked, axis=3))
    weights = jnp.where(allowed, jnp.exp(masked - new_max[..., None]), 0.0)
    denominator = jnp.sum(weights, axis=3)
    weighted_sum = jnp.einsum("ghij,gjhd->ghid", weights, value_heads, precision=HIGHEST)
    return (new_max, denominator, weighted_sum)


def attend_back(
    query_heads,
    keys_back,
    values_back,
    grad_attention,
    attention,
    log_total,
    positions,
    group_lengths,
    score_scale,
):
    groups, tok_rows, heads_local, head_width = query_heads.shape
    seq_len = keys_back.shape[1]
    key_heads = keys_back.reshape(groups, seq_len, heads_local, head_width)
    value_heads = values_back.reshape(groups, seq_len, heads_local, head_width)
    grad_heads = grad_attention.reshape(groups, tok_rows, heads_local, head_width)
    scores = (
        jnp.einsum("gihd,gjhd->ghij", query_heads, key_heads, preferred_element_type=jnp.float32)
        * score_scale
    )
    allowed = key_mask(jnp.arange(seq_len, dtype=jnp.int32), positions, group_lengths)
    weights = jnp.where(
        allowed, jnp.exp(jnp.where(allowed, scores, NEGATIVE) - log_total[..., None]), 0.0
    )
    grad_wide = grad_heads.astype(jnp.float32)
    row_dot = jnp.sum(grad_wide.transpose(0, 2, 1, 3) * attention, axis=3)
    grad_weights = jnp.einsum(
        "gihd,gjhd->ghij", grad_heads, value_heads, preferred_element_type=jnp.float32
    )
    grad_scores = (weights * (grad_weights - row_dot[..., None])).astype(jnp.bfloat16)
    grad_queries = (
        jnp.einsum("ghij,gjhd->gihd", grad_scores, key_heads, preferred_element_type=jnp.float32)
        * score_scale
    )
    grad_keys = (
        jnp.einsum("ghij,gihd->gjhd", grad_scores, query_heads, preferred_element_type=jnp.float32)
        * score_scale
    )
    grad_values = jnp.einsum("ghij,gihd->gjhd", weights, grad_wide, precision=HIGHEST)
    return (
        grad_queries,
        grad_keys.reshape(groups, seq_len, heads_local * head_width),
        grad_values.reshape(groups, seq_len, heads_local * head_width),
    )


def body(
    tokens,
    teacher,
    lengths,
    routes,
    attn_gain,
    ffn_gain,
    router_weight,
    shared_gate,
    qkv_weight,
    qkv_bias,
    out_weight,
    shared_up,
    shared_down,
    expert_up,
    expert_down,
):
    tok_rows = tokens.shape[1]
    model_width = tokens.shape[2]
    groups = lax.axis_size("exp")
    seq_len = tok_rows * lax.axis_size("ctx")
    head_width = HD
    head_columns = qkv_weight.shape[2]
    heads_local = head_columns // head_width
    experts_total = router_weight.shape[1]
    top_count = routes.shape[2]
    capacity = min(tok_rows, tok_rows * top_count * 7 // (experts_total * 5))
    shared_columns = shared_down.shape[1]
    inner_width = expert_down.shape[2]
    weight_rows = qkv_weight.shape[0]
    total_rows = groups * tok_rows
    score_scale = head_width ** (-0.5)
    count_valid = jnp.sum(lengths).astype(jnp.float32)
    factor = lengths.shape[0] * seq_len / count_valid
    group_lengths = lax.dynamic_slice_in_dim(lengths, lax.axis_index("dp") * groups, groups)
    own_length = lax.dynamic_slice_in_dim(group_lengths, lax.axis_index("exp"), 1)
    positions = lax.axis_index("ctx") * tok_rows + jnp.arange(tok_rows, dtype=jnp.int32)
    valid_rows = (positions < own_length).astype(jnp.float32)
    router_full, attn_full, ffn_full, gate_full = (
        lax.all_gather(router_weight, ("dp", "ctx", "exp"), axis=0, tiled=True),
        lax.all_gather(attn_gain, ("dp", "ctx", "exp"), axis=0, tiled=True),
        lax.all_gather(ffn_gain, ("dp", "ctx", "exp"), axis=0, tiled=True),
        lax.all_gather(shared_gate, ("dp", "ctx", "exp"), axis=0, tiled=True),
    )
    attn_factor = attn_full.astype(jnp.float32)
    ffn_factor = ffn_full.astype(jnp.float32)
    inputs = tokens[0].astype(jnp.float32)
    attn_scale = lax.rsqrt(jnp.mean(inputs * inputs, axis=1, keepdims=True) + EPSILON)
    normed_attn = (inputs * attn_scale * attn_factor).astype(jnp.bfloat16)
    attn_rows = gather_rows(normed_attn)
    projected = project_in(attn_rows, qkv_weight) + qkv_bias.astype(jnp.float32)[:, None, :]
    cosine_table, sine_table = rope_tables(positions.astype(jnp.float32), head_width)
    shaped = projected.reshape(3, groups, tok_rows, heads_local, head_width)
    query_heads = rotate(shaped[0], cosine_table, sine_table).astype(jnp.bfloat16)
    keys_flat = (
        rotate(shaped[1], cosine_table, sine_table)
        .astype(jnp.bfloat16)
        .reshape(groups, tok_rows, head_columns)
    )
    values_flat = shaped[2].astype(jnp.bfloat16).reshape(groups, tok_rows, head_columns)
    initial = (
        jnp.full((groups, heads_local, tok_rows), NEGATIVE, jnp.float32),
        jnp.zeros((groups, heads_local, tok_rows), jnp.float32),
        jnp.zeros((groups, heads_local, tok_rows, head_width), jnp.float32),
    )
    running_max, denominator, weighted_sum = attend_block(
        initial,
        (
            lax.all_gather(keys_flat, "ctx", axis=1, tiled=True),
            lax.all_gather(values_flat, "ctx", axis=1, tiled=True),
        ),
        query_heads,
        positions,
        group_lengths,
        score_scale,
    )
    attention = weighted_sum / denominator[..., None]
    log_total = running_max + jnp.log(denominator)
    attn_low = (
        attention.transpose(0, 2, 1, 3).reshape(total_rows, head_columns).astype(jnp.bfloat16)
    )
    out_view = out_weight.reshape(weight_rows, 1, head_columns)
    attn_out = sum_rows(project_out(attn_low[None], out_view, False)[0])
    hidden = inputs + attn_out
    ffn_scale = lax.rsqrt(jnp.mean(hidden * hidden, axis=1, keepdims=True) + EPSILON)
    normed_ffn = (hidden * ffn_scale * ffn_factor).astype(jnp.bfloat16)
    logits = jnp.dot(normed_ffn, router_full, preferred_element_type=jnp.float32)
    router_probs = jax.nn.softmax(logits, axis=1)
    route_pick = (
        routes[0][:, :, None] == jnp.arange(experts_total, dtype=jnp.int32)[None, None, :]
    ).astype(jnp.float32)
    gate_values = jnp.sum(router_probs[:, None, :] * route_pick, axis=2)
    shared_sig = jax.nn.sigmoid(jnp.dot(normed_ffn, gate_full, preferred_element_type=jnp.float32))
    ffn_rows = gather_rows(normed_ffn)
    shared_pre = project_in(ffn_rows, shared_up)
    shared_act = (jax.nn.silu(shared_pre[0]) * shared_pre[1]).astype(jnp.bfloat16)
    down_view = shared_down.reshape(weight_rows, 1, shared_columns)
    shared_out = sum_rows(project_out(shared_act[None], down_view, False)[0])
    flat_routes = routes[0].reshape(tok_rows * top_count)
    route_onehot = (
        flat_routes[:, None] == jnp.arange(experts_total, dtype=jnp.int32)[None, :]
    ).astype(jnp.int32)
    earlier = jnp.cumsum(route_onehot, axis=0) - route_onehot
    slot_index = jnp.sum(earlier * route_onehot, axis=1)
    target = (flat_routes * capacity + slot_index).reshape(tok_rows, top_count)
    slot_match = (
        jnp.arange(experts_total * capacity, dtype=jnp.int32)[:, None, None] == target[None]
    ).astype(jnp.bfloat16)
    dispatch = jnp.sum(slot_match.astype(jnp.float32), axis=2).astype(jnp.bfloat16)
    slot_flat = slot_match.reshape(experts_total * capacity, tok_rows * top_count)
    buffer = (
        jnp.dot(dispatch, normed_ffn, preferred_element_type=jnp.float32)
        .astype(jnp.bfloat16)
        .reshape(experts_total, capacity, model_width)
    )
    expert_in = send_out(buffer)
    expert_pre = project_in(expert_in, expert_up)
    expert_act = (
        jax.nn.silu(expert_pre[..., :inner_width]) * expert_pre[..., inner_width:]
    ).astype(jnp.bfloat16)
    expert_result = project_out(expert_act, expert_down, False)
    returned = send_home(expert_result.astype(jnp.bfloat16)).reshape(
        experts_total * capacity, model_width
    )
    picked = returned[target].astype(jnp.float32)
    routed = jnp.sum(gate_values[:, :, None] * picked, axis=1)
    result = hidden + shared_sig[:, None] * shared_out + routed
    grad_result = factor * valid_rows[:, None] * (result - teacher[0])
    grad_pairs = (
        (gate_values[:, :, None] * grad_result[:, None, :])
        .astype(jnp.bfloat16)
        .reshape(tok_rows * top_count, model_width)
    )
    grad_slots = (
        jnp.dot(slot_flat, grad_pairs, preferred_element_type=jnp.float32)
        .astype(jnp.bfloat16)
        .reshape(experts_total, capacity, model_width)
    )
    grad_gates = jnp.sum(picked * grad_result[:, None, :], axis=2)
    grad_probs = jnp.sum(grad_gates[:, :, None] * route_pick, axis=1)
    grad_logits = router_probs * (
        grad_probs - jnp.sum(router_probs * grad_probs, axis=1, keepdims=True)
    )
    normed_wide = normed_ffn.astype(jnp.float32)
    grad_router_full = jnp.dot(normed_wide.T, grad_logits, precision=HIGHEST)
    grad_sig = jnp.sum(grad_result * shared_out, axis=1) * shared_sig * (1.0 - shared_sig)
    grad_gate_full = jnp.dot(grad_sig, normed_wide, precision=HIGHEST)
    grad_normed = (
        jnp.dot(grad_logits, router_full.astype(jnp.float32).T, precision=HIGHEST)
        + grad_sig[:, None] * gate_full.astype(jnp.float32)[None, :]
    )
    shared_back = gather_rows((shared_sig[:, None] * grad_result).astype(jnp.bfloat16))
    grad_shared_act = project_in(shared_back, down_view)[0]
    shared_gate_grad, shared_up_grad = silu_back(shared_pre[0], shared_pre[1], grad_shared_act)
    grad_shared_pre = jnp.stack([shared_gate_grad, shared_up_grad]).astype(jnp.bfloat16)
    grad_shared_down = weight_grads(shared_back, shared_act[None]).reshape(
        weight_rows, shared_columns
    )
    grad_shared_up = weight_grads(ffn_rows, grad_shared_pre)
    grad_normed = grad_normed + sum_rows(project_out(grad_shared_pre, shared_up, True)[0])
    expert_back_in = send_out(grad_slots)
    grad_expert_act = project_in(expert_back_in, expert_down)
    gate_part, up_part = silu_back(
        expert_pre[..., :inner_width], expert_pre[..., inner_width:], grad_expert_act
    )
    grad_expert_pre = jnp.concatenate([gate_part, up_part], axis=2).astype(jnp.bfloat16)
    grad_expert_down = weight_grads(expert_back_in, expert_act)
    grad_expert_up = weight_grads(expert_in, grad_expert_pre)
    grad_expert_in = project_out(grad_expert_pre, expert_up, False)
    grad_buffer = send_home(grad_expert_in.astype(jnp.bfloat16)).reshape(
        experts_total * capacity, model_width
    )
    grad_normed = grad_normed + jnp.einsum(
        "st,sd->td", dispatch, grad_buffer, preferred_element_type=jnp.float32
    )
    grad_hidden_norm, grad_ffn_full = norm_back(hidden, ffn_scale, ffn_factor, grad_normed)
    grad_hidden = grad_result + grad_hidden_norm
    attn_back = gather_rows(grad_hidden.astype(jnp.bfloat16))
    grad_attention = project_in(attn_back, out_view)[0].astype(jnp.bfloat16)
    grad_out = weight_grads(attn_back, attn_low[None]).reshape(weight_rows, head_columns)
    keys_back, values_back = (
        lax.all_gather(keys_flat, "ctx", axis=1, tiled=True),
        lax.all_gather(values_flat, "ctx", axis=1, tiled=True),
    )
    grad_queries, grad_keys, grad_values = attend_back(
        query_heads,
        keys_back,
        values_back,
        grad_attention,
        attention,
        log_total,
        positions,
        group_lengths,
        score_scale,
    )
    grad_keys_own, grad_values_own = (
        lax.psum_scatter(grad_keys, "ctx", scatter_dimension=1, tiled=True),
        lax.psum_scatter(grad_values, "ctx", scatter_dimension=1, tiled=True),
    )
    rope_query = rotate_back(grad_queries, cosine_table, sine_table)
    rope_key = rotate_back(
        grad_keys_own.reshape(groups, tok_rows, heads_local, head_width), cosine_table, sine_table
    )
    grad_projected = jnp.stack(
        [
            rope_query.reshape(total_rows, head_columns),
            rope_key.reshape(total_rows, head_columns),
            grad_values_own.reshape(total_rows, head_columns),
        ]
    ).astype(jnp.bfloat16)
    grad_qkv = weight_grads(attn_rows, grad_projected)
    bias_local = jnp.sum(grad_projected.astype(jnp.float32), axis=1)
    bias_wide = lax.dynamic_update_slice_in_dim(
        jnp.zeros((3, groups * head_columns), jnp.float32),
        bias_local,
        lax.axis_index("exp") * head_columns,
        1,
    )
    grad_normed_attn = sum_rows(project_out(grad_projected, qkv_weight, True)[0])
    grad_inputs_norm, grad_attn_full = norm_back(inputs, attn_scale, attn_factor, grad_normed_attn)
    grad_tokens = (grad_hidden + grad_inputs_norm)[None]
    grad_router, grad_attn_gain, grad_ffn_gain, grad_shared_gate, grad_bias_all = (
        lax.psum_scatter(grad_router_full, ("dp", "ctx", "exp"), scatter_dimension=0, tiled=True),
        lax.psum_scatter(grad_attn_full, ("dp", "ctx", "exp"), scatter_dimension=0, tiled=True),
        lax.psum_scatter(grad_ffn_full, ("dp", "ctx", "exp"), scatter_dimension=0, tiled=True),
        lax.psum_scatter(grad_gate_full, ("dp", "ctx", "exp"), scatter_dimension=0, tiled=True),
        lax.psum_scatter(bias_wide, ("dp", "ctx", "exp"), scatter_dimension=1, tiled=True),
    )
    grad_qkv_bias = jnp.stack([grad_bias_all[0], grad_bias_all[2]])
    grad_key_bias = grad_bias_all[1]
    return (
        result.astype(jnp.bfloat16)[None],
        grad_tokens,
        grad_attn_gain,
        grad_ffn_gain,
        grad_router,
        grad_shared_gate,
        grad_qkv,
        grad_qkv_bias,
        grad_key_bias,
        grad_out,
        grad_shared_up,
        grad_shared_down,
        grad_expert_up,
        grad_expert_down,
    )


def solution(mesh):
    return jax.shard_map(
        body,
        mesh=mesh,
        in_specs=(
            P(("dp", "exp"), "ctx", None),
            P(("dp", "exp"), "ctx", None),
            P(),
            P(("dp", "exp"), "ctx", None),
            P(("dp", "ctx", "exp")),
            P(("dp", "ctx", "exp")),
            P(("dp", "ctx", "exp"), None),
            P(("dp", "ctx", "exp")),
            P(("dp", "ctx"), None, "exp"),
            P(None, "exp"),
            P(("dp", "ctx"), "exp"),
            P(("dp", "ctx"), None, "exp"),
            P(("dp", "ctx"), "exp"),
            P(("dp", "ctx"), "exp", None),
            P(("dp", "ctx"), "exp", None),
        ),
        out_specs=(
            P(("dp", "exp"), "ctx", None),
            P(("dp", "exp"), "ctx", None),
            P(("dp", "ctx", "exp")),
            P(("dp", "ctx", "exp")),
            P(("dp", "ctx", "exp"), None),
            P(("dp", "ctx", "exp")),
            P(("dp", "ctx"), None, "exp"),
            P(None, ("dp", "ctx", "exp")),
            P(("dp", "ctx", "exp")),
            P(("dp", "ctx"), "exp"),
            P(("dp", "ctx"), None, "exp"),
            P(("dp", "ctx"), "exp"),
            P(("dp", "ctx"), "exp", None),
            P(("dp", "ctx"), "exp", None),
        ),
        check_vma=False,
    )
```

profile of v0, /device:TPU:1, one launch (start us, length us, event | category | flops | bytes accessed | tf_op | source)
XLA Modules:
  0.0 2140.0 jit_solution(7186324105356165370)
XLA Ops:
  11.6 40.7 %all-reduce.7 = (bf16[2048]{0:T(1024)(128)(2,1)S(1)}, bf16[2048]{0:T(1024)(128)(2,1)S(1)}, bf16[2048]{0:T(1024)(128)(2,1)S(1)}) all-reduce(bf16[2048]{0:T(1024)(128)(2,1)S(1)} %dynamic-update-slice, bf16[2048]{0:T(1024)(128)(2,1)S(1)} %dynamic-update-slice.1, ...), channel_id=1, replica_groups=mesh['dp'=4,'ctx'=2,'exp'=4] {'dp','ctx','exp'}, use_global_device_ids=true, to_apply=%add | all-reduce | flops 6144 | bytes 24576
  56.8 44.4 %all-gather.16.cloned.1.call-done = bf16[512,2048]{1,0:T(8,128)(2,1)} async-done(((bf16[128,2048]{1,0:T(8,128)(2,1)}), bf16[512,2048]{1,0:T(8,128)(2,1)}) %all-gather.16.cloned.1.call-update) | async-done | bytes 2097168 | tf_op jit(solution)/shard_map/all_gather | solution.py:53
  101.2 46.6 %all-gather.18.cloned.1.call-done = bf16[2048,3,512]{2,0,1:T(8,128)(2,1)} async-done(((bf16[256,3,512]{2,0,1:T(8,128)(2,1)}), bf16[2048,3,512]{2,0,1:T(8,128)(2,1)}) %all-gather.18.cloned.1.call-update) | async-done | bytes 6291472 | tf_op jit(solution)/shard_map/all_gather | solution.py:77
  147.7 6.2 add_bitcast_fusion
  169.1 8.5 all-gather.22.cloned.1.call-done
  179.1 21.8 %all-gather.20.cloned.1.call-done = bf16[4,256,512]{1,2,0:T(8,128)(2,1)} async-done(((bf16[4,128,512]{1,2,0:T(8,128)(2,1)}), bf16[4,256,512]{1,2,0:T(8,128)(2,1)}) %all-gather.20.cloned.1.call-update) | async-done | bytes 1048592 | tf_op jit(solution)/shard_map/all_gather | solution.py:252
  206.5 24.5 %all-gather.36.cloned.1.call-done = bf16[2048,512]{1,0:T(8,128)(2,1)} async-done(((bf16[256,512]{1,0:T(8,128)(2,1)}), bf16[2048,512]{1,0:T(8,128)(2,1)}) %all-gather.36.cloned.1.call-update) | async-done | bytes 2097168 | tf_op jit(solution)/shard_map/all_gather | solution.py:89
  231.0 4.9 fusion.59
  238.6 73.8 %reduce-scatter.19.cloned.1.call-done = f32[128,2048]{1,0:T(8,128)} async-done(((f32[512,2048]{1,0:T(8,128)}), f32[128,2048]{1,0:T(8,128)}) %reduce-scatter.19.cloned.1.call-update) | async-done | bytes 1048592 | tf_op jit(solution)/shard_map/reduce_scatter | solution.py:57
  327.5 4.6 all-to-all-start
  332.2 51.5 %all-gather.26.cloned.1.call-done = bf16[2048,2,1408]{2,0,1:T(8,128)(2,1)} async-done(((bf16[256,2,1408]{2,0,1:T(8,128)(2,1)}), bf16[2048,2,1408]{2,0,1:T(8,128)(2,1)}) %all-gather.26.cloned.1.call-update) | async-done | bytes 11534352 | tf_op jit(solution)/shard_map/all_gather | solution.py:77
  383.7 54.3 %all-gather.24.cloned.1.call-done = bf16[512,2048]{1,0:T(8,128)(2,1)} async-done(((bf16[128,2048]{1,0:T(8,128)(2,1)}), bf16[512,2048]{1,0:T(8,128)(2,1)}) %all-gather.24.cloned.1.call-update) | async-done | bytes 2097168 | tf_op jit(solution)/shard_map/all_gather | solution.py:53
  438.0 10.1 convolution_bitcast_fusion
  451.5 30.7 %all-gather.38.cloned.1.call-done = bf16[2048,1408]{1,0:T(8,128)(2,1)} async-done(((bf16[256,1408]{1,0:T(8,128)(2,1)}), bf16[2048,1408]{1,0:T(8,128)(2,1)}) %all-gather.38.cloned.1.call-update) | async-done | bytes 5767184 | tf_op jit(solution)/shard_map/all_gather | solution.py:89
  482.3 7.6 fusion.86
  489.9 5.3 copy.164
  495.2 106.0 %all-gather.28.cloned.1.call-done = bf16[2048,2,2816]{2,0,1:T(8,128)(2,1)} async-done(((bf16[256,2,2816]{2,0,1:T(8,128)(2,1)}), bf16[2048,2,2816]{2,0,1:T(8,128)(2,1)}) %all-gather.28.cloned.1.call-update) | async-done | bytes 23068688 | tf_op jit(solution)/shard_map/all_gather | solution.py:77
  601.2 14.3 fusion.8
  621.3 50.3 %all-gather.30.cloned.1.call-done = bf16[2048,2,1408]{2,0,1:T(8,128)(2,1)} async-done(((bf16[256,2,1408]{2,0,1:T(8,128)(2,1)}), bf16[2048,2,1408]{2,0,1:T(8,128)(2,1)}) %all-gather.30.cloned.1.call-update) | async-done | bytes 11534352 | tf_op jit(solution)/shard_map/all_gather | solution.py:89
  671.6 9.7 convolution_convert_fusion.4
  681.3 4.6 copy.168
  685.9 4.5 all-to-all-start.1
  696.0 170.0 %all-gather.2 = bf16[32,64,8]{1,2,0:T(8,128)(2,1)S(1)} all-gather(bf16[1,64,8]{1,2,0:T(8,128)(2,1)S(1)} %bitcast.239), channel_id=1, replica_groups=mesh['dp'=4,'ctx'=2,'exp'=4] {'dp','ctx','exp'}, dimensions={0}, use_global_device_ids=true | all-gather | bytes 33792 | tf_op jit(solution)/shard_map/all_gather | solution.py:223
  873.9 3.7 gather_fusion
  877.6 4.7 reshape.375
  882.3 5.8 multiply_reduce_fusion.1
  895.2 4.3 reshape.347
  899.5 4.7 all-to-all-start.2
  904.3 67.3 %all-gather.32.cloned.1.call-done = bf16[512,2048]{1,0:T(8,128)(2,1)} async-done(((bf16[128,2048]{1,0:T(8,128)(2,1)}), bf16[512,2048]{1,0:T(8,128)(2,1)}) %all-gather.32.cloned.1.call-update) | async-done | bytes 2097168 | tf_op jit(solution)/shard_map/all_gather | solution.py:53
  971.6 9.0 multiply_convert_fusion.5
  982.1 10.5 convolution_bitcast_fusion.1
  992.7 26.2 %all-to-all-done.2 = bf16[8,89,2048]{2,1,0:T(8,128)(2,1)} async-done(((bf16[8,89,2048]{2,1,0:T(8,128)(2,1)}), bf16[8,89,2048]{2,1,0:T(8,128)(2,1)}, u32[]{:S(2)}, u32[]{:S(2)}) %all-to-all-start.2) | async-done | bytes 2916384 | tf_op jit(solution)/shard_map/all_to_all | solution.py:61
  1018.8 4.9 copy.172
  1023.8 14.5 multiply_convert_fusion.2
  1038.3 15.1 convolution_convert_fusion.3
  1053.4 6.4 copy.174
  1059.8 4.7 all-to-all-start.3
  1064.6 4.5 multiply_reduce_fusion
  1069.2 66.9 %all-to-all-done.3 = bf16[2,356,2048]{2,0,1:T(2,128)(2,1)} async-done(((bf16[2,356,2048]{2,0,1:T(2,128)(2,1)}), bf16[2,356,2048]{2,0,1:T(2,128)(2,1)}, u32[]{:S(2)}, u32[]{:S(2)}) %all-to-all-start.3) | async-done | bytes 2916384 | tf_op jit(solution)/shard_map/all_to_all | solution.py:65
  1136.1 4.8 copy.175
  1140.9 4.4 reshape.348
  1152.1 44.9 %all-gather.34.cloned.1.call-done = bf16[512,2048]{1,0:T(8,128)(2,1)} async-done(((bf16[128,2048]{1,0:T(8,128)(2,1)}), bf16[512,2048]{1,0:T(8,128)(2,1)}) %all-gather.34.cloned.1.call-update) | async-done | bytes 2097168 | tf_op jit(solution)/shard_map/all_gather | solution.py:53
  1213.9 7.6 fusion
  1222.6 4.2 fusion.3
  1232.5 3.9 reduce-scatter.27.cloned.1.call-done
  1238.7 32.2 %reduce-scatter.25.cloned.1.call-done = f32[4,128,512]{1,2,0:T(8,128)} async-done(((f32[4,256,512]{1,2,0:T(8,128)}), f32[4,128,512]{1,2,0:T(8,128)}) %reduce-scatter.25.cloned.1.call-update) | async-done | bytes 1048592 | tf_op jit(solution)/shard_map/reduce_scatter | solution.py:380
  1282.0 10.6 convolution_convert_fusion
  1294.4 10.9 convert_bitcast_fusion.1
  1306.7 7.8 convolution_bitcast_fusion.2
  1314.6 7.0 convolution_convert_fusion.2
  1323.4 18.2 convert_bitcast_fusion
  1342.0 61.6 %reduce-scatter.43.cloned.1.call-done = f32[64,8]{1,0:T(8,128)} async-done(((f32[2048,8]{1,0:T(8,128)}), f32[64,8]{1,0:T(8,128)}) %reduce-scatter.43.cloned.1.call-update) | async-done | bytes 2064
  1405.0 63.4 %reduce-scatter.37.cloned.1.call-done = bf16[256,1,1408]{2,0,1:T(8,128)(2,1)} async-done(((bf16[2048,1,1408]{2,0,1:T(8,128)(2,1)}), bf16[256,1,1408]{2,0,1:T(8,128)(2,1)}) %reduce-scatter.37.cloned.1.call-update) | async-done | bytes 720912 | tf_op jit(solution)/shard_map/reduce_scatter | solution.py:102
  1470.8 42.4 %reduce-scatter.33.cloned.1.call-done = bf16[256,1,512]{2,0,1:T(8,128)(2,1)} async-done(((bf16[2048,1,512]{2,0,1:T(8,128)(2,1)}), bf16[256,1,512]{2,0,1:T(8,128)(2,1)}) %reduce-scatter.33.cloned.1.call-update) | async-done | bytes 262160 | tf_op jit(solution)/shard_map/reduce_scatter | solution.py:102
  1515.0 131.5 %reduce-scatter.45.cloned.1.call-done = f32[64,3]{1,0:T(8,128)} async-done(((f32[2048,3]{1,0:T(8,128)}), f32[64,3]{1,0:T(8,128)}) %reduce-scatter.45.cloned.1.call-update) | async-done | bytes 784
  1648.8 90.2 %reduce-scatter.35.cloned.1.call-done = bf16[256,2,1408]{2,0,1:T(8,128)(2,1)} async-done(((bf16[2048,2,1408]{2,0,1:T(8,128)(2,1)}), bf16[256,2,1408]{2,0,1:T(8,128)(2,1)}) %reduce-scatter.35.cloned.1.call-update) | async-done | bytes 1441808 | tf_op jit(solution)/shard_map/reduce_scatter | solution.py:102
  1739.0 4.4 copy.189
  1743.5 86.3 %reduce-scatter.41.cloned.1.call-done = bf16[256,2,1408]{0,2,1:T(8,128)(2,1)} async-done(((bf16[2048,2,1408]{0,2,1:T(8,128)(2,1)}), bf16[256,2,1408]{0,2,1:T(8,128)(2,1)}) %reduce-scatter.41.cloned.1.call-update) | async-done | bytes 1441808 | tf_op jit(solution)/shard_map/reduce_scatter | solution.py:102
  1829.7 5.0 copy.191
  1834.8 74.0 %reduce-scatter.29.cloned.1.call-done = f32[128,2048]{1,0:T(8,128)} async-done(((f32[512,2048]{1,0:T(8,128)}), f32[128,2048]{1,0:T(8,128)}) %reduce-scatter.29.cloned.1.call-update) | async-done | bytes 1048592 | tf_op jit(solution)/shard_map/reduce_scatter | solution.py:57
  1910.3 41.4 %all-reduce.6 = (f32[2048]{0:T(1024)S(1)}, f32[2048]{0:T(1024)S(1)}, f32[2048]{0:T(1024)S(1)}) all-reduce(f32[2048]{0:T(1024)S(1)} %get-tuple-element.72, f32[2048]{0:T(1024)S(1)} %get-tuple-element.70, f32[2048]{0:T(1024)S(1)} %bitcast.236), channel_id=10, replica_groups=mesh['dp'=4,'ctx'=2,'exp'=4] {'dp','ctx','exp'}, use_global_device_ids=true, to_apply=%region_27.28.clone | all-reduce | flops 6144 | bytes 49152
  1956.1 19.0 reduce-scatter.31.cloned.1.call-done
  1977.5 147.4 %reduce-scatter.39.cloned.1.call-done = bf16[256,2,2816]{0,2,1:T(8,128)(2,1)} async-done(((bf16[2048,2,2816]{0,2,1:T(8,128)(2,1)}), bf16[256,2,2816]{0,2,1:T(8,128)(2,1)}) %reduce-scatter.39.cloned.1.call-update) | async-done | bytes 2883600 | tf_op jit(solution)/shard_map/reduce_scatter | solution.py:102
  2124.9 8.4 copy.190
  (332 shorter events, 144.0 us)
Async XLA Ops:
  7.2 48.1 %copy-start.61 = (bf16[3,512]{1,0:T(4,128)(2,1)S(1)}, bf16[3,512]{1,0:T(4,128)(2,1)}, u32[]{:S(2)}) copy-start(bf16[3,512]{1,0:T(4,128)(2,1)} %param.24) | copy-start | bytes 9220
  7.2 94.0 %all-gather.16.cloned.1.call-start = ((), (), s32[]{:S(2)}) async-start(), calls=%async_computation.18 | async-start | bytes 2621440 | tf_op jit(solution)/shard_map/all_gather | solution.py:53
  9.1 46.2 %copy-start.57 = (f32[128]{0:T(128)}, f32[128]{0:T(128)S(1)}, u32[]{:S(2)}) copy-start(f32[128]{0:T(128)S(1)} %get-tuple-element.111) | copy-start | bytes 1540
  52.3 640.6 %copy-start.53 = (bf16[2048]{0:T(1024)(128)(2,1)}, bf16[2048]{0:T(1024)(128)(2,1)S(1)}, u32[]{:S(2)}) copy-start(bf16[2048]{0:T(1024)(128)(2,1)S(1)} %get-tuple-element.79) | copy-start | bytes 12292
  52.4 101.6 %copy-start.44 = (f32[2048]{0:T(1024)}, f32[2048]{0:T(1024)S(1)}, u32[]{:S(2)}) copy-start(f32[2048]{0:T(1024)S(1)} %convert_element_type.180) | copy-start | bytes 24580
  54.4 93.3 %all-gather.18.cloned.1.call-start = ((), (), s32[]{:S(2)}) async-start(), calls=%async_computation.19 | async-start | bytes 7077888 | tf_op jit(solution)/shard_map/all_gather | solution.py:77
  55.2 122.4 %all-gather.22.cloned.1.call-start = ((), (), s32[]{:S(2)}) async-start(), calls=%async_computation.21 | async-start | bytes 1572864 | tf_op jit(solution)/shard_map/all_gather | solution.py:253
  56.1 112.8 %copy-start.40 = (f32[128,128]{0,1:T(8,128)}, f32[128,128]{0,1:T(8,128)S(1)}, u32[]{:S(2)}) copy-start(f32[128,128]{0,1:T(8,128)S(1)} %get-tuple-element.105) | copy-start | bytes 196612
  56.8 112.1 %copy-start.38 = (f32[128,128]{0,1:T(8,128)}, f32[128,128]{0,1:T(8,128)S(1)}, u32[]{:S(2)}) copy-start(f32[128,128]{0,1:T(8,128)S(1)} %get-tuple-element.107) | copy-start | bytes 196612
  156.6 44.3 %all-gather.20.cloned.1.call-start = ((), (), s32[]{:S(2)}) async-start(), calls=%async_computation.20 | async-start | bytes 1572864 | tf_op jit(solution)/shard_map/all_gather | solution.py:252
  165.8 65.1 %all-gather.36.cloned.1.call-start = ((), (), s32[]{:S(2)}) async-start(), calls=%async_computation.40 | async-start | bytes 2359296 | tf_op jit(solution)/shard_map/all_gather | solution.py:89
  166.4 146.0 %reduce-scatter.19.cloned.1.call-start = ((), (), s32[]{:S(2)}) async-start(), calls=%async_computation.22 | async-start | bytes 5242880 | tf_op jit(solution)/shard_map/reduce_scatter | solution.py:57
  166.8 36.7 %copy-start.18 = (pred[4,128,256]{2,1,0:T(8,128)(4,1)}, pred[4,128,256]{2,1,0:T(8,128)(4,1)S(1)}, u32[]{:S(2)}) copy-start(pred[4,128,256]{2,1,0:T(8,128)(4,1)S(1)} %broadcast_and_fusion) | copy-start | bytes 393220
  169.1 33.6 %copy-start.11 = (bf16[4,128,4,128]{1,3,2,0:T(8,128)(2,1)}, bf16[4,128,4,128]{1,3,2,0:T(8,128)(2,1)S(1)}, u32[]{:S(2)}) copy-start(bf16[4,128,4,128]{1,3,2,0:T(8,128)(2,1)S(1)} %fusion.41) | copy-start | bytes 1572868
  179.1 24.4 %copy-start.13 = (bf16[4,256,512]{1,2,0:T(8,128)(2,1)}, bf16[4,256,512]{1,2,0:T(8,128)(2,1)S(1)}, u32[]{:S(2)}) copy-start(bf16[4,256,512]{1,2,0:T(8,128)(2,1)S(1)} %copy.156) | copy-start | bytes 3145732
  206.5 29.4 %copy-start.16 = (bf16[4,128,4,128]{3,2,1,0:T(4,128)(2,1)}, bf16[4,128,4,128]{3,2,1,0:T(4,128)(2,1)S(1)}, u32[]{:S(2)}) copy-start(bf16[4,128,4,128]{3,2,1,0:T(4,128)(2,1)S(1)} %copy.157) | copy-start | bytes 1572868
  235.9 76.5 %copy-start.5 = (bf16[1,128,2048]{2,1,0:T(8,128)(2,1)S(1)}, bf16[1,128,2048]{2,1,0:T(8,128)(2,1)}, u32[]{:S(2)}) copy-start(bf16[1,128,2048]{2,1,0:T(8,128)(2,1)} %param.15) | copy-start | bytes 1572868
  235.9 147.8 %all-gather.26.cloned.1.call-start = ((), (), s32[]{:S(2)}) async-start(), calls=%async_computation.24 | async-start | bytes 12976128 | tf_op jit(solution)/shard_map/all_gather | solution.py:77
  238.5 78.2 %copy-start.24 = (bf16[256,2,2816]{2,1,0:T(2,128)(2,1)S(1)}, bf16[256,2,2816]{2,1,0:T(2,128)(2,1)}, u32[]{:S(2)}) copy-start(bf16[256,2,2816]{2,1,0:T(2,128)(2,1)} %param.28) | copy-start | bytes 8650756
  238.5 199.5 %all-gather.24.cloned.1.call-start = ((), (), s32[]{:S(2)}) async-start(), calls=%async_computation.23 | async-start | bytes 2621440 | tf_op jit(solution)/shard_map/all_gather | solution.py:53
  238.6 80.0 %copy-start.46 = (f32[2048]{0:T(1024)}, f32[2048]{0:T(1024)S(1)}, u32[]{:S(2)}) copy-start(f32[2048]{0:T(1024)S(1)} %convert_element_type.189) | copy-start | bytes 24580
  315.9 166.4 %all-gather.38.cloned.1.call-start = ((), (), s32[]{:S(2)}) async-start(), calls=%async_computation.41 | async-start | bytes 6488064 | tf_op jit(solution)/shard_map/all_gather | solution.py:89
  316.6 284.6 %all-gather.28.cloned.1.call-start = ((), (), s32[]{:S(2)}) async-start(), calls=%async_computation.26 | async-start | bytes 25952256 | tf_op jit(solution)/shard_map/all_gather | solution.py:77
  318.6 5.5 copy-start.4
  318.6 353.0 %all-gather.30.cloned.1.call-start = ((), (), s32[]{:S(2)}) async-start(), calls=%async_computation.27 | async-start | bytes 12976128 | tf_op jit(solution)/shard_map/all_gather | solution.py:89
  327.5 162.4 %all-to-all-start = ((bf16[8,89,2048]{2,1,0:T(8,128)(2,1)}), bf16[8,89,2048]{2,1,0:T(8,128)(2,1)}, u32[]{:S(2)}, u32[]{:S(2)}) async-start(bf16[8,89,2048]{2,1,0:T(8,128)(2,1)} %reshape.345), calls=%async_computation.2 | async-start | bytes 6291456 | tf_op jit(solution)/shard_map/all_to_all | solution.py:61
  332.2 555.9 %reduce-scatter.21.cloned.1.call-start = ((), (), s32[]{:S(2)}) async-start(), calls=%async_computation.25 | async-start | bytes 5242880 | tf_op jit(solution)/shard_map/reduce_scatter | solution.py:57
  451.5 38.3 %copy-start.34 = (bf16[512,1408]{1,0:T(8,128)(2,1)}, bf16[512,1408]{1,0:T(8,128)(2,1)S(1)}, u32[]{:S(2)}) copy-start(bf16[512,1408]{1,0:T(8,128)(2,1)S(1)} %fusion.24) | copy-start | bytes 4325380
  495.2 120.4 %copy-start.20 = (bf16[4,2,89,2048]{3,1,2,0:T(2,128)(2,1)}, bf16[4,2,89,2048]{3,1,2,0:T(2,128)(2,1)S(1)}, u32[]{:S(2)}) copy-start(bf16[4,2,89,2048]{3,1,2,0:T(2,128)(2,1)S(1)} %copy.164) | copy-start | bytes 8749060
  685.9 10.1 copy-start.62
  685.9 182.2 %all-to-all-start.1 = ((bf16[2,356,2048]{2,0,1:T(2,128)(2,1)}), bf16[2,356,2048]{2,0,1:T(2,128)(2,1)S(1)}, u32[]{:S(2)}, u32[]{:S(2)}) async-start(bf16[2,356,2048]{2,0,1:T(2,128)(2,1)} %copy.168), calls=%async_computation.3 | async-start | bytes 5832704 | tf_op jit(solution)/shard_map/all_to_all | solution.py:65
  690.3 281.2 %all-gather.32.cloned.1.call-start = ((), (), s32[]{:S(2)}) async-start(), calls=%async_computation.28 | async-start | bytes 2621440 | tf_op jit(solution)/shard_map/all_gather | solution.py:53
  882.3 5.8 copy-start.3
  899.5 119.3 %all-to-all-start.2 = ((bf16[8,89,2048]{2,1,0:T(8,128)(2,1)}), bf16[8,89,2048]{2,1,0:T(8,128)(2,1)}, u32[]{:S(2)}, u32[]{:S(2)}) async-start(bf16[8,89,2048]{2,1,0:T(8,128)(2,1)} %reshape.347), calls=%async_computation.5 | async-start | bytes 6291456 | tf_op jit(solution)/shard_map/all_to_all | solution.py:61
  904.3 241.1 %reduce-scatter.23.cloned.1.call-start = ((), (), s32[]{:S(2)}) async-start(), calls=%async_computation.29 | async-start | bytes 5242880 | tf_op jit(solution)/shard_map/reduce_scatter | solution.py:57
  1023.7 14.6 copy-start.22
  1059.8 4.8 copy-start.54
  1059.8 76.3 %all-to-all-start.3 = ((bf16[2,356,2048]{2,0,1:T(2,128)(2,1)}), bf16[2,356,2048]{2,0,1:T(2,128)(2,1)}, u32[]{:S(2)}, u32[]{:S(2)}) async-start(bf16[2,356,2048]{2,0,1:T(2,128)(2,1)} %copy.174), calls=%async_computation.6 | async-start | bytes 5832704 | tf_op jit(solution)/shard_map/all_to_all | solution.py:65
  1064.6 132.4 %all-gather.34.cloned.1.call-start = ((), (), s32[]{:S(2)}) async-start(), calls=%async_computation.30 | async-start | bytes 2621440 | tf_op jit(solution)/shard_map/all_gather | solution.py:53
  1140.9 6.4 copy-start.33
  1140.9 6.4 copy-start.47
  1140.9 6.4 copy-start.60
  1151.6 84.8 %reduce-scatter.27.cloned.1.call-start = ((), (), s32[]{:S(2)}) async-start(), calls=%async_computation.32 | async-start | bytes 3145728 | tf_op jit(solution)/shard_map/reduce_scatter | solution.py:381
  1152.1 50.8 %copy-start.19 = (pred[4,128,256]{2,1,0:T(8,128)(4,1)S(1)}, pred[4,128,256]{2,1,0:T(8,128)(4,1)}, u32[]{:S(2)}) copy-start(pred[4,128,256]{2,1,0:T(8,128)(4,1)} %copy-done.18) | copy-start | bytes 393220
  1197.0 5.9 copy-start.1
  1205.7 65.2 %reduce-scatter.25.cloned.1.call-start = ((), (), s32[]{:S(2)}) async-start(), calls=%async_computation.31 | async-start | bytes 3145728 | tf_op jit(solution)/shard_map/reduce_scatter | solution.py:380
  1205.8 4.5 copy-start.12
  1212.1 191.5 %reduce-scatter.43.cloned.1.call-start = ((), (), s32[]{:S(2)}) async-start(), calls=%async_computation.42 | async-start | bytes 1081344
  1213.9 254.6 %reduce-scatter.37.cloned.1.call-start = ((), (), s32[]{:S(2)}) async-start(), calls=%async_computation.37 | async-start | bytes 6488064 | tf_op jit(solution)/shard_map/reduce_scatter | solution.py:102
  1221.5 5.5 copy-start.41
  1221.5 291.7 %reduce-scatter.33.cloned.1.call-start = ((), (), s32[]{:S(2)}) async-start(), calls=%async_computation.35 | async-start | bytes 2359296 | tf_op jit(solution)/shard_map/reduce_scatter | solution.py:102
  1226.8 419.7 %reduce-scatter.45.cloned.1.call-start = ((), (), s32[]{:S(2)}) async-start(), calls=%async_computation.43 | async-start | bytes 1081344
  1231.9 39.0 %copy-start.39 = (f32[128,128]{0,1:T(8,128)S(1)}, f32[128,128]{0,1:T(8,128)}, u32[]{:S(2)}) copy-start(f32[128,128]{0,1:T(8,128)} %copy-done.38) | copy-start | bytes 196612
  1232.5 47.0 %copy-start.28 = (bf16[1,512,512]{2,1,0:T(8,128)(2,1)}, bf16[1,512,512]{2,1,0:T(8,128)(2,1)S(1)}, u32[]{:S(2)}) copy-start(bf16[1,512,512]{2,1,0:T(8,128)(2,1)S(1)} %stack_reshape.9) | copy-start | bytes 1572868
  1281.9 457.1 %reduce-scatter.35.cloned.1.call-start = ((), (), s32[]{:S(2)}) async-start(), calls=%async_computation.36 | async-start | bytes 12976128 | tf_op jit(solution)/shard_map/reduce_scatter | solution.py:102
  1292.6 537.2 %reduce-scatter.41.cloned.1.call-start = ((), (), s32[]{:S(2)}) async-start(), calls=%async_computation.39 | async-start | bytes 12976128 | tf_op jit(solution)/shard_map/reduce_scatter | solution.py:102
  1305.3 603.4 %reduce-scatter.29.cloned.1.call-start = ((), (), s32[]{:S(2)}) async-start(), calls=%async_computation.33 | async-start | bytes 5242880 | tf_op jit(solution)/shard_map/reduce_scatter | solution.py:57
  1314.5 660.5 %reduce-scatter.31.cloned.1.call-start = ((), (), s32[]{:S(2)}) async-start(), calls=%async_computation.34 | async-start | bytes 7077888 | tf_op jit(solution)/shard_map/reduce_scatter | solution.py:102
  1321.6 803.3 %reduce-scatter.39.cloned.1.call-start = ((), (), s32[]{:S(2)}) async-start(), calls=%async_computation.38 | async-start | bytes 25952256 | tf_op jit(solution)/shard_map/reduce_scatter | solution.py:102
  1743.5 165.3 %copy-start.6 = (bf16[1,128,2048]{2,1,0:T(8,128)(2,1)S(1)}, bf16[1,128,2048]{2,1,0:T(8,128)(2,1)}, u32[]{:S(2)}) copy-start(bf16[1,128,2048]{2,1,0:T(8,128)(2,1)} %param.15) | copy-start | bytes 1572868
  1743.5 165.3 %copy-start.45 = (f32[2048]{0:T(1024)S(1)}, f32[2048]{0:T(1024)}, u32[]{:S(2)}) copy-start(f32[2048]{0:T(1024)} %copy-done.44) | copy-start | bytes 24580
  1743.5 165.3 %copy-start.58 = (f32[128]{0:T(128)S(1)}, f32[128]{0:T(128)}, u32[]{:S(2)}) copy-start(f32[128]{0:T(128)} %copy-done.57) | copy-start | bytes 1540
  1743.5 209.9 %copy-start.15 = (f32[128,2048]{1,0:T(8,128)S(1)}, f32[128,2048]{1,0:T(8,128)}, u32[]{:S(2)}) copy-start(f32[128,2048]{1,0:T(8,128)} %get-tuple-element.81) | copy-start | bytes 3145732
  1743.5 209.9 %copy-start.63 = (f32[128]{0:T(128)S(1)}, f32[128]{0:T(128)}, u32[]{:S(2)}) copy-start(f32[128]{0:T(128)} %get-tuple-element.110) | copy-start | bytes 1540
  (35 other events, 74.7 us)
Sparse Core Ops, SparseCore 0:
  54.5 46.5 all-gather.15
  103.0 44.6 all-gather.17
  156.7 20.8 all-gather.21
  179.6 21.2 all-gather.19
  202.6 28.3 all-gather.35
  236.0 76.3 reduce-scatter.18
  315.1 68.5 all-gather.25
  385.9 52.0 all-gather.23
  440.0 42.1 all-gather.37
  484.7 116.4 all-gather.27
  603.9 67.6 all-gather.29
  673.9 122.5 reduce-scatter.20
  892.1 79.4 all-gather.31
  992.8 103.6 reduce-scatter.22
  1151.7 45.2 all-gather.33
  1205.9 30.5 reduce-scatter.26
  1239.1 31.8 reduce-scatter.24
  1273.1 130.4 reduce-scatter.42
  1407.6 60.7 reduce-scatter.36
  1472.0 41.2 reduce-scatter.32
  1516.0 130.4 reduce-scatter.44
  1650.4 88.5 reduce-scatter.34
  1742.9 86.7 reduce-scatter.40
  1832.0 76.7 reduce-scatter.28
  1912.2 62.8 reduce-scatter.30
  1978.9 145.9 reduce-scatter.38
where the time goes:
time: 2150 us; the launch traced here: 2140 us
  waiting for transfers between devices  1470 us (68%)
  blocking collectives  252 us (12%)
  matrix products  196 us (9%)
  local copies, waits for them, and re-layouts  129 us (6%)
  other arithmetic  54.3 us (3%)
    reduce_scatter x6, waiting for transfers between devices, weight_grads(): lax.psum_scatter(partial_value(jnp.int32(0), row_count * lax.axis_size(('...  449 us
    all_gather x4, waiting for transfers between devices, gather_rows(): return lax.all_gather(values, 'exp', axis=0, tiled=True)  211 us
    all_gather x3, waiting for transfers between devices, project_in(): return accumulate(lax.all_gather(weight, ('dp', 'ctx'), axis=0, tiled=True))  204 us
    unnamed x28, waiting for transfers between devices  195 us
    all_gather x1, blocking collectives, body(): lax.all_gather(router_weight, ('dp', 'ctx', 'exp'), axis=0, tiled=True)  170 us
    reduce_scatter x4, waiting for transfers between devices, sum_rows(): lax.psum_scatter(partial_value, 'exp', scatter_dimension=0, tiled=True)  148 us
    all_gather x3, waiting for transfers between devices, project_out(): return produce(lax.all_gather(weight, ('dp', 'ctx'), axis=0, tiled=True))  106 us
    unnamed x2, blocking collectives  82.1 us
  transfers between devices with their start and end apart: 30, of which 26 were waited for; matrix products, arithmetic and copies ran while one was open for 15% of the time, Pallas kernels for 0%

commit v1 on v0

v1 whole, which is shorter than its diff:
```python
import functools

import jax
import jax.numpy as jnp
from jax import lax
from jax.experimental import pallas as pl
from jax.experimental.pallas import tpu as pltpu
from jax.sharding import PartitionSpec as P

HD = 128
EPSILON = 1e-06
ROPE_BASE = 1000000.0
NEGATIVE = -1e30
HIGHEST = lax.Precision.HIGHEST
BF = jnp.bfloat16
F32 = jnp.float32


def core_swap(v):
    n = lax.axis_size("dp")
    return lax.ppermute(v, "dp", [(i, i ^ 1) for i in range(n)])


def y_swap(v):
    n = lax.axis_size("dp")
    return lax.ppermute(v, "dp", [(i, i ^ 2) for i in range(n)])


def shift(v, axis, s):
    n = lax.axis_size(axis)
    return lax.ppermute(v, axis, [(i, (i + s) % n) for i in range(n)])


def after(values, anchors):
    return lax.optimization_barrier((tuple(values), tuple(anchors)))[0]


def gather_shards(v):
    nz = lax.axis_size("exp")
    mine = [v] + [shift(v, "exp", s) for s in range(1, nz)]
    return mine + [core_swap(m) for m in mine]


def gather_rows(v):
    return jnp.concatenate(gather_shards(v), axis=0)


def home_sum(keep, away):
    nz = lax.axis_size("exp")
    rows = keep.shape[0] // nz
    both = (keep.astype(F32) + core_swap(away).astype(F32)).astype(keep.dtype)
    parts = [both[s * rows : (s + 1) * rows] for s in range(nz)]
    total = parts[0].astype(F32)
    for s in range(1, nz):
        total = total + shift(parts[s], "exp", -s).astype(F32)
    return total


def sum_everywhere(v):
    v = v + core_swap(v)
    v = v + y_swap(v)
    for axis in ("ctx", "exp"):
        v = functools.reduce(
            jnp.add, [v] + [shift(v, axis, s) for s in range(1, lax.axis_size(axis))]
        )
    return v


def gather_weight(mine, other, anchors):
    n = lax.axis_size("ctx")
    x, c, y = lax.axis_index("ctx"), lax.axis_index("dp") % 2, lax.axis_index("dp") // 2
    a, b = mine, core_swap(other)
    if anchors:
        a, b = after((a, b), anchors)
    ax = [a] + [shift(a, "ctx", s) for s in range(1, n)]
    by = y_swap(b)
    ay = [y_swap(v) for v in ax]
    bx = [b] + [shift(b, "ctx", s) for s in range(1, n)]
    bxy = [by] + [shift(by, "ctx", s) for s in range(1, n)]
    rows, cols = mine.shape
    out = jnp.zeros((2, 2, n, rows, cols), mine.dtype)
    zero = jnp.int32(0)

    def put(buffer, block, yy, cc, xx):
        return lax.dynamic_update_slice(buffer, block[None, None, None], (yy, cc, xx, zero, zero))

    for s in range(n):
        xs = lax.rem(x + n - s, n)
        out = put(out, ax[s], y, c, xs)
        out = put(out, bx[s], y, 1 - c, xs)
    for s in range(n):
        xs = lax.rem(x + n - s, n)
        out = put(out, ay[s], 1 - y, c, xs)
        out = put(out, bxy[s], 1 - y, 1 - c, xs)
    return out.reshape(4 * n * rows, cols), (ax[-1], by)


def scatter_grad(grad):
    n = lax.axis_size("ctx")
    x, c, y = lax.axis_index("ctx"), lax.axis_index("dp") % 2, lax.axis_index("dp") // 2
    rows = grad.shape[0] // (4 * n)
    blocks = grad.reshape(2, 2, n, rows, grad.shape[1])

    def block(yy, cc, xx):
        return lax.dynamic_slice(
            blocks, (yy, cc, xx, 0, 0), (1, 1, 1, rows, grad.shape[1])
        ).reshape(rows, grad.shape[1])

    def line(yy, cc):
        return lax.dynamic_slice(
            blocks, (yy, cc, 0, 0, 0), (1, 1, n, rows, grad.shape[1])
        ).reshape(n, rows, grad.shape[1])

    def add(*terms):
        return functools.reduce(jnp.add, [t.astype(F32) for t in terms])

    got = y_swap(line(1 - y, c))
    mine = None
    for s in range(n):
        xs = lax.rem(x + n - s, n)
        both = add(
            block(y, c, xs), lax.dynamic_index_in_dim(got, xs, 0, keepdims=False)
        )
        mine = both if s == 0 else mine + shift(both.astype(BF), "ctx", -s).astype(F32)
    away = stay = None
    for s in range(n):
        xs = lax.rem(x + n - s, n)
        far, near = block(1 - y, 1 - c, xs), block(y, 1 - c, xs)
        if s:
            far, near = shift(far, "ctx", -s), shift(near, "ctx", -s)
        away = far.astype(F32) if s == 0 else away + far.astype(F32)
        stay = near.astype(F32) if s == 0 else stay + near.astype(F32)
    theirs = stay + y_swap(away.astype(BF)).astype(F32)
    return mine, core_swap(theirs.astype(BF)).astype(F32)


def turn(v):
    lane = lax.broadcasted_iota(jnp.int32, v.shape, 1)
    rolled = pltpu.roll(v, HD // 2, 1)
    return jnp.where(lane < HD // 2, -rolled, rolled)


def qkv_kernel(rows_ref, weight_ref, bias_ref, cos_ref, sin_ref, q_ref, kv_ref):
    width = q_ref.shape[1]
    cos, sin = cos_ref[...], sin_ref[...]
    tokens = cos.shape[0]
    projected = (
        jnp.dot(rows_ref[...], weight_ref[...], preferred_element_type=F32) + bias_ref[...]
    )
    for t in range(projected.shape[0] // tokens):
        for h in range(2 * width // HD):
            piece = projected[t * tokens : (t + 1) * tokens, h * HD : (h + 1) * HD]
            out = (piece * cos + turn(piece) * sin).astype(BF)
            at = h * HD
            if at < width:
                q_ref[t * tokens : (t + 1) * tokens, at : at + HD] = out
            else:
                kv_ref[t * tokens : (t + 1) * tokens, at - width : at - width + HD] = out
    kv_ref[:, width:] = projected[:, 2 * width :].astype(BF)


def qkv_call(rows, weight, bias, cos, sin, width):
    total, depth = rows.shape
    tile = min(total, 4 * cos.shape[0])
    return pl.pallas_call(
        qkv_kernel,
        grid=(total // tile,),
        in_specs=[
            pl.BlockSpec((tile, depth), lambda i: (i, 0)),
            pl.BlockSpec((depth, 3 * width), lambda i: (0, 0)),
            pl.BlockSpec((1, 3 * width), lambda i: (0, 0)),
            pl.BlockSpec(cos.shape, lambda i: (0, 0)),
            pl.BlockSpec(sin.shape, lambda i: (0, 0)),
        ],
        out_specs=[
            pl.BlockSpec((tile, width), lambda i: (i, 0)),
            pl.BlockSpec((tile, 2 * width), lambda i: (i, 0)),
        ],
        out_shape=[
            jax.ShapeDtypeStruct((total, width), BF),
            jax.ShapeDtypeStruct((total, 2 * width), BF),
        ],
        cost_estimate=pl.CostEstimate(
            flops=2 * total * depth * 3 * width,
            transcendentals=0,
            bytes_accessed=2 * (total * depth + depth * 3 * width + total * 3 * width),
        ),
        name="qkv_rope",
    )(rows, weight, bias, cos, sin)


def probabilities(query, keys, length, x, scale):
    tokens, count = query.shape[0], keys.shape[0]
    scores = (
        lax.dot_general(query, keys, (((1,), (1,)), ((), ())), preferred_element_type=F32) * scale
    )
    row = lax.broadcasted_iota(jnp.int32, (tokens, count), 0) + x * tokens
    col = lax.broadcasted_iota(jnp.int32, (tokens, count), 1)
    place = jnp.zeros((tokens, count), jnp.int32)
    for s in range(count // tokens):
        inside = (col >= s * tokens) & (col < (s + 1) * tokens)
        place = jnp.where(inside, col - s * tokens + (x - s) * tokens, place)
    allowed = (place >= 0) & (place <= row) & (place < length)
    masked = jnp.where(allowed, scores, NEGATIVE)
    top = jnp.max(masked, axis=1, keepdims=True)
    weights = jnp.where(allowed, jnp.exp(masked - top), 0.0)
    return weights / jnp.sum(weights, axis=1, keepdims=True)


def attend_kernel(scale, info_ref, q_ref, *refs):
    kv_refs, out_ref = refs[:-1], refs[-1]
    group = pl.program_id(0)
    width = q_ref.shape[1]
    for h in range(width // HD):
        at = h * HD
        keys = jnp.concatenate([r[:, at : at + HD] for r in kv_refs], axis=0)
        values = jnp.concatenate([r[:, width + at : width + at + HD] for r in kv_refs], axis=0)
        prob = probabilities(
            q_ref[:, at : at + HD], keys, info_ref[group], info_ref[pl.num_programs(0)], scale
        )
        out_ref[:, at : at + HD] = jnp.dot(
            prob.astype(BF), values, preferred_element_type=F32
        ).astype(BF)


def attend_call(info, query, kvs, tokens, scale):
    total, width = query.shape
    groups = total // tokens
    return pl.pallas_call(
        functools.partial(attend_kernel, scale),
        grid_spec=pltpu.PrefetchScalarGridSpec(
            num_scalar_prefetch=1,
            grid=(groups,),
            in_specs=[pl.BlockSpec((tokens, width), lambda i, info: (i, 0))]
            + [pl.BlockSpec((tokens, 2 * width), lambda i, info: (i, 0)) for _ in kvs],
            out_specs=pl.BlockSpec((tokens, width), lambda i, info: (i, 0)),
        ),
        out_shape=jax.ShapeDtypeStruct((total, width), BF),
        cost_estimate=pl.CostEstimate(
            flops=4 * total * width * tokens * len(kvs),
            transcendentals=total * tokens * len(kvs) * width // HD,
            bytes_accessed=2 * total * width * (2 + 2 * len(kvs)),
        ),
        name="attend",
    )(info, query, *kvs)


def unrope(grad, cos, sin):
    return grad * cos - turn(grad * sin)


def attend_back_kernel(scale, count, info_ref, q_ref, da_ref, *refs):
    kv_refs = refs[:count]
    cos_ref, sin_ref = refs[count : count + 2]
    dq_ref = refs[count + 2]
    dkv_refs = refs[count + 3 :]
    group = pl.program_id(0)
    tokens, width = q_ref.shape
    for h in range(width // HD):
        at = h * HD
        keys = jnp.concatenate([r[:, at : at + HD] for r in kv_refs], axis=0)
        values = jnp.concatenate([r[:, width + at : width + at + HD] for r in kv_refs], axis=0)
        query, grad = q_ref[:, at : at + HD], da_ref[:, at : at + HD]
        prob = probabilities(
            query, keys, info_ref[group], info_ref[pl.num_programs(0)], scale
        )
        dprob = lax.dot_general(
            grad, values, (((1,), (1,)), ((), ())), preferred_element_type=F32
        )
        row_dot = jnp.sum(prob * dprob, axis=1, keepdims=True)
        dscore = (prob * (dprob - row_dot)).astype(BF)
        dq = jnp.dot(dscore, keys, preferred_element_type=F32) * scale
        dq_ref[:, at : at + HD] = unrope(dq, cos_ref[:tokens], sin_ref[:tokens]).astype(BF)
        dk = (
            lax.dot_general(dscore, query, (((0,), (0,)), ((), ())), preferred_element_type=F32)
            * scale
        )
        dv = lax.dot_general(
            prob.astype(BF), grad, (((0,), (0,)), ((), ())), preferred_element_type=F32
        )
        for s in range(count):
            part = slice(s * tokens, (s + 1) * tokens)
            dkv_refs[s][:, at : at + HD] = unrope(dk[part], cos_ref[part], sin_ref[part]).astype(
                dkv_refs[s].dtype
            )
            dkv_refs[s][:, width + at : width + at + HD] = dv[part].astype(dkv_refs[s].dtype)


def attend_back_call(info, query, grad, kvs, cos, sin, tokens, scale):
    total, width = query.shape
    groups, count = total // tokens, len(kvs)
    one = pl.BlockSpec((tokens, width), lambda i, info: (i, 0))
    two = pl.BlockSpec((tokens, 2 * width), lambda i, info: (i, 0))
    table = pl.BlockSpec(cos.shape, lambda i, info: (0, 0))
    return pl.pallas_call(
        functools.partial(attend_back_kernel, scale, count),
        grid_spec=pltpu.PrefetchScalarGridSpec(
            num_scalar_prefetch=1,
            grid=(groups,),
            in_specs=[one, one] + [two] * count + [table, table],
            out_specs=[one] + [two] * count,
        ),
        out_shape=[jax.ShapeDtypeStruct((total, width), BF)]
        + [jax.ShapeDtypeStruct((total, 2 * width), F32 if s == 0 else BF) for s in range(count)],
        cost_estimate=pl.CostEstimate(
            flops=10 * total * width * tokens * count,
            transcendentals=total * tokens * count * width // HD,
            bytes_accessed=2 * total * width * (3 + 5 * count),
        ),
        name="attend_back",
    )(info, query, grad, *kvs, cos, sin)


def rope_tables(positions):
    frequency = ROPE_BASE ** (-jnp.arange(0, HD, 2, dtype=F32) / HD)
    angles = positions[:, None] * frequency[None, :]
    return (
        jnp.concatenate([jnp.cos(angles), jnp.cos(angles)], axis=1),
        jnp.concatenate([jnp.sin(angles), jnp.sin(angles)], axis=1),
    )


def dot_t(a, b):
    return lax.dot_general(a, b, (((1,), (1,)), ((), ())), preferred_element_type=F32)


def dot_rows(a, b):
    return lax.dot_general(a, b, (((0,), (0,)), ((), ())), preferred_element_type=F32)


def norm_scale(values):
    return lax.rsqrt(jnp.mean(values * values, axis=1, keepdims=True) + EPSILON)


def norm_back(values, scale, gain, grads):
    weighted = grads * gain
    grad_values = scale * weighted - values * scale**3 * jnp.mean(
        weighted * values, axis=1, keepdims=True
    )
    return grad_values, jnp.sum(grads * values * scale, axis=0)


def body(
    tokens,
    teacher,
    lengths,
    routes,
    attn_gain,
    ffn_gain,
    router_weight,
    shared_gate,
    qkv_weight,
    qkv_bias,
    out_weight,
    shared_up,
    shared_down,
    expert_up,
    expert_down,
):
    tok_rows, model_width = tokens.shape[1:]
    nz, n = lax.axis_size("exp"), lax.axis_size("ctx")
    z, x, dp = lax.axis_index("exp"), lax.axis_index("ctx"), lax.axis_index("dp")
    c = dp % 2
    devices = lax.axis_size(("dp", "ctx", "exp"))
    me = lax.axis_index(("dp", "ctx", "exp"))
    seq_len = tok_rows * n
    experts = router_weight.shape[1]
    own_expert = 2 * z + c
    rows_w = qkv_weight.shape[0]
    width = qkv_weight.shape[2] // 2
    units, shared = expert_down.shape[2], shared_down.shape[1] // 2
    score_scale = HD ** (-0.5)
    first = c == 0

    def halves(v, axis):
        size = v.shape[axis] // 2
        low = lax.slice_in_dim(v, 0, size, axis=axis)
        high = lax.slice_in_dim(v, size, 2 * size, axis=axis)
        return jnp.where(first, low, high), jnp.where(first, high, low)

    token_shards = gather_shards(tokens[0])

    piece = jnp.concatenate(
        [
            router_weight.T,
            attn_gain[None],
            ffn_gain[None],
            shared_gate[None],
        ],
        axis=0,
    )
    span = model_width // devices
    lane = lax.broadcasted_iota(jnp.int32, (experts + 3, model_width), 1)
    vectors = sum_everywhere(
        jnp.where(lane // span == me, jnp.tile(piece, (1, devices)), jnp.zeros((), BF))
    )
    router_t = vectors[:experts]
    attn_factor = vectors[experts].astype(F32)[None]
    ffn_factor = vectors[experts + 1].astype(F32)[None]
    gate_full = vectors[experts + 2]

    chosen = (
        routes[0][:, None, :] == jnp.arange(experts, dtype=jnp.int32)[None, :, None]
    ).any(axis=2)
    chosen_t = chosen.astype(BF).T
    chosen_mine = jnp.concatenate(
        [chosen_t[None]] + [shift(chosen_t, "exp", s)[None] for s in range(1, nz)], axis=0
    )
    chosen_all = jnp.concatenate([chosen_mine, core_swap(chosen_mine)], axis=0)
    routed_own = (
        lax.dynamic_index_in_dim(chosen_all, own_expert, 1, keepdims=False)
        .astype(F32)
        .reshape(-1, 1)
    )

    qkv_halves = halves(qkv_weight, 2)
    out_halves = halves(out_weight, 1)
    shared_halves = halves(shared_up, 2)
    down_halves = halves(shared_down, 1)
    expert_halves = [v[:, 0] for v in halves(expert_up, 1)]
    expert_down_halves = [v[:, 0] for v in halves(expert_down, 1)]
    attn_pair = [
        jnp.concatenate([q[:, 0], q[:, 1], q[:, 2], o], axis=1)
        for q, o in zip(qkv_halves, out_halves)
    ]
    gate_pair = [
        jnp.concatenate([e[:, :units], s[:, 0]], axis=1)
        for e, s in zip(expert_halves, shared_halves)
    ]
    up_pair = [
        jnp.concatenate([e[:, units:], s[:, 1]], axis=1)
        for e, s in zip(expert_halves, shared_halves)
    ]
    down_pair = [
        jnp.concatenate([e, s], axis=1) for e, s in zip(expert_down_halves, down_halves)
    ]
    attn_weight, marks = gather_weight(*attn_pair, ())
    gate_weight, marks = gather_weight(*gate_pair, marks)
    up_weight, marks = gather_weight(*up_pair, marks)
    down_weight, marks = gather_weight(*down_pair, marks)
    out_full = attn_weight[:, 3 * width :]

    count_valid = jnp.sum(lengths).astype(F32)
    factor = lengths.shape[0] * seq_len / count_valid
    positions = x * tok_rows + jnp.arange(tok_rows, dtype=jnp.int32)
    own_length = lengths[dp * nz + z]
    valid_rows = (positions < own_length).astype(F32)[:, None]
    shard_dp = jnp.repeat(jnp.stack([dp, dp ^ 1]), nz)
    shard_z = jnp.tile(lax.rem(z + nz - jnp.arange(nz, dtype=jnp.int32), nz), 2)
    info = jnp.concatenate([lengths[shard_dp * nz + shard_z], x[None].astype(jnp.int32)])
    key_places = jnp.concatenate([positions - s * tok_rows for s in range(n)])
    cos_all, sin_all = rope_tables(key_places.astype(F32))
    cos, sin = cos_all[:tok_rows], sin_all[:tok_rows]

    inputs = tokens[0].astype(F32)
    attn_scale = norm_scale(inputs)
    wide = jnp.concatenate(token_shards, axis=0).astype(F32)
    attn_rows = (wide * norm_scale(wide) * attn_factor).astype(BF)
    bias = jnp.where(first, qkv_bias[:, :width], qkv_bias[:, width:])
    query, kv = qkv_call(
        attn_rows, attn_weight, bias.astype(F32).reshape(1, 3 * width), cos, sin, width
    )
    kvs = [kv] + [
        lax.ppermute(kv, "ctx", [(i, i + s) for i in range(n - s)]) for s in range(1, n)
    ]
    attended = attend_call(info, query, kvs, tok_rows, score_scale)
    half = nz * tok_rows

    def project_home(parts, weights):
        away = sum(dot_t(p[half:], w) for p, w in zip(parts, weights)).astype(BF)
        keep = sum(dot_t(p[:half], w) for p, w in zip(parts, weights)).astype(BF)
        return home_sum(keep, away)

    hidden = inputs + project_home([attended], [out_full])

    ffn_scale = norm_scale(hidden)
    normed_ffn = (hidden * ffn_scale * ffn_factor).astype(BF)
    ffn_rows = gather_rows(normed_ffn)
    small = jnp.concatenate([router_t, gate_full[None]], axis=0)
    logits = dot_t(ffn_rows, small)
    probs_all = jax.nn.softmax(logits[:, :experts], axis=1)
    sig_all = jax.nn.sigmoid(logits[:, experts:])
    own_col = (jnp.arange(experts, dtype=jnp.int32) == own_expert).astype(F32)[None]
    gate_all = jnp.sum(probs_all * own_col, axis=1, keepdims=True) * routed_own
    is_expert = lax.broadcasted_iota(jnp.int32, (1, units + shared), 1) < units
    row_scale = jnp.where(is_expert, gate_all, sig_all)

    gate_pre = jnp.dot(ffn_rows, gate_weight, preferred_element_type=F32)
    up_pre = jnp.dot(ffn_rows, up_weight, preferred_element_type=F32)
    act = jax.nn.silu(gate_pre) * up_pre
    act_scaled = (act * row_scale).astype(BF)
    result = hidden + project_home([act_scaled], [down_weight])
    grad_result = factor * valid_rows * (result - teacher[0])

    back_rows = gather_rows(grad_result.astype(BF))
    grad_act = jnp.dot(back_rows, down_weight, preferred_element_type=F32)
    touched = act * grad_act
    grad_gate_all = jnp.sum(touched[:, :units], axis=1) * routed_own[:, 0]
    grad_sig_all = jnp.sum(touched[:, units:], axis=1)
    scaled = grad_act * row_scale
    sigmoid_gate = jax.nn.sigmoid(gate_pre)
    grad_gate_pre = (
        scaled * up_pre * sigmoid_gate * (1.0 + gate_pre * (1.0 - sigmoid_gate))
    ).astype(BF)
    grad_up_pre = (scaled * gate_pre * sigmoid_gate).astype(BF)
    scalar_rows = jnp.concatenate(
        [own_col.T * grad_gate_all[None], grad_sig_all[None]], axis=0
    ).reshape(experts + 1, 2, nz, tok_rows)
    scalar_both = scalar_rows[:, 0] + core_swap(scalar_rows[:, 1])
    scalar_own = scalar_both[:, 0]
    for s in range(1, nz):
        scalar_own = scalar_own + shift(scalar_both[:, s], "exp", -s)

    grad_normed = project_home([grad_gate_pre, grad_up_pre], [gate_weight, up_weight])
    grad_down = scatter_grad(dot_rows(back_rows, act_scaled).astype(BF))
    grad_gate = scatter_grad(dot_rows(ffn_rows, grad_gate_pre).astype(BF))
    grad_up = scatter_grad(dot_rows(ffn_rows, grad_up_pre).astype(BF))

    own_logits = dot_t(normed_ffn, small)
    probs = jax.nn.softmax(own_logits[:, :experts], axis=1)
    sig = jax.nn.sigmoid(own_logits[:, experts])
    grad_probs = scalar_own[:experts].T
    grad_logits = probs * (grad_probs - jnp.sum(probs * grad_probs, axis=1, keepdims=True))
    grad_sig = scalar_own[experts] * sig * (1.0 - sig)
    grad_small = jnp.concatenate([grad_logits, grad_sig[:, None]], axis=1)
    normed_wide = normed_ffn.astype(F32)
    grad_small_full = lax.dot_general(
        grad_small, normed_wide, (((0,), (0,)), ((), ())), precision=HIGHEST
    )
    grad_normed = grad_normed + jnp.dot(grad_small, small.astype(F32), precision=HIGHEST)
    grad_hidden_norm, grad_ffn_full = norm_back(hidden, ffn_scale, ffn_factor, grad_normed)
    grad_hidden = grad_result + grad_hidden_norm
    ffn_vectors = sum_everywhere(jnp.concatenate([grad_small_full, grad_ffn_full[None]], axis=0))

    attn_back = gather_rows(grad_hidden.astype(BF))
    grad_attended = jnp.dot(attn_back, out_full, preferred_element_type=F32).astype(BF)
    grad_query, grad_kv, *sent = attend_back_call(
        info, query, grad_attended, kvs, cos_all, sin_all, tok_rows, score_scale
    )
    for s, other in enumerate(sent, start=1):
        grad_kv = grad_kv + lax.ppermute(
            other, "ctx", [(i + s, i) for i in range(n - s)]
        ).astype(F32)
    grad_projected = jnp.concatenate([grad_query, grad_kv.astype(BF)], axis=1)
    grad_normed_attn = project_home([grad_projected], [attn_weight[:, : 3 * width]])
    grad_attn = scatter_grad(
        jnp.concatenate(
            [dot_rows(attn_rows, grad_projected), dot_rows(attn_back, attended)], axis=1
        ).astype(BF)
    )
    bias_own = jnp.sum(grad_projected.astype(F32), axis=0).reshape(3, width)
    blocks = model_width // width
    column = lax.broadcasted_iota(jnp.int32, (3, model_width), 1)
    bias_wide = jnp.where(column // width == own_expert, jnp.tile(bias_own, (1, blocks)), 0.0)
    grad_inputs_norm, grad_attn_full = norm_back(inputs, attn_scale, attn_factor, grad_normed_attn)
    grad_tokens = (grad_hidden + grad_inputs_norm)[None]
    attn_vectors = sum_everywhere(jnp.concatenate([bias_wide, grad_attn_full[None]], axis=0))

    def join(pair, axis):
        mine, theirs = pair
        return jnp.concatenate(
            [jnp.where(first, mine, theirs), jnp.where(first, theirs, mine)], axis=axis
        )

    def own_span(v):
        return lax.dynamic_slice_in_dim(v, me * span, span, 1)

    grad_qkv = join([g[:, : 3 * width].reshape(rows_w, 3, width) for g in grad_attn], 2)
    grad_out = join([g[:, 3 * width :] for g in grad_attn], 1)
    grad_expert_up = join(
        [
            jnp.concatenate([g[:, :units], u[:, :units]], axis=1)[:, None]
            for g, u in zip(grad_gate, grad_up)
        ],
        1,
    )
    grad_shared_up = join(
        [
            jnp.concatenate([g[:, None, units:], u[:, None, units:]], axis=1)
            for g, u in zip(grad_gate, grad_up)
        ],
        2,
    )
    grad_expert_down = join([g[:, None, :units] for g in grad_down], 1)
    grad_shared_down = join([g[:, units:] for g in grad_down], 1)
    ffn_own, attn_own = own_span(ffn_vectors), own_span(attn_vectors)
    return (
        result.astype(BF)[None],
        grad_tokens,
        attn_own[3],
        ffn_own[experts + 1],
        ffn_own[:experts].T,
        ffn_own[experts],
        grad_qkv,
        jnp.stack([attn_own[0], attn_own[2]]),
        attn_own[1],
        grad_out,
        grad_shared_up,
        grad_shared_down,
        grad_expert_up,
        grad_expert_down,
    )


def solution(mesh):
    every = ("dp", "ctx", "exp")
    return jax.shard_map(
        body,
        mesh=mesh,
        in_specs=(
            P(("dp", "exp"), "ctx", None),
            P(("dp", "exp"), "ctx", None),
            P(),
            P(("dp", "exp"), "ctx", None),
            P(every),
            P(every),
            P(every, None),
            P(every),
            P(("dp", "ctx"), None, "exp"),
            P(None, "exp"),
            P(("dp", "ctx"), "exp"),
            P(("dp", "ctx"), None, "exp"),
            P(("dp", "ctx"), "exp"),
            P(("dp", "ctx"), "exp", None),
            P(("dp", "ctx"), "exp", None),
        ),
        out_specs=(
            P(("dp", "exp"), "ctx", None),
            P(("dp", "exp"), "ctx", None),
            P(every),
            P(every),
            P(every, None),
            P(every),
            P(("dp", "ctx"), None, "exp"),
            P(None, every),
            P(every),
            P(("dp", "ctx"), "exp"),
            P(("dp", "ctx"), None, "exp"),
            P(("dp", "ctx"), "exp"),
            P(("dp", "ctx"), "exp", None),
            P(("dp", "ctx"), "exp", None),
        ),
        check_vma=False,
    )
```

time: 2150 us -> 1560 us (0.73)
  waiting for transfers between devices: 1470 us -> 596 us
  local copies, waits for them, and re-layouts: 129 us -> 387 us
  blocking collectives: 252 us -> 0 us
  starting transfers between devices: 20.5 us -> 245 us
  other arithmetic: 54.3 us -> 96.3 us
  Pallas kernels: 0 us -> 29.2 us
    reduce_scatter x12 -> x0, waiting for transfers between devices: 633 us -> none  [the longest x6 449 us: weight_grads(): lax.psum_scatter(partial_value(jnp.int32(0), row_count * lax.axis_size(('...]
    ppermute x0 -> x124, waiting for transfers between devices: none -> 596 us  [the longest x66 422 us: shift(): return lax.ppermute(v, axis, [(i, (i + s) % n) for i in range(n)])]
    all_gather x12 -> x0, waiting for transfers between devices: 551 us -> none  [the longest x4 211 us: gather_rows(): return lax.all_gather(values, 'exp', axis=0, tiled=True)]
    ppermute x0 -> x124, starting transfers between devices: none -> 245 us  [the longest x66 142 us: shift(): return lax.ppermute(v, axis, [(i, (i + s) % n) for i in range(n)])]
    unnamed x28 -> x0, waiting for transfers between devices: 195 us -> none
    all_gather x1 -> x0, blocking collectives: 170 us -> none  [body(): lax.all_gather(router_weight, ('dp', 'ctx', 'exp'), axis=0, tiled=True)]
    all_to_all x4 -> x0, waiting for transfers between devices: 93.1 us -> none  [the longest x2 66.9 us: send_home(): lax.all_to_all(buffer, 'exp', split_axis=1, concat_axis=0, tiled=True)]
    unnamed x2 -> x0, blocking collectives: 82.1 us -> none
  transfers between devices with their start and end apart: 30 -> 124, of which waited for: 26 -> 46; matrix products, arithmetic and copies ran while one was open for 15% -> 30% of each run, Pallas kernels for 0% -> 1%
where the time goes in v1:
time: 1560 us; the launch traced here: 1540 us
  waiting for transfers between devices  596 us (38%)
  local copies, waits for them, and re-layouts  387 us (25%)
  starting transfers between devices  245 us (16%)
  matrix products  182 us (12%)
  other arithmetic  96.3 us (6%)
  Pallas kernels  29.2 us (2%)
    ppermute x66, waiting for transfers between devices, shift(): return lax.ppermute(v, axis, [(i, (i + s) % n) for i in range(n)])  422 us
    ppermute x23, waiting for transfers between devices, y_swap(): return lax.ppermute(v, 'dp', [(i, i ^ 2) for i in range(n)])  155 us
    ppermute x66, starting transfers between devices, shift(): return lax.ppermute(v, axis, [(i, (i + s) % n) for i in range(n)])  142 us
    unnamed x354, local copies, waits for them, and re-layouts  100 us
    ppermute x33, starting transfers between devices, core_swap(): return lax.ppermute(v, 'dp', [(i, i ^ 1) for i in range(n)])  76.1 us
    dot_general x12, matrix products, dot_t(): lax.dot_general(a, b, (((1,), (1,)), ((), ())), preferred_element_type=F32)  75.2 us
    reshape x3, local copies, waits for them, and re-layouts, scatter_grad(): blocks = grad.reshape(2, 2, n, rows, grad.shape[1])  60.4 us
    broadcast_in_dim x29, local copies, waits for them, and re-layouts, put(): block[None, None, None]  53.2 us
  transfers between devices with their start and end apart: 124, of which 46 were waited for; matrix products, arithmetic and copies ran while one was open for 30% of the time, Pallas kernels for 1%

profile of v1, /device:TPU:1, one launch (start us, length us, event | category | flops | bytes accessed | tf_op | source)
XLA Modules:
  0.0 1539.5 jit_solution(6889891211708840041)
XLA Ops:
  76.8 6.6 collective-permute-done
  83.5 9.4 collective-permute-start.3
  94.7 15.5 %collective-permute-done.1 = bf16[128,2048]{1,0:T(8,128)(2,1)} collective-permute-done((bf16[128,2048]{1,0:T(8,128)(2,1)S(1)}, bf16[128,2048]{1,0:T(8,128)(2,1)}, u32[]{:S(2)}, u32[]{:S(2)}) %collective-permute-start.1) | collective-permute-done | bytes 524320 | tf_op jit(solution)/shard_map/ppermute | solution.py:31
  130.9 6.1 collective-permute-done.18
  176.6 7.1 qkv_rope.1
  185.4 26.0 %collective-permute-done.33 = bf16[256,2112]{0,1:T(8,128)(2,1)S(1)} collective-permute-done((bf16[256,2112]{0,1:T(8,128)(2,1)}, bf16[256,2112]{0,1:T(8,128)(2,1)S(1)}, u32[]{:S(2)}, u32[]{:S(2)}) %collective-permute-start.33) | collective-permute-done | bytes 1081376 | tf_op jit(solution)/shard_map/ppermute | solution.py:31
  242.4 9.5 attend.1
  251.9 30.7 %collective-permute-done.40 = bf16[256,2112]{0,1:T(8,128)(2,1)} collective-permute-done((bf16[256,2112]{0,1:T(8,128)(2,1)}, bf16[256,2112]{0,1:T(8,128)(2,1)}, u32[]{:S(2)}, u32[]{:S(2)}) %collective-permute-start.40) | collective-permute-done | bytes 1081376 | tf_op jit(solution)/shard_map/ppermute | solution.py:31
  297.5 8.3 collective-permute-done.38
  330.3 21.8 %collective-permute-done.51 = bf16[256,2112]{0,1:T(8,128)(2,1)} collective-permute-done((bf16[256,2112]{0,1:T(8,128)(2,1)}, bf16[256,2112]{0,1:T(8,128)(2,1)}, u32[]{:S(2)}, u32[]{:S(2)}) %collective-permute-start.51) | collective-permute-done | bytes 1081376 | tf_op jit(solution)/shard_map/ppermute | solution.py:31
  365.6 9.4 collective-permute-done.44
  385.2 6.2 collective-permute-start.24
  404.0 25.5 %collective-permute-done.23 = bf16[128,2048]{1,0:T(8,128)(2,1)S(1)} collective-permute-done((bf16[128,2048]{1,0:T(8,128)(2,1)}, bf16[128,2048]{1,0:T(8,128)(2,1)S(1)}, u32[]{:S(2)}, u32[]{:S(2)}) %collective-permute-start.23) | collective-permute-done | bytes 524320 | tf_op jit(solution)/shard_map/ppermute | solution.py:31
  433.9 10.8 collective-permute-start.25
  459.8 15.4 collective-permute-done.26
  488.3 14.5 fusion.133
  503.0 20.0 %fusion = (bf16[1024,2112]{0,1:T(8,128)(2,1)}, f32[1024,2112]{0,1:T(8,128)}) fusion(f32[1024]{0:T(1024)S(1)} %bitcast.395, f32[1024]{0:T(1024)S(1)} %mul.318, pred[2112]{0:T(1024)(128)(4,1)S(1)} %copy-done.130, f32[1024,2112]{0,1:T(8,128)} %fusion.133, bf16[1024,2048]{1,0:T(8,128)(2,1)} %constant_dynamic-update-slice_fusion.8, bf16[2048,2112]{1,0:T(8,128)(2,1)} %bitcast.355), kind=kOutput, calls=%fused_computation.15 | convolution fusion | flops 8875671552 | bytes 34482240 | tf_op jit(solution)/shard_map/dot_general | solution.py:489
  523.0 9.3 convolution_convert_fusion.8
  537.6 8.7 add_convert_fusion.4
  546.4 13.6 collective-permute-start.60
  564.3 11.1 collective-permute-done.60
  575.3 22.6 %collective-permute-done.59 = bf16[128,2048]{1,0:T(8,128)(2,1)S(1)} collective-permute-done((bf16[128,2048]{1,0:T(8,128)(2,1)S(1)}, bf16[128,2048]{1,0:T(8,128)(2,1)S(1)}, u32[]{:S(2)}, u32[]{:S(2)}) %collective-permute-start.59) | collective-permute-done | bytes 524320 | tf_op jit(solution)/shard_map/ppermute | solution.py:31
  598.5 11.6 collective-permute-start.61
  614.7 6.2 collective-permute-done.61
  623.1 20.6 %collective-permute-done.62 = bf16[128,2048]{1,0:T(8,128)(2,1)S(1)} collective-permute-done((bf16[128,2048]{1,0:T(8,128)(2,1)S(1)}, bf16[128,2048]{1,0:T(8,128)(2,1)S(1)}, u32[]{:S(2)}, u32[]{:S(2)}) %collective-permute-start.62) | collective-permute-done | bytes 524320 | tf_op jit(solution)/shard_map/ppermute | solution.py:31
  648.6 22.8 %fusion.119 = (f32[1024,2112]{0,1:T(8,128)}, bf16[1024,2112]{0,1:T(8,128)(2,1)}, bf16[1024,2112]{0,1:T(8,128)(2,1)}) fusion(f32[1024,2112]{0,1:T(8,128)} %get-tuple-element.231, f32[1024,2112]{0,1:T(8,128)} %fusion.133, f32[1024]{0:T(1024)S(1)} %bitcast.396, f32[1024]{0:T(1024)S(1)} %mul.318, pred[2112]{0:T(1024)(128)(4,1)S(1)} %copy-done.130, ...), kind=kOutput, calls=%fused_computation.449 | convolution fusion | flops 8897298432 | bytes 47458368 | tf_op jit(solution)/shard_map/dot_general | solution.py:496
  676.8 10.4 fusion.13
  687.2 6.7 fusion.16
  693.9 11.3 convolution_convert_fusion.1
  705.2 20.1 %reshape.474 = bf16[2,2,2,256,2112]{3,2,1,0,4:T(2,128)(2,1)} reshape(bf16[2048,2112]{0,1:T(8,128)(2,1)} %convolution_convert_fusion.1) | data formatting | bytes 17301504 | tf_op jit(solution)/shard_map/reshape | solution.py:102
  725.3 16.8 %constant_dynamic-slice_fusion.23 = (bf16[1,1,1,256,2112]{3,2,1,0,4:T(2,128)(2,1)}, bf16[1,1,1,256,2112]{3,2,1,0,4:T(2,128)(2,1)}, bf16[1,1,1,256,2112]{3,2,1,0,...) fusion(bf16[2,2,2,256,2112]{3,2,1,0,4:T(2,128)(2,1)} %reshape.4, ...), kind=kLoop, calls=%fused_computation.315 | loop fusion | bytes 12976152 | tf_op jit(solution)/shard_map/dynamic_slice | solution.py:105
  746.3 13.6 convolution_convert_fusion
  760.4 11.7 convolution_convert_fusion.2
  772.1 10.0 add_convert_fusion.2
  782.0 20.1 %reshape.472 = bf16[2,2,2,256,2112]{3,2,1,0,4:T(2,128)(2,1)} reshape(bf16[2048,2112]{0,1:T(8,128)(2,1)} %convolution_convert_fusion.2) | data formatting | bytes 17301504 | tf_op jit(solution)/shard_map/reshape | solution.py:102
  802.2 16.8 %constant_dynamic-slice_fusion.27 = (bf16[1,1,1,256,2112]{3,2,1,0,4:T(2,128)(2,1)}, bf16[1,1,1,256,2112]{3,2,1,0,4:T(2,128)(2,1)}, bf16[1,1,1,256,2112]{3,2,1,0,...) fusion(bf16[2,2,2,256,2112]{3,2,1,0,4:T(2,128)(2,1)} %reshape.4, ...), kind=kLoop, calls=%fused_computation.319 | loop fusion | bytes 12976152 | tf_op jit(solution)/shard_map/dynamic_slice | solution.py:105
  819.0 20.1 %reshape.480 = bf16[2,2,2,256,2112]{3,2,1,0,4:T(2,128)(2,1)} reshape(bf16[2048,2112]{0,1:T(8,128)(2,1)} %convolution_convert_fusion) | data formatting | bytes 17301504 | tf_op jit(solution)/shard_map/reshape | solution.py:102
  839.1 17.0 %constant_dynamic-slice_fusion.11 = (bf16[1,1,1,256,2112]{3,2,1,0,4:T(2,128)(2,1)}, bf16[1,1,1,256,2112]{3,2,1,0,4:T(2,128)(2,1)}, bf16[1,1,1,256,2112]{3,2,1,0,...) fusion(bf16[2,2,2,256,2112]{3,2,1,0,4:T(2,128)(2,1)} %reshape.4, ...), kind=kLoop, calls=%fused_computation.303 | loop fusion | bytes 12976152 | tf_op jit(solution)/shard_map/dynamic_slice | solution.py:105
  864.2 11.7 collective-permute-start.75
  890.4 6.1 copy.377
  898.1 6.2 copy.374
  909.2 6.2 copy.388
  920.4 43.9 %collective-permute-done.111 = bf16[256,2112]{0,1:T(8,128)(2,1)S(1)} collective-permute-done((bf16[256,2112]{0,1:T(8,128)(2,1)}, bf16[256,2112]{0,1:T(8,128)(2,1)S(1)}, u32[]{:S(2)}, u32[]{:S(2)}) %collective-permute-start.111) | collective-permute-done | bytes 1081376 | tf_op jit(solution)/shard_map/ppermute | solution.py:31
  965.7 44.9 %collective-permute-done.121 = bf16[256,2112]{0,1:T(8,128)(2,1)S(1)} collective-permute-done((bf16[256,2112]{0,1:T(8,128)(2,1)}, bf16[256,2112]{0,1:T(8,128)(2,1)S(1)}, u32[]{:S(2)}, u32[]{:S(2)}) %collective-permute-start.121) | collective-permute-done | bytes 1081376 | tf_op jit(solution)/shard_map/ppermute | solution.py:31
  1012.5 9.7 add_convert_fusion.1
  1022.6 59.0 %collective-permute-done.116 = bf16[256,2112]{0,1:T(8,128)(2,1)S(1)} collective-permute-done((bf16[256,2112]{0,1:T(8,128)(2,1)S(1)}, bf16[256,2112]{0,1:T(8,128)(2,1)S(1)}, u32[]{:S(2)}, u32[]{:S(2)}) %collective-permute-start.116) | collective-permute-done | bytes 1081376 | tf_op jit(solution)/shard_map/ppermute | solution.py:26
  1090.0 61.6 %collective-permute-done.112 = bf16[256,2112]{0,1:T(8,128)(2,1)S(1)} collective-permute-done((bf16[256,2112]{0,1:T(8,128)(2,1)S(1)}, bf16[256,2112]{0,1:T(8,128)(2,1)S(1)}, u32[]{:S(2)}, u32[]{:S(2)}) %collective-permute-start.112) | collective-permute-done | bytes 1081376 | tf_op jit(solution)/shard_map/ppermute | solution.py:26
  1156.9 17.8 %collective-permute-done.122 = bf16[256,2112]{0,1:T(8,128)(2,1)S(1)} collective-permute-done((bf16[256,2112]{0,1:T(8,128)(2,1)S(1)}, bf16[256,2112]{0,1:T(8,128)(2,1)S(1)}, u32[]{:S(2)}, u32[]{:S(2)}) %collective-permute-start.122) | collective-permute-done | bytes 1081376 | tf_op jit(solution)/shard_map/ppermute | solution.py:26
  1197.1 9.4 collective-permute-start.99
  1211.8 22.9 %collective-permute-done.98 = f32[10,2048]{1,0:T(8,128)S(1)} collective-permute-done((f32[10,2048]{1,0:T(8,128)S(1)}, f32[10,2048]{1,0:T(8,128)S(1)}, u32[]{:S(2)}, u32[]{:S(2)}) %collective-permute-start.98) | collective-permute-done | bytes 81952 | tf_op jit(solution)/shard_map/ppermute | solution.py:31
  1235.9 11.6 collective-permute-start.79
  1276.6 8.5 collective-permute-start.81
  1292.0 7.4 collective-permute-done.107
  1299.3 9.0 collective-permute-start.82
  1346.4 12.6 attend_back.1
  1366.4 15.0 collective-permute-done.83
  1412.6 7.0 copy.362
  1419.5 5.7 copy.363
  1431.4 8.5 collective-permute-done.103
  1442.9 8.0 collective-permute-done.102
  1451.0 11.2 collective-permute-done.101
  1477.1 8.9 collective-permute-done.87
  1486.0 21.8 %collective-permute-done.86 = bf16[128,2048]{1,0:T(8,128)(2,1)S(1)} collective-permute-done((bf16[128,2048]{1,0:T(8,128)(2,1)S(1)}, bf16[128,2048]{1,0:T(8,128)(2,1)S(1)}, u32[]{:S(2)}, u32[]{:S(2)}) %collective-permute-start.86) | collective-permute-done | bytes 524320 | tf_op jit(solution)/shard_map/ppermute | solution.py:31
  1519.4 14.1 collective-permute-start.93
  (824 shorter events, 543.3 us)
Async XLA Ops:
  1.9 56.0 %collective-permute-start.46 = (bf16[8,128]{1,0:T(8,128)(2,1)}, bf16[8,128]{1,0:T(8,128)(2,1)}, u32[]{:S(2)}, u32[]{:S(2)}) collective-permute-start(bf16[8,128]{1,0:T(8,128)(2,1)} %get-tuple-element.225), channel_id=1, source_target_pairs={{0,1},{1,2},{2,3},{3,0},{4,5},{5,6},{6,7},{7,4},{8,9},{9,10},{10,1... | collective-permute-start | bytes 6152 | tf_op jit(solution)/shard_map/ppermute | solution.py:31
  4.0 54.1 %collective-permute-start.47 = (bf16[8,128]{1,0:T(8,128)(2,1)}, bf16[8,128]{1,0:T(8,128)(2,1)}, u32[]{:S(2)}, u32[]{:S(2)}) collective-permute-start(bf16[8,128]{1,0:T(8,128)(2,1)} %get-tuple-element.225), channel_id=1, source_target_pairs={{0,2},{1,3},{2,0},{3,1},{4,6},{5,7},{6,4},{7,5},{8,10},{9,11},{10,... | collective-permute-start | bytes 6152 | tf_op jit(solution)/shard_map/ppermute | solution.py:31
  6.4 51.8 %collective-permute-start.48 = (bf16[8,128]{1,0:T(8,128)(2,1)}, bf16[8,128]{1,0:T(8,128)(2,1)}, u32[]{:S(2)}, u32[]{:S(2)}) collective-permute-start(bf16[8,128]{1,0:T(8,128)(2,1)} %get-tuple-element.225), channel_id=1, source_target_pairs={{0,3},{1,0},{2,1},{3,2},{4,7},{5,4},{6,5},{7,6},{8,11},{9,8},{10,9... | collective-permute-start | bytes 6152 | tf_op jit(solution)/shard_map/ppermute | solution.py:31
  11.2 62.5 %collective-permute-start.13 = (bf16[256,1024]{0,1:T(8,128)(2,1)}, bf16[256,1024]{0,1:T(8,128)(2,1)}, u32[]{:S(2)}, u32[]{:S(2)}) collective-permute-start(bf16[256,1024]{0,1:T(8,128)(2,1)} %pad_maximum_fusion.18), channel_id=1, source_target_pairs={{0,8},{8,0},{16,24},{24,16},{1,9},{9,1},{17,25},{25,17},{2,10},{10... | collective-permute-start | bytes 1572872 | tf_op jit(solution)/shard_map/ppermute | solution.py:21
  13.6 99.2 %collective-permute-start.14 = (bf16[256,1024]{0,1:T(8,128)(2,1)}, bf16[256,1024]{0,1:T(8,128)(2,1)}, u32[]{:S(2)}, u32[]{:S(2)}) collective-permute-start(bf16[256,1024]{0,1:T(8,128)(2,1)} %get-tuple-element.198), channel_id=1, source_target_pairs={{0,4},{4,0},{1,5},{5,1},{2,6},{6,2},{3,7},{7,3},{8,12},{12,8},{9,1... | collective-permute-start | bytes 1572872 | tf_op jit(solution)/shard_map/ppermute | solution.py:31
  70.1 43.8 %collective-permute-start.16 = (bf16[256,1024]{0,1:T(8,128)(2,1)}, bf16[256,1024]{0,1:T(8,128)(2,1)S(1)}, u32[]{:S(2)}, u32[]{:S(2)}) collective-permute-start(bf16[256,1024]{0,1:T(8,128)(2,1)} %get-tuple-element.198), channel_id=1, source_target_pairs={{0,16},{8,24},{16,0},{24,8},{1,17},{9,25},{17,1},{25,9},{2,18},{10... | collective-permute-start | bytes 1572872 | tf_op jit(solution)/shard_map/ppermute | solution.py:26
  73.7 36.6 %collective-permute-start.1 = (bf16[128,2048]{1,0:T(8,128)(2,1)S(1)}, bf16[128,2048]{1,0:T(8,128)(2,1)}, u32[]{:S(2)}, u32[]{:S(2)}) collective-permute-start(bf16[128,2048]{1,0:T(8,128)(2,1)S(1)} %bitcast.361), channel_id=1, source_target_pairs={{0,2},{1,3},{2,0},{3,1},{4,6},{5,7},{6,4},{7,5},{8,10},{9,11},{10,... | collective-permute-start | bytes 1572872 | tf_op jit(solution)/shard_map/ppermute | solution.py:31
  73.7 41.3 %collective-permute-start.2 = (bf16[128,2048]{1,0:T(8,128)(2,1)S(1)}, bf16[128,2048]{1,0:T(8,128)(2,1)S(1)}, u32[]{:S(2)}, u32[]{:S(2)}) collective-permute-start(bf16[128,2048]{1,0:T(8,128)(2,1)S(1)} %bitcast.362), channel_id=1, source_target_pairs={{0,3},{1,0},{2,1},{3,2},{4,7},{5,4},{6,5},{7,6},{8,11},{9,8},{10,9... | collective-permute-start | bytes 1572872 | tf_op jit(solution)/shard_map/ppermute | solution.py:31
  128.3 55.5 %collective-permute-start.39 = (bf16[256,2112]{0,1:T(8,128)(2,1)}, bf16[256,2112]{0,1:T(8,128)(2,1)}, u32[]{:S(2)}, u32[]{:S(2)}) collective-permute-start(bf16[256,2112]{0,1:T(8,128)(2,1)} %copy.305), channel_id=1, source_target_pairs={{0,8},{8,0},{16,24},{24,16},{1,9},{9,1},{17,25},{25,17},{2,10},{10... | collective-permute-start | bytes 3244040 | tf_op jit(solution)/shard_map/ppermute | solution.py:21
  156.8 58.5 %collective-permute-start.36 = (bf16[256,2112]{0,1:T(8,128)(2,1)}, bf16[256,2112]{0,1:T(8,128)(2,1)}, u32[]{:S(2)}, u32[]{:S(2)}) collective-permute-start(bf16[256,2112]{0,1:T(8,128)(2,1)} %collective-permute-done.32), channel_id=1, source_target_pairs={{0,16},{8,24},{16,0},{24,8},{1,17},{9,25},{17,1},{25,9},{2,18},{10... | collective-permute-start | bytes 3244040 | tf_op jit(solution)/shard_map/ppermute | solution.py:26
  158.0 61.6 %collective-permute-start.34 = (bf16[256,2112]{0,1:T(8,128)(2,1)}, bf16[256,2112]{0,1:T(8,128)(2,1)}, u32[]{:S(2)}, u32[]{:S(2)}) collective-permute-start(bf16[256,2112]{0,1:T(8,128)(2,1)} %collective-permute-done.32), channel_id=1, source_target_pairs={{0,4},{4,0},{1,5},{5,1},{2,6},{6,2},{3,7},{7,3},{8,12},{12,8},{9,1... | collective-permute-start | bytes 3244040 | tf_op jit(solution)/shard_map/ppermute | solution.py:31
  159.9 51.5 %collective-permute-start.33 = (bf16[256,2112]{0,1:T(8,128)(2,1)}, bf16[256,2112]{0,1:T(8,128)(2,1)S(1)}, u32[]{:S(2)}, u32[]{:S(2)}) collective-permute-start(bf16[256,2112]{0,1:T(8,128)(2,1)} %copy.297), channel_id=1, source_target_pairs={{0,4},{4,0},{1,5},{5,1},{2,6},{6,2},{3,7},{7,3},{8,12},{12,8},{9,1... | collective-permute-start | bytes 3244040 | tf_op jit(solution)/shard_map/ppermute | solution.py:31
  165.1 57.0 %collective-permute-start.35 = (bf16[256,2112]{0,1:T(8,128)(2,1)}, bf16[256,2112]{0,1:T(8,128)(2,1)}, u32[]{:S(2)}, u32[]{:S(2)}) collective-permute-start(bf16[256,2112]{0,1:T(8,128)(2,1)} %copy.297), channel_id=1, source_target_pairs={{0,16},{8,24},{16,0},{24,8},{1,17},{9,25},{17,1},{25,9},{2,18},{10... | collective-permute-start | bytes 3244040 | tf_op jit(solution)/shard_map/ppermute | solution.py:26
  183.8 52.4 %collective-permute-start.50 = (bf16[256,2112]{0,1:T(8,128)(2,1)}, bf16[256,2112]{0,1:T(8,128)(2,1)}, u32[]{:S(2)}, u32[]{:S(2)}) collective-permute-start(bf16[256,2112]{0,1:T(8,128)(2,1)} %copy.317), channel_id=1, source_target_pairs={{0,8},{8,0},{16,24},{24,16},{1,9},{9,1},{17,25},{25,17},{2,10},{10... | collective-permute-start | bytes 3244040 | tf_op jit(solution)/shard_map/ppermute | solution.py:21
  216.8 73.7 %collective-permute-start.43 = (bf16[256,2112]{0,1:T(8,128)(2,1)}, bf16[256,2112]{0,1:T(8,128)(2,1)}, u32[]{:S(2)}, u32[]{:S(2)}) collective-permute-start(bf16[256,2112]{0,1:T(8,128)(2,1)} %collective-permute-done.39), channel_id=1, source_target_pairs={{0,16},{8,24},{16,0},{24,8},{1,17},{9,25},{17,1},{25,9},{2,18},{10... | collective-permute-start | bytes 3244040 | tf_op jit(solution)/shard_map/ppermute | solution.py:26
  219.6 91.9 %collective-permute-start.41 = (bf16[256,2112]{0,1:T(8,128)(2,1)}, bf16[256,2112]{0,1:T(8,128)(2,1)}, u32[]{:S(2)}, u32[]{:S(2)}) collective-permute-start(bf16[256,2112]{0,1:T(8,128)(2,1)} %collective-permute-done.39), channel_id=1, source_target_pairs={{0,4},{4,0},{1,5},{5,1},{2,6},{6,2},{3,7},{7,3},{8,12},{12,8},{9,1... | collective-permute-start | bytes 3244040 | tf_op jit(solution)/shard_map/ppermute | solution.py:31
  222.1 60.5 %collective-permute-start.40 = (bf16[256,2112]{0,1:T(8,128)(2,1)}, bf16[256,2112]{0,1:T(8,128)(2,1)}, u32[]{:S(2)}, u32[]{:S(2)}) collective-permute-start(bf16[256,2112]{0,1:T(8,128)(2,1)} %copy.307), channel_id=1, source_target_pairs={{0,4},{4,0},{1,5},{5,1},{2,6},{6,2},{3,7},{7,3},{8,12},{12,8},{9,1... | collective-permute-start | bytes 3244040 | tf_op jit(solution)/shard_map/ppermute | solution.py:31
  236.2 59.6 %collective-permute-start.37 = (bf16[256,2112]{0,1:T(8,128)(2,1)S(1)}, bf16[256,2112]{0,1:T(8,128)(2,1)}, u32[]{:S(2)}, u32[]{:S(2)}) collective-permute-start(bf16[256,2112]{0,1:T(8,128)(2,1)S(1)} %copy-done.89), channel_id=1, source_target_pairs={{0,16},{8,24},{16,0},{24,8},{1,17},{9,25},{17,1},{25,9},{2,18},{10... | collective-permute-start | bytes 3244040 | tf_op jit(solution)/shard_map/ppermute | solution.py:26
  236.5 69.3 %collective-permute-start.38 = (bf16[256,2112]{0,1:T(8,128)(2,1)}, bf16[256,2112]{0,1:T(8,128)(2,1)}, u32[]{:S(2)}, u32[]{:S(2)}) collective-permute-start(bf16[256,2112]{0,1:T(8,128)(2,1)} %collective-permute-done.36), channel_id=1, source_target_pairs={{0,4},{4,0},{1,5},{5,1},{2,6},{6,2},{3,7},{7,3},{8,12},{12,8},{9,1... | collective-permute-start | bytes 3244040 | tf_op jit(solution)/shard_map/ppermute | solution.py:31
  282.6 36.4 %collective-permute-start.42 = (bf16[256,2112]{0,1:T(8,128)(2,1)}, bf16[256,2112]{0,1:T(8,128)(2,1)}, u32[]{:S(2)}, u32[]{:S(2)}) collective-permute-start(bf16[256,2112]{0,1:T(8,128)(2,1)} %copy.307), channel_id=1, source_target_pairs={{0,16},{8,24},{16,0},{24,8},{1,17},{9,25},{17,1},{25,9},{2,18},{10... | collective-permute-start | bytes 3244040 | tf_op jit(solution)/shard_map/ppermute | solution.py:26
  290.5 67.2 %collective-permute-start.52 = (bf16[256,2112]{0,1:T(8,128)(2,1)}, bf16[256,2112]{0,1:T(8,128)(2,1)}, u32[]{:S(2)}, u32[]{:S(2)}) collective-permute-start(bf16[256,2112]{0,1:T(8,128)(2,1)} %collective-permute-done.50), channel_id=1, source_target_pairs={{0,4},{4,0},{1,5},{5,1},{2,6},{6,2},{3,7},{7,3},{8,12},{12,8},{9,1... | collective-permute-start | bytes 3244040 | tf_op jit(solution)/shard_map/ppermute | solution.py:31
  295.8 56.3 %collective-permute-start.51 = (bf16[256,2112]{0,1:T(8,128)(2,1)}, bf16[256,2112]{0,1:T(8,128)(2,1)}, u32[]{:S(2)}, u32[]{:S(2)}) collective-permute-start(bf16[256,2112]{0,1:T(8,128)(2,1)} %copy.319), channel_id=1, source_target_pairs={{0,4},{4,0},{1,5},{5,1},{2,6},{6,2},{3,7},{7,3},{8,12},{12,8},{9,1... | collective-permute-start | bytes 3244040 | tf_op jit(solution)/shard_map/ppermute | solution.py:31
  305.8 55.8 %collective-permute-start.53 = (bf16[256,2112]{0,1:T(8,128)(2,1)}, bf16[256,2112]{0,1:T(8,128)(2,1)}, u32[]{:S(2)}, u32[]{:S(2)}) collective-permute-start(bf16[256,2112]{0,1:T(8,128)(2,1)} %copy.319), channel_id=1, source_target_pairs={{0,16},{8,24},{16,0},{24,8},{1,17},{9,25},{17,1},{25,9},{2,18},{10... | collective-permute-start | bytes 3244040 | tf_op jit(solution)/shard_map/ppermute | solution.py:26
  311.6 51.6 %collective-permute-start.54 = (bf16[256,2112]{0,1:T(8,128)(2,1)}, bf16[256,2112]{0,1:T(8,128)(2,1)}, u32[]{:S(2)}, u32[]{:S(2)}) collective-permute-start(bf16[256,2112]{0,1:T(8,128)(2,1)} %collective-permute-done.50), channel_id=1, source_target_pairs={{0,16},{8,24},{16,0},{24,8},{1,17},{9,25},{17,1},{25,9},{2,18},{10... | collective-permute-start | bytes 3244040 | tf_op jit(solution)/shard_map/ppermute | solution.py:26
  325.9 49.1 %collective-permute-start.44 = (bf16[256,2112]{0,1:T(8,128)(2,1)}, bf16[256,2112]{0,1:T(8,128)(2,1)}, u32[]{:S(2)}, u32[]{:S(2)}) collective-permute-start(bf16[256,2112]{0,1:T(8,128)(2,1)} %collective-permute-done.40), channel_id=1, source_target_pairs={{0,16},{8,24},{16,0},{24,8},{1,17},{9,25},{17,1},{25,9},{2,18},{10... | collective-permute-start | bytes 3244040 | tf_op jit(solution)/shard_map/ppermute | solution.py:26
  357.7 38.3 %collective-permute-start.45 = (bf16[256,2112]{0,1:T(8,128)(2,1)}, bf16[256,2112]{0,1:T(8,128)(2,1)}, u32[]{:S(2)}, u32[]{:S(2)}) collective-permute-start(bf16[256,2112]{0,1:T(8,128)(2,1)} %collective-permute-done.43), channel_id=1, source_target_pairs={{0,4},{4,0},{1,5},{5,1},{2,6},{6,2},{3,7},{7,3},{8,12},{12,8},{9,1... | collective-permute-start | bytes 3244040 | tf_op jit(solution)/shard_map/ppermute | solution.py:31
  391.5 38.0 %collective-permute-start.23 = (bf16[128,2048]{1,0:T(8,128)(2,1)}, bf16[128,2048]{1,0:T(8,128)(2,1)S(1)}, u32[]{:S(2)}, u32[]{:S(2)}) collective-permute-start(bf16[128,2048]{1,0:T(8,128)(2,1)} %get-tuple-element.176), channel_id=1, source_target_pairs={{0,2},{1,3},{2,0},{3,1},{4,6},{5,7},{6,4},{7,5},{8,10},{9,11},{10,... | collective-permute-start | bytes 1572872 | tf_op jit(solution)/shard_map/ppermute | solution.py:31
  394.7 35.6 %collective-permute-start.22 = (bf16[128,2048]{1,0:T(8,128)(2,1)}, bf16[128,2048]{1,0:T(8,128)(2,1)}, u32[]{:S(2)}, u32[]{:S(2)}) collective-permute-start(bf16[128,2048]{1,0:T(8,128)(2,1)} %get-tuple-element.174), channel_id=1, source_target_pairs={{0,3},{1,0},{2,1},{3,2},{4,7},{5,4},{6,5},{7,6},{8,11},{9,8},{10,9... | collective-permute-start | bytes 1572872 | tf_op jit(solution)/shard_map/ppermute | solution.py:31
  398.3 48.5 %collective-permute-start.55 = (bf16[256,2112]{0,1:T(8,128)(2,1)}, bf16[256,2112]{0,1:T(8,128)(2,1)S(1)}, u32[]{:S(2)}, u32[]{:S(2)}) collective-permute-start(bf16[256,2112]{0,1:T(8,128)(2,1)} %collective-permute-done.51), channel_id=1, source_target_pairs={{0,16},{8,24},{16,0},{24,8},{1,17},{9,25},{17,1},{25,9},{2,18},{10... | collective-permute-start | bytes 3244040 | tf_op jit(solution)/shard_map/ppermute | solution.py:26
  401.7 48.9 %collective-permute-start.56 = (bf16[256,2112]{0,1:T(8,128)(2,1)}, bf16[256,2112]{0,1:T(8,128)(2,1)}, u32[]{:S(2)}, u32[]{:S(2)}) collective-permute-start(bf16[256,2112]{0,1:T(8,128)(2,1)} %collective-permute-done.54), channel_id=1, source_target_pairs={{0,4},{4,0},{1,5},{5,1},{2,6},{6,2},{3,7},{7,3},{8,12},{12,8},{9,1... | collective-permute-start | bytes 3244040 | tf_op jit(solution)/shard_map/ppermute | solution.py:31
  444.7 33.3 %collective-permute-start.27 = (bf16[128,2048]{1,0:T(8,128)(2,1)S(1)}, bf16[128,2048]{1,0:T(8,128)(2,1)S(1)}, u32[]{:S(2)}, u32[]{:S(2)}) collective-permute-start(bf16[128,2048]{1,0:T(8,128)(2,1)S(1)} %get-tuple-element.117), channel_id=1, source_target_pairs={{0,3},{1,0},{2,1},{3,2},{4,7},{5,4},{6,5},{7,6},{8,11},{9,8},{10,9... | collective-permute-start | bytes 1572872 | tf_op jit(solution)/shard_map/ppermute | solution.py:31
  446.8 33.4 %collective-permute-start.28 = (bf16[128,2048]{1,0:T(8,128)(2,1)S(1)}, bf16[128,2048]{1,0:T(8,128)(2,1)}, u32[]{:S(2)}, u32[]{:S(2)}) collective-permute-start(bf16[128,2048]{1,0:T(8,128)(2,1)S(1)} %get-tuple-element.117), channel_id=1, source_target_pairs={{0,8},{8,0},{16,24},{24,16},{1,9},{9,1},{17,25},{25,17},{2,10},{10... | collective-permute-start | bytes 1572872 | tf_op jit(solution)/shard_map/ppermute | solution.py:21
  560.1 37.9 %collective-permute-start.59 = (bf16[128,2048]{1,0:T(8,128)(2,1)S(1)}, bf16[128,2048]{1,0:T(8,128)(2,1)S(1)}, u32[]{:S(2)}, u32[]{:S(2)}) collective-permute-start(bf16[128,2048]{1,0:T(8,128)(2,1)S(1)} %get-tuple-element.173), channel_id=1, source_target_pairs={{0,2},{1,3},{2,0},{3,1},{4,6},{5,7},{6,4},{7,5},{8,10},{9,11},{10,... | collective-permute-start | bytes 1572872 | tf_op jit(solution)/shard_map/ppermute | solution.py:31
  563.3 34.7 %collective-permute-start.58 = (bf16[128,2048]{1,0:T(8,128)(2,1)S(1)}, bf16[128,2048]{1,0:T(8,128)(2,1)S(1)}, u32[]{:S(2)}, u32[]{:S(2)}) collective-permute-start(bf16[128,2048]{1,0:T(8,128)(2,1)S(1)} %get-tuple-element.171), channel_id=1, source_target_pairs={{0,3},{1,0},{2,1},{3,2},{4,7},{5,4},{6,5},{7,6},{8,11},{9,8},{10,9... | collective-permute-start | bytes 1572872 | tf_op jit(solution)/shard_map/ppermute | solution.py:31
  610.6 33.7 %collective-permute-start.63 = (bf16[128,2048]{1,0:T(8,128)(2,1)S(1)}, bf16[128,2048]{1,0:T(8,128)(2,1)S(1)}, u32[]{:S(2)}, u32[]{:S(2)}) collective-permute-start(bf16[128,2048]{1,0:T(8,128)(2,1)S(1)} %get-tuple-element.114), channel_id=1, source_target_pairs={{0,3},{1,0},{2,1},{3,2},{4,7},{5,4},{6,5},{7,6},{8,11},{9,8},{10,9... | collective-permute-start | bytes 1572872 | tf_op jit(solution)/shard_map/ppermute | solution.py:31
  760.0 104.2 %collective-permute-start.72 = (f32[9,4,128]{2,0,1:T(8,128)S(1)}, f32[9,4,128]{2,0,1:T(8,128)S(1)}, u32[]{:S(2)}, u32[]{:S(2)}) collective-permute-start(f32[9,4,128]{2,0,1:T(8,128)S(1)} %fusion.78), channel_id=1, source_target_pairs={{0,8},{8,0},{16,24},{24,16},{1,9},{9,1},{17,25},{25,17},{2,10},{10... | collective-permute-start | bytes 55304 | tf_op jit(solution)/shard_map/ppermute | solution.py:21
  861.9 55.4 %collective-permute-start.115 = (bf16[256,2112]{0,1:T(8,128)(2,1)}, bf16[256,2112]{0,1:T(8,128)(2,1)}, u32[]{:S(2)}, u32[]{:S(2)}) collective-permute-start(bf16[256,2112]{0,1:T(8,128)(2,1)} %bitcast.346), channel_id=1, source_target_pairs={{0,4},{4,0},{1,5},{5,1},{2,6},{6,2},{3,7},{7,3},{8,12},{12,8},{9,1... | collective-permute-start | bytes 3244040 | tf_op jit(solution)/shard_map/ppermute | solution.py:31
  864.2 51.2 %collective-permute-start.75 = (f32[9,128]{1,0:T(8,128)S(1)}, f32[9,128]{1,0:T(8,128)S(1)}, u32[]{:S(2)}, u32[]{:S(2)}) collective-permute-start(f32[9,128]{1,0:T(8,128)S(1)} %get-tuple-element.214), channel_id=1, source_target_pairs={{0,1},{1,2},{2,3},{3,0},{4,5},{5,6},{6,7},{7,4},{8,9},{9,10},{10,1... | collective-permute-start | bytes 13832 | tf_op jit(solution)/shard_map/ppermute | solution.py:31
  875.9 39.5 %collective-permute-start.74 = (f32[9,128]{1,0:T(8,128)S(1)}, f32[9,128]{1,0:T(8,128)S(1)}, u32[]{:S(2)}, u32[]{:S(2)}) collective-permute-start(f32[9,128]{1,0:T(8,128)S(1)} %get-tuple-element.215), channel_id=1, source_target_pairs={{0,2},{1,3},{2,0},{3,1},{4,6},{5,7},{6,4},{7,5},{8,10},{9,11},{10,... | collective-permute-start | bytes 13832 | tf_op jit(solution)/shard_map/ppermute | solution.py:31
  879.0 37.9 %collective-permute-start.73 = (f32[9,128]{1,0:T(8,128)S(1)}, f32[9,128]{1,0:T(8,128)S(1)}, u32[]{:S(2)}, u32[]{:S(2)}) collective-permute-start(f32[9,128]{1,0:T(8,128)S(1)} %get-tuple-element.213), channel_id=1, source_target_pairs={{0,3},{1,0},{2,1},{3,2},{4,7},{5,4},{6,5},{7,6},{8,11},{9,8},{10,9... | collective-permute-start | bytes 13832 | tf_op jit(solution)/shard_map/ppermute | solution.py:31
  883.5 128.5 %collective-permute-start.68 = (bf16[512,2048]{1,0:T(8,128)(2,1)}, bf16[512,2048]{1,0:T(8,128)(2,1)}, u32[]{:S(2)}, u32[]{:S(2)}) collective-permute-start(bf16[512,2048]{1,0:T(8,128)(2,1)} %add_convert_fusion.2), channel_id=1, source_target_pairs={{0,8},{8,0},{16,24},{24,16},{1,9},{9,1},{17,25},{25,17},{2,10},{10... | collective-permute-start | bytes 6291464 | tf_op jit(solution)/shard_map/ppermute | solution.py:21
  915.4 107.0 %collective-permute-start.114 = (bf16[256,2112]{0,1:T(8,128)(2,1)}, bf16[256,2112]{0,1:T(8,128)(2,1)S(1)}, u32[]{:S(2)}, u32[]{:S(2)}) collective-permute-start(bf16[256,2112]{0,1:T(8,128)(2,1)} %bitcast.372), channel_id=1, source_target_pairs={{0,4},{4,0},{1,5},{5,1},{2,6},{6,2},{3,7},{7,3},{8,12},{12,8},{9,1... | collective-permute-start | bytes 3244040 | tf_op jit(solution)/shard_map/ppermute | solution.py:31
  915.4 48.9 %collective-permute-start.111 = (bf16[256,2112]{0,1:T(8,128)(2,1)}, bf16[256,2112]{0,1:T(8,128)(2,1)S(1)}, u32[]{:S(2)}, u32[]{:S(2)}) collective-permute-start(bf16[256,2112]{0,1:T(8,128)(2,1)} %bitcast.373), channel_id=1, source_target_pairs={{0,4},{4,0},{1,5},{5,1},{2,6},{6,2},{3,7},{7,3},{8,12},{12,8},{9,1... | collective-permute-start | bytes 3244040 | tf_op jit(solution)/shard_map/ppermute | solution.py:31
  916.9 171.4 %collective-permute-start.110 = (bf16[256,2112]{0,1:T(8,128)(2,1)}, bf16[256,2112]{0,1:T(8,128)(2,1)S(1)}, u32[]{:S(2)}, u32[]{:S(2)}) collective-permute-start(bf16[256,2112]{0,1:T(8,128)(2,1)} %bitcast.371), channel_id=1, source_target_pairs={{0,4},{4,0},{1,5},{5,1},{2,6},{6,2},{3,7},{7,3},{8,12},{12,8},{9,1... | collective-permute-start | bytes 3244040 | tf_op jit(solution)/shard_map/ppermute | solution.py:31
  917.4 93.2 %collective-permute-start.121 = (bf16[256,2112]{0,1:T(8,128)(2,1)}, bf16[256,2112]{0,1:T(8,128)(2,1)S(1)}, u32[]{:S(2)}, u32[]{:S(2)}) collective-permute-start(bf16[256,2112]{0,1:T(8,128)(2,1)} %bitcast.374), channel_id=1, source_target_pairs={{0,4},{4,0},{1,5},{5,1},{2,6},{6,2},{3,7},{7,3},{8,12},{12,8},{9,1... | collective-permute-start | bytes 3244040 | tf_op jit(solution)/shard_map/ppermute | solution.py:31
  964.3 119.8 %collective-permute-start.108 = (bf16[2,256,2112]{1,2,0:T(8,128)(2,1)S(1)}, bf16[2,256,2112]{1,2,0:T(8,128)(2,1)S(1)}, u32[]{:S(2)}, u32[]{:S(2)}) collective-permute-start(bf16[2,256,2112]{1,2,0:T(8,128)(2,1)S(1)} %bitcast.369), channel_id=1, source_target_pairs={{0,16},{8,24},{16,0},{24,8},{1,17},{9,25},{17,1},{25,9},{2,18},{10... | collective-permute-start | bytes 6488072 | tf_op jit(solution)/shard_map/ppermute | solution.py:26
  1010.6 75.3 %collective-permute-start.106 = (bf16[2,256,2112]{1,2,0:T(8,128)(2,1)S(1)}, bf16[2,256,2112]{1,2,0:T(8,128)(2,1)S(1)}, u32[]{:S(2)}, u32[]{:S(2)}) collective-permute-start(bf16[2,256,2112]{1,2,0:T(8,128)(2,1)S(1)} %bitcast.368), channel_id=1, source_target_pairs={{0,16},{8,24},{16,0},{24,8},{1,17},{9,25},{17,1},{25,9},{2,18},{10... | collective-permute-start | bytes 6488072 | tf_op jit(solution)/shard_map/ppermute | solution.py:26
  1012.0 69.5 %collective-permute-start.116 = (bf16[256,2112]{0,1:T(8,128)(2,1)S(1)}, bf16[256,2112]{0,1:T(8,128)(2,1)S(1)}, u32[]{:S(2)}, u32[]{:S(2)}) collective-permute-start(bf16[256,2112]{0,1:T(8,128)(2,1)S(1)} %fusion.25), channel_id=1, source_target_pairs={{0,16},{8,24},{16,0},{24,8},{1,17},{9,25},{17,1},{25,9},{2,18},{10... | collective-permute-start | bytes 3244040 | tf_op jit(solution)/shard_map/ppermute | solution.py:26
  1022.4 132.0 %collective-permute-start.120 = (bf16[256,2112]{0,1:T(8,128)(2,1)S(1)}, bf16[256,2112]{0,1:T(8,128)(2,1)S(1)}, u32[]{:S(2)}, u32[]{:S(2)}) collective-permute-start(bf16[256,2112]{0,1:T(8,128)(2,1)S(1)} %bitcast.370), channel_id=1, source_target_pairs={{0,4},{4,0},{1,5},{5,1},{2,6},{6,2},{3,7},{7,3},{8,12},{12,8},{9,1... | collective-permute-start | bytes 3244040 | tf_op jit(solution)/shard_map/ppermute | solution.py:31
  1081.6 97.3 %collective-permute-start.118 = (bf16[2,256,2112]{1,2,0:T(8,128)(2,1)S(1)}, bf16[2,256,2112]{1,2,0:T(8,128)(2,1)S(1)}, u32[]{:S(2)}, u32[]{:S(2)}) collective-permute-start(bf16[2,256,2112]{1,2,0:T(8,128)(2,1)S(1)} %bitcast.367), channel_id=1, source_target_pairs={{0,16},{8,24},{16,0},{24,8},{1,17},{9,25},{17,1},{25,9},{2,18},{10... | collective-permute-start | bytes 6488072 | tf_op jit(solution)/shard_map/ppermute | solution.py:26
  1084.1 67.5 %collective-permute-start.112 = (bf16[256,2112]{0,1:T(8,128)(2,1)S(1)}, bf16[256,2112]{0,1:T(8,128)(2,1)S(1)}, u32[]{:S(2)}, u32[]{:S(2)}) collective-permute-start(bf16[256,2112]{0,1:T(8,128)(2,1)S(1)} %fusion.28), channel_id=1, source_target_pairs={{0,16},{8,24},{16,0},{24,8},{1,17},{9,25},{17,1},{25,9},{2,18},{10... | collective-permute-start | bytes 3244040 | tf_op jit(solution)/shard_map/ppermute | solution.py:26
  1085.9 88.9 %collective-permute-start.122 = (bf16[256,2112]{0,1:T(8,128)(2,1)S(1)}, bf16[256,2112]{0,1:T(8,128)(2,1)S(1)}, u32[]{:S(2)}, u32[]{:S(2)}) collective-permute-start(bf16[256,2112]{0,1:T(8,128)(2,1)S(1)} %fusion.21), channel_id=1, source_target_pairs={{0,16},{8,24},{16,0},{24,8},{1,17},{9,25},{17,1},{25,9},{2,18},{10... | collective-permute-start | bytes 3244040 | tf_op jit(solution)/shard_map/ppermute | solution.py:26
  1088.3 92.5 %collective-permute-start.71 = (bf16[128,2048]{1,0:T(8,128)(2,1)S(1)}, bf16[128,2048]{1,0:T(8,128)(2,1)S(1)}, u32[]{:S(2)}, u32[]{:S(2)}) collective-permute-start(bf16[128,2048]{1,0:T(8,128)(2,1)S(1)} %get-tuple-element.169), channel_id=1, source_target_pairs={{0,1},{1,2},{2,3},{3,0},{4,5},{5,6},{6,7},{7,4},{8,9},{9,10},{10,1... | collective-permute-start | bytes 1572872 | tf_op jit(solution)/shard_map/ppermute | solution.py:31
  1174.8 91.0 %collective-permute-start.117 = (bf16[256,2112]{0,1:T(8,128)(2,1)}, bf16[256,2112]{0,1:T(8,128)(2,1)}, u32[]{:S(2)}, u32[]{:S(2)}) collective-permute-start(bf16[256,2112]{0,1:T(8,128)(2,1)} %fusion.27), channel_id=1, source_target_pairs={{0,8},{8,0},{16,24},{24,16},{1,9},{9,1},{17,25},{25,17},{2,10},{10... | collective-permute-start | bytes 3244040 | tf_op jit(solution)/shard_map/ppermute | solution.py:21
  1178.8 93.0 %collective-permute-start.113 = (bf16[256,2112]{0,1:T(8,128)(2,1)}, bf16[256,2112]{0,1:T(8,128)(2,1)}, u32[]{:S(2)}, u32[]{:S(2)}) collective-permute-start(bf16[256,2112]{0,1:T(8,128)(2,1)} %fusion.30), channel_id=1, source_target_pairs={{0,8},{8,0},{16,24},{24,16},{1,9},{9,1},{17,25},{25,17},{2,10},{10... | collective-permute-start | bytes 3244040 | tf_op jit(solution)/shard_map/ppermute | solution.py:21
  1258.4 40.9 %collective-permute-start.107 = (bf16[256,2112]{0,1:T(8,128)(2,1)}, bf16[256,2112]{0,1:T(8,128)(2,1)}, u32[]{:S(2)}, u32[]{:S(2)}) collective-permute-start(bf16[256,2112]{0,1:T(8,128)(2,1)} %fusion.32), channel_id=1, source_target_pairs={{0,4},{4,0},{1,5},{5,1},{2,6},{6,2},{3,7},{7,3},{8,12},{12,8},{9,1... | collective-permute-start | bytes 3244040 | tf_op jit(solution)/shard_map/ppermute | solution.py:31
  1260.1 72.9 %collective-permute-start.123 = (bf16[256,2112]{0,1:T(8,128)(2,1)}, bf16[256,2112]{0,1:T(8,128)(2,1)}, u32[]{:S(2)}, u32[]{:S(2)}) collective-permute-start(bf16[256,2112]{0,1:T(8,128)(2,1)} %fusion.23), channel_id=1, source_target_pairs={{0,8},{8,0},{16,24},{24,16},{1,9},{9,1},{17,25},{25,17},{2,10},{10... | collective-permute-start | bytes 3244040 | tf_op jit(solution)/shard_map/ppermute | solution.py:21
  1267.8 54.7 %collective-permute-start.119 = (bf16[256,2112]{0,1:T(8,128)(2,1)}, bf16[256,2112]{0,1:T(8,128)(2,1)}, u32[]{:S(2)}, u32[]{:S(2)}) collective-permute-start(bf16[256,2112]{0,1:T(8,128)(2,1)} %fusion.24), channel_id=1, source_target_pairs={{0,4},{4,0},{1,5},{5,1},{2,6},{6,2},{3,7},{7,3},{8,12},{12,8},{9,1... | collective-permute-start | bytes 3244040 | tf_op jit(solution)/shard_map/ppermute | solution.py:31
  1271.9 64.3 %collective-permute-start.80 = (bf16[128,2048]{1,0:T(8,128)(2,1)}, bf16[128,2048]{1,0:T(8,128)(2,1)}, u32[]{:S(2)}, u32[]{:S(2)}) collective-permute-start(bf16[128,2048]{1,0:T(8,128)(2,1)} %collective-permute-done.76), channel_id=1, source_target_pairs={{0,8},{8,0},{16,24},{24,16},{1,9},{9,1},{17,25},{25,17},{2,10},{10... | collective-permute-start | bytes 1572872 | tf_op jit(solution)/shard_map/ppermute | solution.py:21
  1276.6 61.5 %collective-permute-start.81 = (bf16[128,2048]{1,0:T(8,128)(2,1)}, bf16[128,2048]{1,0:T(8,128)(2,1)}, u32[]{:S(2)}, u32[]{:S(2)}) collective-permute-start(bf16[128,2048]{1,0:T(8,128)(2,1)} %collective-permute-done.77), channel_id=1, source_target_pairs={{0,8},{8,0},{16,24},{24,16},{1,9},{9,1},{17,25},{25,17},{2,10},{10... | collective-permute-start | bytes 1572872 | tf_op jit(solution)/shard_map/ppermute | solution.py:21
  1299.3 40.7 %collective-permute-start.82 = (bf16[128,2048]{1,0:T(8,128)(2,1)}, bf16[128,2048]{1,0:T(8,128)(2,1)}, u32[]{:S(2)}, u32[]{:S(2)}) collective-permute-start(bf16[128,2048]{1,0:T(8,128)(2,1)} %collective-permute-done.78), channel_id=1, source_target_pairs={{0,8},{8,0},{16,24},{24,16},{1,9},{9,1},{17,25},{25,17},{2,10},{10... | collective-permute-start | bytes 1572872 | tf_op jit(solution)/shard_map/ppermute | solution.py:21
  1393.3 71.5 %collective-permute-start.84 = (bf16[512,2048]{1,0:T(8,128)(2,1)}, bf16[512,2048]{1,0:T(8,128)(2,1)}, u32[]{:S(2)}, u32[]{:S(2)}) collective-permute-start(bf16[512,2048]{1,0:T(8,128)(2,1)} %convolution_convert_fusion.6), channel_id=1, source_target_pairs={{0,8},{8,0},{16,24},{24,16},{1,9},{9,1},{17,25},{25,17},{2,10},{10... | collective-permute-start | bytes 6291464 | tf_op jit(solution)/shard_map/ppermute | solution.py:21
  1404.6 35.2 %collective-permute-start.100 = (bf16[2,256,1024]{1,2,0:T(8,128)(2,1)}, bf16[2,256,1024]{1,2,0:T(8,128)(2,1)}, u32[]{:S(2)}, u32[]{:S(2)}) collective-permute-start(bf16[2,256,1024]{1,2,0:T(8,128)(2,1)} %fusion.44), channel_id=1, source_target_pairs={{0,16},{8,24},{16,0},{24,8},{1,17},{9,25},{17,1},{25,9},{2,18},{10... | collective-permute-start | bytes 3145736 | tf_op jit(solution)/shard_map/ppermute | solution.py:26
  1474.7 33.8 %collective-permute-start.85 = (bf16[128,2048]{1,0:T(8,128)(2,1)S(1)}, bf16[128,2048]{1,0:T(8,128)(2,1)S(1)}, u32[]{:S(2)}, u32[]{:S(2)}) collective-permute-start(bf16[128,2048]{1,0:T(8,128)(2,1)S(1)} %get-tuple-element.165), channel_id=1, source_target_pairs={{0,3},{1,0},{2,1},{3,2},{4,7},{5,4},{6,5},{7,6},{8,11},{9,8},{10,9... | collective-permute-start | bytes 1572872 | tf_op jit(solution)/shard_map/ppermute | solution.py:31
  (211 other events, 3775.7 us)

commit v2 on v1

v2 whole, which is shorter than its diff:
```python
import functools

import jax
import jax.numpy as jnp
from jax import lax
from jax.experimental import pallas as pl
from jax.experimental.pallas import tpu as pltpu
from jax.sharding import PartitionSpec as P

HD = 128
EPSILON = 1e-06
ROPE_BASE = 1000000.0
NEGATIVE = -1e30
HIGHEST = lax.Precision.HIGHEST
BF = jnp.bfloat16
F32 = jnp.float32
TILE_M = 512
TILE_N = 256
PACE = 8


def core_swap(v):
    n = lax.axis_size("dp")
    return lax.ppermute(v, "dp", [(i, i ^ 1) for i in range(n)])


def y_swap(v):
    n = lax.axis_size("dp")
    return lax.ppermute(v, "dp", [(i, i ^ 2) for i in range(n)])


def shift(v, axis, s):
    n = lax.axis_size(axis)
    return lax.ppermute(v, axis, [(i, (i + s) % n) for i in range(n)])


def after(values, anchors):
    return lax.optimization_barrier((tuple(values), tuple(anchors)))[0]


def meet(*trees):
    return lax.optimization_barrier(trees)


def exchange(v):
    return lax.all_to_all(v, "exp", split_axis=0, concat_axis=0, tiled=True)


def gather_exp(v):
    nz = lax.axis_size("exp")
    wide = jnp.broadcast_to(v[None], (nz, *v.shape)).reshape(nz * v.shape[0], *v.shape[1:])
    return exchange(wide)


def gather_rows(v):
    return both_cores(gather_exp(v))


def both_cores(mine):
    return [mine, core_swap(mine)]


def home_start(keep, got):
    nz = lax.axis_size("exp")
    both = (keep.astype(F32) + got.astype(F32)).astype(keep.dtype)
    return both, list(exchange(both).reshape(nz, keep.shape[0] // nz, *keep.shape[1:]))


def total(parts):
    return functools.reduce(jnp.add, [p.astype(F32) for p in parts])


def sum_shifts(v, axis):
    return functools.reduce(
        jnp.add, [v] + [shift(v, axis, s) for s in range(1, lax.axis_size(axis))]
    )


def spread(v, size, index):
    place = lax.broadcasted_iota(jnp.int32, (size, *(1,) * v.ndim), 0)
    return jnp.where(place == index, v[None], jnp.zeros((), v.dtype))


def gather_group(v):
    v = sum_shifts(spread(v, lax.axis_size("exp"), lax.axis_index("exp")), "exp")
    v = spread(v, 2, lax.axis_index("dp") % 2)
    return v + core_swap(v)


def gather_plane(v):
    v = spread(v, 2, lax.axis_index("dp") // 2)
    v = v + y_swap(v)
    return sum_shifts(spread(v, lax.axis_size("ctx"), lax.axis_index("ctx")), "ctx")


def own_of(v, axis, size, index):
    return total(
        [
            shift(lax.dynamic_index_in_dim(v, lax.rem(index + s, size), 0, False), axis, s)
            if s
            else lax.dynamic_index_in_dim(v, index, 0, False)
            for s in range(size)
        ]
    )


def scatter_everywhere(v):
    y, c = lax.axis_index("dp") // 2, lax.axis_index("dp") % 2
    v = own_of(v, "ctx", lax.axis_size("ctx"), lax.axis_index("ctx"))
    pick = lax.dynamic_index_in_dim
    v = pick(v, y, 0, False) + y_swap(pick(v, 1 - y, 0, False))
    v = pick(v, c, 0, False) + core_swap(pick(v, 1 - c, 0, False))
    return own_of(v, "exp", lax.axis_size("exp"), lax.axis_index("exp"))


def weight_ctx(pair):
    return [shift(pair, "ctx", s) for s in range(1, lax.axis_size("ctx"))]


def weight_first(pair):
    return weight_ctx(pair), y_swap(pair)


def weight_second(px, py):
    n = lax.axis_size("ctx")
    return [y_swap(v[0])[None] for v in px], [shift(py[1], "ctx", s)[None] for s in range(1, n)]


def weight_blocks(pair, px, py, axy, bxy):
    near = [pair, *px]
    return (
        [(v, 0) for v in near]
        + [(v, 1) for v in near]
        + [(py, 0)]
        + [(v, 0) for v in axy]
        + [(py, 1)]
        + [(v, 0) for v in bxy]
    )


def block_spec(block, cols, at):
    array, index = block
    return pl.BlockSpec((None, array.shape[1], cols), lambda i, p: (index, 0, at(i)))


def arrays(blocks):
    return [array for array, _ in blocks]


def grad_first_y(groups):
    return y_swap(groups[1])


def grad_first_ctx(groups, anchors=()):
    lines = list(groups[3:])
    if anchors:
        lines = after(lines, anchors)
    return [shift(v, "ctx", -s) for s, v in enumerate(lines, start=1)]


def grad_first(groups):
    return grad_first_y(groups), grad_first_ctx(groups)


def grad_second(groups, far, sent):
    near, _, line, *_ = groups
    lines = [line, *sent]
    mine_sent = [
        shift(total([near[s], far[s]]).astype(BF), "ctx", -s) for s in range(1, near.shape[0])
    ]
    theirs_sent = y_swap(total([v[1] for v in lines]).astype(BF))
    return ([near[0], far[0]], [v[0] for v in lines]), (mine_sent, [theirs_sent])


def grad_last(kept, sent):
    mine, theirs = total(kept[0] + sent[0]), total(kept[1] + sent[1])
    return mine, core_swap(theirs.astype(BF)).astype(F32)


def cost(flops, transcendentals, bytes_accessed):
    return pl.CostEstimate(
        flops=flops // PACE,
        transcendentals=transcendentals // PACE,
        bytes_accessed=bytes_accessed // PACE,
    )


def whole(v):
    return pl.BlockSpec(v.shape, lambda *_: (0,) * v.ndim)


def window(places_ref, j, size):
    return pl.ds(pl.multiple_of(places_ref[j] * size, size), size)


def reorder(places_ref, row_refs, scratch, blocks):
    start = 0
    size = scratch.shape[1] // blocks
    for ref in row_refs:
        rows = ref.shape[0]
        for j in range(blocks):
            scratch[start : start + rows, j * size : (j + 1) * size] = ref[
                :, window(places_ref, j, size)
            ]
        start += rows


def turn(v):
    lane = lax.broadcasted_iota(jnp.int32, v.shape, 1)
    rolled = pltpu.roll(v, HD // 2, 1)
    return jnp.where(lane < HD // 2, -rolled, rolled)


def tiles_of(total_rows):
    tile = min(TILE_M, total_rows)
    return tile, total_rows // tile


def qkv_kernel(shards, blocks, places_ref, *refs):
    token_refs, refs = refs[:shards], refs[shards:]
    weight_refs, refs = refs[:blocks], refs[blocks:]
    gain_ref, bias_ref, cos_ref, sin_ref, rows_ref, q_ref, kv_ref, scratch = refs
    width = q_ref.shape[1]
    tokens = cos_ref.shape[0]
    piece = min(32, tokens)
    low = 0
    for ref in token_refs:

        def norm(i, _, ref=ref, low=low):
            at = pl.multiple_of(i * piece, piece)
            wide = ref[pl.ds(at, piece), :].astype(F32)
            scale = lax.rsqrt(jnp.mean(wide * wide, axis=1, keepdims=True) + EPSILON)
            rows_ref[pl.ds(low + at, piece), :] = (wide * scale * gain_ref[...]).astype(BF)
            return 0

        lax.fori_loop(0, ref.shape[0] // piece, norm, 0)
        low += ref.shape[0]
    reorder(places_ref, [rows_ref], scratch, blocks)
    tile, count = tiles_of(rows_ref.shape[0])
    cos = jnp.concatenate([cos_ref[...]] * (tile // tokens), axis=0)
    sin = jnp.concatenate([sin_ref[...]] * (tile // tokens), axis=0)

    def step(m, _):
        at = pl.ds(pl.multiple_of(m * tile, tile), tile)
        rows = scratch[at, :]
        for part in range(3):
            cols = slice(part * width, (part + 1) * width)
            weight = jnp.concatenate([w[:, cols] for w in weight_refs], axis=0)
            out = jnp.dot(rows, weight, preferred_element_type=F32) + bias_ref[:, cols]
            if part == 2:
                kv_ref[at, width:] = out.astype(BF)
                continue
            for h in range(width // HD):
                head = out[:, h * HD : (h + 1) * HD]
                head = (head * cos + turn(head) * sin).astype(BF)
                if part == 0:
                    q_ref[at, h * HD : (h + 1) * HD] = head
                else:
                    kv_ref[at, h * HD : (h + 1) * HD] = head
        return 0

    lax.fori_loop(0, count, step, 0)


def qkv_call(places, shards, weights, gain, bias, cos, sin, width):
    tokens, depth = shards[0].shape
    total_rows = tokens * len(shards)
    return pl.pallas_call(
        functools.partial(qkv_kernel, len(shards), len(weights)),
        grid_spec=pltpu.PrefetchScalarGridSpec(
            num_scalar_prefetch=1,
            grid=(1,),
            in_specs=[whole(s) for s in shards]
            + [block_spec(w, 3 * width, lambda i: 0) for w in weights]
            + [whole(v) for v in (gain, bias, cos, sin)],
            out_specs=[
                pl.BlockSpec((total_rows, depth), lambda i, p: (0, 0)),
                pl.BlockSpec((total_rows, width), lambda i, p: (0, 0)),
                pl.BlockSpec((total_rows, 2 * width), lambda i, p: (0, 0)),
            ],
            scratch_shapes=[pltpu.VMEM((total_rows, depth), BF)],
        ),
        out_shape=[
            jax.ShapeDtypeStruct((total_rows, depth), BF),
            jax.ShapeDtypeStruct((total_rows, width), BF),
            jax.ShapeDtypeStruct((total_rows, 2 * width), BF),
        ],
        cost_estimate=cost(
            flops=2 * total_rows * depth * 3 * width,
            transcendentals=0,
            bytes_accessed=2 * (2 * total_rows * depth + depth * 3 * width),
        ),
        name="qkv_rope",
    )(places, *shards, *arrays(weights), gain, bias, cos, sin)


def up_kernel(shards, blocks, experts, info_ref, *refs):
    row_refs, refs = refs[:shards], refs[shards:]
    gate_refs, up_refs, refs = refs[:blocks], refs[blocks : 2 * blocks], refs[2 * blocks :]
    small_ref, chosen_ref, act_ref, gate_ref, up_ref, scale_ref, scratch = refs
    step_n = pl.program_id(0)
    own = info_ref[blocks]
    units = info_ref[blocks + 1]
    tile, count = tiles_of(scratch.shape[0])

    @pl.when(step_n == 0)
    def _():
        tokens = row_refs[0].shape[0]
        for k, ref in enumerate(row_refs):
            logits = lax.dot_general(
                ref[...], small_ref[...], (((1,), (1,)), ((), ())), preferred_element_type=F32
            )
            lane = lax.broadcasted_iota(jnp.int32, logits.shape, 1)
            kept = jnp.where(lane < experts, logits, NEGATIVE)
            raised = jnp.exp(kept - jnp.max(kept, axis=1, keepdims=True))
            prob = raised / jnp.sum(raised, axis=1, keepdims=True)
            chosen = chosen_ref[k * tokens : (k + 1) * tokens, :].astype(F32)
            routed = jnp.sum(jnp.where(lane == own, chosen, 0.0), axis=1, keepdims=True)
            gate = jnp.sum(jnp.where(lane == own, prob, 0.0), axis=1, keepdims=True) * routed
            sig = jax.nn.sigmoid(
                jnp.sum(jnp.where(lane == experts, logits, 0.0), axis=1, keepdims=True)
            )
            place = lax.broadcasted_iota(jnp.int32, (tokens, HD), 1)
            scale_ref[k * tokens : (k + 1) * tokens, :] = jnp.where(
                place == 0, gate, jnp.where(place == 1, sig, routed)
            )
        reorder(info_ref, row_refs, scratch, blocks)

    def step(m, _):
        at = pl.ds(pl.multiple_of(m * tile, tile), tile)
        rows = scratch[at, :]
        gate = jnp.dot(
            rows, jnp.concatenate([w[...] for w in gate_refs], axis=0), preferred_element_type=F32
        )
        up = jnp.dot(
            rows, jnp.concatenate([w[...] for w in up_refs], axis=0), preferred_element_type=F32
        )
        gate_ref[at, :] = gate
        up_ref[at, :] = up
        col = lax.broadcasted_iota(jnp.int32, gate.shape, 1) + step_n * gate.shape[1]
        scale = jnp.where(col < units, scale_ref[at, 0:1], scale_ref[at, 1:2])
        act_ref[at, :] = (gate * jax.nn.sigmoid(gate) * up * scale).astype(BF)
        return 0

    lax.fori_loop(0, count, step, 0)


def up_call(info, shards, gates, ups, small, chosen, experts):
    tokens, depth = shards[0].shape
    total_rows, cols = tokens * len(shards), gates[0][0].shape[2]
    out = pl.BlockSpec((total_rows, TILE_N), lambda i, p: (0, i))
    return pl.pallas_call(
        functools.partial(up_kernel, len(shards), len(gates), experts),
        grid_spec=pltpu.PrefetchScalarGridSpec(
            num_scalar_prefetch=1,
            grid=(pl.cdiv(cols, TILE_N),),
            in_specs=[whole(s) for s in shards]
            + [block_spec(w, TILE_N, lambda i: i) for w in gates + ups]
            + [whole(small), whole(chosen)],
            out_specs=[out, out, out, pl.BlockSpec((total_rows, HD), lambda i, p: (0, 0))],
            scratch_shapes=[pltpu.VMEM((total_rows, depth), BF)],
        ),
        out_shape=[
            jax.ShapeDtypeStruct((total_rows, cols), BF),
            jax.ShapeDtypeStruct((total_rows, cols), F32),
            jax.ShapeDtypeStruct((total_rows, cols), F32),
            jax.ShapeDtypeStruct((total_rows, HD), F32),
        ],
        cost_estimate=cost(
            flops=4 * total_rows * depth * cols,
            transcendentals=total_rows * cols,
            bytes_accessed=2 * (total_rows * depth + 2 * depth * cols) + 10 * total_rows * cols,
        ),
        name="expert_up",
    )(info, *shards, *arrays(gates + ups), small, chosen)


def down_back_kernel(shards, blocks, cols, info_ref, *refs):
    row_refs, refs = refs[:shards], refs[shards:]
    weight_refs, refs = refs[:blocks], refs[blocks:]
    gate_ref, up_ref, scale_ref, dgate_ref, dup_ref, sums_ref, scratch = refs
    step_n = pl.program_id(0)
    units = info_ref[blocks + 1]
    tile, count = tiles_of(scratch.shape[0])

    @pl.when(step_n == 0)
    def _():
        reorder(info_ref, row_refs, scratch, blocks)
        sums_ref[...] = jnp.zeros_like(sums_ref)

    def step(m, _):
        at = pl.ds(pl.multiple_of(m * tile, tile), tile)
        back = jnp.dot(
            scratch[at, :],
            jnp.concatenate([w[...] for w in weight_refs], axis=0),
            preferred_element_type=F32,
        )
        gate, up = gate_ref[at, :], up_ref[at, :]
        sig = jax.nn.sigmoid(gate)
        act = gate * sig
        col = lax.broadcasted_iota(jnp.int32, gate.shape, 1) + step_n * gate.shape[1]
        inside = col < units
        touched = act * up * back
        expert_sum = jnp.sum(jnp.where(inside, touched, 0.0), axis=1, keepdims=True)
        shared_sum = jnp.sum(
            jnp.where(jnp.logical_not(inside) & (col < cols), touched, 0.0), axis=1, keepdims=True
        )
        place = lax.broadcasted_iota(jnp.int32, (tile, HD), 1)
        sums_ref[at, :] += jnp.where(
            place == 0, expert_sum * scale_ref[at, 2:3], jnp.where(place == 1, shared_sum, 0.0)
        )
        scaled = back * jnp.where(inside, scale_ref[at, 0:1], scale_ref[at, 1:2])
        dup_ref[at, :] = (scaled * act).astype(BF)
        dgate_ref[at, :] = (scaled * up * sig * (1.0 + gate * (1.0 - sig))).astype(BF)
        return 0

    lax.fori_loop(0, count, step, 0)


def down_back_call(info, shards, weights, gate, up, scales):
    tokens, depth = shards[0].shape
    total_rows, cols = gate.shape
    out = pl.BlockSpec((total_rows, TILE_N), lambda i, p: (0, i))
    return pl.pallas_call(
        functools.partial(down_back_kernel, len(shards), len(weights), cols),
        grid_spec=pltpu.PrefetchScalarGridSpec(
            num_scalar_prefetch=1,
            grid=(pl.cdiv(cols, TILE_N),),
            in_specs=[whole(s) for s in shards]
            + [block_spec(w, TILE_N, lambda i: i) for w in weights]
            + [out, out, whole(scales)],
            out_specs=[out, out, whole(scales)],
            scratch_shapes=[pltpu.VMEM((total_rows, depth), BF)],
        ),
        out_shape=[
            jax.ShapeDtypeStruct((total_rows, cols), BF),
            jax.ShapeDtypeStruct((total_rows, cols), BF),
            jax.ShapeDtypeStruct((total_rows, HD), F32),
        ],
        cost_estimate=cost(
            flops=2 * total_rows * depth * cols,
            transcendentals=total_rows * cols,
            bytes_accessed=2 * (total_rows * depth + depth * cols) + 12 * total_rows * cols,
        ),
        name="down_back",
    )(info, *shards, *arrays(weights), gate, up, scales)


def out_back_kernel(shards, blocks, places_ref, *refs):
    row_refs, refs = refs[:shards], refs[shards:]
    weight_refs, (out_ref, rows_ref, scratch) = refs[:blocks], refs[blocks:]
    tokens = row_refs[0].shape[0]
    for k, ref in enumerate(row_refs):
        rows_ref[k * tokens : (k + 1) * tokens, :] = ref[...]
    reorder(places_ref, row_refs, scratch, blocks)
    tile, count = tiles_of(scratch.shape[0])

    def step(m, _):
        at = pl.ds(pl.multiple_of(m * tile, tile), tile)
        out_ref[at, :] = jnp.dot(
            scratch[at, :],
            jnp.concatenate([w[...] for w in weight_refs], axis=0),
            preferred_element_type=F32,
        ).astype(BF)
        return 0

    lax.fori_loop(0, count, step, 0)


def out_back_call(places, shards, weights, width):
    tokens, depth = shards[0].shape
    total_rows = tokens * len(shards)
    return pl.pallas_call(
        functools.partial(out_back_kernel, len(shards), len(weights)),
        grid_spec=pltpu.PrefetchScalarGridSpec(
            num_scalar_prefetch=1,
            grid=(1,),
            in_specs=[whole(s) for s in shards]
            + [block_spec(w, width, lambda i: 3) for w in weights],
            out_specs=[
                pl.BlockSpec((total_rows, width), lambda i, p: (0, 0)),
                pl.BlockSpec((total_rows, depth), lambda i, p: (0, 0)),
            ],
            scratch_shapes=[pltpu.VMEM((total_rows, depth), BF)],
        ),
        out_shape=[
            jax.ShapeDtypeStruct((total_rows, width), BF),
            jax.ShapeDtypeStruct((total_rows, depth), BF),
        ],
        cost_estimate=cost(
            flops=2 * total_rows * depth * width,
            transcendentals=0,
            bytes_accessed=2 * (2 * total_rows * depth + depth * width),
        ),
        name="out_back",
    )(places, *shards, *arrays(weights))


def home_kernel(pairs, indices, start, places_ref, *refs):
    blocks = len(indices) // pairs
    act_refs, refs = refs[:pairs], refs[pairs:]
    weight_refs, refs = refs[: pairs * blocks], refs[pairs * blocks :]
    keep_ref, away_ref, held, sems = refs
    size, cols = held.shape[2:]

    def copy(p, j, source, index):
        return pltpu.make_async_copy(
            source.at[index, :, start : start + cols], held.at[p, j], sems.at[p, j]
        )

    for j in range(blocks):
        for p in range(pairs):
            copy(p, j, weight_refs[p * blocks + j], indices[p * blocks + j]).start()
    half = keep_ref.shape[0]
    tile, count = tiles_of(half)

    def step(j, _):
        for p in range(pairs):
            copy(p, j, weight_refs[p * blocks], 0).wait()
        to = window(places_ref, j, size)
        for h, out_ref in enumerate((keep_ref, away_ref)):
            for m in range(count):
                at = slice(h * half + m * tile, h * half + (m + 1) * tile)
                out = functools.reduce(
                    jnp.add,
                    [
                        lax.dot_general(
                            act_refs[p][at, :],
                            held[p, j],
                            (((1,), (1,)), ((), ())),
                            preferred_element_type=F32,
                        )
                        for p in range(pairs)
                    ],
                )
                out_ref[m * tile : (m + 1) * tile, to] = out.astype(BF)
        return 0

    lax.fori_loop(0, blocks, step, 0)


def project_home(places, acts, weights, depth, start=0):
    total_rows, cols = acts[0].shape
    blocks, size = len(weights[0]), weights[0][0][0].shape[1]
    every = [w for blocks_of in weights for w in blocks_of]
    half = pl.BlockSpec((total_rows // 2, depth), lambda i, p: (0, 0))
    keep, away = pl.pallas_call(
        functools.partial(home_kernel, len(acts), [i for _, i in every], start),
        grid_spec=pltpu.PrefetchScalarGridSpec(
            num_scalar_prefetch=1,
            grid=(1,),
            in_specs=[whole(a) for a in acts]
            + [pl.BlockSpec(memory_space=pl.ANY)] * (len(acts) * blocks),
            out_specs=[half, half],
            scratch_shapes=[
                pltpu.VMEM((len(acts), blocks, size, cols), BF),
                pltpu.SemaphoreType.DMA((len(acts), blocks)),
            ],
        ),
        out_shape=[jax.ShapeDtypeStruct((total_rows // 2, depth), BF)] * 2,
        cost_estimate=cost(
            flops=2 * total_rows * depth * cols * len(acts),
            transcendentals=0,
            bytes_accessed=2 * (total_rows * depth + len(acts) * cols * (depth + total_rows)),
        ),
        name="project_home",
    )(places, *acts, *arrays(every))
    return keep, away


def weight_grad_kernel(n, lists, places_ref, *refs):
    row_refs, out_refs = [], refs[-(2 + n) :]
    at = 0
    for count in lists:
        row_refs.append(refs[at : at + count])
        at += count
    part_refs = refs[at : at + len(lists)]
    j = pl.program_id(0)
    low = 0
    for rows, part in zip(row_refs, part_refs):
        left = jnp.concatenate([r[...] for r in rows], axis=0)
        out = lax.dot_general(
            left, part[...], (((0,), (0,)), ((), ())), preferred_element_type=F32
        ).astype(BF)
        cols = slice(low, low + part.shape[1])
        low += part.shape[1]
        for g, ref in enumerate(out_refs):
            first = g * n if g < 2 else 2 * n + (g - 2) * 2
            last = first + (n if g < 2 else 2)

            @pl.when((j >= first) & (j < last))
            def _(ref=ref, out=out, cols=cols):
                ref[0, :, cols] = out


def weight_grad(order, pairs):
    n = lax.axis_size("ctx")
    blocks = 4 * n
    depth = pairs[0][0][0].shape[1]
    size = depth // blocks
    cols = sum(p.shape[1] for _, p in pairs)
    total_rows = pairs[0][1].shape[0]
    in_specs, operands = [], []
    for rows, _ in pairs:
        for r in rows:
            in_specs.append(pl.BlockSpec((r.shape[0], size), lambda j, o: (0, o[j])))
            operands.append(r)
    for _, part in pairs:
        in_specs.append(whole(part))
        operands.append(part)
    out_specs, out_shape = [], []
    for g in range(2 + n):
        first = g * n if g < 2 else 2 * n + (g - 2) * 2
        count = n if g < 2 else 2
        out_specs.append(
            pl.BlockSpec(
                (1, size, cols),
                lambda j, o, first=first, count=count: (
                    jnp.clip(j - first, 0, count - 1),
                    0,
                    0,
                ),
            )
        )
        out_shape.append(jax.ShapeDtypeStruct((count, size, cols), BF))
    return pl.pallas_call(
        functools.partial(weight_grad_kernel, n, [len(rows) for rows, _ in pairs]),
        grid_spec=pltpu.PrefetchScalarGridSpec(
            num_scalar_prefetch=1, grid=(blocks,), in_specs=in_specs, out_specs=out_specs
        ),
        out_shape=out_shape,
        cost_estimate=cost(
            flops=2 * total_rows * depth * cols,
            transcendentals=0,
            bytes_accessed=2 * (total_rows * (depth + cols) + depth * cols),
        ),
        name="weight_grad",
    )(order, *operands)


def probabilities(query, keys, length, x, scale):
    tokens, count = query.shape[0], keys.shape[0]
    scores = (
        lax.dot_general(query, keys, (((1,), (1,)), ((), ())), preferred_element_type=F32) * scale
    )
    row = lax.broadcasted_iota(jnp.int32, (tokens, count), 0) + x * tokens
    col = lax.broadcasted_iota(jnp.int32, (tokens, count), 1)
    place = jnp.zeros((tokens, count), jnp.int32)
    for s in range(count // tokens):
        inside = (col >= s * tokens) & (col < (s + 1) * tokens)
        place = jnp.where(inside, col - s * tokens + (x - s) * tokens, place)
    allowed = (place >= 0) & (place <= row) & (place < length)
    masked = jnp.where(allowed, scores, NEGATIVE)
    top = jnp.max(masked, axis=1, keepdims=True)
    weights = jnp.where(allowed, jnp.exp(masked - top), 0.0)
    return weights / jnp.sum(weights, axis=1, keepdims=True)


def attend_kernel(scale, info_ref, q_ref, *refs):
    kv_refs, out_ref = refs[:-1], refs[-1]
    group = pl.program_id(0)
    width = q_ref.shape[1]
    for h in range(width // HD):
        at = h * HD
        keys = jnp.concatenate([r[:, at : at + HD] for r in kv_refs], axis=0)
        values = jnp.concatenate([r[:, width + at : width + at + HD] for r in kv_refs], axis=0)
        prob = probabilities(
            q_ref[:, at : at + HD], keys, info_ref[group], info_ref[pl.num_programs(0)], scale
        )
        out_ref[:, at : at + HD] = jnp.dot(
            prob.astype(BF), values, preferred_element_type=F32
        ).astype(BF)


def attend_call(info, query, kvs, tokens, scale):
    total, width = query.shape
    groups = total // tokens
    return pl.pallas_call(
        functools.partial(attend_kernel, scale),
        grid_spec=pltpu.PrefetchScalarGridSpec(
            num_scalar_prefetch=1,
            grid=(groups,),
            in_specs=[pl.BlockSpec((tokens, width), lambda i, info: (i, 0))]
            + [pl.BlockSpec((tokens, 2 * width), lambda i, info: (i, 0)) for _ in kvs],
            out_specs=pl.BlockSpec((tokens, width), lambda i, info: (i, 0)),
        ),
        out_shape=jax.ShapeDtypeStruct((total, width), BF),
        cost_estimate=cost(
            flops=4 * total * width * tokens * len(kvs),
            transcendentals=total * tokens * len(kvs) * width // HD,
            bytes_accessed=2 * total * width * (2 + 2 * len(kvs)),
        ),
        name="attend",
    )(info, query, *kvs)


def unrope(grad, cos, sin):
    return grad * cos - turn(grad * sin)


def attend_back_kernel(scale, count, info_ref, q_ref, da_ref, *refs):
    kv_refs = refs[:count]
    cos_ref, sin_ref = refs[count : count + 2]
    dq_ref = refs[count + 2]
    dkv_refs = refs[count + 3 :]
    group = pl.program_id(0)
    tokens, width = q_ref.shape
    for h in range(width // HD):
        at = h * HD
        keys = jnp.concatenate([r[:, at : at + HD] for r in kv_refs], axis=0)
        values = jnp.concatenate([r[:, width + at : width + at + HD] for r in kv_refs], axis=0)
        query, grad = q_ref[:, at : at + HD], da_ref[:, at : at + HD]
        prob = probabilities(
            query, keys, info_ref[group], info_ref[pl.num_programs(0)], scale
        )
        dprob = lax.dot_general(
            grad, values, (((1,), (1,)), ((), ())), preferred_element_type=F32
        )
        row_dot = jnp.sum(prob * dprob, axis=1, keepdims=True)
        dscore = (prob * (dprob - row_dot)).astype(BF)
        dq = jnp.dot(dscore, keys, preferred_element_type=F32) * scale
        dq_ref[:, at : at + HD] = unrope(dq, cos_ref[:tokens], sin_ref[:tokens]).astype(BF)
        dk = (
            lax.dot_general(dscore, query, (((0,), (0,)), ((), ())), preferred_element_type=F32)
            * scale
        )
        dv = lax.dot_general(
            prob.astype(BF), grad, (((0,), (0,)), ((), ())), preferred_element_type=F32
        )
        for s in range(count):
            part = slice(s * tokens, (s + 1) * tokens)
            dkv_refs[s][:, at : at + HD] = unrope(dk[part], cos_ref[part], sin_ref[part]).astype(
                dkv_refs[s].dtype
            )
            dkv_refs[s][:, width + at : width + at + HD] = dv[part].astype(dkv_refs[s].dtype)


def attend_back_call(info, query, grad, kvs, cos, sin, tokens, scale):
    total, width = query.shape
    groups, count = total // tokens, len(kvs)
    one = pl.BlockSpec((tokens, width), lambda i, info: (i, 0))
    two = pl.BlockSpec((tokens, 2 * width), lambda i, info: (i, 0))
    table = pl.BlockSpec(cos.shape, lambda i, info: (0, 0))
    return pl.pallas_call(
        functools.partial(attend_back_kernel, scale, count),
        grid_spec=pltpu.PrefetchScalarGridSpec(
            num_scalar_prefetch=1,
            grid=(groups,),
            in_specs=[one, one] + [two] * count + [table, table],
            out_specs=[one] + [two] * count,
        ),
        out_shape=[jax.ShapeDtypeStruct((total, width), BF)]
        + [jax.ShapeDtypeStruct((total, 2 * width), F32 if s == 0 else BF) for s in range(count)],
        cost_estimate=cost(
            flops=10 * total * width * tokens * count,
            transcendentals=total * tokens * count * width // HD,
            bytes_accessed=2 * total * width * (3 + 5 * count),
        ),
        name="attend_back",
    )(info, query, grad, *kvs, cos, sin)


def rope_tables(positions):
    frequency = ROPE_BASE ** (-jnp.arange(0, HD, 2, dtype=F32) / HD)
    angles = positions[:, None] * frequency[None, :]
    return (
        jnp.concatenate([jnp.cos(angles), jnp.cos(angles)], axis=1),
        jnp.concatenate([jnp.sin(angles), jnp.sin(angles)], axis=1),
    )


def dot_t(a, b):
    return lax.dot_general(a, b, (((1,), (1,)), ((), ())), preferred_element_type=F32)


def norm_scale(values):
    return lax.rsqrt(jnp.mean(values * values, axis=1, keepdims=True) + EPSILON)


def norm_back(values, scale, gain, grads):
    weighted = grads * gain
    grad_values = scale * weighted - values * scale**3 * jnp.mean(
        weighted * values, axis=1, keepdims=True
    )
    return grad_values, jnp.sum(grads * values * scale, axis=0)


def body(
    tokens,
    teacher,
    lengths,
    routes,
    attn_gain,
    ffn_gain,
    router_weight,
    shared_gate,
    qkv_weight,
    qkv_bias,
    out_weight,
    shared_up,
    shared_down,
    expert_up,
    expert_down,
):
    tok_rows, model_width = tokens.shape[1:]
    nz, n = lax.axis_size("exp"), lax.axis_size("ctx")
    z, x, dp = lax.axis_index("exp"), lax.axis_index("ctx"), lax.axis_index("dp")
    c = dp % 2
    devices = lax.axis_size(("dp", "ctx", "exp"))
    seq_len = tok_rows * n
    experts = router_weight.shape[1]
    own_expert = 2 * z + c
    rows_w = qkv_weight.shape[0]
    width = qkv_weight.shape[2] // 2
    units, shared = expert_down.shape[2], shared_down.shape[1] // 2
    score_scale = HD ** (-0.5)
    first = c == 0

    def halves(v, axis):
        size = v.shape[axis] // 2
        low = lax.slice_in_dim(v, 0, size, axis=axis)
        high = lax.slice_in_dim(v, size, 2 * size, axis=axis)
        return jnp.where(first, low, high), jnp.where(first, high, low)

    token_mine = gather_exp(tokens[0])

    lanes = pl.cdiv(experts + 1, 16) * 16
    span = model_width // devices
    piece = jnp.concatenate(
        [router_weight.T, shared_gate[None], attn_gain[None], ffn_gain[None]], axis=0
    )
    held = pl.cdiv(experts + 3, 16) * 16
    piece = jnp.pad(piece, ((0, held - experts - 3), (0, tok_rows - span)))
    chosen = (
        (routes[0][None, :, :] == jnp.arange(lanes, dtype=jnp.int32)[:, None, None])
        .any(axis=2)
        .astype(BF)
    )
    grouped = gather_group(jnp.concatenate([piece, chosen], axis=0))
    vectors = gather_plane(grouped[:, :, : experts + 3, :span])
    chosen = grouped[:, :, held:]
    chosen = jnp.where(first, chosen, chosen[::-1])
    chosen_all = jnp.swapaxes(chosen, 2, 3).reshape(2 * nz * tok_rows, lanes)

    attn_halves = [
        jnp.concatenate([q[:, 0], q[:, 1], q[:, 2], o], axis=1)
        for q, o in zip(halves(qkv_weight, 2), halves(out_weight, 1))
    ]
    blank = jnp.zeros((rows_w, -(units + shared) % HD), BF)

    def pack(experts_of, shared_of):
        mine, other = [
            jnp.concatenate([e, s, blank], axis=1) for e, s in zip(experts_of, shared_of)
        ]
        return jnp.stack([mine, core_swap(other)])

    def up_pair(anchors, part):
        up_e, up_s = after((expert_up, shared_up), anchors)
        return pack(
            [v[:, 0] for v in halves(up_e[:, :, part * units : (part + 1) * units], 1)],
            halves(up_s[:, part], 1),
        )

    def down_pair(anchors):
        down_e, down_s = after((expert_down, shared_down), anchors)
        return pack([v[:, 0] for v in halves(down_e, 1)], halves(down_s, 1))

    attn_pair = jnp.stack([attn_halves[0], core_swap(attn_halves[1])])
    attn_near = weight_first(attn_pair)
    attn_far = weight_second(*attn_near)
    gate_pair = up_pair([attn_pair], 0)
    gate_near = weight_first(after((gate_pair,), attn_near)[0])
    token_mine, attn_near, attn_far, gate_pair, vectors = meet(
        token_mine, attn_near, attn_far, gate_pair, vectors
    )
    attn_weight = weight_blocks(attn_pair, *attn_near, *attn_far)
    vectors = vectors.transpose(4, 1, 2, 0, 3, 5).reshape(experts + 3, model_width)
    small = jnp.pad(vectors[: experts + 1], ((0, lanes - experts - 1), (0, 0)))
    attn_factor = vectors[experts + 1].astype(F32)[None]
    ffn_factor = vectors[experts + 2].astype(F32)[None]

    count_valid = jnp.sum(lengths).astype(F32)
    factor = lengths.shape[0] * seq_len / count_valid
    positions = x * tok_rows + jnp.arange(tok_rows, dtype=jnp.int32)
    own_length = lengths[dp * nz + z]
    valid_rows = (positions < own_length).astype(F32)[:, None]
    shard_dp = jnp.repeat(jnp.stack([dp, dp ^ 1]), nz)
    shard_z = jnp.tile(jnp.arange(nz, dtype=jnp.int32), 2)
    info = jnp.concatenate([lengths[shard_dp * nz + shard_z], x[None].astype(jnp.int32)])
    key_places = jnp.concatenate([positions - s * tok_rows for s in range(n)])
    cos_all, sin_all = rope_tables(key_places.astype(F32))
    cos, sin = cos_all[:tok_rows], sin_all[:tok_rows]

    def place(dy, dc, s):
        return (((dp // 2) ^ dy) * 2 + (c ^ dc)) * n + lax.rem(x + n - s, n)

    blocks = 4 * n
    places = jnp.stack(
        [place(dy, dc, s) for dy in range(2) for dc in range(2) for s in range(n)]
    ).astype(jnp.int32)
    order = jnp.stack(
        [place(dy, 0, s) for dy in range(2) for s in range(n)]
        + [place(dy, 1, s) for s in range(n) for dy in range(2)]
    ).astype(jnp.int32)
    facts = jnp.concatenate(
        [places, jnp.stack([own_expert, jnp.int32(units)]).astype(jnp.int32)]
    )

    inputs = tokens[0].astype(F32)
    attn_scale = norm_scale(inputs)
    bias = jnp.where(first, qkv_bias[:, :width], qkv_bias[:, width:])
    attn_rows, query, kv = qkv_call(
        places,
        both_cores(token_mine),
        attn_weight,
        attn_factor,
        bias.astype(F32).reshape(1, 3 * width),
        cos,
        sin,
        width,
    )
    kvs = [kv] + [
        lax.ppermute(kv, "ctx", [(i, i + s) for i in range(n - s)]) for s in range(1, n)
    ]
    upper_pair = up_pair([kv], 1)
    kvs, gate_near, upper_pair = meet(kvs, gate_near, upper_pair)
    gate_far = weight_second(*gate_near)
    upper_near = weight_first(upper_pair)
    attended = attend_call(info, query, kvs, tok_rows, score_scale)
    keep, away = project_home(places, [attended], [attn_weight], model_width, 3 * width)
    keep, away, gate_far = meet(keep, away, gate_far)
    gate_weight = weight_blocks(gate_pair, *gate_near, *gate_far)
    both, parts = home_start(keep, core_swap(away))
    lower_pair = down_pair([both])
    parts, upper_near, lower_pair = meet(parts, upper_near, lower_pair)
    upper_far = weight_second(*upper_near)
    lower_near = weight_first(lower_pair)
    hidden = inputs + total(parts)

    ffn_scale = norm_scale(hidden)
    normed_ffn = (hidden * ffn_scale * ffn_factor).astype(BF)
    ffn_mine, upper_far, lower_near = meet(gather_exp(normed_ffn), upper_far, lower_near)
    up_weight = weight_blocks(upper_pair, *upper_near, *upper_far)
    lower_far = weight_second(*lower_near)
    ffn_shards = both_cores(ffn_mine)
    act_scaled, gate_pre, up_pre, scales = up_call(
        facts, ffn_shards, gate_weight, up_weight, small, chosen_all, experts
    )
    down_weight = weight_blocks(lower_pair, *lower_near, *lower_far)
    keep, away = project_home(places, [act_scaled], [down_weight], model_width)
    _, parts = home_start(keep, core_swap(away))
    result = hidden + total(parts)
    grad_result = factor * valid_rows * (result - teacher[0])

    back_shards = gather_rows(grad_result.astype(BF))
    down_groups = weight_grad(order, [(back_shards, act_scaled)])
    down_moves = grad_first(down_groups)
    back_shards, down_groups = meet(back_shards, down_groups)
    grad_gate_pre, grad_up_pre, sums = down_back_call(
        facts, back_shards, down_weight, gate_pre, up_pre, scales
    )
    keep, away = project_home(
        places, [grad_gate_pre, grad_up_pre], [gate_weight, up_weight], model_width
    )
    got, down_moves = meet(core_swap(away), down_moves)
    both, parts = home_start(keep, got)
    own_col = (jnp.arange(experts, dtype=jnp.int32) == own_expert).astype(F32)[:, None]
    scalar_rows = jnp.concatenate(
        [own_col * sums[:, 0][None], sums[:, 1][None]], axis=0
    ).reshape(experts + 1, 2, nz, tok_rows)
    scalar_both = scalar_rows[:, 0] + core_swap(scalar_rows[:, 1])
    grad_gate_pre, grad_up_pre = after((grad_gate_pre, grad_up_pre), [both])
    gate_groups = weight_grad(order, [(ffn_shards, grad_gate_pre)])
    gate_moves = grad_first(gate_groups)
    (scalar_both,) = after((jnp.swapaxes(scalar_both, 0, 1),), [gate_groups])
    scalar_own = own_of(scalar_both, "exp", nz, z)
    down_kept, down_moves = grad_second(down_groups, *down_moves)
    parts, scalar_own, gate_groups, down_moves = meet(parts, scalar_own, gate_groups, down_moves)
    grad_normed = total(parts)

    own_logits = dot_t(normed_ffn, small)
    probs = jax.nn.softmax(own_logits[:, :experts], axis=1)
    sig = jax.nn.sigmoid(own_logits[:, experts])
    grad_probs = scalar_own[:experts].T
    grad_logits = probs * (grad_probs - jnp.sum(probs * grad_probs, axis=1, keepdims=True))
    grad_sig = scalar_own[experts] * sig * (1.0 - sig)
    grad_small = jnp.concatenate([grad_logits, grad_sig[:, None]], axis=1)
    normed_wide = normed_ffn.astype(F32)
    grad_small_full = lax.dot_general(
        grad_small, normed_wide, (((0,), (0,)), ((), ())), precision=HIGHEST
    )
    grad_normed = grad_normed + jnp.dot(
        grad_small, small[: experts + 1].astype(F32), precision=HIGHEST
    )
    grad_hidden_norm, grad_ffn_full = norm_back(hidden, ffn_scale, ffn_factor, grad_normed)
    grad_hidden = grad_result + grad_hidden_norm
    grad_hidden_low = grad_hidden.astype(BF)

    back_mine = gather_exp(grad_hidden_low)
    grad_up_pre = after((grad_up_pre,), [grad_hidden_low])[0]
    up_groups = weight_grad(order, [(ffn_shards, grad_up_pre)])
    back_mine, up_groups, gate_moves = meet(back_mine, up_groups, gate_moves)
    up_y = grad_first_y(up_groups)
    gate_kept, gate_moves = grad_second(gate_groups, *gate_moves)
    grad_attended, attn_back = out_back_call(places, both_cores(back_mine), attn_weight, width)
    grad_query, grad_kv, *sent = attend_back_call(
        info, query, grad_attended, kvs, cos_all, sin_all, tok_rows, score_scale
    )
    sent = [
        lax.ppermute(v, "ctx", [(i + s, i) for i in range(n - s)])
        for s, v in enumerate(sent, start=1)
    ]
    sent, gate_moves = meet(sent, gate_moves)
    up_ctx = grad_first_ctx(up_groups, [sent])
    grad_kv = total([grad_kv, *sent])
    grad_projected = jnp.concatenate([grad_query, grad_kv.astype(BF)], axis=1)
    keep, away = project_home(places, [grad_projected], [attn_weight], model_width)
    both, parts = home_start(keep, core_swap(away))
    up_y, up_ctx = after((up_y, up_ctx), [both])
    up_kept, up_moves = grad_second(up_groups, up_y, up_ctx)
    attn_groups = weight_grad(
        order,
        [
            ([attn_rows], after((grad_projected,), [up_y, up_ctx])[0]),
            ([attn_back], attended),
        ],
    )
    attn_moves = grad_first(attn_groups)
    down_kept, gate_kept = after((down_kept, gate_kept), [attn_groups])
    grad_down = grad_last(down_kept, down_moves)
    grad_gate = grad_last(gate_kept, gate_moves)
    bias_own = jnp.sum(grad_projected.astype(F32), axis=0).reshape(3, width)
    columns = 2 * nz
    column = lax.broadcasted_iota(jnp.int32, (3, columns * width), 1)
    bias_wide = jnp.where(column // width == own_expert, jnp.tile(bias_own, (1, columns)), 0.0)
    parts, attn_groups = meet(parts, attn_groups)
    grad_normed_attn = total(parts)
    grad_inputs_norm, grad_attn_full = norm_back(inputs, attn_scale, attn_factor, grad_normed_attn)
    grad_tokens = (grad_hidden + grad_inputs_norm)[None]
    vectors = jnp.concatenate(
        [bias_wide, grad_attn_full[None], grad_small_full, grad_ffn_full[None]], axis=0
    )
    vectors = scatter_everywhere(
        vectors.reshape(-1, 2, 2, n, nz, span).transpose(3, 1, 2, 4, 0, 5)
    )
    attn_kept, attn_moves = grad_second(attn_groups, *attn_moves)
    grad_up = grad_last(up_kept, up_moves)
    grad_attn = grad_last(attn_kept, attn_moves)

    def join(pair, axis):
        mine, theirs = pair
        return jnp.concatenate(
            [jnp.where(first, mine, theirs), jnp.where(first, theirs, mine)], axis=axis
        )

    grad_qkv = join([g[:, : 3 * width].reshape(rows_w, 3, width) for g in grad_attn], 2)
    grad_out = join([g[:, 3 * width :] for g in grad_attn], 1)
    grad_expert_up = join(
        [
            jnp.concatenate([g[:, :units], u[:, :units]], axis=1)[:, None]
            for g, u in zip(grad_gate, grad_up)
        ],
        1,
    )
    grad_shared_up = join(
        [
            jnp.concatenate([g[:, None, units : units + shared], u[:, None, units : units + shared]], axis=1)
            for g, u in zip(grad_gate, grad_up)
        ],
        2,
    )
    grad_expert_down = join([g[:, None, :units] for g in grad_down], 1)
    grad_shared_down = join([g[:, units : units + shared] for g in grad_down], 1)
    attn_own, ffn_own = vectors[:4], vectors[4:]
    return (
        result.astype(BF)[None],
        grad_tokens,
        attn_own[3],
        ffn_own[experts + 1],
        ffn_own[:experts].T,
        ffn_own[experts],
        grad_qkv,
        jnp.stack([attn_own[0], attn_own[2]]),
        attn_own[1],
        grad_out,
        grad_shared_up,
        grad_shared_down,
        grad_expert_up,
        grad_expert_down,
    )


def solution(mesh):
    every = ("dp", "ctx", "exp")
    return jax.shard_map(
        body,
        mesh=mesh,
        in_specs=(
            P(("dp", "exp"), "ctx", None),
            P(("dp", "exp"), "ctx", None),
            P(),
            P(("dp", "exp"), "ctx", None),
            P(every),
            P(every),
            P(every, None),
            P(every),
            P(("dp", "ctx"), None, "exp"),
            P(None, "exp"),
            P(("dp", "ctx"), "exp"),
            P(("dp", "ctx"), None, "exp"),
            P(("dp", "ctx"), "exp"),
            P(("dp", "ctx"), "exp", None),
            P(("dp", "ctx"), "exp", None),
        ),
        out_specs=(
            P(("dp", "exp"), "ctx", None),
            P(("dp", "exp"), "ctx", None),
            P(every),
            P(every),
            P(every, None),
            P(every),
            P(("dp", "ctx"), None, "exp"),
            P(None, every),
            P(every),
            P(("dp", "ctx"), "exp"),
            P(("dp", "ctx"), None, "exp"),
            P(("dp", "ctx"), "exp"),
            P(("dp", "ctx"), "exp", None),
            P(("dp", "ctx"), "exp", None),
        ),
        check_vma=False,
    )
```

time: 1560 us -> 967 us (0.62)
  local copies, waits for them, and re-layouts: 387 us -> 98.4 us
  waiting for transfers between devices: 596 us -> 369 us
  Pallas kernels: 29.2 us -> 238 us
  matrix products: 182 us -> 2.21 us
  starting transfers between devices: 245 us -> 108 us
  blocking collectives: 0 us -> 50.1 us
    ppermute x66 -> x27, waiting for transfers between devices: 422 us -> 53.8 us  [shift(): return lax.ppermute(v, axis, [(i, (i + s) % n) for i in range(n)])]
    pallas_call x1 -> x12, Pallas kernels: 7.12 us -> 216 us  [the longest x4 69.4 us: weight_grad(): pl.pallas_call(functools.partial(weight_grad_kernel, n, [len(rows) for ro...]
    ppermute x66 -> x27, starting transfers between devices: 142 us -> 32.9 us  [shift(): return lax.ppermute(v, axis, [(i, (i + s) % n) for i in range(n)])]
    dot_general x10 -> x1, matrix products: 107 us -> 1.66 us  [body(): jnp.dot(grad_small, small[:experts + 1].astype(F32), precision=HIGHEST)]
    all_to_all x0 -> x7, waiting for transfers between devices: none -> 87.7 us  [exchange(): return lax.all_to_all(v, 'exp', split_axis=0, concat_axis=0, tiled=True)]
    dot_general x12 -> x1, matrix products: 75.2 us -> 0.24 us  [dot_t(): lax.dot_general(a, b, (((1,), (1,)), ((), ())), preferred_element_type=F32)]
    unnamed x354 -> x129, local copies, waits for them, and re-layouts: 100 us -> 27.2 us
    dynamic_slice x12 -> x2, local copies, waits for them, and re-layouts: 70 us -> 0.02 us  [scatter_everywhere(): v = pick(v, c, 0, False) + core_swap(pick(v, 1 - c, 0, False))]
  transfers between devices with their start and end apart: 124 -> 73, of which waited for: 46 -> 33; matrix products, arithmetic and copies ran while one was open for 30% -> 15% of each run, Pallas kernels for 1% -> 20%
where the time goes in v2:
time: 967 us; the launch traced here: 956 us
  waiting for transfers between devices  369 us (38%)
  Pallas kernels  238 us (25%)
  starting transfers between devices  108 us (11%)
  local copies, waits for them, and re-layouts  98.4 us (10%)
  other arithmetic  87.1 us (9%)
  blocking collectives  50.1 us (5%)
    ppermute x18, waiting for transfers between devices, y_swap(): return lax.ppermute(v, 'dp', [(i, i ^ 2) for i in range(n)])  166 us
    all_to_all x7, waiting for transfers between devices, exchange(): return lax.all_to_all(v, 'exp', split_axis=0, concat_axis=0, tiled=True)  87.7 us
    pallas_call x4, Pallas kernels, weight_grad(): pl.pallas_call(functools.partial(weight_grad_kernel, n, [len(rows) for ro...  69.4 us
    pallas_call x4, Pallas kernels, project_home(): pl.pallas_call(functools.partial(home_kernel, len(acts), [i for _, i in e...  64 us
    ppermute x27, waiting for transfers between devices, shift(): return lax.ppermute(v, axis, [(i, (i + s) % n) for i in range(n)])  53.8 us
    all_to_all x1, blocking collectives, exchange(): return lax.all_to_all(v, 'exp', split_axis=0, concat_axis=0, tiled=True)  50.1 us
    ppermute x27, starting transfers between devices, shift(): return lax.ppermute(v, axis, [(i, (i + s) % n) for i in range(n)])  32.9 us
    all_to_all x7, starting transfers between devices, exchange(): return lax.all_to_all(v, 'exp', split_axis=0, concat_axis=0, tiled=True)  32 us
  transfers between devices with their start and end apart: 73, of which 33 were waited for; matrix products, arithmetic and copies ran while one was open for 15% of the time, Pallas kernels for 20%

profile of v2, /device:TPU:1, one launch (start us, length us, event | category | flops | bytes accessed | tf_op | source)
XLA Modules:
  0.0 956.5 jit_solution(16393365605216648130)
XLA Ops:
  13.4 4.5 all-to-all-start
  28.4 3.3 concatenate.142
  33.2 13.6 %collective-permute-done.1.refs_3_.refs_5_.refs_2_.refs_4_ = bf16[2,256,1024]{2,1,0:T(8,128)(2,1)S(1)} collective-permute-done((bf16[2,256,1024]{2,1,0:T(8,128)(2,1)S(1)}, bf16[2,256,1024]{2,1,0:T(8,128)(2,1)S(1)}, u32[]{:S(2)}, u32[]{:S(2)}) %collective-permute-start.1) | collective-permute-done | bytes 1048608 | tf_op jit(solution)/shard_map/ppermute | solution.py:34
  50.8 3.2 concatenate.141
  55.9 3.5 collective-permute-done.3
  60.2 6.0 all-to-all-done
  74.2 13.5 %qkv_rope.1 = (bf16[1024,2048]{1,0:T(8,128)(2,1)}, bf16[1024,256]{1,0:T(8,128)(2,1)}, bf16[1024,512]{1,0:T(8,128)(2,1)}) custom-call(s32[8]{0:T(128)} %stack.97.places_ref, bf16[512,2048]{1,0:T(8,128)(2,1)} %bitcast.13.refs_0_, bf16[512,2048]{1,0:T(8,128)(2,1)} %collective-permute-done.12.refs_1_, bf16[2,256,1024]{2,1,0:T(8,128)(2,1)} %copy-done.1, ...), custom_call_target="tpu_custom_call" | custom-call | flops 402653184 | bytes 1441792 | tf_op jit(solution)/shard_map/qkv_rope/pallas_call | solution.py:268
  92.5 3.2 concatenate.149
  96.0 3.1 collective-permute-start.13
  99.2 3.2 concatenate.148
  102.4 3.2 pad_maximum_fusion.6.refs_10_.refs_12_
  105.6 14.9 %collective-permute-done.14.refs_3_.refs_5_ = bf16[2,256,2176]{2,1,0:T(8,128)(2,1)} collective-permute-done((bf16[2,256,2176]{2,1,0:T(8,128)(2,1)S(1)}, bf16[2,256,2176]{2,1,0:T(8,128)(2,1)}, u32[]{:S(2)}, u32[]{:S(2)}) %collective-permute-start.14) | collective-permute-done | bytes 2228256 | tf_op jit(solution)/shard_map/ppermute | solution.py:34
  121.4 20.5 %collective-permute-done.13.refs_1_ = bf16[1024,512]{1,0:T(8,128)(2,1)} collective-permute-done((bf16[1024,512]{1,0:T(8,128)(2,1)S(1)}, bf16[1024,512]{1,0:T(8,128)(2,1)}, u32[]{:S(2)}, u32[]{:S(2)}) %collective-permute-start.13) | collective-permute-done | bytes 1048608 | tf_op jit(solution)/shard_map/ppermute | solution.py:923
  151.5 9.5 attend.1.refs_0_.refs_3_
  161.1 7.3 project_home.4
  169.7 4.4 collective-permute-done.18
  175.8 4.0 collective-permute-done.19
  179.8 3.7 add_convert_fusion.3
  183.5 4.8 all-to-all-start.1
  199.7 36.6 %all-to-all-done.1 = bf16[4,128,2048]{2,1,0:T(8,128)(2,1)} async-done(((bf16[4,128,2048]{2,1,0:T(8,128)(2,1)}), bf16[4,128,2048]{2,1,0:T(8,128)(2,1)}, u32[]{:S(2)}, u32[]{:S(2)}) %all-to-all-start.1) | async-done | bytes 2097184 | tf_op jit(solution)/shard_map/all_to_all | solution.py:46
  243.6 4.4 all-to-all-start.2
  253.8 66.6 %collective-permute-done.23 = bf16[256,2176]{1,0:T(8,128)(2,1)S(1)} collective-permute-done((bf16[256,2176]{1,0:T(8,128)(2,1)S(1)}, bf16[256,2176]{1,0:T(8,128)(2,1)S(1)}, u32[]{:S(2)}, u32[]{:S(2)}) %collective-permute-start.23) | collective-permute-done | bytes 1114144 | tf_op jit(solution)/shard_map/ppermute | solution.py:29
  323.2 2.8 collective-permute-start.27
  326.0 2.4 slice_bitcast_fusion.13
  336.6 31.8 %expert_up.1 = (bf16[1024,2176]{1,0:T(8,128)(2,1)}, f32[1024,2176]{1,0:T(8,128)}, f32[1024,2176]{1,0:T(8,128)}, f32[1024,128]{1,0:T(8,128)}) custom-call(s32[10]{0:T(128)} %concatenate.152.info_ref, bf16[512,2048]{1,0:T(8,128)(2,1)} %bitcast.56.refs_0_, bf16[512,2048]{1,0:T(8,128)(2,1)} %copy-done.7, bf16[2,256,2176]{2,1,0:T(8,128)(2,1)} %copy-done.5, ...), custom_call_target="tpu_custom_call" | custom-call | flops 2281701376 | bytes 5537792 | tf_op jit(solution)/shard_map/expert_up/pallas_call | solution.py:352
  368.4 17.6 %project_home.5 = (bf16[512,2048]{1,0:T(8,128)(2,1)}, bf16[512,2048]{1,0:T(8,128)(2,1)}) custom-call(s32[8]{0:T(128)} %stack.97.places_ref, bf16[1024,2176]{1,0:T(8,128)(2,1)} %get-tuple-element.173.refs_0_.refs_2_, bf16[2,256,2176]{2,1,0:T(8,128)(2,1)} %copy-done.4, bf16[2,256,2176]{2,1,0:T(8,128)(2,1)} %copy-done.6, bf16[2,256,2176]{2,1,0:T(8,128)(2,1)} %copy-done.4, ...), custom_call_target="tpu_custom_call" | custom-call | flops 1140850688 | bytes 2195456 | tf_op jit(solution)/shard_map/project_home/pallas_call | solution.py:547
  387.1 4.0 collective-permute-done.30
  391.0 3.7 add_convert_fusion.2
  394.8 4.4 all-to-all-start.3
  401.9 45.0 %all-to-all-done.3 = bf16[4,128,2048]{2,1,0:T(8,128)(2,1)S(1)} async-done(((bf16[4,128,2048]{2,1,0:T(8,128)(2,1)}), bf16[4,128,2048]{2,1,0:T(8,128)(2,1)S(1)}, u32[]{:S(2)}, u32[]{:S(2)}) %all-to-all-start.3) | async-done | bytes 2097184 | tf_op jit(solution)/shard_map/all_to_all | solution.py:46
  446.9 2.7 fusion.23
  449.9 50.1 %all_to_all.71 = bf16[4,128,2048]{2,1,0:T(8,128)(2,1)S(1)} all-to-all(bf16[4,128,2048]{2,1,0:T(8,128)(2,1)S(1)} %broadcast_in_dim.222), channel_id=1, replica_groups=mesh['dp'=4,'ctx'=2,'exp'=4] {'exp'}, dimensions={0} | all-to-all | bytes 4194304 | tf_op jit(solution)/shard_map/all_to_all | solution.py:46
  502.6 3.2 collective-permute-done.31.refs_1_
  505.9 18.2 %weight_grad.4 = (bf16[2,256,2176]{2,1,0:T(8,128)(2,1)}, bf16[2,256,2176]{2,1,0:T(8,128)(2,1)}, bf16[2,256,2176]{2,1,0:T(8,128)(2,1)}, bf16[2,256,2176]{2,1,0:T(8,128)(2,1)}) custom-call(s32[8]{0:T(128)} %stack.114.places_ref, bf16[512,2048]{1,0:T(8,128)(2,1)} %bitcast.292, bf16[512,2048]{1,0:T(8,128)(2,1)} %collective-permute-done.31.refs_1_, ...), custom_call_target="tpu_custom_call" | custom-call | flops 1140850688 | bytes 2195456 | tf_op jit(solution)/shard_map/weight_grad/pallas_call | solution.py:626
  525.2 30.9 %down_back.1 = (bf16[1024,2176]{1,0:T(8,128)(2,1)}, bf16[1024,2176]{1,0:T(8,128)(2,1)}, f32[1024,128]{1,0:T(8,128)}) custom-call(s32[10]{0:T(128)} %concatenate.152.info_ref, bf16[512,2048]{1,0:T(8,128)(2,1)} %bitcast.293, bf16[512,2048]{1,0:T(8,128)(2,1)} %collective-permute-done.31.refs_1_, bf16[2,256,2176]{2,1,0:T(8,128)(2,1)} %copy-done.4, ...), custom_call_target="tpu_custom_call" | custom-call | flops 1140850688 | bytes 4980736 | tf_op jit(solution)/shard_map/down_back/pallas_call | solution.py:424
  556.1 29.0 %project_home.6 = (bf16[512,2048]{1,0:T(8,128)(2,1)}, bf16[512,2048]{1,0:T(8,128)(2,1)}) custom-call(s32[8]{0:T(128)} %stack.97.places_ref, bf16[1024,2176]{1,0:T(8,128)(2,1)} %get-tuple-element.193.refs_0_.refs_2_, bf16[1024,2176]{1,0:T(8,128)(2,1)} %get-tuple-element.209.refs_1_.refs_2_, bf16[2,256,2176]{2,1,0:T(8,128)(2,1)} %copy-done.5, ...), custom_call_target="tpu_custom_call" | custom-call | flops 2281701376 | bytes 3866624 | tf_op jit(solution)/shard_map/project_home/pallas_call | solution.py:547
  586.5 4.1 collective-permute-done.32
  590.7 5.2 add_convert_fusion.1
  595.9 4.6 all-to-all-start.5
  601.8 2.8 fusion.6
  604.7 2.5 fusion.5
  608.6 18.2 %weight_grad.5 = (bf16[2,256,2176]{2,1,0:T(8,128)(2,1)}, bf16[2,256,2176]{2,1,0:T(8,128)(2,1)}, bf16[2,256,2176]{2,1,0:T(8,128)(2,1)}, bf16[2,256,2176]{2,1,0:T(8,128)(2,1)}) custom-call(s32[8]{0:T(128)} %stack.114.places_ref, bf16[512,2048]{1,0:T(8,128)(2,1)} %bitcast.56.refs_0_, bf16[512,2048]{1,0:T(8,128)(2,1)} %copy-done.7, ...), custom_call_target="tpu_custom_call" | custom-call | flops 1140850688 | bytes 2195456 | tf_op jit(solution)/shard_map/weight_grad/pallas_call | solution.py:626
  631.8 6.3 collective-permute-done.36
  638.1 10.9 %collective-permute-done.37 = f32[9,128]{1,0:T(8,128)S(1)} collective-permute-done((f32[9,128]{1,0:T(8,128)S(1)}, f32[9,128]{1,0:T(8,128)S(1)}, u32[]{:S(2)}, u32[]{:S(2)}) %collective-permute-start.37) | collective-permute-done | bytes 4640 | tf_op jit(solution)/shard_map/ppermute | solution.py:34
  656.0 4.8 all-to-all-start.6
  665.8 2.4 slice_bitcast_fusion.9
  668.2 18.2 %weight_grad.6 = (bf16[2,256,2176]{2,1,0:T(8,128)(2,1)}, bf16[2,256,2176]{2,1,0:T(8,128)(2,1)}, bf16[2,256,2176]{2,1,0:T(8,128)(2,1)}, bf16[2,256,2176]{2,1,0:T(8,128)(2,1)}) custom-call(s32[8]{0:T(128)} %stack.114.places_ref, bf16[512,2048]{1,0:T(8,128)(2,1)} %bitcast.56.refs_0_, bf16[512,2048]{1,0:T(8,128)(2,1)} %copy-done.7, ...), custom_call_target="tpu_custom_call" | custom-call | flops 1140850688 | bytes 2195456 | tf_op jit(solution)/shard_map/weight_grad/pallas_call | solution.py:626
  686.4 23.5 %collective-permute-done.41 = bf16[2,256,2176]{2,1,0:T(8,128)(2,1)} collective-permute-done((bf16[2,256,2176]{2,1,0:T(8,128)(2,1)}, bf16[2,256,2176]{2,1,0:T(8,128)(2,1)}, u32[]{:S(2)}, u32[]{:S(2)}) %collective-permute-start.41) | collective-permute-done | bytes 2228256 | tf_op jit(solution)/shard_map/ppermute | solution.py:29
  714.4 2.7 fusion.8
  718.5 2.5 fusion.7
  721.7 6.9 out_back.1
  728.6 12.5 %attend_back.1 = (bf16[1024,256]{1,0:T(8,128)(2,1)}, f32[1024,512]{1,0:T(8,128)}, bf16[1024,512]{1,0:T(8,128)(2,1)}) custom-call(s32[9]{0:T(128)} %pad_add_fusion.info_ref, bf16[1024,256]{1,0:T(8,128)(2,1)} %get-tuple-element.144.q_ref, bf16[1024,256]{1,0:T(8,128)(2,1)} %get-tuple-element.215.da_ref, bf16[1024,512]{1,0:T(8,128)(2,1)} %get-tuple-element.149.refs_0_, ...), custom_call_target="tpu_custom_call" | custom-call | flops 83886080 | bytes 851968 | tf_op jit(solution)/shard_map/attend_back/pallas_call | solution.py:744
  747.0 22.4 %collective-permute-done.44 = bf16[1024,512]{1,0:T(8,128)(2,1)S(1)} collective-permute-done((bf16[1024,512]{1,0:T(8,128)(2,1)}, bf16[1024,512]{1,0:T(8,128)(2,1)S(1)}, u32[]{:S(2)}, u32[]{:S(2)}) %collective-permute-start.44) | collective-permute-done | bytes 1048608 | tf_op jit(solution)/shard_map/ppermute | solution.py:1010
  771.7 10.0 %project_home.7 = (bf16[512,2048]{1,0:T(8,128)(2,1)}, bf16[512,2048]{1,0:T(8,128)(2,1)}) custom-call(s32[8]{0:T(128)} %stack.97.places_ref, bf16[1024,768]{1,0:T(8,128)(2,1)} %pad_maximum_fusion.8.refs_0_.refs_2_, bf16[2,256,1024]{2,1,0:T(8,128)(2,1)} %copy-done.1, bf16[2,256,1024]{2,1,0:T(8,128)(2,1)} %copy-done.2, bf16[2,256,1024]{2,1,0:T(8,128)(2,1)} %copy-done.1, ...), custom_call_target="tpu_custom_call" | custom-call | flops 402653184 | bytes 1114112 | tf_op jit(solution)/shard_map/project_home/pallas_call | solution.py:547
  791.2 4.5 add_convert_fusion
  795.6 4.5 all-to-all-start.7
  800.1 36.2 %collective-permute-done.48 = bf16[2,256,2176]{2,1,0:T(8,128)(2,1)} collective-permute-done((bf16[2,256,2176]{2,1,0:T(8,128)(2,1)}, bf16[2,256,2176]{2,1,0:T(8,128)(2,1)}, u32[]{:S(2)}, u32[]{:S(2)}) %collective-permute-start.48) | collective-permute-done | bytes 2228256 | tf_op jit(solution)/shard_map/ppermute | solution.py:29
  836.4 14.8 %weight_grad.7 = (bf16[2,256,1024]{2,1,0:T(8,128)(2,1)}, bf16[2,256,1024]{2,1,0:T(8,128)(2,1)}, bf16[2,256,1024]{2,1,0:T(8,128)(2,1)}, bf16[2,256,1024]{2,1,0:T(8,128)(2,1)}) custom-call(s32[8]{0:T(128)} %stack.114.places_ref, bf16[1024,2048]{1,0:T(8,128)(2,1)} %get-tuple-element.226.refs_0_, bf16[1024,2048]{1,0:T(8,128)(2,1)} %get-tuple-element.227.refs_1_, ...), custom_call_target="tpu_custom_call" | custom-call | flops 536870912 | bytes 1310720 | tf_op jit(solution)/shard_map/weight_grad/pallas_call | solution.py:626
  866.7 32.4 %collective-permute-done.63 = bf16[256,2176]{1,0:T(8,128)(2,1)S(1)} collective-permute-done((bf16[256,2176]{1,0:T(8,128)(2,1)S(1)}, bf16[256,2176]{1,0:T(8,128)(2,1)S(1)}, u32[]{:S(2)}, u32[]{:S(2)}) %collective-permute-start.63) | collective-permute-done | bytes 1114144 | tf_op jit(solution)/shard_map/ppermute | solution.py:29
  905.1 3.8 copy.89
  912.5 7.2 copy.88
  919.7 3.8 copy.87
  933.9 3.7 collective-permute-start.52
  946.8 2.5 collective-permute-start.60
  (422 shorter events, 196.3 us)
Async XLA Ops:
  2.3 15.6 %collective-permute-start.6 = (bf16[4,32,128]{1,2,0:T(8,128)(2,1)S(1)}, bf16[4,32,128]{1,2,0:T(8,128)(2,1)S(1)}, u32[]{:S(2)}, u32[]{:S(2)}) collective-permute-start(bf16[4,32,128]{1,2,0:T(8,128)(2,1)S(1)} %broadcast_select_fusion.9), channel_id=1, source_target_pairs={{0,1},{1,2},{2,3},{3,0},{4,5},{5,6},{6,7},{7,4},{8,9},{9,10},{10,1... | collective-permute-start | bytes 98312 | tf_op jit(solution)/shard_map/ppermute | solution.py:34
  4.5 13.5 %collective-permute-start.7 = (bf16[4,32,128]{1,2,0:T(8,128)(2,1)S(1)}, bf16[4,32,128]{1,2,0:T(8,128)(2,1)S(1)}, u32[]{:S(2)}, u32[]{:S(2)}) collective-permute-start(bf16[4,32,128]{1,2,0:T(8,128)(2,1)S(1)} %broadcast_select_fusion.9), channel_id=1, source_target_pairs={{0,2},{1,3},{2,0},{3,1},{4,6},{5,7},{6,4},{7,5},{8,10},{9,11},{10,... | collective-permute-start | bytes 98312 | tf_op jit(solution)/shard_map/ppermute | solution.py:34
  6.8 11.2 %collective-permute-start.8 = (bf16[4,32,128]{1,2,0:T(8,128)(2,1)S(1)}, bf16[4,32,128]{1,2,0:T(8,128)(2,1)S(1)}, u32[]{:S(2)}, u32[]{:S(2)}) collective-permute-start(bf16[4,32,128]{1,2,0:T(8,128)(2,1)S(1)} %broadcast_select_fusion.9), channel_id=1, source_target_pairs={{0,3},{1,0},{2,1},{3,2},{4,7},{5,4},{6,5},{7,6},{8,11},{9,8},{10,9... | collective-permute-start | bytes 98312 | tf_op jit(solution)/shard_map/ppermute | solution.py:34
  10.2 11.9 %collective-permute-start = (bf16[256,1024]{1,0:T(8,128)(2,1)S(1)}, bf16[256,1024]{1,0:T(8,128)(2,1)S(1)}, u32[]{:S(2)}, u32[]{:S(2)}) collective-permute-start(bf16[256,1024]{1,0:T(8,128)(2,1)S(1)} %pad_maximum_fusion.14), channel_id=1, source_target_pairs={{0,8},{8,0},{16,24},{24,16},{1,9},{9,1},{17,25},{25,17},{2,10},{10... | collective-permute-start | bytes 1572872 | tf_op jit(solution)/shard_map/ppermute | solution.py:24
  13.4 52.9 %all-to-all-start = ((bf16[4,128,2048]{2,1,0:T(8,128)(2,1)}), bf16[4,128,2048]{2,1,0:T(8,128)(2,1)}, u32[]{:S(2)}, u32[]{:S(2)}) async-start(bf16[4,128,2048]{2,1,0:T(8,128)(2,1)} %broadcast_in_dim.195), calls=%async_computation | async-start | bytes 4194304 | tf_op jit(solution)/shard_map/all_to_all | solution.py:46
  20.9 11.8 %collective-permute-start.10 = (bf16[2,2,4,11,64]{4,2,1,0,3:T(4,128)(2,1)S(1)}, bf16[2,2,4,11,64]{4,2,1,0,3:T(4,128)(2,1)S(1)}, u32[]{:S(2)}, u32[]{:S(2)}) collective-permute-start(bf16[2,2,4,11,64]{4,2,1,0,3:T(4,128)(2,1)S(1)} %broadcast_select_fusion.13), channel_id=1, source_target_pairs={{0,16},{8,24},{16,0},{24,8},{1,17},{9,25},{17,1},{25,9},{2,18},{10... | collective-permute-start | bytes 67592 | tf_op jit(solution)/shard_map/ppermute | solution.py:29
  22.3 24.5 %collective-permute-start.1 = (bf16[2,256,1024]{2,1,0:T(8,128)(2,1)S(1)}, bf16[2,256,1024]{2,1,0:T(8,128)(2,1)S(1)}, u32[]{:S(2)}, u32[]{:S(2)}) collective-permute-start(bf16[2,256,1024]{2,1,0:T(8,128)(2,1)S(1)} %pad_maximum_fusion.13.refs_2_.refs_4_.refs_1_.refs_3_), channel_id=1, source_target_pairs={{0,4},{4,0},{1,5},{5,1},{2,6},{6,2},{3,7},{7,3},{8,12},{12,8},{9,1... | collective-permute-start | bytes 3145736 | tf_op jit(solution)/shard_map/ppermute | solution.py:34
  23.6 24.4 %collective-permute-start.2 = (bf16[2,256,1024]{2,1,0:T(8,128)(2,1)S(1)}, bf16[2,256,1024]{2,1,0:T(8,128)(2,1)S(1)}, u32[]{:S(2)}, u32[]{:S(2)}) collective-permute-start(bf16[2,256,1024]{2,1,0:T(8,128)(2,1)S(1)} %pad_maximum_fusion.13.refs_2_.refs_4_.refs_1_.refs_3_), channel_id=1, source_target_pairs={{0,16},{8,24},{16,0},{24,8},{1,17},{9,25},{17,1},{25,9},{2,18},{10... | collective-permute-start | bytes 3145736 | tf_op jit(solution)/shard_map/ppermute | solution.py:29
  31.7 22.4 %collective-permute-start.5 = (bf16[256,2176]{1,0:T(8,128)(2,1)}, bf16[256,2176]{1,0:T(8,128)(2,1)}, u32[]{:S(2)}, u32[]{:S(2)}) collective-permute-start(bf16[256,2176]{1,0:T(8,128)(2,1)} %concatenate.142), channel_id=1, source_target_pairs={{0,8},{8,0},{16,24},{24,16},{1,9},{9,1},{17,25},{25,17},{2,10},{10... | collective-permute-start | bytes 3342344 | tf_op jit(solution)/shard_map/ppermute | solution.py:24
  32.9 17.2 %collective-permute-start.11 = (bf16[2,2,2,4,11,64]{5,3,0,2,1,4:T(4,128)(2,1)S(1)}, bf16[2,2,2,4,11,64]{5,3,0,2,1,4:T(4,128)(2,1)S(1)}, u32[]{:S(2)}, u32[]{:S(2)}) collective-permute-start(bf16[2,2,2,4,11,64]{5,3,0,2,1,4:T(4,128)(2,1)S(1)} %broadcast_select_fusion.12), channel_id=1, source_target_pairs={{0,4},{4,0},{1,5},{5,1},{2,6},{6,2},{3,7},{7,3},{8,12},{12,8},{9,1... | collective-permute-start | bytes 135176 | tf_op jit(solution)/shard_map/ppermute | solution.py:34
  47.7 11.7 %collective-permute-start.3 = (bf16[256,1024]{1,0:T(8,128)(2,1)}, bf16[256,1024]{1,0:T(8,128)(2,1)}, u32[]{:S(2)}, u32[]{:S(2)}) collective-permute-start(bf16[256,1024]{1,0:T(8,128)(2,1)} %slice_bitcast_fusion.37), channel_id=1, source_target_pairs={{0,16},{8,24},{16,0},{24,8},{1,17},{9,25},{17,1},{25,9},{2,18},{10... | collective-permute-start | bytes 1572872 | tf_op jit(solution)/shard_map/ppermute | solution.py:29
  48.8 11.4 %collective-permute-start.4 = (bf16[256,1024]{1,0:T(8,128)(2,1)}, bf16[256,1024]{1,0:T(8,128)(2,1)}, u32[]{:S(2)}, u32[]{:S(2)}) collective-permute-start(bf16[256,1024]{1,0:T(8,128)(2,1)} %slice_bitcast_fusion.36), channel_id=1, source_target_pairs={{0,4},{4,0},{1,5},{5,1},{2,6},{6,2},{3,7},{7,3},{8,12},{12,8},{9,1... | collective-permute-start | bytes 1572872 | tf_op jit(solution)/shard_map/ppermute | solution.py:34
  66.3 7.9 collective-permute-start.12
  70.3 50.2 %collective-permute-start.14 = (bf16[2,256,2176]{2,1,0:T(8,128)(2,1)S(1)}, bf16[2,256,2176]{2,1,0:T(8,128)(2,1)}, u32[]{:S(2)}, u32[]{:S(2)}) collective-permute-start(bf16[2,256,2176]{2,1,0:T(8,128)(2,1)S(1)} %pad_maximum_fusion.5.refs_2_.refs_4_), channel_id=1, source_target_pairs={{0,4},{4,0},{1,5},{5,1},{2,6},{6,2},{3,7},{7,3},{8,12},{12,8},{9,1... | collective-permute-start | bytes 6684680 | tf_op jit(solution)/shard_map/ppermute | solution.py:34
  71.5 49.9 %collective-permute-start.15 = (bf16[2,256,2176]{2,1,0:T(8,128)(2,1)S(1)}, bf16[2,256,2176]{2,1,0:T(8,128)(2,1)}, u32[]{:S(2)}, u32[]{:S(2)}) collective-permute-start(bf16[2,256,2176]{2,1,0:T(8,128)(2,1)S(1)} %pad_maximum_fusion.5.refs_2_.refs_4_), channel_id=1, source_target_pairs={{0,16},{8,24},{16,0},{24,8},{1,17},{9,25},{17,1},{25,9},{2,18},{10... | collective-permute-start | bytes 6684680 | tf_op jit(solution)/shard_map/ppermute | solution.py:29
  95.7 6.7 collective-permute-start.16
  96.0 45.9 %collective-permute-start.13 = (bf16[1024,512]{1,0:T(8,128)(2,1)S(1)}, bf16[1024,512]{1,0:T(8,128)(2,1)}, u32[]{:S(2)}, u32[]{:S(2)}) collective-permute-start(bf16[1024,512]{1,0:T(8,128)(2,1)S(1)} %copy-done.26), channel_id=1, source_target_pairs={{0,4},{1,5},{2,6},{3,7},{8,12},{9,13},{10,14},{11,15},{16,20},{17,... | collective-permute-start | bytes 3145736 | tf_op jit(solution)/shard_map/ppermute | solution.py:923
  144.2 25.5 %collective-permute-start.17 = (bf16[256,2176]{1,0:T(8,128)(2,1)}, bf16[256,2176]{1,0:T(8,128)(2,1)S(1)}, u32[]{:S(2)}, u32[]{:S(2)}) collective-permute-start(bf16[256,2176]{1,0:T(8,128)(2,1)} %slice_bitcast_fusion.17), channel_id=1, source_target_pairs={{0,16},{8,24},{16,0},{24,8},{1,17},{9,25},{17,1},{25,9},{2,18},{10... | collective-permute-start | bytes 3342344 | tf_op jit(solution)/shard_map/ppermute | solution.py:29
  147.7 26.4 %collective-permute-start.18 = (bf16[256,2176]{1,0:T(8,128)(2,1)}, bf16[256,2176]{1,0:T(8,128)(2,1)S(1)}, u32[]{:S(2)}, u32[]{:S(2)}) collective-permute-start(bf16[256,2176]{1,0:T(8,128)(2,1)} %slice_bitcast_fusion.16), channel_id=1, source_target_pairs={{0,4},{4,0},{1,5},{5,1},{2,6},{6,2},{3,7},{7,3},{8,12},{12,8},{9,1... | collective-permute-start | bytes 3342344 | tf_op jit(solution)/shard_map/ppermute | solution.py:34
  174.1 5.7 collective-permute-start.19
  183.5 52.8 %all-to-all-start.1 = ((bf16[4,128,2048]{2,1,0:T(8,128)(2,1)}), bf16[4,128,2048]{2,1,0:T(8,128)(2,1)}, u32[]{:S(2)}, u32[]{:S(2)}) async-start(bf16[4,128,2048]{2,1,0:T(8,128)(2,1)} %bitcast.46), calls=%async_computation.1 | async-start | bytes 4194304 | tf_op jit(solution)/shard_map/all_to_all | solution.py:46
  188.3 50.0 %collective-permute-start.20 = (bf16[2,256,2176]{2,1,0:T(8,128)(2,1)}, bf16[2,256,2176]{2,1,0:T(8,128)(2,1)}, u32[]{:S(2)}, u32[]{:S(2)}) collective-permute-start(bf16[2,256,2176]{2,1,0:T(8,128)(2,1)} %pad_maximum_fusion.6.refs_10_.refs_12_), channel_id=1, source_target_pairs={{0,4},{4,0},{1,5},{5,1},{2,6},{6,2},{3,7},{7,3},{8,12},{12,8},{9,1... | collective-permute-start | bytes 6684680 | tf_op jit(solution)/shard_map/ppermute | solution.py:34
  189.8 49.6 %collective-permute-start.21 = (bf16[2,256,2176]{2,1,0:T(8,128)(2,1)}, bf16[2,256,2176]{2,1,0:T(8,128)(2,1)}, u32[]{:S(2)}, u32[]{:S(2)}) collective-permute-start(bf16[2,256,2176]{2,1,0:T(8,128)(2,1)} %pad_maximum_fusion.6.refs_10_.refs_12_), channel_id=1, source_target_pairs={{0,16},{8,24},{16,0},{24,8},{1,17},{9,25},{17,1},{25,9},{2,18},{10... | collective-permute-start | bytes 6684680 | tf_op jit(solution)/shard_map/ppermute | solution.py:29
  243.6 79.6 %all-to-all-start.2 = ((bf16[4,128,2048]{2,1,0:T(8,128)(2,1)}), bf16[4,128,2048]{2,1,0:T(8,128)(2,1)}, u32[]{:S(2)}, u32[]{:S(2)}) async-start(bf16[4,128,2048]{2,1,0:T(8,128)(2,1)} %broadcast_in_dim.216), calls=%async_computation.2 | async-start | bytes 4194304 | tf_op jit(solution)/shard_map/all_to_all | solution.py:46
  248.0 72.4 %collective-permute-start.25 = (bf16[2,256,2176]{2,1,0:T(8,128)(2,1)S(1)}, bf16[2,256,2176]{2,1,0:T(8,128)(2,1)S(1)}, u32[]{:S(2)}, u32[]{:S(2)}) collective-permute-start(bf16[2,256,2176]{2,1,0:T(8,128)(2,1)S(1)} %pad_maximum_fusion.7.refs_1_.refs_3_.refs_2_.refs_4_), channel_id=1, source_target_pairs={{0,4},{4,0},{1,5},{5,1},{2,6},{6,2},{3,7},{7,3},{8,12},{12,8},{9,1... | collective-permute-start | bytes 6684680 | tf_op jit(solution)/shard_map/ppermute | solution.py:34
  248.4 74.7 %collective-permute-start.26 = (bf16[2,256,2176]{2,1,0:T(8,128)(2,1)S(1)}, bf16[2,256,2176]{2,1,0:T(8,128)(2,1)}, u32[]{:S(2)}, u32[]{:S(2)}) collective-permute-start(bf16[2,256,2176]{2,1,0:T(8,128)(2,1)S(1)} %pad_maximum_fusion.7.refs_1_.refs_3_.refs_2_.refs_4_), channel_id=1, source_target_pairs={{0,16},{8,24},{16,0},{24,8},{1,17},{9,25},{17,1},{25,9},{2,18},{10... | collective-permute-start | bytes 6684680 | tf_op jit(solution)/shard_map/ppermute | solution.py:29
  250.0 70.4 %collective-permute-start.23 = (bf16[256,2176]{1,0:T(8,128)(2,1)S(1)}, bf16[256,2176]{1,0:T(8,128)(2,1)S(1)}, u32[]{:S(2)}, u32[]{:S(2)}) collective-permute-start(bf16[256,2176]{1,0:T(8,128)(2,1)S(1)} %slice_bitcast_fusion.15), channel_id=1, source_target_pairs={{0,16},{8,24},{16,0},{24,8},{1,17},{9,25},{17,1},{25,9},{2,18},{10... | collective-permute-start | bytes 3342344 | tf_op jit(solution)/shard_map/ppermute | solution.py:29
  252.6 67.8 %collective-permute-start.24 = (bf16[256,2176]{1,0:T(8,128)(2,1)S(1)}, bf16[256,2176]{1,0:T(8,128)(2,1)S(1)}, u32[]{:S(2)}, u32[]{:S(2)}) collective-permute-start(bf16[256,2176]{1,0:T(8,128)(2,1)S(1)} %slice_bitcast_fusion.14), channel_id=1, source_target_pairs={{0,4},{4,0},{1,5},{5,1},{2,6},{6,2},{3,7},{7,3},{8,12},{12,8},{9,1... | collective-permute-start | bytes 3342344 | tf_op jit(solution)/shard_map/ppermute | solution.py:34
  323.2 12.1 %collective-permute-start.27 = (bf16[512,2048]{1,0:T(8,128)(2,1)}, bf16[512,2048]{1,0:T(8,128)(2,1)S(1)}, u32[]{:S(2)}, u32[]{:S(2)}) collective-permute-start(bf16[512,2048]{1,0:T(8,128)(2,1)} %bitcast.56.refs_0_), channel_id=1, source_target_pairs={{0,8},{8,0},{16,24},{24,16},{1,9},{9,1},{17,25},{25,17},{2,10},{10... | collective-permute-start | bytes 6291464 | tf_op jit(solution)/shard_map/ppermute | solution.py:24
  328.3 40.0 %collective-permute-start.28 = (bf16[256,2176]{1,0:T(8,128)(2,1)}, bf16[256,2176]{1,0:T(8,128)(2,1)}, u32[]{:S(2)}, u32[]{:S(2)}) collective-permute-start(bf16[256,2176]{1,0:T(8,128)(2,1)} %slice_bitcast_fusion.13), channel_id=1, source_target_pairs={{0,16},{8,24},{16,0},{24,8},{1,17},{9,25},{17,1},{25,9},{2,18},{10... | collective-permute-start | bytes 3342344 | tf_op jit(solution)/shard_map/ppermute | solution.py:29
  330.9 37.5 %collective-permute-start.29 = (bf16[256,2176]{1,0:T(8,128)(2,1)}, bf16[256,2176]{1,0:T(8,128)(2,1)}, u32[]{:S(2)}, u32[]{:S(2)}) collective-permute-start(bf16[256,2176]{1,0:T(8,128)(2,1)} %slice_bitcast_fusion.12), channel_id=1, source_target_pairs={{0,4},{4,0},{1,5},{5,1},{2,6},{6,2},{3,7},{7,3},{8,12},{12,8},{9,1... | collective-permute-start | bytes 3342344 | tf_op jit(solution)/shard_map/ppermute | solution.py:34
  394.8 52.2 %all-to-all-start.3 = ((bf16[4,128,2048]{2,1,0:T(8,128)(2,1)}), bf16[4,128,2048]{2,1,0:T(8,128)(2,1)S(1)}, u32[]{:S(2)}, u32[]{:S(2)}) async-start(bf16[4,128,2048]{2,1,0:T(8,128)(2,1)} %bitcast.294), calls=%async_computation.3 | async-start | bytes 4194304 | tf_op jit(solution)/shard_map/all_to_all | solution.py:46
  500.0 5.8 collective-permute-start.31
  524.1 66.6 %collective-permute-start.33 = (bf16[2,256,2176]{2,1,0:T(8,128)(2,1)}, bf16[2,256,2176]{2,1,0:T(8,128)(2,1)}, u32[]{:S(2)}, u32[]{:S(2)}) collective-permute-start(bf16[2,256,2176]{2,1,0:T(8,128)(2,1)} %get-tuple-element.179), channel_id=1, source_target_pairs={{0,16},{8,24},{16,0},{24,8},{1,17},{9,25},{17,1},{25,9},{2,18},{10... | collective-permute-start | bytes 6684680 | tf_op jit(solution)/shard_map/ppermute | solution.py:29
  524.9 65.8 %collective-permute-start.34 = (bf16[2,256,2176]{2,1,0:T(8,128)(2,1)}, bf16[2,256,2176]{2,1,0:T(8,128)(2,1)S(1)}, u32[]{:S(2)}, u32[]{:S(2)}) collective-permute-start(bf16[2,256,2176]{2,1,0:T(8,128)(2,1)} %get-tuple-element.181), channel_id=1, source_target_pairs={{0,4},{4,0},{1,5},{5,1},{2,6},{6,2},{3,7},{7,3},{8,12},{12,8},{9,1... | collective-permute-start | bytes 6684680 | tf_op jit(solution)/shard_map/ppermute | solution.py:34
  585.1 5.6 collective-permute-start.32
  595.9 53.1 %all-to-all-start.5 = ((bf16[4,128,2048]{2,1,0:T(8,128)(2,1)}), bf16[4,128,2048]{2,1,0:T(8,128)(2,1)}, u32[]{:S(2)}, u32[]{:S(2)}) async-start(bf16[4,128,2048]{2,1,0:T(8,128)(2,1)} %bitcast.73), calls=%async_computation.5 | async-start | bytes 4194304 | tf_op jit(solution)/shard_map/all_to_all | solution.py:46
  601.4 7.2 collective-permute-start.35
  604.7 46.1 %collective-permute-start.40 = (bf16[256,2176]{1,0:T(8,128)(2,1)}, bf16[256,2176]{1,0:T(8,128)(2,1)}, u32[]{:S(2)}, u32[]{:S(2)}) collective-permute-start(bf16[256,2176]{1,0:T(8,128)(2,1)} %fusion.6), channel_id=1, source_target_pairs={{0,16},{8,24},{16,0},{24,8},{1,17},{9,25},{17,1},{25,9},{2,18},{10... | collective-permute-start | bytes 3342344 | tf_op jit(solution)/shard_map/ppermute | solution.py:29
  607.2 43.5 %collective-permute-start.39 = (bf16[256,2176]{1,0:T(8,128)(2,1)}, bf16[256,2176]{1,0:T(8,128)(2,1)S(1)}, u32[]{:S(2)}, u32[]{:S(2)}) collective-permute-start(bf16[256,2176]{1,0:T(8,128)(2,1)} %fusion.5), channel_id=1, source_target_pairs={{0,4},{4,0},{1,5},{5,1},{2,6},{6,2},{3,7},{7,3},{8,12},{12,8},{9,1... | collective-permute-start | bytes 3342344 | tf_op jit(solution)/shard_map/ppermute | solution.py:34
  626.7 11.4 %collective-permute-start.36 = (f32[9,128]{1,0:T(8,128)S(1)}, f32[9,128]{1,0:T(8,128)S(1)}, u32[]{:S(2)}, u32[]{:S(2)}) collective-permute-start(f32[9,128]{1,0:T(8,128)S(1)} %get-tuple-element.367), channel_id=1, source_target_pairs={{0,1},{1,2},{2,3},{3,0},{4,5},{5,6},{6,7},{7,4},{8,9},{9,10},{10,1... | collective-permute-start | bytes 13832 | tf_op jit(solution)/shard_map/ppermute | solution.py:34
  628.5 20.6 %collective-permute-start.37 = (f32[9,128]{1,0:T(8,128)S(1)}, f32[9,128]{1,0:T(8,128)S(1)}, u32[]{:S(2)}, u32[]{:S(2)}) collective-permute-start(f32[9,128]{1,0:T(8,128)S(1)} %get-tuple-element.369), channel_id=1, source_target_pairs={{0,2},{1,3},{2,0},{3,1},{4,6},{5,7},{6,4},{7,5},{8,10},{9,11},{10,... | collective-permute-start | bytes 13832 | tf_op jit(solution)/shard_map/ppermute | solution.py:34
  630.6 18.5 %collective-permute-start.38 = (f32[9,128]{1,0:T(8,128)S(1)}, f32[9,128]{1,0:T(8,128)S(1)}, u32[]{:S(2)}, u32[]{:S(2)}) collective-permute-start(f32[9,128]{1,0:T(8,128)S(1)} %get-tuple-element.368), channel_id=1, source_target_pairs={{0,3},{1,0},{2,1},{3,2},{4,7},{5,4},{6,5},{7,6},{8,11},{9,8},{10,9... | collective-permute-start | bytes 13832 | tf_op jit(solution)/shard_map/ppermute | solution.py:34
  656.0 53.9 %all-to-all-start.6 = ((bf16[4,128,2048]{2,1,0:T(8,128)(2,1)}), bf16[4,128,2048]{2,1,0:T(8,128)(2,1)}, u32[]{:S(2)}, u32[]{:S(2)}) async-start(bf16[4,128,2048]{2,1,0:T(8,128)(2,1)} %broadcast_in_dim.223), calls=%async_computation.6 | async-start | bytes 4194304 | tf_op jit(solution)/shard_map/all_to_all | solution.py:46
  660.8 49.1 %collective-permute-start.41 = (bf16[2,256,2176]{2,1,0:T(8,128)(2,1)}, bf16[2,256,2176]{2,1,0:T(8,128)(2,1)}, u32[]{:S(2)}, u32[]{:S(2)}) collective-permute-start(bf16[2,256,2176]{2,1,0:T(8,128)(2,1)} %get-tuple-element.195), channel_id=1, source_target_pairs={{0,16},{8,24},{16,0},{24,8},{1,17},{9,25},{17,1},{25,9},{2,18},{10... | collective-permute-start | bytes 6684680 | tf_op jit(solution)/shard_map/ppermute | solution.py:29
  660.8 49.1 %collective-permute-start.42 = (bf16[2,256,2176]{2,1,0:T(8,128)(2,1)}, bf16[2,256,2176]{2,1,0:T(8,128)(2,1)}, u32[]{:S(2)}, u32[]{:S(2)}) collective-permute-start(bf16[2,256,2176]{2,1,0:T(8,128)(2,1)} %get-tuple-element.197), channel_id=1, source_target_pairs={{0,4},{4,0},{1,5},{5,1},{2,6},{6,2},{3,7},{7,3},{8,12},{12,8},{9,1... | collective-permute-start | bytes 6684680 | tf_op jit(solution)/shard_map/ppermute | solution.py:34
  709.9 11.8 %collective-permute-start.43 = (bf16[512,2048]{1,0:T(8,128)(2,1)}, bf16[512,2048]{1,0:T(8,128)(2,1)}, u32[]{:S(2)}, u32[]{:S(2)}) collective-permute-start(bf16[512,2048]{1,0:T(8,128)(2,1)} %bitcast.90.refs_0_), channel_id=1, source_target_pairs={{0,8},{8,0},{16,24},{24,16},{1,9},{9,1},{17,25},{25,17},{2,10},{10... | collective-permute-start | bytes 6291464 | tf_op jit(solution)/shard_map/ppermute | solution.py:24
  717.1 29.0 %collective-permute-start.46 = (bf16[256,2176]{1,0:T(8,128)(2,1)}, bf16[256,2176]{1,0:T(8,128)(2,1)}, u32[]{:S(2)}, u32[]{:S(2)}) collective-permute-start(bf16[256,2176]{1,0:T(8,128)(2,1)} %fusion.8), channel_id=1, source_target_pairs={{0,16},{8,24},{16,0},{24,8},{1,17},{9,25},{17,1},{25,9},{2,18},{10... | collective-permute-start | bytes 3342344 | tf_op jit(solution)/shard_map/ppermute | solution.py:29
  721.0 26.0 %collective-permute-start.45 = (bf16[256,2176]{1,0:T(8,128)(2,1)}, bf16[256,2176]{1,0:T(8,128)(2,1)}, u32[]{:S(2)}, u32[]{:S(2)}) collective-permute-start(bf16[256,2176]{1,0:T(8,128)(2,1)} %fusion.7), channel_id=1, source_target_pairs={{0,4},{4,0},{1,5},{5,1},{2,6},{6,2},{3,7},{7,3},{8,12},{12,8},{9,1... | collective-permute-start | bytes 3342344 | tf_op jit(solution)/shard_map/ppermute | solution.py:34
  741.1 28.3 %collective-permute-start.44 = (bf16[1024,512]{1,0:T(8,128)(2,1)}, bf16[1024,512]{1,0:T(8,128)(2,1)S(1)}, u32[]{:S(2)}, u32[]{:S(2)}) collective-permute-start(bf16[1024,512]{1,0:T(8,128)(2,1)} %get-tuple-element.218), channel_id=1, source_target_pairs={{4,0},{5,1},{6,2},{7,3},{12,8},{13,9},{14,10},{15,11},{20,16},{21,... | collective-permute-start | bytes 3145736 | tf_op jit(solution)/shard_map/ppermute | solution.py:1010
  781.8 9.4 collective-permute-start.47
  786.0 50.4 %collective-permute-start.48 = (bf16[2,256,2176]{2,1,0:T(8,128)(2,1)}, bf16[2,256,2176]{2,1,0:T(8,128)(2,1)}, u32[]{:S(2)}, u32[]{:S(2)}) collective-permute-start(bf16[2,256,2176]{2,1,0:T(8,128)(2,1)} %get-tuple-element.228), channel_id=1, source_target_pairs={{0,16},{8,24},{16,0},{24,8},{1,17},{9,25},{17,1},{25,9},{2,18},{10... | collective-permute-start | bytes 6684680 | tf_op jit(solution)/shard_map/ppermute | solution.py:29
  786.1 50.3 %collective-permute-start.49 = (bf16[2,256,2176]{2,1,0:T(8,128)(2,1)}, bf16[2,256,2176]{2,1,0:T(8,128)(2,1)}, u32[]{:S(2)}, u32[]{:S(2)}) collective-permute-start(bf16[2,256,2176]{2,1,0:T(8,128)(2,1)} %get-tuple-element.230), channel_id=1, source_target_pairs={{0,4},{4,0},{1,5},{5,1},{2,6},{6,2},{3,7},{7,3},{8,12},{12,8},{9,1... | collective-permute-start | bytes 6684680 | tf_op jit(solution)/shard_map/ppermute | solution.py:34
  795.6 127.9 %all-to-all-start.7 = ((bf16[4,128,2048]{2,1,0:T(8,128)(2,1)}), bf16[4,128,2048]{2,1,0:T(8,128)(2,1)}, u32[]{:S(2)}, u32[]{:S(2)}) async-start(bf16[4,128,2048]{2,1,0:T(8,128)(2,1)} %bitcast.93), calls=%async_computation.7 | async-start | bytes 4194304 | tf_op jit(solution)/shard_map/all_to_all | solution.py:46
  851.2 75.1 %collective-permute-start.56 = (bf16[2,256,1024]{2,1,0:T(8,128)(2,1)}, bf16[2,256,1024]{2,1,0:T(8,128)(2,1)}, u32[]{:S(2)}, u32[]{:S(2)}) collective-permute-start(bf16[2,256,1024]{2,1,0:T(8,128)(2,1)} %get-tuple-element.235), channel_id=1, source_target_pairs={{0,16},{8,24},{16,0},{24,8},{1,17},{9,25},{17,1},{25,9},{2,18},{10... | collective-permute-start | bytes 3145736 | tf_op jit(solution)/shard_map/ppermute | solution.py:29
  852.4 79.3 %collective-permute-start.58 = (bf16[2,256,1024]{2,1,0:T(8,128)(2,1)}, bf16[2,256,1024]{2,1,0:T(8,128)(2,1)}, u32[]{:S(2)}, u32[]{:S(2)}) collective-permute-start(bf16[2,256,1024]{2,1,0:T(8,128)(2,1)} %get-tuple-element.237), channel_id=1, source_target_pairs={{0,4},{4,0},{1,5},{5,1},{2,6},{6,2},{3,7},{7,3},{8,12},{12,8},{9,1... | collective-permute-start | bytes 3145736 | tf_op jit(solution)/shard_map/ppermute | solution.py:34
  854.8 47.7 %collective-permute-start.65 = (bf16[256,2176]{1,0:T(8,128)(2,1)S(1)}, bf16[256,2176]{1,0:T(8,128)(2,1)S(1)}, u32[]{:S(2)}, u32[]{:S(2)}) collective-permute-start(bf16[256,2176]{1,0:T(8,128)(2,1)S(1)} %add_convert_fusion.4), channel_id=1, source_target_pairs={{0,8},{8,0},{16,24},{24,16},{1,9},{9,1},{17,25},{25,17},{2,10},{10... | collective-permute-start | bytes 3342344 | tf_op jit(solution)/shard_map/ppermute | solution.py:24
  861.2 42.0 %collective-permute-start.61 = (bf16[256,2176]{1,0:T(8,128)(2,1)S(1)}, bf16[256,2176]{1,0:T(8,128)(2,1)S(1)}, u32[]{:S(2)}, u32[]{:S(2)}) collective-permute-start(bf16[256,2176]{1,0:T(8,128)(2,1)S(1)} %fusion.9), channel_id=1, source_target_pairs={{0,4},{4,0},{1,5},{5,1},{2,6},{6,2},{3,7},{7,3},{8,12},{12,8},{9,1... | collective-permute-start | bytes 3342344 | tf_op jit(solution)/shard_map/ppermute | solution.py:34
  864.3 34.8 %collective-permute-start.63 = (bf16[256,2176]{1,0:T(8,128)(2,1)S(1)}, bf16[256,2176]{1,0:T(8,128)(2,1)S(1)}, u32[]{:S(2)}, u32[]{:S(2)}) collective-permute-start(bf16[256,2176]{1,0:T(8,128)(2,1)S(1)} %fusion.10), channel_id=1, source_target_pairs={{0,16},{8,24},{16,0},{24,8},{1,17},{9,25},{17,1},{25,9},{2,18},{10... | collective-permute-start | bytes 3342344 | tf_op jit(solution)/shard_map/ppermute | solution.py:29
  899.1 9.8 %collective-permute-start.62 = (bf16[256,2176]{1,0:T(8,128)(2,1)S(1)}, bf16[256,2176]{1,0:T(8,128)(2,1)S(1)}, u32[]{:S(2)}, u32[]{:S(2)}) collective-permute-start(bf16[256,2176]{1,0:T(8,128)(2,1)S(1)} %add_convert_fusion.6), channel_id=1, source_target_pairs={{0,8},{8,0},{16,24},{24,16},{1,9},{9,1},{17,25},{25,17},{2,10},{10... | collective-permute-start | bytes 3342344 | tf_op jit(solution)/shard_map/ppermute | solution.py:24
  902.5 8.0 collective-permute-start.64
  927.8 22.8 %collective-permute-start.57 = (bf16[256,1024]{1,0:T(8,128)(2,1)S(1)}, bf16[256,1024]{1,0:T(8,128)(2,1)S(1)}, u32[]{:S(2)}, u32[]{:S(2)}) collective-permute-start(bf16[256,1024]{1,0:T(8,128)(2,1)S(1)} %fusion.21), channel_id=1, source_target_pairs={{0,4},{4,0},{1,5},{5,1},{2,6},{6,2},{3,7},{7,3},{8,12},{12,8},{9,1... | collective-permute-start | bytes 1572872 | tf_op jit(solution)/shard_map/ppermute | solution.py:34
  933.0 12.5 %collective-permute-start.59 = (bf16[256,1024]{1,0:T(8,128)(2,1)S(1)}, bf16[256,1024]{1,0:T(8,128)(2,1)S(1)}, u32[]{:S(2)}, u32[]{:S(2)}) collective-permute-start(bf16[256,1024]{1,0:T(8,128)(2,1)S(1)} %fusion.22), channel_id=1, source_target_pairs={{0,16},{8,24},{16,0},{24,8},{1,17},{9,25},{17,1},{25,9},{2,18},{10... | collective-permute-start | bytes 1572872 | tf_op jit(solution)/shard_map/ppermute | solution.py:29
  938.5 6.2 collective-permute-start.53
  (71 other events, 500.7 us)

commit v3 on v2

--- a/solution.py
+++ b/solution.py
@@ -162,14 +162,24 @@
     return grad_first_y(groups), grad_first_ctx(groups)
 
 
-def grad_second(groups, far, sent):
+def grad_addends(groups, far, sent):
     near, _, line, *_ = groups
     lines = [line, *sent]
-    mine_sent = [
-        shift(total([near[s], far[s]]).astype(BF), "ctx", -s) for s in range(1, near.shape[0])
-    ]
-    theirs_sent = y_swap(total([v[1] for v in lines]).astype(BF))
-    return ([near[0], far[0]], [v[0] for v in lines]), (mine_sent, [theirs_sent])
+    kept = ([near[0], far[0]], [v[0] for v in lines])
+    onward = (
+        [total([near[s], far[s]]).astype(BF) for s in range(1, near.shape[0])],
+        total([v[1] for v in lines]).astype(BF),
+    )
+    return kept, onward
+
+
+def grad_moves(onward):
+    return [shift(v, "ctx", -s) for s, v in enumerate(onward[0], start=1)], [y_swap(onward[1])]
+
+
+def grad_second(groups, far, sent):
+    kept, onward = grad_addends(groups, far, sent)
+    return kept, grad_moves(onward)
 
 
 def grad_last(kept, sent):
@@ -297,7 +307,7 @@
 def up_kernel(shards, blocks, experts, info_ref, *refs):
     row_refs, refs = refs[:shards], refs[shards:]
     gate_refs, up_refs, refs = refs[:blocks], refs[blocks : 2 * blocks], refs[2 * blocks :]
-    small_ref, chosen_ref, act_ref, gate_ref, up_ref, scale_ref, scratch = refs
+    small_ref, chosen_ref, act_ref, silu_ref, slope_ref, plain_ref, scale_ref, scratch = refs
     step_n = pl.program_id(0)
     own = info_ref[blocks]
     units = info_ref[blocks + 1]
@@ -326,8 +336,8 @@
             )
         reorder(info_ref, row_refs, scratch, blocks)
 
-    def step(m, _):
-        at = pl.ds(pl.multiple_of(m * tile, tile), tile)
+    for m in range(count):
+        at = slice(m * tile, (m + 1) * tile)
         rows = scratch[at, :]
         gate = jnp.dot(
             rows, jnp.concatenate([w[...] for w in gate_refs], axis=0), preferred_element_type=F32
@@ -335,14 +345,17 @@
         up = jnp.dot(
             rows, jnp.concatenate([w[...] for w in up_refs], axis=0), preferred_element_type=F32
         )
-        gate_ref[at, :] = gate
-        up_ref[at, :] = up
-        col = lax.broadcasted_iota(jnp.int32, gate.shape, 1) + step_n * gate.shape[1]
-        scale = jnp.where(col < units, scale_ref[at, 0:1], scale_ref[at, 1:2])
-        act_ref[at, :] = (gate * jax.nn.sigmoid(gate) * up * scale).astype(BF)
-        return 0
-
-    lax.fori_loop(0, count, step, 0)
+        sig = jax.nn.sigmoid(gate)
+        act = gate * sig
+        plain = act * up
+        silu_ref[at, :] = act.astype(BF)
+        slope_ref[at, :] = (up * (sig + act * (1.0 - sig))).astype(BF)
+        plain_ref[at, :] = plain.astype(BF)
+        for h in range(TILE_N // HD):
+            cols = slice(h * HD, (h + 1) * HD)
+            expert = step_n * (TILE_N // HD) + h < units // HD
+            scale = jnp.where(expert, scale_ref[at, 0:1], scale_ref[at, 1:2])
+            act_ref[at, cols] = (plain[:, cols] * scale).astype(BF)
 
 
 def up_call(info, shards, gates, ups, small, chosen, experts):
@@ -357,19 +370,15 @@
             in_specs=[whole(s) for s in shards]
             + [block_spec(w, TILE_N, lambda i: i) for w in gates + ups]
             + [whole(small), whole(chosen)],
-            out_specs=[out, out, out, pl.BlockSpec((total_rows, HD), lambda i, p: (0, 0))],
+            out_specs=[out] * 4 + [pl.BlockSpec((total_rows, HD), lambda i, p: (0, 0))],
             scratch_shapes=[pltpu.VMEM((total_rows, depth), BF)],
         ),
-        out_shape=[
-            jax.ShapeDtypeStruct((total_rows, cols), BF),
-            jax.ShapeDtypeStruct((total_rows, cols), F32),
-            jax.ShapeDtypeStruct((total_rows, cols), F32),
-            jax.ShapeDtypeStruct((total_rows, HD), F32),
-        ],
+        out_shape=[jax.ShapeDtypeStruct((total_rows, cols), BF)] * 4
+        + [jax.ShapeDtypeStruct((total_rows, HD), F32)],
         cost_estimate=cost(
             flops=4 * total_rows * depth * cols,
             transcendentals=total_rows * cols,
-            bytes_accessed=2 * (total_rows * depth + 2 * depth * cols) + 10 * total_rows * cols,
+            bytes_accessed=2 * (total_rows * depth + 2 * depth * cols) + 8 * total_rows * cols,
         ),
         name="expert_up",
     )(info, *shards, *arrays(gates + ups), small, chosen)
@@ -378,7 +387,7 @@
 def down_back_kernel(shards, blocks, cols, info_ref, *refs):
     row_refs, refs = refs[:shards], refs[shards:]
     weight_refs, refs = refs[:blocks], refs[blocks:]
-    gate_ref, up_ref, scale_ref, dgate_ref, dup_ref, sums_ref, scratch = refs
+    silu_ref, slope_ref, plain_ref, scale_ref, dgate_ref, dup_ref, sums_ref, scratch, sums = refs
     step_n = pl.program_id(0)
     units = info_ref[blocks + 1]
     tile, count = tiles_of(scratch.shape[0])
@@ -386,40 +395,42 @@
     @pl.when(step_n == 0)
     def _():
         reorder(info_ref, row_refs, scratch, blocks)
-        sums_ref[...] = jnp.zeros_like(sums_ref)
-
-    def step(m, _):
-        at = pl.ds(pl.multiple_of(m * tile, tile), tile)
+        sums[...] = jnp.zeros_like(sums)
+
+    for m in range(count):
+        at = slice(m * tile, (m + 1) * tile)
         back = jnp.dot(
             scratch[at, :],
             jnp.concatenate([w[...] for w in weight_refs], axis=0),
             preferred_element_type=F32,
         )
-        gate, up = gate_ref[at, :], up_ref[at, :]
-        sig = jax.nn.sigmoid(gate)
-        act = gate * sig
-        col = lax.broadcasted_iota(jnp.int32, gate.shape, 1) + step_n * gate.shape[1]
-        inside = col < units
-        touched = act * up * back
-        expert_sum = jnp.sum(jnp.where(inside, touched, 0.0), axis=1, keepdims=True)
-        shared_sum = jnp.sum(
-            jnp.where(jnp.logical_not(inside) & (col < cols), touched, 0.0), axis=1, keepdims=True
-        )
-        place = lax.broadcasted_iota(jnp.int32, (tile, HD), 1)
-        sums_ref[at, :] += jnp.where(
-            place == 0, expert_sum * scale_ref[at, 2:3], jnp.where(place == 1, shared_sum, 0.0)
-        )
-        scaled = back * jnp.where(inside, scale_ref[at, 0:1], scale_ref[at, 1:2])
-        dup_ref[at, :] = (scaled * act).astype(BF)
-        dgate_ref[at, :] = (scaled * up * sig * (1.0 + gate * (1.0 - sig))).astype(BF)
-        return 0
-
-    lax.fori_loop(0, count, step, 0)
-
-
-def down_back_call(info, shards, weights, gate, up, scales):
+        for h in range(TILE_N // HD):
+            lane = slice(h * HD, (h + 1) * HD)
+            group = step_n * (TILE_N // HD) + h
+            expert = group < units // HD
+            part = back[:, lane]
+            touched = jnp.where(group < cols // HD, part * plain_ref[at, lane].astype(F32), 0.0)
+            kind = jnp.where(expert, 0, 1)
+            sums[kind, at, :] += touched
+            scaled = part * jnp.where(expert, scale_ref[at, 0:1], scale_ref[at, 1:2])
+            dup_ref[at, lane] = (scaled * silu_ref[at, lane].astype(F32)).astype(BF)
+            dgate_ref[at, lane] = (scaled * slope_ref[at, lane].astype(F32)).astype(BF)
+
+    @pl.when(step_n == pl.num_programs(0) - 1)
+    def _():
+        for m in range(count):
+            at = slice(m * tile, (m + 1) * tile)
+            place = lax.broadcasted_iota(jnp.int32, (tile, HD), 1)
+            expert_sum = jnp.sum(sums[0, at, :], axis=1, keepdims=True) * scale_ref[at, 2:3]
+            shared_sum = jnp.sum(sums[1, at, :], axis=1, keepdims=True)
+            sums_ref[at, :] = jnp.where(
+                place == 0, expert_sum, jnp.where(place == 1, shared_sum, 0.0)
+            )
+
+
+def down_back_call(info, shards, weights, silu, slope, plain, scales):
     tokens, depth = shards[0].shape
-    total_rows, cols = gate.shape
+    total_rows, cols = silu.shape
     out = pl.BlockSpec((total_rows, TILE_N), lambda i, p: (0, i))
     return pl.pallas_call(
         functools.partial(down_back_kernel, len(shards), len(weights), cols),
@@ -428,9 +439,12 @@
             grid=(pl.cdiv(cols, TILE_N),),
             in_specs=[whole(s) for s in shards]
             + [block_spec(w, TILE_N, lambda i: i) for w in weights]
-            + [out, out, whole(scales)],
+            + [out, out, out, whole(scales)],
             out_specs=[out, out, whole(scales)],
-            scratch_shapes=[pltpu.VMEM((total_rows, depth), BF)],
+            scratch_shapes=[
+                pltpu.VMEM((total_rows, depth), BF),
+                pltpu.VMEM((2, total_rows, HD), F32),
+            ],
         ),
         out_shape=[
             jax.ShapeDtypeStruct((total_rows, cols), BF),
@@ -439,11 +453,11 @@
         ],
         cost_estimate=cost(
             flops=2 * total_rows * depth * cols,
-            transcendentals=total_rows * cols,
-            bytes_accessed=2 * (total_rows * depth + depth * cols) + 12 * total_rows * cols,
+            transcendentals=0,
+            bytes_accessed=2 * (total_rows * depth + depth * cols) + 10 * total_rows * cols,
         ),
         name="down_back",
-    )(info, *shards, *arrays(weights), gate, up, scales)
+    )(info, *shards, *arrays(weights), silu, slope, plain, scales)
 
 
 def out_back_kernel(shards, blocks, places_ref, *refs):
@@ -638,18 +652,20 @@
     )(order, *operands)
 
 
-def probabilities(query, keys, length, x, scale):
-    tokens, count = query.shape[0], keys.shape[0]
+def allowed_keys(tokens, count, length, x):
+    row = lax.broadcasted_iota(jnp.int32, (tokens, tokens), 0) + x * tokens
+    col = lax.broadcasted_iota(jnp.int32, (tokens, tokens), 1)
+    parts = []
+    for s in range(count):
+        place = col + (x - s) * tokens
+        parts.append((place >= 0) & (place <= row) & (place < length))
+    return jnp.concatenate(parts, axis=1)
+
+
+def probabilities(query, keys, allowed, scale):
     scores = (
         lax.dot_general(query, keys, (((1,), (1,)), ((), ())), preferred_element_type=F32) * scale
     )
-    row = lax.broadcasted_iota(jnp.int32, (tokens, count), 0) + x * tokens
-    col = lax.broadcasted_iota(jnp.int32, (tokens, count), 1)
-    place = jnp.zeros((tokens, count), jnp.int32)
-    for s in range(count // tokens):
-        inside = (col >= s * tokens) & (col < (s + 1) * tokens)
-        place = jnp.where(inside, col - s * tokens + (x - s) * tokens, place)
-    allowed = (place >= 0) & (place <= row) & (place < length)
     masked = jnp.where(allowed, scores, NEGATIVE)
     top = jnp.max(masked, axis=1, keepdims=True)
     weights = jnp.where(allowed, jnp.exp(masked - top), 0.0)
@@ -659,14 +675,13 @@
 def attend_kernel(scale, info_ref, q_ref, *refs):
     kv_refs, out_ref = refs[:-1], refs[-1]
     group = pl.program_id(0)
-    width = q_ref.shape[1]
+    tokens, width = q_ref.shape
+    allowed = allowed_keys(tokens, len(kv_refs), info_ref[group], info_ref[pl.num_programs(0)])
     for h in range(width // HD):
         at = h * HD
         keys = jnp.concatenate([r[:, at : at + HD] for r in kv_refs], axis=0)
         values = jnp.concatenate([r[:, width + at : width + at + HD] for r in kv_refs], axis=0)
-        prob = probabilities(
-            q_ref[:, at : at + HD], keys, info_ref[group], info_ref[pl.num_programs(0)], scale
-        )
+        prob = probabilities(q_ref[:, at : at + HD], keys, allowed, scale)
         out_ref[:, at : at + HD] = jnp.dot(
             prob.astype(BF), values, preferred_element_type=F32
         ).astype(BF)
@@ -705,14 +720,13 @@
     dkv_refs = refs[count + 3 :]
     group = pl.program_id(0)
     tokens, width = q_ref.shape
+    allowed = allowed_keys(tokens, count, info_ref[group], info_ref[pl.num_programs(0)])
     for h in range(width // HD):
         at = h * HD
         keys = jnp.concatenate([r[:, at : at + HD] for r in kv_refs], axis=0)
         values = jnp.concatenate([r[:, width + at : width + at + HD] for r in kv_refs], axis=0)
         query, grad = q_ref[:, at : at + HD], da_ref[:, at : at + HD]
-        prob = probabilities(
-            query, keys, info_ref[group], info_ref[pl.num_programs(0)], scale
-        )
+        prob = probabilities(query, keys, allowed, scale)
         dprob = lax.dot_general(
             grad, values, (((1,), (1,)), ((), ())), preferred_element_type=F32
         )
@@ -943,7 +957,7 @@
     up_weight = weight_blocks(upper_pair, *upper_near, *upper_far)
     lower_far = weight_second(*lower_near)
     ffn_shards = both_cores(ffn_mine)
-    act_scaled, gate_pre, up_pre, scales = up_call(
+    act_scaled, silu, slope, plain, scales = up_call(
         facts, ffn_shards, gate_weight, up_weight, small, chosen_all, experts
     )
     down_weight = weight_blocks(lower_pair, *lower_near, *lower_far)
@@ -957,7 +971,7 @@
     down_moves = grad_first(down_groups)
     back_shards, down_groups = meet(back_shards, down_groups)
     grad_gate_pre, grad_up_pre, sums = down_back_call(
-        facts, back_shards, down_weight, gate_pre, up_pre, scales
+        facts, back_shards, down_weight, silu, slope, plain, scales
     )
     keep, away = project_home(
         places, [grad_gate_pre, grad_up_pre], [gate_weight, up_weight], model_width
@@ -970,12 +984,12 @@
     ).reshape(experts + 1, 2, nz, tok_rows)
     scalar_both = scalar_rows[:, 0] + core_swap(scalar_rows[:, 1])
     grad_gate_pre, grad_up_pre = after((grad_gate_pre, grad_up_pre), [both])
-    gate_groups = weight_grad(order, [(ffn_shards, grad_gate_pre)])
-    gate_moves = grad_first(gate_groups)
-    (scalar_both,) = after((jnp.swapaxes(scalar_both, 0, 1),), [gate_groups])
+    wide_groups = weight_grad(order, [(ffn_shards, grad_gate_pre), (ffn_shards, grad_up_pre)])
+    wide_moves = grad_first(wide_groups)
+    (scalar_both,) = after((jnp.swapaxes(scalar_both, 0, 1),), [wide_groups])
     scalar_own = own_of(scalar_both, "exp", nz, z)
     down_kept, down_moves = grad_second(down_groups, *down_moves)
-    parts, scalar_own, gate_groups, down_moves = meet(parts, scalar_own, gate_groups, down_moves)
+    parts, scalar_own, wide_groups, down_moves = meet(parts, scalar_own, wide_groups, down_moves)
     grad_normed = total(parts)
 
     own_logits = dot_t(normed_ffn, small)
@@ -996,12 +1010,8 @@
     grad_hidden = grad_result + grad_hidden_norm
     grad_hidden_low = grad_hidden.astype(BF)
 
-    back_mine = gather_exp(grad_hidden_low)
-    grad_up_pre = after((grad_up_pre,), [grad_hidden_low])[0]
-    up_groups = weight_grad(order, [(ffn_shards, grad_up_pre)])
-    back_mine, up_groups, gate_moves = meet(back_mine, up_groups, gate_moves)
-    up_y = grad_first_y(up_groups)
-    gate_kept, gate_moves = grad_second(gate_groups, *gate_moves)
+    down_kept, down_moves = after((down_kept, down_moves), [grad_hidden_low])
+    back_mine, grad_down = meet(gather_exp(grad_hidden_low), grad_last(down_kept, down_moves))
     grad_attended, attn_back = out_back_call(places, both_cores(back_mine), attn_weight, width)
     grad_query, grad_kv, *sent = attend_back_call(
         info, query, grad_attended, kvs, cos_all, sin_all, tok_rows, score_scale
@@ -1010,25 +1020,21 @@
         lax.ppermute(v, "ctx", [(i + s, i) for i in range(n - s)])
         for s, v in enumerate(sent, start=1)
     ]
-    sent, gate_moves = meet(sent, gate_moves)
-    up_ctx = grad_first_ctx(up_groups, [sent])
+    wide_kept, onward = grad_addends(wide_groups, *after(wide_moves, [grad_query]))
+    sent, onward = meet(sent, onward)
+    wide_moves = grad_moves(onward)
     grad_kv = total([grad_kv, *sent])
     grad_projected = jnp.concatenate([grad_query, grad_kv.astype(BF)], axis=1)
     keep, away = project_home(places, [grad_projected], [attn_weight], model_width)
     both, parts = home_start(keep, core_swap(away))
-    up_y, up_ctx = after((up_y, up_ctx), [both])
-    up_kept, up_moves = grad_second(up_groups, up_y, up_ctx)
     attn_groups = weight_grad(
         order,
         [
-            ([attn_rows], after((grad_projected,), [up_y, up_ctx])[0]),
+            ([attn_rows], after((grad_projected,), [both])[0]),
             ([attn_back], attended),
         ],
     )
     attn_moves = grad_first(attn_groups)
-    down_kept, gate_kept = after((down_kept, gate_kept), [attn_groups])
-    grad_down = grad_last(down_kept, down_moves)
-    grad_gate = grad_last(gate_kept, gate_moves)
     bias_own = jnp.sum(grad_projected.astype(F32), axis=0).reshape(3, width)
     columns = 2 * nz
     column = lax.broadcasted_iota(jnp.int32, (3, columns * width), 1)
@@ -1044,7 +1050,9 @@
         vectors.reshape(-1, 2, 2, n, nz, span).transpose(3, 1, 2, 4, 0, 5)
     )
     attn_kept, attn_moves = grad_second(attn_groups, *attn_moves)
-    grad_up = grad_last(up_kept, up_moves)
+    grad_wide = grad_last(wide_kept, wide_moves)
+    grad_gate = [g[:, : act_scaled.shape[1]] for g in grad_wide]
+    grad_up = [g[:, act_scaled.shape[1] :] for g in grad_wide]
     grad_attn = grad_last(attn_kept, attn_moves)
 
     def join(pair, axis):

time: 967 us -> 903 us (0.934)
  waiting for transfers between devices: 369 us -> 323 us
  Pallas kernels: 238 us -> 226 us
  local copies, waits for them, and re-layouts: 98.4 us -> 86.5 us
    ppermute x18 -> x16, waiting for transfers between devices: 166 us -> 100 us  [y_swap(): return lax.ppermute(v, 'dp', [(i, i ^ 2) for i in range(n)])]
    all_to_all x7, waiting for transfers between devices: 87.7 us -> 131 us  [exchange(): return lax.all_to_all(v, 'exp', split_axis=0, concat_axis=0, tiled=True)]
    ppermute x27 -> x25, waiting for transfers between devices: 53.8 us -> 39.3 us  [shift(): return lax.ppermute(v, axis, [(i, (i + s) % n) for i in range(n)])]
    ppermute x19 -> x18, starting transfers between devices: 27.1 us -> 30.6 us  [core_swap(): return lax.ppermute(v, 'dp', [(i, i ^ 1) for i in range(n)])]
    pallas_call x4 -> x3, Pallas kernels: 69.4 us -> 66.4 us  [weight_grad(): pl.pallas_call(functools.partial(weight_grad_kernel, n, [len(rows) for ro...]
    ppermute x27 -> x25, starting transfers between devices: 32.9 us -> 30.1 us  [shift(): return lax.ppermute(v, axis, [(i, (i + s) % n) for i in range(n)])]
    unnamed x129 -> x117, local copies, waits for them, and re-layouts: 27.2 us -> 24.4 us
  transfers between devices with their start and end apart: 73 -> 68, of which waited for: 33 -> 33; matrix products, arithmetic and copies ran while one was open for 15% -> 17% of each run, Pallas kernels for 20% -> 20%
where the time goes in v3:
time: 903 us; the launch traced here: 892 us
  waiting for transfers between devices  323 us (36%)
  Pallas kernels  226 us (25%)
  starting transfers between devices  107 us (12%)
  other arithmetic  92.4 us (10%)
  local copies, waits for them, and re-layouts  86.5 us (10%)
  blocking collectives  50.1 us (6%)
    all_to_all x7, waiting for transfers between devices, exchange(): return lax.all_to_all(v, 'exp', split_axis=0, concat_axis=0, tiled=True)  131 us
    ppermute x16, waiting for transfers between devices, y_swap(): return lax.ppermute(v, 'dp', [(i, i ^ 2) for i in range(n)])  100 us
    pallas_call x3, Pallas kernels, weight_grad(): pl.pallas_call(functools.partial(weight_grad_kernel, n, [len(rows) for ro...  66.4 us
    pallas_call x4, Pallas kernels, project_home(): pl.pallas_call(functools.partial(home_kernel, len(acts), [i for _, i in e...  64.1 us
    all_to_all x1, blocking collectives, exchange(): return lax.all_to_all(v, 'exp', split_axis=0, concat_axis=0, tiled=True)  50.1 us
    ppermute x25, waiting for transfers between devices, shift(): return lax.ppermute(v, axis, [(i, (i + s) % n) for i in range(n)])  39.3 us
    pallas_call x1, Pallas kernels, up_call(): pl.pallas_call(functools.partial(up_kernel, len(shards), len(gates), expe...  31.2 us
    all_to_all x7, starting transfers between devices, exchange(): return lax.all_to_all(v, 'exp', split_axis=0, concat_axis=0, tiled=True)  30.9 us
  transfers between devices with their start and end apart: 68, of which 33 were waited for; matrix products, arithmetic and copies ran while one was open for 17% of the time, Pallas kernels for 20%

profile of v3, /device:TPU:1, one launch (start us, length us, event | category | flops | bytes accessed | tf_op | source)
XLA Modules:
  0.0 891.9 jit_solution(9736710239700131460)
XLA Ops:
  13.4 4.5 all-to-all-start
  28.4 3.3 concatenate.142
  33.2 13.6 %collective-permute-done.1.refs_3_.refs_5_.refs_2_.refs_4_ = bf16[2,256,1024]{2,1,0:T(8,128)(2,1)S(1)} collective-permute-done((bf16[2,256,1024]{2,1,0:T(8,128)(2,1)S(1)}, bf16[2,256,1024]{2,1,0:T(8,128)(2,1)S(1)}, u32[]{:S(2)}, u32[]{:S(2)}) %collective-permute-start.1) | collective-permute-done | bytes 1048608 | tf_op jit(solution)/shard_map/ppermute | solution.py:34
  50.8 3.2 concatenate.141
  55.9 3.5 collective-permute-done.3
  60.2 6.1 all-to-all-done
  74.2 13.5 %qkv_rope.1 = (bf16[1024,2048]{1,0:T(8,128)(2,1)}, bf16[1024,256]{1,0:T(8,128)(2,1)}, bf16[1024,512]{1,0:T(8,128)(2,1)}) custom-call(s32[8]{0:T(128)} %stack.97.places_ref, bf16[512,2048]{1,0:T(8,128)(2,1)} %bitcast.13.refs_0_, bf16[512,2048]{1,0:T(8,128)(2,1)} %collective-permute-done.12.refs_1_, bf16[2,256,1024]{2,1,0:T(8,128)(2,1)} %copy-done.1, ...), custom_call_target="tpu_custom_call" | custom-call | flops 402653184 | bytes 1441792 | tf_op jit(solution)/shard_map/qkv_rope/pallas_call | solution.py:278
  92.5 3.2 concatenate.149
  96.0 3.2 collective-permute-start.13
  99.2 3.2 concatenate.148
  102.4 3.2 pad_maximum_fusion.6.refs_10_.refs_12_
  105.6 14.9 %collective-permute-done.14.refs_3_.refs_5_ = bf16[2,256,2176]{2,1,0:T(8,128)(2,1)} collective-permute-done((bf16[2,256,2176]{2,1,0:T(8,128)(2,1)S(1)}, bf16[2,256,2176]{2,1,0:T(8,128)(2,1)}, u32[]{:S(2)}, u32[]{:S(2)}) %collective-permute-start.14) | collective-permute-done | bytes 2228256 | tf_op jit(solution)/shard_map/ppermute | solution.py:34
  121.4 20.5 %collective-permute-done.13.refs_1_ = bf16[1024,512]{1,0:T(8,128)(2,1)} collective-permute-done((bf16[1024,512]{1,0:T(8,128)(2,1)S(1)}, bf16[1024,512]{1,0:T(8,128)(2,1)}, u32[]{:S(2)}, u32[]{:S(2)}) %collective-permute-start.13) | collective-permute-done | bytes 1048608 | tf_op jit(solution)/shard_map/ppermute | solution.py:937
  151.6 9.5 %attend.1.refs_0_.refs_3_ = bf16[1024,256]{1,0:T(8,128)(2,1)} custom-call(s32[9]{0:T(128)} %pad_add_fusion.info_ref, bf16[1024,256]{1,0:T(8,128)(2,1)} %get-tuple-element.133.q_ref, bf16[1024,512]{1,0:T(8,128)(2,1)} %get-tuple-element.138.refs_0_, bf16[1024,512]{1,0:T(8,128)(2,1)} %collective-permute-done.13.refs_1_), custom_call_target="tpu_custom_call" | custom-call | flops 33554432 | bytes 393216 | tf_op jit(solution)/shard_map/attend/pallas_call | solution.py:693
  161.1 7.5 project_home.4
  169.7 4.4 collective-permute-done.18
  175.8 4.0 collective-permute-done.19
  179.8 3.7 add_convert_fusion.5
  183.5 4.8 all-to-all-start.1
  198.8 37.5 %all-to-all-done.1 = bf16[4,128,2048]{2,1,0:T(8,128)(2,1)} async-done(((bf16[4,128,2048]{2,1,0:T(8,128)(2,1)}), bf16[4,128,2048]{2,1,0:T(8,128)(2,1)}, u32[]{:S(2)}, u32[]{:S(2)}) %all-to-all-start.1) | async-done | bytes 2097184 | tf_op jit(solution)/shard_map/all_to_all | solution.py:46
  243.5 4.5 all-to-all-start.2
  253.8 66.6 %collective-permute-done.23 = bf16[256,2176]{1,0:T(8,128)(2,1)S(1)} collective-permute-done((bf16[256,2176]{1,0:T(8,128)(2,1)S(1)}, bf16[256,2176]{1,0:T(8,128)(2,1)S(1)}, u32[]{:S(2)}, u32[]{:S(2)}) %collective-permute-start.23) | collective-permute-done | bytes 1114144 | tf_op jit(solution)/shard_map/ppermute | solution.py:29
  323.2 2.8 collective-permute-start.27
  336.5 31.2 %expert_up.1 = (bf16[1024,2176]{1,0:T(8,128)(2,1)}, bf16[1024,2176]{1,0:T(8,128)(2,1)}, bf16[1024,2176]{1,0:T(8,128)(2,1)}, bf16[1024,2176]{1,0:T(8,128)(2,1)}, f32[1024,128]{1,0:T(8,128)}) custom-call(s32[10]{0:T(128)} %concatenate.152.info_ref, bf16[512,2048]{1,0:T(8,128)(2,1)} %bitcast.56.refs_0_.refs_2_, bf16[512,2048]{1,0:T(8,128)(2,1)} %copy-done.7, ...), custom_call_target="tpu_custom_call" | custom-call | flops 2281701376 | bytes 4980736 | tf_op jit(solution)/shard_map/expert_up/pallas_call | solution.py:365
  367.7 17.5 %project_home.5 = (bf16[512,2048]{1,0:T(8,128)(2,1)}, bf16[512,2048]{1,0:T(8,128)(2,1)}) custom-call(s32[8]{0:T(128)} %stack.97.places_ref, bf16[1024,2176]{1,0:T(8,128)(2,1)} %get-tuple-element.162.refs_0_.refs_2_, bf16[2,256,2176]{2,1,0:T(8,128)(2,1)} %copy-done.4, bf16[2,256,2176]{2,1,0:T(8,128)(2,1)} %copy-done.6, bf16[2,256,2176]{2,1,0:T(8,128)(2,1)} %copy-done.4, ...), custom_call_target="tpu_custom_call" | custom-call | flops 1140850688 | bytes 2195456 | tf_op jit(solution)/shard_map/project_home/pallas_call | solution.py:561
  386.3 4.0 collective-permute-done.30
  390.3 3.7 add_convert_fusion.4
  394.0 4.4 all-to-all-start.3
  401.1 45.1 %all-to-all-done.3 = bf16[4,128,2048]{2,1,0:T(8,128)(2,1)S(1)} async-done(((bf16[4,128,2048]{2,1,0:T(8,128)(2,1)}), bf16[4,128,2048]{2,1,0:T(8,128)(2,1)S(1)}, u32[]{:S(2)}, u32[]{:S(2)}) %all-to-all-start.3) | async-done | bytes 2097184 | tf_op jit(solution)/shard_map/all_to_all | solution.py:46
  446.2 2.7 fusion.21
  449.1 50.1 %all_to_all.71 = bf16[4,128,2048]{2,1,0:T(8,128)(2,1)S(1)} all-to-all(bf16[4,128,2048]{2,1,0:T(8,128)(2,1)S(1)} %broadcast_in_dim.222), channel_id=1, replica_groups=mesh['dp'=4,'ctx'=2,'exp'=4] {'exp'}, dimensions={0} | all-to-all | bytes 4194304 | tf_op jit(solution)/shard_map/all_to_all | solution.py:46
  501.8 3.2 collective-permute-done.31.refs_1_
  505.1 18.2 %weight_grad.3 = (bf16[2,256,2176]{2,1,0:T(8,128)(2,1)}, bf16[2,256,2176]{2,1,0:T(8,128)(2,1)}, bf16[2,256,2176]{2,1,0:T(8,128)(2,1)}, bf16[2,256,2176]{2,1,0:T(8,128)(2,1)}) custom-call(s32[8]{0:T(128)} %stack.114.places_ref, bf16[512,2048]{1,0:T(8,128)(2,1)} %bitcast.280, bf16[512,2048]{1,0:T(8,128)(2,1)} %collective-permute-done.31.refs_1_, ...), custom_call_target="tpu_custom_call" | custom-call | flops 1140850688 | bytes 2195456 | tf_op jit(solution)/shard_map/weight_grad/pallas_call | solution.py:640
  524.4 22.5 %down_back.1 = (bf16[1024,2176]{1,0:T(8,128)(2,1)}, bf16[1024,2176]{1,0:T(8,128)(2,1)}, f32[1024,128]{1,0:T(8,128)}) custom-call(s32[10]{0:T(128)} %concatenate.152.info_ref, bf16[512,2048]{1,0:T(8,128)(2,1)} %bitcast.281, bf16[512,2048]{1,0:T(8,128)(2,1)} %collective-permute-done.31.refs_1_, bf16[2,256,2176]{2,1,0:T(8,128)(2,1)} %copy-done.4, ...), custom_call_target="tpu_custom_call" | custom-call | flops 1140850688 | bytes 4423680 | tf_op jit(solution)/shard_map/down_back/pallas_call | solution.py:435
  547.0 29.1 %project_home.6 = (bf16[512,2048]{1,0:T(8,128)(2,1)}, bf16[512,2048]{1,0:T(8,128)(2,1)}) custom-call(s32[8]{0:T(128)} %stack.97.places_ref, bf16[1024,2176]{1,0:T(8,128)(2,1)} %get-tuple-element.183.refs_0_.refs_4_, bf16[1024,2176]{1,0:T(8,128)(2,1)} %get-tuple-element.184.refs_1_.refs_5_, bf16[2,256,2176]{2,1,0:T(8,128)(2,1)} %copy-done.5, ...), custom_call_target="tpu_custom_call" | custom-call | flops 2281701376 | bytes 3866624 | tf_op jit(solution)/shard_map/project_home/pallas_call | solution.py:561
  578.5 3.1 collective-permute-done.32
  581.6 4.4 add_convert_fusion.3
  586.1 3.6 all-to-all-start.5
  592.2 2.7 fusion.8
  598.8 33.6 %weight_grad.4 = (bf16[2,256,4352]{2,1,0:T(8,128)(2,1)}, bf16[2,256,4352]{2,1,0:T(8,128)(2,1)}, bf16[2,256,4352]{2,1,0:T(8,128)(2,1)}, bf16[2,256,4352]{2,1,0:T(8,128)(2,1)}) custom-call(s32[8]{0:T(128)} %stack.114.places_ref, bf16[512,2048]{1,0:T(8,128)(2,1)} %bitcast.56.refs_0_.refs_2_, bf16[512,2048]{1,0:T(8,128)(2,1)} %copy-done.7, ...), custom_call_target="tpu_custom_call" | custom-call | flops 2281701376 | bytes 3866624 | tf_op jit(solution)/shard_map/weight_grad/pallas_call | solution.py:640
  646.6 4.4 all-to-all-start.6
  655.6 2.6 collective-permute-start.41
  662.0 36.8 %all-to-all-done.6 = bf16[4,128,2048]{2,1,0:T(8,128)(2,1)} async-done(((bf16[4,128,2048]{2,1,0:T(8,128)(2,1)}), bf16[4,128,2048]{2,1,0:T(8,128)(2,1)}, u32[]{:S(2)}, u32[]{:S(2)}) %all-to-all-start.6) | async-done | bytes 2097184 | tf_op jit(solution)/shard_map/all_to_all | solution.py:46
  704.4 6.8 out_back.1
  711.3 12.4 %attend_back.1 = (bf16[1024,256]{1,0:T(8,128)(2,1)}, f32[1024,512]{1,0:T(8,128)}, bf16[1024,512]{1,0:T(8,128)(2,1)}) custom-call(s32[9]{0:T(128)} %pad_add_fusion.info_ref, bf16[1024,256]{1,0:T(8,128)(2,1)} %get-tuple-element.133.q_ref, bf16[1024,256]{1,0:T(8,128)(2,1)} %get-tuple-element.208.da_ref, bf16[1024,512]{1,0:T(8,128)(2,1)} %get-tuple-element.138.refs_0_, ...), custom_call_target="tpu_custom_call" | custom-call | flops 83886080 | bytes 851968 | tf_op jit(solution)/shard_map/attend_back/pallas_call | solution.py:758
  723.7 12.0 %collective-permute-done.44 = bf16[2,256,4352]{2,1,0:T(8,128)(2,1)} collective-permute-done((bf16[2,256,4352]{2,1,0:T(8,128)(2,1)}, bf16[2,256,4352]{2,1,0:T(8,128)(2,1)}, u32[]{:S(2)}, u32[]{:S(2)}) %collective-permute-start.44) | collective-permute-done | bytes 4456480 | tf_op jit(solution)/shard_map/ppermute | solution.py:29
  737.5 4.2 fusion.4
  741.7 4.3 fusion.3
  746.0 13.7 %collective-permute-done.43 = bf16[1024,512]{1,0:T(8,128)(2,1)S(1)} collective-permute-done((bf16[1024,512]{1,0:T(8,128)(2,1)}, bf16[1024,512]{1,0:T(8,128)(2,1)S(1)}, u32[]{:S(2)}, u32[]{:S(2)}) %collective-permute-start.43) | collective-permute-done | bytes 1048608 | tf_op jit(solution)/shard_map/ppermute | solution.py:1020
  761.4 10.0 %project_home.7 = (bf16[512,2048]{1,0:T(8,128)(2,1)}, bf16[512,2048]{1,0:T(8,128)(2,1)}) custom-call(s32[8]{0:T(128)} %stack.97.places_ref, bf16[1024,768]{1,0:T(8,128)(2,1)} %pad_maximum_fusion.8.refs_0_.refs_2_, bf16[2,256,1024]{2,1,0:T(8,128)(2,1)} %copy-done.1, bf16[2,256,1024]{2,1,0:T(8,128)(2,1)} %copy-done.2, bf16[2,256,1024]{2,1,0:T(8,128)(2,1)} %copy-done.1, ...), custom_call_target="tpu_custom_call" | custom-call | flops 402653184 | bytes 1114112 | tf_op jit(solution)/shard_map/project_home/pallas_call | solution.py:561
  771.4 4.2 collective-permute-start.46
  780.2 3.8 copy.89
  787.9 4.4 add_convert_fusion.2
  792.3 14.5 %weight_grad.5 = (bf16[2,256,1024]{2,1,0:T(8,128)(2,1)}, bf16[2,256,1024]{2,1,0:T(8,128)(2,1)}, bf16[2,256,1024]{2,1,0:T(8,128)(2,1)}, bf16[2,256,1024]{2,1,0:T(8,128)(2,1)}) custom-call(s32[8]{0:T(128)} %stack.114.places_ref, bf16[1024,2048]{1,0:T(8,128)(2,1)} %get-tuple-element.219.refs_0_, bf16[1024,2048]{1,0:T(8,128)(2,1)} %get-tuple-element.220.refs_1_, ...), custom_call_target="tpu_custom_call" | custom-call | flops 536870912 | bytes 1310720 | tf_op jit(solution)/shard_map/weight_grad/pallas_call | solution.py:640
  807.7 4.7 all-to-all-start.7
  813.8 14.4 %collective-permute-done.59 = bf16[256,4352]{1,0:T(8,128)(2,1)} collective-permute-done((bf16[256,4352]{1,0:T(8,128)(2,1)}, bf16[256,4352]{1,0:T(8,128)(2,1)}, u32[]{:S(2)}, u32[]{:S(2)}) %collective-permute-start.59) | collective-permute-done | bytes 2228256 | tf_op jit(solution)/shard_map/ppermute | solution.py:29
  828.2 3.8 fusion
  833.3 4.0 collective-permute-done.58
  837.3 3.3 bitcast_add_fusion.1
  843.1 7.0 copy.88
  850.1 3.8 copy.87
  853.9 6.1 all-to-all-done.7
  869.7 4.8 collective-permute-start.49
  882.2 2.7 collective-permute-start.57
  (387 shorter events, 179.9 us)
Async XLA Ops:
  2.3 15.6 %collective-permute-start.6 = (bf16[4,32,128]{1,2,0:T(8,128)(2,1)S(1)}, bf16[4,32,128]{1,2,0:T(8,128)(2,1)S(1)}, u32[]{:S(2)}, u32[]{:S(2)}) collective-permute-start(bf16[4,32,128]{1,2,0:T(8,128)(2,1)S(1)} %broadcast_select_fusion.9), channel_id=1, source_target_pairs={{0,1},{1,2},{2,3},{3,0},{4,5},{5,6},{6,7},{7,4},{8,9},{9,10},{10,1... | collective-permute-start | bytes 98312 | tf_op jit(solution)/shard_map/ppermute | solution.py:34
  4.5 13.5 %collective-permute-start.7 = (bf16[4,32,128]{1,2,0:T(8,128)(2,1)S(1)}, bf16[4,32,128]{1,2,0:T(8,128)(2,1)S(1)}, u32[]{:S(2)}, u32[]{:S(2)}) collective-permute-start(bf16[4,32,128]{1,2,0:T(8,128)(2,1)S(1)} %broadcast_select_fusion.9), channel_id=1, source_target_pairs={{0,2},{1,3},{2,0},{3,1},{4,6},{5,7},{6,4},{7,5},{8,10},{9,11},{10,... | collective-permute-start | bytes 98312 | tf_op jit(solution)/shard_map/ppermute | solution.py:34
  6.8 11.2 %collective-permute-start.8 = (bf16[4,32,128]{1,2,0:T(8,128)(2,1)S(1)}, bf16[4,32,128]{1,2,0:T(8,128)(2,1)S(1)}, u32[]{:S(2)}, u32[]{:S(2)}) collective-permute-start(bf16[4,32,128]{1,2,0:T(8,128)(2,1)S(1)} %broadcast_select_fusion.9), channel_id=1, source_target_pairs={{0,3},{1,0},{2,1},{3,2},{4,7},{5,4},{6,5},{7,6},{8,11},{9,8},{10,9... | collective-permute-start | bytes 98312 | tf_op jit(solution)/shard_map/ppermute | solution.py:34
  10.2 11.9 %collective-permute-start = (bf16[256,1024]{1,0:T(8,128)(2,1)S(1)}, bf16[256,1024]{1,0:T(8,128)(2,1)S(1)}, u32[]{:S(2)}, u32[]{:S(2)}) collective-permute-start(bf16[256,1024]{1,0:T(8,128)(2,1)S(1)} %pad_maximum_fusion.14), channel_id=1, source_target_pairs={{0,8},{8,0},{16,24},{24,16},{1,9},{9,1},{17,25},{25,17},{2,10},{10... | collective-permute-start | bytes 1572872 | tf_op jit(solution)/shard_map/ppermute | solution.py:24
  13.4 52.9 %all-to-all-start = ((bf16[4,128,2048]{2,1,0:T(8,128)(2,1)}), bf16[4,128,2048]{2,1,0:T(8,128)(2,1)}, u32[]{:S(2)}, u32[]{:S(2)}) async-start(bf16[4,128,2048]{2,1,0:T(8,128)(2,1)} %broadcast_in_dim.195), calls=%async_computation | async-start | bytes 4194304 | tf_op jit(solution)/shard_map/all_to_all | solution.py:46
  20.9 11.8 %collective-permute-start.10 = (bf16[2,2,4,11,64]{4,2,1,0,3:T(4,128)(2,1)S(1)}, bf16[2,2,4,11,64]{4,2,1,0,3:T(4,128)(2,1)S(1)}, u32[]{:S(2)}, u32[]{:S(2)}) collective-permute-start(bf16[2,2,4,11,64]{4,2,1,0,3:T(4,128)(2,1)S(1)} %broadcast_select_fusion.13), channel_id=1, source_target_pairs={{0,16},{8,24},{16,0},{24,8},{1,17},{9,25},{17,1},{25,9},{2,18},{10... | collective-permute-start | bytes 67592 | tf_op jit(solution)/shard_map/ppermute | solution.py:29
  22.3 24.5 %collective-permute-start.1 = (bf16[2,256,1024]{2,1,0:T(8,128)(2,1)S(1)}, bf16[2,256,1024]{2,1,0:T(8,128)(2,1)S(1)}, u32[]{:S(2)}, u32[]{:S(2)}) collective-permute-start(bf16[2,256,1024]{2,1,0:T(8,128)(2,1)S(1)} %pad_maximum_fusion.13.refs_2_.refs_4_.refs_1_.refs_3_), channel_id=1, source_target_pairs={{0,4},{4,0},{1,5},{5,1},{2,6},{6,2},{3,7},{7,3},{8,12},{12,8},{9,1... | collective-permute-start | bytes 3145736 | tf_op jit(solution)/shard_map/ppermute | solution.py:34
  23.6 24.4 %collective-permute-start.2 = (bf16[2,256,1024]{2,1,0:T(8,128)(2,1)S(1)}, bf16[2,256,1024]{2,1,0:T(8,128)(2,1)S(1)}, u32[]{:S(2)}, u32[]{:S(2)}) collective-permute-start(bf16[2,256,1024]{2,1,0:T(8,128)(2,1)S(1)} %pad_maximum_fusion.13.refs_2_.refs_4_.refs_1_.refs_3_), channel_id=1, source_target_pairs={{0,16},{8,24},{16,0},{24,8},{1,17},{9,25},{17,1},{25,9},{2,18},{10... | collective-permute-start | bytes 3145736 | tf_op jit(solution)/shard_map/ppermute | solution.py:29
  31.7 22.3 %collective-permute-start.5 = (bf16[256,2176]{1,0:T(8,128)(2,1)}, bf16[256,2176]{1,0:T(8,128)(2,1)}, u32[]{:S(2)}, u32[]{:S(2)}) collective-permute-start(bf16[256,2176]{1,0:T(8,128)(2,1)} %concatenate.142), channel_id=1, source_target_pairs={{0,8},{8,0},{16,24},{24,16},{1,9},{9,1},{17,25},{25,17},{2,10},{10... | collective-permute-start | bytes 3342344 | tf_op jit(solution)/shard_map/ppermute | solution.py:24
  32.9 17.1 %collective-permute-start.11 = (bf16[2,2,2,4,11,64]{5,3,0,2,1,4:T(4,128)(2,1)S(1)}, bf16[2,2,2,4,11,64]{5,3,0,2,1,4:T(4,128)(2,1)S(1)}, u32[]{:S(2)}, u32[]{:S(2)}) collective-permute-start(bf16[2,2,2,4,11,64]{5,3,0,2,1,4:T(4,128)(2,1)S(1)} %broadcast_select_fusion.12), channel_id=1, source_target_pairs={{0,4},{4,0},{1,5},{5,1},{2,6},{6,2},{3,7},{7,3},{8,12},{12,8},{9,1... | collective-permute-start | bytes 135176 | tf_op jit(solution)/shard_map/ppermute | solution.py:34
  47.7 11.7 %collective-permute-start.3 = (bf16[256,1024]{1,0:T(8,128)(2,1)}, bf16[256,1024]{1,0:T(8,128)(2,1)}, u32[]{:S(2)}, u32[]{:S(2)}) collective-permute-start(bf16[256,1024]{1,0:T(8,128)(2,1)} %slice_bitcast_fusion.33), channel_id=1, source_target_pairs={{0,16},{8,24},{16,0},{24,8},{1,17},{9,25},{17,1},{25,9},{2,18},{10... | collective-permute-start | bytes 1572872 | tf_op jit(solution)/shard_map/ppermute | solution.py:29
  48.8 11.4 %collective-permute-start.4 = (bf16[256,1024]{1,0:T(8,128)(2,1)}, bf16[256,1024]{1,0:T(8,128)(2,1)}, u32[]{:S(2)}, u32[]{:S(2)}) collective-permute-start(bf16[256,1024]{1,0:T(8,128)(2,1)} %slice_bitcast_fusion.32), channel_id=1, source_target_pairs={{0,4},{4,0},{1,5},{5,1},{2,6},{6,2},{3,7},{7,3},{8,12},{12,8},{9,1... | collective-permute-start | bytes 1572872 | tf_op jit(solution)/shard_map/ppermute | solution.py:34
  66.3 7.9 collective-permute-start.12
  70.3 50.2 %collective-permute-start.14 = (bf16[2,256,2176]{2,1,0:T(8,128)(2,1)S(1)}, bf16[2,256,2176]{2,1,0:T(8,128)(2,1)}, u32[]{:S(2)}, u32[]{:S(2)}) collective-permute-start(bf16[2,256,2176]{2,1,0:T(8,128)(2,1)S(1)} %pad_maximum_fusion.5.refs_2_.refs_4_), channel_id=1, source_target_pairs={{0,4},{4,0},{1,5},{5,1},{2,6},{6,2},{3,7},{7,3},{8,12},{12,8},{9,1... | collective-permute-start | bytes 6684680 | tf_op jit(solution)/shard_map/ppermute | solution.py:34
  71.5 49.9 %collective-permute-start.15 = (bf16[2,256,2176]{2,1,0:T(8,128)(2,1)S(1)}, bf16[2,256,2176]{2,1,0:T(8,128)(2,1)}, u32[]{:S(2)}, u32[]{:S(2)}) collective-permute-start(bf16[2,256,2176]{2,1,0:T(8,128)(2,1)S(1)} %pad_maximum_fusion.5.refs_2_.refs_4_), channel_id=1, source_target_pairs={{0,16},{8,24},{16,0},{24,8},{1,17},{9,25},{17,1},{25,9},{2,18},{10... | collective-permute-start | bytes 6684680 | tf_op jit(solution)/shard_map/ppermute | solution.py:29
  95.7 6.7 collective-permute-start.16
  96.0 45.9 %collective-permute-start.13 = (bf16[1024,512]{1,0:T(8,128)(2,1)S(1)}, bf16[1024,512]{1,0:T(8,128)(2,1)}, u32[]{:S(2)}, u32[]{:S(2)}) collective-permute-start(bf16[1024,512]{1,0:T(8,128)(2,1)S(1)} %copy-done.22), channel_id=1, source_target_pairs={{0,4},{1,5},{2,6},{3,7},{8,12},{9,13},{10,14},{11,15},{16,20},{17,... | collective-permute-start | bytes 3145736 | tf_op jit(solution)/shard_map/ppermute | solution.py:937
  144.2 25.5 %collective-permute-start.17 = (bf16[256,2176]{1,0:T(8,128)(2,1)}, bf16[256,2176]{1,0:T(8,128)(2,1)S(1)}, u32[]{:S(2)}, u32[]{:S(2)}) collective-permute-start(bf16[256,2176]{1,0:T(8,128)(2,1)} %slice_bitcast_fusion.13), channel_id=1, source_target_pairs={{0,16},{8,24},{16,0},{24,8},{1,17},{9,25},{17,1},{25,9},{2,18},{10... | collective-permute-start | bytes 3342344 | tf_op jit(solution)/shard_map/ppermute | solution.py:29
  147.7 26.4 %collective-permute-start.18 = (bf16[256,2176]{1,0:T(8,128)(2,1)}, bf16[256,2176]{1,0:T(8,128)(2,1)S(1)}, u32[]{:S(2)}, u32[]{:S(2)}) collective-permute-start(bf16[256,2176]{1,0:T(8,128)(2,1)} %slice_bitcast_fusion.12), channel_id=1, source_target_pairs={{0,4},{4,0},{1,5},{5,1},{2,6},{6,2},{3,7},{7,3},{8,12},{12,8},{9,1... | collective-permute-start | bytes 3342344 | tf_op jit(solution)/shard_map/ppermute | solution.py:34
  174.1 5.7 collective-permute-start.19
  183.5 52.8 %all-to-all-start.1 = ((bf16[4,128,2048]{2,1,0:T(8,128)(2,1)}), bf16[4,128,2048]{2,1,0:T(8,128)(2,1)}, u32[]{:S(2)}, u32[]{:S(2)}) async-start(bf16[4,128,2048]{2,1,0:T(8,128)(2,1)} %bitcast.46), calls=%async_computation.1 | async-start | bytes 4194304 | tf_op jit(solution)/shard_map/all_to_all | solution.py:46
  188.3 50.0 %collective-permute-start.20 = (bf16[2,256,2176]{2,1,0:T(8,128)(2,1)}, bf16[2,256,2176]{2,1,0:T(8,128)(2,1)}, u32[]{:S(2)}, u32[]{:S(2)}) collective-permute-start(bf16[2,256,2176]{2,1,0:T(8,128)(2,1)} %pad_maximum_fusion.6.refs_10_.refs_12_), channel_id=1, source_target_pairs={{0,4},{4,0},{1,5},{5,1},{2,6},{6,2},{3,7},{7,3},{8,12},{12,8},{9,1... | collective-permute-start | bytes 6684680 | tf_op jit(solution)/shard_map/ppermute | solution.py:34
  189.8 49.6 %collective-permute-start.21 = (bf16[2,256,2176]{2,1,0:T(8,128)(2,1)}, bf16[2,256,2176]{2,1,0:T(8,128)(2,1)}, u32[]{:S(2)}, u32[]{:S(2)}) collective-permute-start(bf16[2,256,2176]{2,1,0:T(8,128)(2,1)} %pad_maximum_fusion.6.refs_10_.refs_12_), channel_id=1, source_target_pairs={{0,16},{8,24},{16,0},{24,8},{1,17},{9,25},{17,1},{25,9},{2,18},{10... | collective-permute-start | bytes 6684680 | tf_op jit(solution)/shard_map/ppermute | solution.py:29
  243.5 79.7 %all-to-all-start.2 = ((bf16[4,128,2048]{2,1,0:T(8,128)(2,1)}), bf16[4,128,2048]{2,1,0:T(8,128)(2,1)}, u32[]{:S(2)}, u32[]{:S(2)}) async-start(bf16[4,128,2048]{2,1,0:T(8,128)(2,1)} %broadcast_in_dim.216), calls=%async_computation.2 | async-start | bytes 4194304 | tf_op jit(solution)/shard_map/all_to_all | solution.py:46
  248.0 72.4 %collective-permute-start.25 = (bf16[2,256,2176]{2,1,0:T(8,128)(2,1)S(1)}, bf16[2,256,2176]{2,1,0:T(8,128)(2,1)S(1)}, u32[]{:S(2)}, u32[]{:S(2)}) collective-permute-start(bf16[2,256,2176]{2,1,0:T(8,128)(2,1)S(1)} %pad_maximum_fusion.7.refs_1_.refs_3_.refs_2_.refs_4_), channel_id=1, source_target_pairs={{0,4},{4,0},{1,5},{5,1},{2,6},{6,2},{3,7},{7,3},{8,12},{12,8},{9,1... | collective-permute-start | bytes 6684680 | tf_op jit(solution)/shard_map/ppermute | solution.py:34
  248.4 74.8 %collective-permute-start.26 = (bf16[2,256,2176]{2,1,0:T(8,128)(2,1)S(1)}, bf16[2,256,2176]{2,1,0:T(8,128)(2,1)}, u32[]{:S(2)}, u32[]{:S(2)}) collective-permute-start(bf16[2,256,2176]{2,1,0:T(8,128)(2,1)S(1)} %pad_maximum_fusion.7.refs_1_.refs_3_.refs_2_.refs_4_), channel_id=1, source_target_pairs={{0,16},{8,24},{16,0},{24,8},{1,17},{9,25},{17,1},{25,9},{2,18},{10... | collective-permute-start | bytes 6684680 | tf_op jit(solution)/shard_map/ppermute | solution.py:29
  250.0 70.4 %collective-permute-start.23 = (bf16[256,2176]{1,0:T(8,128)(2,1)S(1)}, bf16[256,2176]{1,0:T(8,128)(2,1)S(1)}, u32[]{:S(2)}, u32[]{:S(2)}) collective-permute-start(bf16[256,2176]{1,0:T(8,128)(2,1)S(1)} %slice_bitcast_fusion.11), channel_id=1, source_target_pairs={{0,16},{8,24},{16,0},{24,8},{1,17},{9,25},{17,1},{25,9},{2,18},{10... | collective-permute-start | bytes 3342344 | tf_op jit(solution)/shard_map/ppermute | solution.py:29
  252.6 67.8 %collective-permute-start.24 = (bf16[256,2176]{1,0:T(8,128)(2,1)S(1)}, bf16[256,2176]{1,0:T(8,128)(2,1)S(1)}, u32[]{:S(2)}, u32[]{:S(2)}) collective-permute-start(bf16[256,2176]{1,0:T(8,128)(2,1)S(1)} %slice_bitcast_fusion.10), channel_id=1, source_target_pairs={{0,4},{4,0},{1,5},{5,1},{2,6},{6,2},{3,7},{7,3},{8,12},{12,8},{9,1... | collective-permute-start | bytes 3342344 | tf_op jit(solution)/shard_map/ppermute | solution.py:34
  323.2 11.9 %collective-permute-start.27 = (bf16[512,2048]{1,0:T(8,128)(2,1)}, bf16[512,2048]{1,0:T(8,128)(2,1)S(1)}, u32[]{:S(2)}, u32[]{:S(2)}) collective-permute-start(bf16[512,2048]{1,0:T(8,128)(2,1)} %bitcast.56.refs_0_.refs_2_), channel_id=1, source_target_pairs={{0,8},{8,0},{16,24},{24,16},{1,9},{9,1},{17,25},{25,17},{2,10},{10... | collective-permute-start | bytes 6291464 | tf_op jit(solution)/shard_map/ppermute | solution.py:24
  328.3 39.4 %collective-permute-start.28 = (bf16[256,2176]{1,0:T(8,128)(2,1)}, bf16[256,2176]{1,0:T(8,128)(2,1)}, u32[]{:S(2)}, u32[]{:S(2)}) collective-permute-start(bf16[256,2176]{1,0:T(8,128)(2,1)} %slice_bitcast_fusion.9), channel_id=1, source_target_pairs={{0,16},{8,24},{16,0},{24,8},{1,17},{9,25},{17,1},{25,9},{2,18},{10... | collective-permute-start | bytes 3342344 | tf_op jit(solution)/shard_map/ppermute | solution.py:29
  330.9 36.9 %collective-permute-start.29 = (bf16[256,2176]{1,0:T(8,128)(2,1)}, bf16[256,2176]{1,0:T(8,128)(2,1)}, u32[]{:S(2)}, u32[]{:S(2)}) collective-permute-start(bf16[256,2176]{1,0:T(8,128)(2,1)} %slice_bitcast_fusion.8), channel_id=1, source_target_pairs={{0,4},{4,0},{1,5},{5,1},{2,6},{6,2},{3,7},{7,3},{8,12},{12,8},{9,1... | collective-permute-start | bytes 3342344 | tf_op jit(solution)/shard_map/ppermute | solution.py:34
  385.2 5.1 collective-permute-start.30
  394.0 52.2 %all-to-all-start.3 = ((bf16[4,128,2048]{2,1,0:T(8,128)(2,1)}), bf16[4,128,2048]{2,1,0:T(8,128)(2,1)S(1)}, u32[]{:S(2)}, u32[]{:S(2)}) async-start(bf16[4,128,2048]{2,1,0:T(8,128)(2,1)} %bitcast.282), calls=%async_computation.3 | async-start | bytes 4194304 | tf_op jit(solution)/shard_map/all_to_all | solution.py:46
  499.2 5.8 collective-permute-start.31
  523.3 58.3 %collective-permute-start.33 = (bf16[2,256,2176]{2,1,0:T(8,128)(2,1)}, bf16[2,256,2176]{2,1,0:T(8,128)(2,1)}, u32[]{:S(2)}, u32[]{:S(2)}) collective-permute-start(bf16[2,256,2176]{2,1,0:T(8,128)(2,1)} %get-tuple-element.168), channel_id=1, source_target_pairs={{0,16},{8,24},{16,0},{24,8},{1,17},{9,25},{17,1},{25,9},{2,18},{10... | collective-permute-start | bytes 6684680 | tf_op jit(solution)/shard_map/ppermute | solution.py:29
  524.1 57.5 %collective-permute-start.34 = (bf16[2,256,2176]{2,1,0:T(8,128)(2,1)}, bf16[2,256,2176]{2,1,0:T(8,128)(2,1)}, u32[]{:S(2)}, u32[]{:S(2)}) collective-permute-start(bf16[2,256,2176]{2,1,0:T(8,128)(2,1)} %get-tuple-element.170), channel_id=1, source_target_pairs={{0,4},{4,0},{1,5},{5,1},{2,6},{6,2},{3,7},{7,3},{8,12},{12,8},{9,1... | collective-permute-start | bytes 6684680 | tf_op jit(solution)/shard_map/ppermute | solution.py:34
  576.1 5.5 collective-permute-start.32
  578.4 13.8 %collective-permute-start.35 = (f32[9,4,128]{2,0,1:T(8,128)S(1)}, f32[9,4,128]{2,0,1:T(8,128)S(1)}, u32[]{:S(2)}, u32[]{:S(2)}) collective-permute-start(f32[9,4,128]{2,0,1:T(8,128)S(1)} %fusion.29), channel_id=1, source_target_pairs={{0,8},{8,0},{16,24},{24,16},{1,9},{9,1},{17,25},{25,17},{2,10},{10... | collective-permute-start | bytes 55304 | tf_op jit(solution)/shard_map/ppermute | solution.py:24
  586.1 55.3 %all-to-all-start.5 = ((bf16[4,128,2048]{2,1,0:T(8,128)(2,1)}), bf16[4,128,2048]{2,1,0:T(8,128)(2,1)S(1)}, u32[]{:S(2)}, u32[]{:S(2)}) async-start(bf16[4,128,2048]{2,1,0:T(8,128)(2,1)} %bitcast.73), calls=%async_computation.5 | async-start | bytes 4194304 | tf_op jit(solution)/shard_map/all_to_all | solution.py:46
  594.9 46.8 %collective-permute-start.40 = (bf16[256,2176]{1,0:T(8,128)(2,1)}, bf16[256,2176]{1,0:T(8,128)(2,1)}, u32[]{:S(2)}, u32[]{:S(2)}) collective-permute-start(bf16[256,2176]{1,0:T(8,128)(2,1)} %fusion.8), channel_id=1, source_target_pairs={{0,16},{8,24},{16,0},{24,8},{1,17},{9,25},{17,1},{25,9},{2,18},{10... | collective-permute-start | bytes 3342344 | tf_op jit(solution)/shard_map/ppermute | solution.py:29
  597.4 44.2 %collective-permute-start.39 = (bf16[256,2176]{1,0:T(8,128)(2,1)}, bf16[256,2176]{1,0:T(8,128)(2,1)}, u32[]{:S(2)}, u32[]{:S(2)}) collective-permute-start(bf16[256,2176]{1,0:T(8,128)(2,1)} %fusion.7), channel_id=1, source_target_pairs={{0,4},{4,0},{1,5},{5,1},{2,6},{6,2},{3,7},{7,3},{8,12},{12,8},{9,1... | collective-permute-start | bytes 3342344 | tf_op jit(solution)/shard_map/ppermute | solution.py:34
  632.5 7.2 collective-permute-start.36
  634.0 6.6 collective-permute-start.37
  636.0 5.3 collective-permute-start.38
  639.7 96.0 %collective-permute-start.44 = (bf16[2,256,4352]{2,1,0:T(8,128)(2,1)}, bf16[2,256,4352]{2,1,0:T(8,128)(2,1)}, u32[]{:S(2)}, u32[]{:S(2)}) collective-permute-start(bf16[2,256,4352]{2,1,0:T(8,128)(2,1)} %get-tuple-element.186), channel_id=1, source_target_pairs={{0,16},{8,24},{16,0},{24,8},{1,17},{9,25},{17,1},{25,9},{2,18},{10... | collective-permute-start | bytes 13369352 | tf_op jit(solution)/shard_map/ppermute | solution.py:29
  640.5 95.7 %collective-permute-start.45 = (bf16[2,256,4352]{2,1,0:T(8,128)(2,1)}, bf16[2,256,4352]{2,1,0:T(8,128)(2,1)}, u32[]{:S(2)}, u32[]{:S(2)}) collective-permute-start(bf16[2,256,4352]{2,1,0:T(8,128)(2,1)} %get-tuple-element.188), channel_id=1, source_target_pairs={{0,4},{4,0},{1,5},{5,1},{2,6},{6,2},{3,7},{7,3},{8,12},{12,8},{9,1... | collective-permute-start | bytes 13369352 | tf_op jit(solution)/shard_map/ppermute | solution.py:34
  646.6 52.2 %all-to-all-start.6 = ((bf16[4,128,2048]{2,1,0:T(8,128)(2,1)}), bf16[4,128,2048]{2,1,0:T(8,128)(2,1)}, u32[]{:S(2)}, u32[]{:S(2)}) async-start(bf16[4,128,2048]{2,1,0:T(8,128)(2,1)} %broadcast_in_dim.223), calls=%async_computation.6 | async-start | bytes 4194304 | tf_op jit(solution)/shard_map/all_to_all | solution.py:46
  655.6 4.9 collective-permute-start.41
  698.8 5.6 collective-permute-start.42
  736.2 23.5 %collective-permute-start.43 = (bf16[1024,512]{1,0:T(8,128)(2,1)}, bf16[1024,512]{1,0:T(8,128)(2,1)S(1)}, u32[]{:S(2)}, u32[]{:S(2)}) collective-permute-start(bf16[1024,512]{1,0:T(8,128)(2,1)} %get-tuple-element.211), channel_id=1, source_target_pairs={{4,0},{5,1},{6,2},{7,3},{12,8},{13,9},{14,10},{15,11},{20,16},{21,... | collective-permute-start | bytes 3145736 | tf_op jit(solution)/shard_map/ppermute | solution.py:1020
  771.4 16.5 %collective-permute-start.46 = (bf16[512,2048]{1,0:T(8,128)(2,1)}, bf16[512,2048]{1,0:T(8,128)(2,1)}, u32[]{:S(2)}, u32[]{:S(2)}) collective-permute-start(bf16[512,2048]{1,0:T(8,128)(2,1)} %get-tuple-element.218), channel_id=1, source_target_pairs={{0,8},{8,0},{16,24},{24,16},{1,9},{9,1},{17,25},{25,17},{2,10},{10... | collective-permute-start | bytes 6291464 | tf_op jit(solution)/shard_map/ppermute | solution.py:24
  777.9 50.4 %collective-permute-start.59 = (bf16[256,4352]{1,0:T(8,128)(2,1)}, bf16[256,4352]{1,0:T(8,128)(2,1)}, u32[]{:S(2)}, u32[]{:S(2)}) collective-permute-start(bf16[256,4352]{1,0:T(8,128)(2,1)} %fusion.4), channel_id=1, source_target_pairs={{0,16},{8,24},{16,0},{24,8},{1,17},{9,25},{17,1},{25,9},{2,18},{10... | collective-permute-start | bytes 6684680 | tf_op jit(solution)/shard_map/ppermute | solution.py:29
  787.4 49.8 %collective-permute-start.58 = (bf16[256,4352]{1,0:T(8,128)(2,1)S(1)}, bf16[256,4352]{1,0:T(8,128)(2,1)}, u32[]{:S(2)}, u32[]{:S(2)}) collective-permute-start(bf16[256,4352]{1,0:T(8,128)(2,1)S(1)} %copy-done.28), channel_id=1, source_target_pairs={{0,4},{4,0},{1,5},{5,1},{2,6},{6,2},{3,7},{7,3},{8,12},{12,8},{9,1... | collective-permute-start | bytes 6684680 | tf_op jit(solution)/shard_map/ppermute | solution.py:34
  806.8 57.3 %collective-permute-start.53 = (bf16[2,256,1024]{2,1,0:T(8,128)(2,1)}, bf16[2,256,1024]{2,1,0:T(8,128)(2,1)}, u32[]{:S(2)}, u32[]{:S(2)}) collective-permute-start(bf16[2,256,1024]{2,1,0:T(8,128)(2,1)} %get-tuple-element.223), channel_id=1, source_target_pairs={{0,16},{8,24},{16,0},{24,8},{1,17},{9,25},{17,1},{25,9},{2,18},{10... | collective-permute-start | bytes 3145736 | tf_op jit(solution)/shard_map/ppermute | solution.py:29
  807.7 52.3 %all-to-all-start.7 = ((bf16[4,128,2048]{2,1,0:T(8,128)(2,1)}), bf16[4,128,2048]{2,1,0:T(8,128)(2,1)}, u32[]{:S(2)}, u32[]{:S(2)}) async-start(bf16[4,128,2048]{2,1,0:T(8,128)(2,1)} %bitcast.97), calls=%async_computation.7 | async-start | bytes 4194304 | tf_op jit(solution)/shard_map/all_to_all | solution.py:46
  812.4 54.8 %collective-permute-start.55 = (bf16[2,256,1024]{2,1,0:T(8,128)(2,1)}, bf16[2,256,1024]{2,1,0:T(8,128)(2,1)}, u32[]{:S(2)}, u32[]{:S(2)}) collective-permute-start(bf16[2,256,1024]{2,1,0:T(8,128)(2,1)} %get-tuple-element.225), channel_id=1, source_target_pairs={{0,4},{4,0},{1,5},{5,1},{2,6},{6,2},{3,7},{7,3},{8,12},{12,8},{9,1... | collective-permute-start | bytes 3145736 | tf_op jit(solution)/shard_map/ppermute | solution.py:34
  832.0 8.9 collective-permute-start.60
  862.7 3.7 collective-permute-start.47
  865.5 20.4 %collective-permute-start.54 = (bf16[256,1024]{1,0:T(8,128)(2,1)S(1)}, bf16[256,1024]{1,0:T(8,128)(2,1)S(1)}, u32[]{:S(2)}, u32[]{:S(2)}) collective-permute-start(bf16[256,1024]{1,0:T(8,128)(2,1)S(1)} %fusion.19), channel_id=1, source_target_pairs={{0,4},{4,0},{1,5},{5,1},{2,6},{6,2},{3,7},{7,3},{8,12},{12,8},{9,1... | collective-permute-start | bytes 1572872 | tf_op jit(solution)/shard_map/ppermute | solution.py:34
  868.4 12.4 %collective-permute-start.56 = (bf16[256,1024]{1,0:T(8,128)(2,1)S(1)}, bf16[256,1024]{1,0:T(8,128)(2,1)S(1)}, u32[]{:S(2)}, u32[]{:S(2)}) collective-permute-start(bf16[256,1024]{1,0:T(8,128)(2,1)S(1)} %fusion.20), channel_id=1, source_target_pairs={{0,16},{8,24},{16,0},{24,8},{1,17},{9,25},{17,1},{25,9},{2,18},{10... | collective-permute-start | bytes 1572872 | tf_op jit(solution)/shard_map/ppermute | solution.py:29
  869.7 5.7 collective-permute-start.49
  875.4 4.8 collective-permute-start.50
  875.4 4.8 collective-permute-start.51
  882.2 5.1 collective-permute-start.57
  (60 other events, 626.5 us)

commit v4 on v3

--- a/solution.py
+++ b/solution.py
@@ -1035,6 +1035,7 @@
         ],
     )
     attn_moves = grad_first(attn_groups)
+    (grad_down,) = after((grad_down,), [wide_moves[1]])
     bias_own = jnp.sum(grad_projected.astype(F32), axis=0).reshape(3, width)
     columns = 2 * nz
     column = lax.broadcasted_iota(jnp.int32, (3, columns * width), 1)

time: 903 us -> 898 us (level)
    unnamed x117 -> x109, local copies, waits for them, and re-layouts: 24.4 us -> 25.4 us
  transfers between devices with their start and end apart: 68 -> 68, of which waited for: 33 -> 32; matrix products, arithmetic and copies ran while one was open for 17% -> 17% of each run, Pallas kernels for 20% -> 20%
where the time goes in v4:
time: 898 us; the launch traced here: 888 us
  waiting for transfers between devices  318 us (35%)
  Pallas kernels  227 us (25%)
  starting transfers between devices  107 us (12%)
  other arithmetic  91.5 us (10%)
  local copies, waits for them, and re-layouts  87.6 us (10%)
  blocking collectives  50.1 us (6%)
    all_to_all x7, waiting for transfers between devices, exchange(): return lax.all_to_all(v, 'exp', split_axis=0, concat_axis=0, tiled=True)  126 us
    ppermute x16, waiting for transfers between devices, y_swap(): return lax.ppermute(v, 'dp', [(i, i ^ 2) for i in range(n)])  102 us
    pallas_call x3, Pallas kernels, weight_grad(): pl.pallas_call(functools.partial(weight_grad_kernel, n, [len(rows) for ro...  66.4 us
    pallas_call x4, Pallas kernels, project_home(): pl.pallas_call(functools.partial(home_kernel, len(acts), [i for _, i in e...  64.3 us
    all_to_all x1, blocking collectives, exchange(): return lax.all_to_all(v, 'exp', split_axis=0, concat_axis=0, tiled=True)  50.1 us
    ppermute x25, waiting for transfers between devices, shift(): return lax.ppermute(v, axis, [(i, (i + s) % n) for i in range(n)])  35.3 us
    pallas_call x1, Pallas kernels, up_call(): pl.pallas_call(functools.partial(up_kernel, len(shards), len(gates), expe...  31.2 us
    ppermute x18, starting transfers between devices, core_swap(): return lax.ppermute(v, 'dp', [(i, i ^ 1) for i in range(n)])  30.9 us
  transfers between devices with their start and end apart: 68, of which 32 were waited for; matrix products, arithmetic and copies ran while one was open for 17% of the time, Pallas kernels for 20%

profile of v4, /device:TPU:1, one launch (start us, length us, event | category | flops | bytes accessed | tf_op | source)
XLA Modules:
  0.0 887.5 jit_solution(17720654988343525035)
XLA Ops:
  13.4 4.4 all-to-all-start
  28.4 3.3 concatenate.142
  33.2 13.6 %collective-permute-done.1.refs_3_.refs_5_.refs_2_.refs_4_ = bf16[2,256,1024]{2,1,0:T(8,128)(2,1)S(1)} collective-permute-done((bf16[2,256,1024]{2,1,0:T(8,128)(2,1)S(1)}, bf16[2,256,1024]{2,1,0:T(8,128)(2,1)S(1)}, u32[]{:S(2)}, u32[]{:S(2)}) %collective-permute-start.1) | collective-permute-done | bytes 1048608 | tf_op jit(solution)/shard_map/ppermute | solution.py:34
  50.7 3.2 concatenate.141
  55.8 3.5 collective-permute-done.3
  60.2 6.1 all-to-all-done
  74.1 13.5 %qkv_rope.1 = (bf16[1024,2048]{1,0:T(8,128)(2,1)}, bf16[1024,256]{1,0:T(8,128)(2,1)}, bf16[1024,512]{1,0:T(8,128)(2,1)}) custom-call(s32[8]{0:T(128)} %stack.97.places_ref, bf16[512,2048]{1,0:T(8,128)(2,1)} %bitcast.13.refs_0_, bf16[512,2048]{1,0:T(8,128)(2,1)} %collective-permute-done.12.refs_1_, bf16[2,256,1024]{2,1,0:T(8,128)(2,1)} %copy-done.1, ...), custom_call_target="tpu_custom_call" | custom-call | flops 402653184 | bytes 1441792 | tf_op jit(solution)/shard_map/qkv_rope/pallas_call | solution.py:278
  92.4 3.2 concatenate.149
  96.0 3.2 collective-permute-start.13
  99.1 3.2 concatenate.148
  102.4 3.2 pad_maximum_fusion.6.refs_10_.refs_12_
  105.5 14.9 %collective-permute-done.14.refs_3_.refs_5_ = bf16[2,256,2176]{2,1,0:T(8,128)(2,1)} collective-permute-done((bf16[2,256,2176]{2,1,0:T(8,128)(2,1)S(1)}, bf16[2,256,2176]{2,1,0:T(8,128)(2,1)}, u32[]{:S(2)}, u32[]{:S(2)}) %collective-permute-start.14) | collective-permute-done | bytes 2228256 | tf_op jit(solution)/shard_map/ppermute | solution.py:34
  121.3 20.5 %collective-permute-done.13.refs_1_ = bf16[1024,512]{1,0:T(8,128)(2,1)} collective-permute-done((bf16[1024,512]{1,0:T(8,128)(2,1)S(1)}, bf16[1024,512]{1,0:T(8,128)(2,1)}, u32[]{:S(2)}, u32[]{:S(2)}) %collective-permute-start.13) | collective-permute-done | bytes 1048608 | tf_op jit(solution)/shard_map/ppermute | solution.py:937
  151.5 9.5 %attend.1.refs_0_.refs_3_ = bf16[1024,256]{1,0:T(8,128)(2,1)} custom-call(s32[9]{0:T(128)} %pad_add_fusion.info_ref, bf16[1024,256]{1,0:T(8,128)(2,1)} %get-tuple-element.135.q_ref, bf16[1024,512]{1,0:T(8,128)(2,1)} %get-tuple-element.140.refs_0_, bf16[1024,512]{1,0:T(8,128)(2,1)} %collective-permute-done.13.refs_1_), custom_call_target="tpu_custom_call" | custom-call | flops 33554432 | bytes 393216 | tf_op jit(solution)/shard_map/attend/pallas_call | solution.py:693
  161.0 7.4 project_home.4
  169.7 4.4 collective-permute-done.18
  175.7 4.0 collective-permute-done.19
  179.7 3.7 add_convert_fusion.5
  183.4 4.8 all-to-all-start.1
  198.8 37.5 %all-to-all-done.1 = bf16[4,128,2048]{2,1,0:T(8,128)(2,1)} async-done(((bf16[4,128,2048]{2,1,0:T(8,128)(2,1)}), bf16[4,128,2048]{2,1,0:T(8,128)(2,1)}, u32[]{:S(2)}, u32[]{:S(2)}) %all-to-all-start.1) | async-done | bytes 2097184 | tf_op jit(solution)/shard_map/all_to_all | solution.py:46
  243.6 4.4 all-to-all-start.2
  253.8 66.6 %collective-permute-done.23 = bf16[256,2176]{1,0:T(8,128)(2,1)S(1)} collective-permute-done((bf16[256,2176]{1,0:T(8,128)(2,1)S(1)}, bf16[256,2176]{1,0:T(8,128)(2,1)S(1)}, u32[]{:S(2)}, u32[]{:S(2)}) %collective-permute-start.23) | collective-permute-done | bytes 1114144 | tf_op jit(solution)/shard_map/ppermute | solution.py:29
  323.3 2.8 collective-permute-start.27
  336.7 31.2 %expert_up.1 = (bf16[1024,2176]{1,0:T(8,128)(2,1)}, bf16[1024,2176]{1,0:T(8,128)(2,1)}, bf16[1024,2176]{1,0:T(8,128)(2,1)}, bf16[1024,2176]{1,0:T(8,128)(2,1)}, f32[1024,128]{1,0:T(8,128)}) custom-call(s32[10]{0:T(128)} %concatenate.152.info_ref, bf16[512,2048]{1,0:T(8,128)(2,1)} %bitcast.56.refs_0_.refs_2_, bf16[512,2048]{1,0:T(8,128)(2,1)} %copy-done.7, ...), custom_call_target="tpu_custom_call" | custom-call | flops 2281701376 | bytes 4980736 | tf_op jit(solution)/shard_map/expert_up/pallas_call | solution.py:365
  368.0 17.5 %project_home.5 = (bf16[512,2048]{1,0:T(8,128)(2,1)}, bf16[512,2048]{1,0:T(8,128)(2,1)}) custom-call(s32[8]{0:T(128)} %stack.97.places_ref, bf16[1024,2176]{1,0:T(8,128)(2,1)} %get-tuple-element.164.refs_0_.refs_2_, bf16[2,256,2176]{2,1,0:T(8,128)(2,1)} %copy-done.4, bf16[2,256,2176]{2,1,0:T(8,128)(2,1)} %copy-done.6, bf16[2,256,2176]{2,1,0:T(8,128)(2,1)} %copy-done.4, ...), custom_call_target="tpu_custom_call" | custom-call | flops 1140850688 | bytes 2195456 | tf_op jit(solution)/shard_map/project_home/pallas_call | solution.py:561
  386.6 4.0 collective-permute-done.30
  390.6 3.7 add_convert_fusion.4
  394.3 4.4 all-to-all-start.3
  401.3 45.2 %all-to-all-done.3 = bf16[4,128,2048]{2,1,0:T(8,128)(2,1)S(1)} async-done(((bf16[4,128,2048]{2,1,0:T(8,128)(2,1)}), bf16[4,128,2048]{2,1,0:T(8,128)(2,1)S(1)}, u32[]{:S(2)}, u32[]{:S(2)}) %all-to-all-start.3) | async-done | bytes 2097184 | tf_op jit(solution)/shard_map/all_to_all | solution.py:46
  446.5 2.7 fusion.21
  449.4 50.1 %all_to_all.71 = bf16[4,128,2048]{2,1,0:T(8,128)(2,1)S(1)} all-to-all(bf16[4,128,2048]{2,1,0:T(8,128)(2,1)S(1)} %broadcast_in_dim.222), channel_id=1, replica_groups=mesh['dp'=4,'ctx'=2,'exp'=4] {'exp'}, dimensions={0} | all-to-all | bytes 4194304 | tf_op jit(solution)/shard_map/all_to_all | solution.py:46
  502.1 3.3 collective-permute-done.31.refs_1_
  505.4 18.2 %weight_grad.3 = (bf16[2,256,2176]{2,1,0:T(8,128)(2,1)}, bf16[2,256,2176]{2,1,0:T(8,128)(2,1)}, bf16[2,256,2176]{2,1,0:T(8,128)(2,1)}, bf16[2,256,2176]{2,1,0:T(8,128)(2,1)}) custom-call(s32[8]{0:T(128)} %stack.114.places_ref, bf16[512,2048]{1,0:T(8,128)(2,1)} %bitcast.280, bf16[512,2048]{1,0:T(8,128)(2,1)} %collective-permute-done.31.refs_1_, ...), custom_call_target="tpu_custom_call" | custom-call | flops 1140850688 | bytes 2195456 | tf_op jit(solution)/shard_map/weight_grad/pallas_call | solution.py:640
  524.8 22.5 %down_back.1 = (bf16[1024,2176]{1,0:T(8,128)(2,1)}, bf16[1024,2176]{1,0:T(8,128)(2,1)}, f32[1024,128]{1,0:T(8,128)}) custom-call(s32[10]{0:T(128)} %concatenate.152.info_ref, bf16[512,2048]{1,0:T(8,128)(2,1)} %bitcast.281, bf16[512,2048]{1,0:T(8,128)(2,1)} %collective-permute-done.31.refs_1_, bf16[2,256,2176]{2,1,0:T(8,128)(2,1)} %copy-done.4, ...), custom_call_target="tpu_custom_call" | custom-call | flops 1140850688 | bytes 4423680 | tf_op jit(solution)/shard_map/down_back/pallas_call | solution.py:435
  547.3 29.1 %project_home.6 = (bf16[512,2048]{1,0:T(8,128)(2,1)}, bf16[512,2048]{1,0:T(8,128)(2,1)}) custom-call(s32[8]{0:T(128)} %stack.97.places_ref, bf16[1024,2176]{1,0:T(8,128)(2,1)} %get-tuple-element.185.refs_0_.refs_4_, bf16[1024,2176]{1,0:T(8,128)(2,1)} %get-tuple-element.186.refs_1_.refs_5_, bf16[2,256,2176]{2,1,0:T(8,128)(2,1)} %copy-done.5, ...), custom_call_target="tpu_custom_call" | custom-call | flops 2281701376 | bytes 3866624 | tf_op jit(solution)/shard_map/project_home/pallas_call | solution.py:561
  578.9 3.1 collective-permute-done.32
  582.0 4.4 add_convert_fusion.3
  586.4 3.6 all-to-all-start.5
  590.1 2.5 slice_bitcast_fusion.5
  592.5 2.7 fusion.8
  595.2 2.5 fusion.7
  599.2 33.7 %weight_grad.4 = (bf16[2,256,4352]{2,1,0:T(8,128)(2,1)}, bf16[2,256,4352]{2,1,0:T(8,128)(2,1)}, bf16[2,256,4352]{2,1,0:T(8,128)(2,1)}, bf16[2,256,4352]{2,1,0:T(8,128)(2,1)}) custom-call(s32[8]{0:T(128)} %stack.114.places_ref, bf16[512,2048]{1,0:T(8,128)(2,1)} %bitcast.56.refs_0_.refs_2_, bf16[512,2048]{1,0:T(8,128)(2,1)} %copy-done.7, ...), custom_call_target="tpu_custom_call" | custom-call | flops 2281701376 | bytes 3866624 | tf_op jit(solution)/shard_map/weight_grad/pallas_call | solution.py:640
  647.0 4.5 all-to-all-start.6
  656.0 2.6 collective-permute-start.41
  662.5 36.8 %all-to-all-done.6 = bf16[4,128,2048]{2,1,0:T(8,128)(2,1)} async-done(((bf16[4,128,2048]{2,1,0:T(8,128)(2,1)}), bf16[4,128,2048]{2,1,0:T(8,128)(2,1)}, u32[]{:S(2)}, u32[]{:S(2)}) %all-to-all-start.6) | async-done | bytes 2097184 | tf_op jit(solution)/shard_map/all_to_all | solution.py:46
  702.2 2.6 collective-permute-done.42.refs_1_
  704.8 6.8 out_back.1
  711.7 12.4 %attend_back.1 = (bf16[1024,256]{1,0:T(8,128)(2,1)}, f32[1024,512]{1,0:T(8,128)}, bf16[1024,512]{1,0:T(8,128)(2,1)}) custom-call(s32[9]{0:T(128)} %pad_add_fusion.info_ref, bf16[1024,256]{1,0:T(8,128)(2,1)} %get-tuple-element.135.q_ref, bf16[1024,256]{1,0:T(8,128)(2,1)} %get-tuple-element.210.da_ref, bf16[1024,512]{1,0:T(8,128)(2,1)} %get-tuple-element.140.refs_0_, ...), custom_call_target="tpu_custom_call" | custom-call | flops 83886080 | bytes 851968 | tf_op jit(solution)/shard_map/attend_back/pallas_call | solution.py:758
  724.1 11.9 %collective-permute-done.44 = bf16[2,256,4352]{2,1,0:T(8,128)(2,1)} collective-permute-done((bf16[2,256,4352]{2,1,0:T(8,128)(2,1)}, bf16[2,256,4352]{2,1,0:T(8,128)(2,1)}, u32[]{:S(2)}, u32[]{:S(2)}) %collective-permute-start.44) | collective-permute-done | bytes 4456480 | tf_op jit(solution)/shard_map/ppermute | solution.py:29
  737.9 4.2 fusion.4
  742.1 4.3 fusion.3
  746.4 13.7 %collective-permute-done.43 = bf16[1024,512]{1,0:T(8,128)(2,1)S(1)} collective-permute-done((bf16[1024,512]{1,0:T(8,128)(2,1)}, bf16[1024,512]{1,0:T(8,128)(2,1)S(1)}, u32[]{:S(2)}, u32[]{:S(2)}) %collective-permute-start.43) | collective-permute-done | bytes 1048608 | tf_op jit(solution)/shard_map/ppermute | solution.py:1020
  761.7 10.2 %project_home.7 = (bf16[512,2048]{1,0:T(8,128)(2,1)}, bf16[512,2048]{1,0:T(8,128)(2,1)}) custom-call(s32[8]{0:T(128)} %stack.97.places_ref, bf16[1024,768]{1,0:T(8,128)(2,1)} %pad_maximum_fusion.8.refs_0_.refs_2_, bf16[2,256,1024]{2,1,0:T(8,128)(2,1)} %copy-done.1, bf16[2,256,1024]{2,1,0:T(8,128)(2,1)} %copy-done.2, bf16[2,256,1024]{2,1,0:T(8,128)(2,1)} %copy-done.1, ...), custom_call_target="tpu_custom_call" | custom-call | flops 402653184 | bytes 1114112 | tf_op jit(solution)/shard_map/project_home/pallas_call | solution.py:561
  771.9 4.2 collective-permute-start.46
  783.6 4.5 add_convert_fusion.2
  788.2 14.5 %weight_grad.5 = (bf16[2,256,1024]{2,1,0:T(8,128)(2,1)}, bf16[2,256,1024]{2,1,0:T(8,128)(2,1)}, bf16[2,256,1024]{2,1,0:T(8,128)(2,1)}, bf16[2,256,1024]{2,1,0:T(8,128)(2,1)}) custom-call(s32[8]{0:T(128)} %stack.114.places_ref, bf16[1024,2048]{1,0:T(8,128)(2,1)} %get-tuple-element.221.refs_0_, bf16[1024,2048]{1,0:T(8,128)(2,1)} %get-tuple-element.222.refs_1_, ...), custom_call_target="tpu_custom_call" | custom-call | flops 536870912 | bytes 1310720 | tf_op jit(solution)/shard_map/weight_grad/pallas_call | solution.py:640
  803.5 4.7 all-to-all-start.7
  809.7 16.8 %collective-permute-done.59 = bf16[256,4352]{1,0:T(8,128)(2,1)} collective-permute-done((bf16[256,4352]{1,0:T(8,128)(2,1)}, bf16[256,4352]{1,0:T(8,128)(2,1)}, u32[]{:S(2)}, u32[]{:S(2)}) %collective-permute-start.59) | collective-permute-done | bytes 2228256 | tf_op jit(solution)/shard_map/ppermute | solution.py:29
  826.5 3.8 fusion
  831.6 3.3 bitcast_add_fusion.1
  838.4 3.8 copy.89
  844.6 7.2 copy.88
  851.9 3.8 copy.87
  865.3 5.3 collective-permute-start.49
  (379 shorter events, 177.2 us)
Async XLA Ops:
  2.3 15.6 %collective-permute-start.6 = (bf16[4,32,128]{1,2,0:T(8,128)(2,1)S(1)}, bf16[4,32,128]{1,2,0:T(8,128)(2,1)S(1)}, u32[]{:S(2)}, u32[]{:S(2)}) collective-permute-start(bf16[4,32,128]{1,2,0:T(8,128)(2,1)S(1)} %broadcast_select_fusion.9), channel_id=1, source_target_pairs={{0,1},{1,2},{2,3},{3,0},{4,5},{5,6},{6,7},{7,4},{8,9},{9,10},{10,1... | collective-permute-start | bytes 98312 | tf_op jit(solution)/shard_map/ppermute | solution.py:34
  4.5 13.5 %collective-permute-start.7 = (bf16[4,32,128]{1,2,0:T(8,128)(2,1)S(1)}, bf16[4,32,128]{1,2,0:T(8,128)(2,1)S(1)}, u32[]{:S(2)}, u32[]{:S(2)}) collective-permute-start(bf16[4,32,128]{1,2,0:T(8,128)(2,1)S(1)} %broadcast_select_fusion.9), channel_id=1, source_target_pairs={{0,2},{1,3},{2,0},{3,1},{4,6},{5,7},{6,4},{7,5},{8,10},{9,11},{10,... | collective-permute-start | bytes 98312 | tf_op jit(solution)/shard_map/ppermute | solution.py:34
  6.8 11.2 %collective-permute-start.8 = (bf16[4,32,128]{1,2,0:T(8,128)(2,1)S(1)}, bf16[4,32,128]{1,2,0:T(8,128)(2,1)S(1)}, u32[]{:S(2)}, u32[]{:S(2)}) collective-permute-start(bf16[4,32,128]{1,2,0:T(8,128)(2,1)S(1)} %broadcast_select_fusion.9), channel_id=1, source_target_pairs={{0,3},{1,0},{2,1},{3,2},{4,7},{5,4},{6,5},{7,6},{8,11},{9,8},{10,9... | collective-permute-start | bytes 98312 | tf_op jit(solution)/shard_map/ppermute | solution.py:34
  10.2 11.9 %collective-permute-start = (bf16[256,1024]{1,0:T(8,128)(2,1)S(1)}, bf16[256,1024]{1,0:T(8,128)(2,1)S(1)}, u32[]{:S(2)}, u32[]{:S(2)}) collective-permute-start(bf16[256,1024]{1,0:T(8,128)(2,1)S(1)} %pad_maximum_fusion.14), channel_id=1, source_target_pairs={{0,8},{8,0},{16,24},{24,16},{1,9},{9,1},{17,25},{25,17},{2,10},{10... | collective-permute-start | bytes 1572872 | tf_op jit(solution)/shard_map/ppermute | solution.py:24
  13.4 52.9 %all-to-all-start = ((bf16[4,128,2048]{2,1,0:T(8,128)(2,1)}), bf16[4,128,2048]{2,1,0:T(8,128)(2,1)}, u32[]{:S(2)}, u32[]{:S(2)}) async-start(bf16[4,128,2048]{2,1,0:T(8,128)(2,1)} %broadcast_in_dim.195), calls=%async_computation | async-start | bytes 4194304 | tf_op jit(solution)/shard_map/all_to_all | solution.py:46
  20.8 11.8 %collective-permute-start.10 = (bf16[2,2,4,11,64]{4,2,1,0,3:T(4,128)(2,1)S(1)}, bf16[2,2,4,11,64]{4,2,1,0,3:T(4,128)(2,1)S(1)}, u32[]{:S(2)}, u32[]{:S(2)}) collective-permute-start(bf16[2,2,4,11,64]{4,2,1,0,3:T(4,128)(2,1)S(1)} %broadcast_select_fusion.13), channel_id=1, source_target_pairs={{0,16},{8,24},{16,0},{24,8},{1,17},{9,25},{17,1},{25,9},{2,18},{10... | collective-permute-start | bytes 67592 | tf_op jit(solution)/shard_map/ppermute | solution.py:29
  22.3 24.5 %collective-permute-start.1 = (bf16[2,256,1024]{2,1,0:T(8,128)(2,1)S(1)}, bf16[2,256,1024]{2,1,0:T(8,128)(2,1)S(1)}, u32[]{:S(2)}, u32[]{:S(2)}) collective-permute-start(bf16[2,256,1024]{2,1,0:T(8,128)(2,1)S(1)} %pad_maximum_fusion.13.refs_2_.refs_4_.refs_1_.refs_3_), channel_id=1, source_target_pairs={{0,4},{4,0},{1,5},{5,1},{2,6},{6,2},{3,7},{7,3},{8,12},{12,8},{9,1... | collective-permute-start | bytes 3145736 | tf_op jit(solution)/shard_map/ppermute | solution.py:34
  23.5 24.3 %collective-permute-start.2 = (bf16[2,256,1024]{2,1,0:T(8,128)(2,1)S(1)}, bf16[2,256,1024]{2,1,0:T(8,128)(2,1)S(1)}, u32[]{:S(2)}, u32[]{:S(2)}) collective-permute-start(bf16[2,256,1024]{2,1,0:T(8,128)(2,1)S(1)} %pad_maximum_fusion.13.refs_2_.refs_4_.refs_1_.refs_3_), channel_id=1, source_target_pairs={{0,16},{8,24},{16,0},{24,8},{1,17},{9,25},{17,1},{25,9},{2,18},{10... | collective-permute-start | bytes 3145736 | tf_op jit(solution)/shard_map/ppermute | solution.py:29
  31.6 22.3 %collective-permute-start.5 = (bf16[256,2176]{1,0:T(8,128)(2,1)}, bf16[256,2176]{1,0:T(8,128)(2,1)}, u32[]{:S(2)}, u32[]{:S(2)}) collective-permute-start(bf16[256,2176]{1,0:T(8,128)(2,1)} %concatenate.142), channel_id=1, source_target_pairs={{0,8},{8,0},{16,24},{24,16},{1,9},{9,1},{17,25},{25,17},{2,10},{10... | collective-permute-start | bytes 3342344 | tf_op jit(solution)/shard_map/ppermute | solution.py:24
  32.9 17.1 %collective-permute-start.11 = (bf16[2,2,2,4,11,64]{5,3,0,2,1,4:T(4,128)(2,1)S(1)}, bf16[2,2,2,4,11,64]{5,3,0,2,1,4:T(4,128)(2,1)S(1)}, u32[]{:S(2)}, u32[]{:S(2)}) collective-permute-start(bf16[2,2,2,4,11,64]{5,3,0,2,1,4:T(4,128)(2,1)S(1)} %broadcast_select_fusion.12), channel_id=1, source_target_pairs={{0,4},{4,0},{1,5},{5,1},{2,6},{6,2},{3,7},{7,3},{8,12},{12,8},{9,1... | collective-permute-start | bytes 135176 | tf_op jit(solution)/shard_map/ppermute | solution.py:34
  47.7 11.7 %collective-permute-start.3 = (bf16[256,1024]{1,0:T(8,128)(2,1)}, bf16[256,1024]{1,0:T(8,128)(2,1)}, u32[]{:S(2)}, u32[]{:S(2)}) collective-permute-start(bf16[256,1024]{1,0:T(8,128)(2,1)} %slice_bitcast_fusion.33), channel_id=1, source_target_pairs={{0,16},{8,24},{16,0},{24,8},{1,17},{9,25},{17,1},{25,9},{2,18},{10... | collective-permute-start | bytes 1572872 | tf_op jit(solution)/shard_map/ppermute | solution.py:29
  48.8 11.4 %collective-permute-start.4 = (bf16[256,1024]{1,0:T(8,128)(2,1)}, bf16[256,1024]{1,0:T(8,128)(2,1)}, u32[]{:S(2)}, u32[]{:S(2)}) collective-permute-start(bf16[256,1024]{1,0:T(8,128)(2,1)} %slice_bitcast_fusion.32), channel_id=1, source_target_pairs={{0,4},{4,0},{1,5},{5,1},{2,6},{6,2},{3,7},{7,3},{8,12},{12,8},{9,1... | collective-permute-start | bytes 1572872 | tf_op jit(solution)/shard_map/ppermute | solution.py:34
  66.3 7.9 collective-permute-start.12
  70.3 50.2 %collective-permute-start.14 = (bf16[2,256,2176]{2,1,0:T(8,128)(2,1)S(1)}, bf16[2,256,2176]{2,1,0:T(8,128)(2,1)}, u32[]{:S(2)}, u32[]{:S(2)}) collective-permute-start(bf16[2,256,2176]{2,1,0:T(8,128)(2,1)S(1)} %pad_maximum_fusion.5.refs_2_.refs_4_), channel_id=1, source_target_pairs={{0,4},{4,0},{1,5},{5,1},{2,6},{6,2},{3,7},{7,3},{8,12},{12,8},{9,1... | collective-permute-start | bytes 6684680 | tf_op jit(solution)/shard_map/ppermute | solution.py:34
  71.5 49.9 %collective-permute-start.15 = (bf16[2,256,2176]{2,1,0:T(8,128)(2,1)S(1)}, bf16[2,256,2176]{2,1,0:T(8,128)(2,1)}, u32[]{:S(2)}, u32[]{:S(2)}) collective-permute-start(bf16[2,256,2176]{2,1,0:T(8,128)(2,1)S(1)} %pad_maximum_fusion.5.refs_2_.refs_4_), channel_id=1, source_target_pairs={{0,16},{8,24},{16,0},{24,8},{1,17},{9,25},{17,1},{25,9},{2,18},{10... | collective-permute-start | bytes 6684680 | tf_op jit(solution)/shard_map/ppermute | solution.py:29
  95.7 6.7 collective-permute-start.16
  96.0 45.8 %collective-permute-start.13 = (bf16[1024,512]{1,0:T(8,128)(2,1)S(1)}, bf16[1024,512]{1,0:T(8,128)(2,1)}, u32[]{:S(2)}, u32[]{:S(2)}) collective-permute-start(bf16[1024,512]{1,0:T(8,128)(2,1)S(1)} %copy-done.23), channel_id=1, source_target_pairs={{0,4},{1,5},{2,6},{3,7},{8,12},{9,13},{10,14},{11,15},{16,20},{17,... | collective-permute-start | bytes 3145736 | tf_op jit(solution)/shard_map/ppermute | solution.py:937
  144.1 25.5 %collective-permute-start.17 = (bf16[256,2176]{1,0:T(8,128)(2,1)}, bf16[256,2176]{1,0:T(8,128)(2,1)S(1)}, u32[]{:S(2)}, u32[]{:S(2)}) collective-permute-start(bf16[256,2176]{1,0:T(8,128)(2,1)} %slice_bitcast_fusion.13), channel_id=1, source_target_pairs={{0,16},{8,24},{16,0},{24,8},{1,17},{9,25},{17,1},{25,9},{2,18},{10... | collective-permute-start | bytes 3342344 | tf_op jit(solution)/shard_map/ppermute | solution.py:29
  147.7 26.4 %collective-permute-start.18 = (bf16[256,2176]{1,0:T(8,128)(2,1)}, bf16[256,2176]{1,0:T(8,128)(2,1)S(1)}, u32[]{:S(2)}, u32[]{:S(2)}) collective-permute-start(bf16[256,2176]{1,0:T(8,128)(2,1)} %slice_bitcast_fusion.12), channel_id=1, source_target_pairs={{0,4},{4,0},{1,5},{5,1},{2,6},{6,2},{3,7},{7,3},{8,12},{12,8},{9,1... | collective-permute-start | bytes 3342344 | tf_op jit(solution)/shard_map/ppermute | solution.py:34
  174.1 5.7 collective-permute-start.19
  183.4 52.8 %all-to-all-start.1 = ((bf16[4,128,2048]{2,1,0:T(8,128)(2,1)}), bf16[4,128,2048]{2,1,0:T(8,128)(2,1)}, u32[]{:S(2)}, u32[]{:S(2)}) async-start(bf16[4,128,2048]{2,1,0:T(8,128)(2,1)} %bitcast.46), calls=%async_computation.1 | async-start | bytes 4194304 | tf_op jit(solution)/shard_map/all_to_all | solution.py:46
  188.3 50.0 %collective-permute-start.20 = (bf16[2,256,2176]{2,1,0:T(8,128)(2,1)}, bf16[2,256,2176]{2,1,0:T(8,128)(2,1)}, u32[]{:S(2)}, u32[]{:S(2)}) collective-permute-start(bf16[2,256,2176]{2,1,0:T(8,128)(2,1)} %pad_maximum_fusion.6.refs_10_.refs_12_), channel_id=1, source_target_pairs={{0,4},{4,0},{1,5},{5,1},{2,6},{6,2},{3,7},{7,3},{8,12},{12,8},{9,1... | collective-permute-start | bytes 6684680 | tf_op jit(solution)/shard_map/ppermute | solution.py:34
  189.8 49.6 %collective-permute-start.21 = (bf16[2,256,2176]{2,1,0:T(8,128)(2,1)}, bf16[2,256,2176]{2,1,0:T(8,128)(2,1)}, u32[]{:S(2)}, u32[]{:S(2)}) collective-permute-start(bf16[2,256,2176]{2,1,0:T(8,128)(2,1)} %pad_maximum_fusion.6.refs_10_.refs_12_), channel_id=1, source_target_pairs={{0,16},{8,24},{16,0},{24,8},{1,17},{9,25},{17,1},{25,9},{2,18},{10... | collective-permute-start | bytes 6684680 | tf_op jit(solution)/shard_map/ppermute | solution.py:29
  243.6 79.7 %all-to-all-start.2 = ((bf16[4,128,2048]{2,1,0:T(8,128)(2,1)}), bf16[4,128,2048]{2,1,0:T(8,128)(2,1)}, u32[]{:S(2)}, u32[]{:S(2)}) async-start(bf16[4,128,2048]{2,1,0:T(8,128)(2,1)} %broadcast_in_dim.216), calls=%async_computation.2 | async-start | bytes 4194304 | tf_op jit(solution)/shard_map/all_to_all | solution.py:46
  248.1 72.4 %collective-permute-start.25 = (bf16[2,256,2176]{2,1,0:T(8,128)(2,1)S(1)}, bf16[2,256,2176]{2,1,0:T(8,128)(2,1)S(1)}, u32[]{:S(2)}, u32[]{:S(2)}) collective-permute-start(bf16[2,256,2176]{2,1,0:T(8,128)(2,1)S(1)} %pad_maximum_fusion.7.refs_1_.refs_3_.refs_2_.refs_4_), channel_id=1, source_target_pairs={{0,4},{4,0},{1,5},{5,1},{2,6},{6,2},{3,7},{7,3},{8,12},{12,8},{9,1... | collective-permute-start | bytes 6684680 | tf_op jit(solution)/shard_map/ppermute | solution.py:34
  248.5 74.8 %collective-permute-start.26 = (bf16[2,256,2176]{2,1,0:T(8,128)(2,1)S(1)}, bf16[2,256,2176]{2,1,0:T(8,128)(2,1)}, u32[]{:S(2)}, u32[]{:S(2)}) collective-permute-start(bf16[2,256,2176]{2,1,0:T(8,128)(2,1)S(1)} %pad_maximum_fusion.7.refs_1_.refs_3_.refs_2_.refs_4_), channel_id=1, source_target_pairs={{0,16},{8,24},{16,0},{24,8},{1,17},{9,25},{17,1},{25,9},{2,18},{10... | collective-permute-start | bytes 6684680 | tf_op jit(solution)/shard_map/ppermute | solution.py:29
  250.0 70.4 %collective-permute-start.23 = (bf16[256,2176]{1,0:T(8,128)(2,1)S(1)}, bf16[256,2176]{1,0:T(8,128)(2,1)S(1)}, u32[]{:S(2)}, u32[]{:S(2)}) collective-permute-start(bf16[256,2176]{1,0:T(8,128)(2,1)S(1)} %slice_bitcast_fusion.11), channel_id=1, source_target_pairs={{0,16},{8,24},{16,0},{24,8},{1,17},{9,25},{17,1},{25,9},{2,18},{10... | collective-permute-start | bytes 3342344 | tf_op jit(solution)/shard_map/ppermute | solution.py:29
  252.6 67.8 %collective-permute-start.24 = (bf16[256,2176]{1,0:T(8,128)(2,1)S(1)}, bf16[256,2176]{1,0:T(8,128)(2,1)S(1)}, u32[]{:S(2)}, u32[]{:S(2)}) collective-permute-start(bf16[256,2176]{1,0:T(8,128)(2,1)S(1)} %slice_bitcast_fusion.10), channel_id=1, source_target_pairs={{0,4},{4,0},{1,5},{5,1},{2,6},{6,2},{3,7},{7,3},{8,12},{12,8},{9,1... | collective-permute-start | bytes 3342344 | tf_op jit(solution)/shard_map/ppermute | solution.py:34
  323.3 12.1 %collective-permute-start.27 = (bf16[512,2048]{1,0:T(8,128)(2,1)}, bf16[512,2048]{1,0:T(8,128)(2,1)S(1)}, u32[]{:S(2)}, u32[]{:S(2)}) collective-permute-start(bf16[512,2048]{1,0:T(8,128)(2,1)} %bitcast.56.refs_0_.refs_2_), channel_id=1, source_target_pairs={{0,8},{8,0},{16,24},{24,16},{1,9},{9,1},{17,25},{25,17},{2,10},{10... | collective-permute-start | bytes 6291464 | tf_op jit(solution)/shard_map/ppermute | solution.py:24
  328.4 39.5 %collective-permute-start.28 = (bf16[256,2176]{1,0:T(8,128)(2,1)}, bf16[256,2176]{1,0:T(8,128)(2,1)}, u32[]{:S(2)}, u32[]{:S(2)}) collective-permute-start(bf16[256,2176]{1,0:T(8,128)(2,1)} %slice_bitcast_fusion.9), channel_id=1, source_target_pairs={{0,16},{8,24},{16,0},{24,8},{1,17},{9,25},{17,1},{25,9},{2,18},{10... | collective-permute-start | bytes 3342344 | tf_op jit(solution)/shard_map/ppermute | solution.py:29
  331.0 37.0 %collective-permute-start.29 = (bf16[256,2176]{1,0:T(8,128)(2,1)}, bf16[256,2176]{1,0:T(8,128)(2,1)}, u32[]{:S(2)}, u32[]{:S(2)}) collective-permute-start(bf16[256,2176]{1,0:T(8,128)(2,1)} %slice_bitcast_fusion.8), channel_id=1, source_target_pairs={{0,4},{4,0},{1,5},{5,1},{2,6},{6,2},{3,7},{7,3},{8,12},{12,8},{9,1... | collective-permute-start | bytes 3342344 | tf_op jit(solution)/shard_map/ppermute | solution.py:34
  385.5 5.1 collective-permute-start.30
  394.3 52.2 %all-to-all-start.3 = ((bf16[4,128,2048]{2,1,0:T(8,128)(2,1)}), bf16[4,128,2048]{2,1,0:T(8,128)(2,1)S(1)}, u32[]{:S(2)}, u32[]{:S(2)}) async-start(bf16[4,128,2048]{2,1,0:T(8,128)(2,1)} %bitcast.283), calls=%async_computation.3 | async-start | bytes 4194304 | tf_op jit(solution)/shard_map/all_to_all | solution.py:46
  499.6 5.8 collective-permute-start.31
  523.6 58.4 %collective-permute-start.33 = (bf16[2,256,2176]{2,1,0:T(8,128)(2,1)}, bf16[2,256,2176]{2,1,0:T(8,128)(2,1)}, u32[]{:S(2)}, u32[]{:S(2)}) collective-permute-start(bf16[2,256,2176]{2,1,0:T(8,128)(2,1)} %get-tuple-element.170), channel_id=1, source_target_pairs={{0,16},{8,24},{16,0},{24,8},{1,17},{9,25},{17,1},{25,9},{2,18},{10... | collective-permute-start | bytes 6684680 | tf_op jit(solution)/shard_map/ppermute | solution.py:29
  524.4 57.5 %collective-permute-start.34 = (bf16[2,256,2176]{2,1,0:T(8,128)(2,1)}, bf16[2,256,2176]{2,1,0:T(8,128)(2,1)}, u32[]{:S(2)}, u32[]{:S(2)}) collective-permute-start(bf16[2,256,2176]{2,1,0:T(8,128)(2,1)} %get-tuple-element.172), channel_id=1, source_target_pairs={{0,4},{4,0},{1,5},{5,1},{2,6},{6,2},{3,7},{7,3},{8,12},{12,8},{9,1... | collective-permute-start | bytes 6684680 | tf_op jit(solution)/shard_map/ppermute | solution.py:34
  576.4 5.5 collective-permute-start.32
  578.7 13.8 %collective-permute-start.35 = (f32[9,4,128]{2,0,1:T(8,128)S(1)}, f32[9,4,128]{2,0,1:T(8,128)S(1)}, u32[]{:S(2)}, u32[]{:S(2)}) collective-permute-start(f32[9,4,128]{2,0,1:T(8,128)S(1)} %fusion.29), channel_id=1, source_target_pairs={{0,8},{8,0},{16,24},{24,16},{1,9},{9,1},{17,25},{25,17},{2,10},{10... | collective-permute-start | bytes 55304 | tf_op jit(solution)/shard_map/ppermute | solution.py:24
  586.4 55.3 %all-to-all-start.5 = ((bf16[4,128,2048]{2,1,0:T(8,128)(2,1)}), bf16[4,128,2048]{2,1,0:T(8,128)(2,1)S(1)}, u32[]{:S(2)}, u32[]{:S(2)}) async-start(bf16[4,128,2048]{2,1,0:T(8,128)(2,1)} %bitcast.73), calls=%async_computation.5 | async-start | bytes 4194304 | tf_op jit(solution)/shard_map/all_to_all | solution.py:46
  595.2 46.8 %collective-permute-start.40 = (bf16[256,2176]{1,0:T(8,128)(2,1)}, bf16[256,2176]{1,0:T(8,128)(2,1)}, u32[]{:S(2)}, u32[]{:S(2)}) collective-permute-start(bf16[256,2176]{1,0:T(8,128)(2,1)} %fusion.8), channel_id=1, source_target_pairs={{0,16},{8,24},{16,0},{24,8},{1,17},{9,25},{17,1},{25,9},{2,18},{10... | collective-permute-start | bytes 3342344 | tf_op jit(solution)/shard_map/ppermute | solution.py:29
  597.8 44.3 %collective-permute-start.39 = (bf16[256,2176]{1,0:T(8,128)(2,1)}, bf16[256,2176]{1,0:T(8,128)(2,1)}, u32[]{:S(2)}, u32[]{:S(2)}) collective-permute-start(bf16[256,2176]{1,0:T(8,128)(2,1)} %fusion.7), channel_id=1, source_target_pairs={{0,4},{4,0},{1,5},{5,1},{2,6},{6,2},{3,7},{7,3},{8,12},{12,8},{9,1... | collective-permute-start | bytes 3342344 | tf_op jit(solution)/shard_map/ppermute | solution.py:34
  632.9 7.2 collective-permute-start.36
  634.4 6.6 collective-permute-start.37
  636.5 5.3 collective-permute-start.38
  640.1 95.9 %collective-permute-start.44 = (bf16[2,256,4352]{2,1,0:T(8,128)(2,1)}, bf16[2,256,4352]{2,1,0:T(8,128)(2,1)}, u32[]{:S(2)}, u32[]{:S(2)}) collective-permute-start(bf16[2,256,4352]{2,1,0:T(8,128)(2,1)} %get-tuple-element.188), channel_id=1, source_target_pairs={{0,16},{8,24},{16,0},{24,8},{1,17},{9,25},{17,1},{25,9},{2,18},{10... | collective-permute-start | bytes 13369352 | tf_op jit(solution)/shard_map/ppermute | solution.py:29
  640.9 95.7 %collective-permute-start.45 = (bf16[2,256,4352]{2,1,0:T(8,128)(2,1)}, bf16[2,256,4352]{2,1,0:T(8,128)(2,1)}, u32[]{:S(2)}, u32[]{:S(2)}) collective-permute-start(bf16[2,256,4352]{2,1,0:T(8,128)(2,1)} %get-tuple-element.190), channel_id=1, source_target_pairs={{0,4},{4,0},{1,5},{5,1},{2,6},{6,2},{3,7},{7,3},{8,12},{12,8},{9,1... | collective-permute-start | bytes 13369352 | tf_op jit(solution)/shard_map/ppermute | solution.py:34
  647.0 52.2 %all-to-all-start.6 = ((bf16[4,128,2048]{2,1,0:T(8,128)(2,1)}), bf16[4,128,2048]{2,1,0:T(8,128)(2,1)}, u32[]{:S(2)}, u32[]{:S(2)}) async-start(bf16[4,128,2048]{2,1,0:T(8,128)(2,1)} %broadcast_in_dim.223), calls=%async_computation.6 | async-start | bytes 4194304 | tf_op jit(solution)/shard_map/all_to_all | solution.py:46
  656.0 5.0 collective-permute-start.41
  699.2 5.6 collective-permute-start.42
  736.6 23.5 %collective-permute-start.43 = (bf16[1024,512]{1,0:T(8,128)(2,1)}, bf16[1024,512]{1,0:T(8,128)(2,1)S(1)}, u32[]{:S(2)}, u32[]{:S(2)}) collective-permute-start(bf16[1024,512]{1,0:T(8,128)(2,1)} %get-tuple-element.213), channel_id=1, source_target_pairs={{4,0},{5,1},{6,2},{7,3},{12,8},{13,9},{14,10},{15,11},{20,16},{21,... | collective-permute-start | bytes 3145736 | tf_op jit(solution)/shard_map/ppermute | solution.py:1020
  771.9 11.7 %collective-permute-start.46 = (bf16[512,2048]{1,0:T(8,128)(2,1)}, bf16[512,2048]{1,0:T(8,128)(2,1)}, u32[]{:S(2)}, u32[]{:S(2)}) collective-permute-start(bf16[512,2048]{1,0:T(8,128)(2,1)} %get-tuple-element.220), channel_id=1, source_target_pairs={{0,8},{8,0},{16,24},{24,16},{1,9},{9,1},{17,25},{25,17},{2,10},{10... | collective-permute-start | bytes 6291464 | tf_op jit(solution)/shard_map/ppermute | solution.py:24
  776.1 50.3 %collective-permute-start.59 = (bf16[256,4352]{1,0:T(8,128)(2,1)}, bf16[256,4352]{1,0:T(8,128)(2,1)}, u32[]{:S(2)}, u32[]{:S(2)}) collective-permute-start(bf16[256,4352]{1,0:T(8,128)(2,1)} %fusion.4), channel_id=1, source_target_pairs={{0,16},{8,24},{16,0},{24,8},{1,17},{9,25},{17,1},{25,9},{2,18},{10... | collective-permute-start | bytes 6684680 | tf_op jit(solution)/shard_map/ppermute | solution.py:29
  781.4 50.2 %collective-permute-start.58 = (bf16[256,4352]{1,0:T(8,128)(2,1)}, bf16[256,4352]{1,0:T(8,128)(2,1)}, u32[]{:S(2)}, u32[]{:S(2)}) collective-permute-start(bf16[256,4352]{1,0:T(8,128)(2,1)} %fusion.3), channel_id=1, source_target_pairs={{0,4},{4,0},{1,5},{5,1},{2,6},{6,2},{3,7},{7,3},{8,12},{12,8},{9,1... | collective-permute-start | bytes 6684680 | tf_op jit(solution)/shard_map/ppermute | solution.py:34
  802.6 57.1 %collective-permute-start.53 = (bf16[2,256,1024]{2,1,0:T(8,128)(2,1)}, bf16[2,256,1024]{2,1,0:T(8,128)(2,1)}, u32[]{:S(2)}, u32[]{:S(2)}) collective-permute-start(bf16[2,256,1024]{2,1,0:T(8,128)(2,1)} %get-tuple-element.225), channel_id=1, source_target_pairs={{0,16},{8,24},{16,0},{24,8},{1,17},{9,25},{17,1},{25,9},{2,18},{10... | collective-permute-start | bytes 3145736 | tf_op jit(solution)/shard_map/ppermute | solution.py:29
  803.5 52.3 %all-to-all-start.7 = ((bf16[4,128,2048]{2,1,0:T(8,128)(2,1)}), bf16[4,128,2048]{2,1,0:T(8,128)(2,1)}, u32[]{:S(2)}, u32[]{:S(2)}) async-start(bf16[4,128,2048]{2,1,0:T(8,128)(2,1)} %bitcast.282), calls=%async_computation.7 | async-start | bytes 4194304 | tf_op jit(solution)/shard_map/all_to_all | solution.py:46
  808.2 54.6 %collective-permute-start.55 = (bf16[2,256,1024]{2,1,0:T(8,128)(2,1)}, bf16[2,256,1024]{2,1,0:T(8,128)(2,1)}, u32[]{:S(2)}, u32[]{:S(2)}) collective-permute-start(bf16[2,256,1024]{2,1,0:T(8,128)(2,1)} %get-tuple-element.227), channel_id=1, source_target_pairs={{0,4},{4,0},{1,5},{5,1},{2,6},{6,2},{3,7},{7,3},{8,12},{12,8},{9,1... | collective-permute-start | bytes 3145736 | tf_op jit(solution)/shard_map/ppermute | solution.py:34
  830.2 12.2 %collective-permute-start.60 = (bf16[256,4352]{1,0:T(8,128)(2,1)S(1)}, bf16[256,4352]{1,0:T(8,128)(2,1)S(1)}, u32[]{:S(2)}, u32[]{:S(2)}) collective-permute-start(bf16[256,4352]{1,0:T(8,128)(2,1)S(1)} %fusion), channel_id=1, source_target_pairs={{0,8},{8,0},{16,24},{24,16},{1,9},{9,1},{17,25},{25,17},{2,10},{10... | collective-permute-start | bytes 6684680 | tf_op jit(solution)/shard_map/ppermute | solution.py:24
  858.4 3.7 collective-permute-start.47
  861.2 20.4 %collective-permute-start.54 = (bf16[256,1024]{1,0:T(8,128)(2,1)S(1)}, bf16[256,1024]{1,0:T(8,128)(2,1)S(1)}, u32[]{:S(2)}, u32[]{:S(2)}) collective-permute-start(bf16[256,1024]{1,0:T(8,128)(2,1)S(1)} %fusion.19), channel_id=1, source_target_pairs={{0,4},{4,0},{1,5},{5,1},{2,6},{6,2},{3,7},{7,3},{8,12},{12,8},{9,1... | collective-permute-start | bytes 1572872 | tf_op jit(solution)/shard_map/ppermute | solution.py:34
  864.0 12.9 %collective-permute-start.56 = (bf16[256,1024]{1,0:T(8,128)(2,1)S(1)}, bf16[256,1024]{1,0:T(8,128)(2,1)S(1)}, u32[]{:S(2)}, u32[]{:S(2)}) collective-permute-start(bf16[256,1024]{1,0:T(8,128)(2,1)S(1)} %fusion.20), channel_id=1, source_target_pairs={{0,16},{8,24},{16,0},{24,8},{1,17},{9,25},{17,1},{25,9},{2,18},{10... | collective-permute-start | bytes 1572872 | tf_op jit(solution)/shard_map/ppermute | solution.py:29
  865.3 6.2 collective-permute-start.49
  871.5 4.9 collective-permute-start.50
  872.4 3.9 collective-permute-start.51
  878.3 4.7 collective-permute-start.57
  (56 other events, 541.6 us)

commit v5 on v4

--- a/solution.py
+++ b/solution.py
@@ -102,6 +102,16 @@
             for s in range(size)
         ]
     )
+
+
+def own_by_halves(v, axis):
+    index, count = lax.axis_index(axis), lax.axis_size(axis)
+    while v.shape[0] > 1:
+        half = v.shape[0] // 2
+        low = lax.rem(index // half, 2) == 0
+        kept, sent = jnp.where(low, v[:half], v[half:]), jnp.where(low, v[half:], v[:half])
+        v = kept + lax.ppermute(sent, axis, [(i, i ^ half) for i in range(count)])
+    return v[0]
 
 
 def scatter_everywhere(v):
@@ -986,8 +996,7 @@
     grad_gate_pre, grad_up_pre = after((grad_gate_pre, grad_up_pre), [both])
     wide_groups = weight_grad(order, [(ffn_shards, grad_gate_pre), (ffn_shards, grad_up_pre)])
     wide_moves = grad_first(wide_groups)
-    (scalar_both,) = after((jnp.swapaxes(scalar_both, 0, 1),), [wide_groups])
-    scalar_own = own_of(scalar_both, "exp", nz, z)
+    scalar_own = own_by_halves(jnp.swapaxes(scalar_both, 0, 1), "exp")
     down_kept, down_moves = grad_second(down_groups, *down_moves)
     parts, scalar_own, wide_groups, down_moves = meet(parts, scalar_own, wide_groups, down_moves)
     grad_normed = total(parts)

time: 898 us -> 916 us (1.020)
  waiting for transfers between devices: 318 us -> 343 us
    ppermute x0 -> x2, waiting for transfers between devices: none -> 24.1 us  [own_by_halves(): v = kept + lax.ppermute(sent, axis, [(i, i ^ half) for i in range(count)])]
    ppermute x25 -> x22, starting transfers between devices: 30.2 us -> 29.5 us  [shift(): return lax.ppermute(v, axis, [(i, (i + s) % n) for i in range(n)])]
    ppermute x25 -> x22, waiting for transfers between devices: 35.3 us -> 35.5 us  [shift(): return lax.ppermute(v, axis, [(i, (i + s) % n) for i in range(n)])]
  transfers between devices with their start and end apart: 68 -> 67, of which waited for: 32 -> 33; matrix products, arithmetic and copies ran while one was open for 17% -> 16% of each run, Pallas kernels for 20% -> 20%
where the time goes in v5:
time: 916 us; the launch traced here: 905 us
  waiting for transfers between devices  343 us (37%)
  Pallas kernels  227 us (25%)
  starting transfers between devices  104 us (11%)
  other arithmetic  89.3 us (10%)
  local copies, waits for them, and re-layouts  86.1 us (9%)
  blocking collectives  50.1 us (5%)
    all_to_all x7, waiting for transfers between devices, exchange(): return lax.all_to_all(v, 'exp', split_axis=0, concat_axis=0, tiled=True)  129 us
    ppermute x16, waiting for transfers between devices, y_swap(): return lax.ppermute(v, 'dp', [(i, i ^ 2) for i in range(n)])  101 us
    pallas_call x3, Pallas kernels, weight_grad(): pl.pallas_call(functools.partial(weight_grad_kernel, n, [len(rows) for ro...  66.4 us
    pallas_call x4, Pallas kernels, project_home(): pl.pallas_call(functools.partial(home_kernel, len(acts), [i for _, i in e...  64.2 us
    all_to_all x1, blocking collectives, exchange(): return lax.all_to_all(v, 'exp', split_axis=0, concat_axis=0, tiled=True)  50.1 us
    ppermute x22, waiting for transfers between devices, shift(): return lax.ppermute(v, axis, [(i, (i + s) % n) for i in range(n)])  35.5 us
    all_to_all x7, starting transfers between devices, exchange(): return lax.all_to_all(v, 'exp', split_axis=0, concat_axis=0, tiled=True)  32.3 us
    pallas_call x1, Pallas kernels, up_call(): pl.pallas_call(functools.partial(up_kernel, len(shards), len(gates), expe...  31.2 us
  transfers between devices with their start and end apart: 67, of which 33 were waited for; matrix products, arithmetic and copies ran while one was open for 16% of the time, Pallas kernels for 20%

profile of v5, /device:TPU:1, one launch (start us, length us, event | category | flops | bytes accessed | tf_op | source)
XLA Modules:
  0.0 905.2 jit_solution(12915487192251835451)
XLA Ops:
  13.4 4.4 all-to-all-start
  28.4 3.3 concatenate.142
  33.2 13.6 %collective-permute-done.1.refs_3_.refs_5_.refs_2_.refs_4_ = bf16[2,256,1024]{2,1,0:T(8,128)(2,1)S(1)} collective-permute-done((bf16[2,256,1024]{2,1,0:T(8,128)(2,1)S(1)}, bf16[2,256,1024]{2,1,0:T(8,128)(2,1)S(1)}, u32[]{:S(2)}, u32[]{:S(2)}) %collective-permute-start.1) | collective-permute-done | bytes 1048608 | tf_op jit(solution)/shard_map/ppermute | solution.py:34
  50.7 3.2 concatenate.141
  55.8 3.5 collective-permute-done.3
  60.2 6.1 all-to-all-done
  74.2 13.5 %qkv_rope.1 = (bf16[1024,2048]{1,0:T(8,128)(2,1)}, bf16[1024,256]{1,0:T(8,128)(2,1)}, bf16[1024,512]{1,0:T(8,128)(2,1)}) custom-call(s32[8]{0:T(128)} %stack.97.places_ref, bf16[512,2048]{1,0:T(8,128)(2,1)} %bitcast.13.refs_0_, bf16[512,2048]{1,0:T(8,128)(2,1)} %collective-permute-done.12.refs_1_, bf16[2,256,1024]{2,1,0:T(8,128)(2,1)} %copy-done.1, ...), custom_call_target="tpu_custom_call" | custom-call | flops 402653184 | bytes 1441792 | tf_op jit(solution)/shard_map/qkv_rope/pallas_call | solution.py:288
  92.4 3.2 concatenate.149
  96.0 3.2 collective-permute-start.13
  99.2 3.2 concatenate.148
  102.4 3.2 pad_maximum_fusion.6.refs_10_.refs_12_
  105.6 14.9 %collective-permute-done.14.refs_3_.refs_5_ = bf16[2,256,2176]{2,1,0:T(8,128)(2,1)} collective-permute-done((bf16[2,256,2176]{2,1,0:T(8,128)(2,1)S(1)}, bf16[2,256,2176]{2,1,0:T(8,128)(2,1)}, u32[]{:S(2)}, u32[]{:S(2)}) %collective-permute-start.14) | collective-permute-done | bytes 2228256 | tf_op jit(solution)/shard_map/ppermute | solution.py:34
  121.4 20.5 %collective-permute-done.13.refs_1_ = bf16[1024,512]{1,0:T(8,128)(2,1)} collective-permute-done((bf16[1024,512]{1,0:T(8,128)(2,1)S(1)}, bf16[1024,512]{1,0:T(8,128)(2,1)}, u32[]{:S(2)}, u32[]{:S(2)}) %collective-permute-start.13) | collective-permute-done | bytes 1048608 | tf_op jit(solution)/shard_map/ppermute | solution.py:947
  141.8 2.3 slice_bitcast_fusion.13
  151.5 9.5 %attend.1.refs_0_.refs_3_ = bf16[1024,256]{1,0:T(8,128)(2,1)} custom-call(s32[9]{0:T(128)} %pad_add_fusion.info_ref, bf16[1024,256]{1,0:T(8,128)(2,1)} %get-tuple-element.134.q_ref, bf16[1024,512]{1,0:T(8,128)(2,1)} %get-tuple-element.139.refs_0_, bf16[1024,512]{1,0:T(8,128)(2,1)} %collective-permute-done.13.refs_1_), custom_call_target="tpu_custom_call" | custom-call | flops 33554432 | bytes 393216 | tf_op jit(solution)/shard_map/attend/pallas_call | solution.py:703
  161.0 7.4 project_home.4
  169.7 4.4 collective-permute-done.18
  175.8 4.0 collective-permute-done.19
  179.8 3.7 add_convert_fusion.5
  183.4 4.8 all-to-all-start.1
  198.8 37.5 %all-to-all-done.1 = bf16[4,128,2048]{2,1,0:T(8,128)(2,1)} async-done(((bf16[4,128,2048]{2,1,0:T(8,128)(2,1)}), bf16[4,128,2048]{2,1,0:T(8,128)(2,1)}, u32[]{:S(2)}, u32[]{:S(2)}) %all-to-all-start.1) | async-done | bytes 2097184 | tf_op jit(solution)/shard_map/all_to_all | solution.py:46
  243.6 4.4 all-to-all-start.2
  253.8 66.6 %collective-permute-done.23 = bf16[256,2176]{1,0:T(8,128)(2,1)S(1)} collective-permute-done((bf16[256,2176]{1,0:T(8,128)(2,1)S(1)}, bf16[256,2176]{1,0:T(8,128)(2,1)S(1)}, u32[]{:S(2)}, u32[]{:S(2)}) %collective-permute-start.23) | collective-permute-done | bytes 1114144 | tf_op jit(solution)/shard_map/ppermute | solution.py:29
  323.2 2.8 collective-permute-start.27
  336.5 31.2 %expert_up.1 = (bf16[1024,2176]{1,0:T(8,128)(2,1)}, bf16[1024,2176]{1,0:T(8,128)(2,1)}, bf16[1024,2176]{1,0:T(8,128)(2,1)}, bf16[1024,2176]{1,0:T(8,128)(2,1)}, f32[1024,128]{1,0:T(8,128)}) custom-call(s32[10]{0:T(128)} %concatenate.152.info_ref, bf16[512,2048]{1,0:T(8,128)(2,1)} %bitcast.56.refs_0_.refs_2_, bf16[512,2048]{1,0:T(8,128)(2,1)} %copy-done.7, ...), custom_call_target="tpu_custom_call" | custom-call | flops 2281701376 | bytes 4980736 | tf_op jit(solution)/shard_map/expert_up/pallas_call | solution.py:375
  367.8 17.5 %project_home.5 = (bf16[512,2048]{1,0:T(8,128)(2,1)}, bf16[512,2048]{1,0:T(8,128)(2,1)}) custom-call(s32[8]{0:T(128)} %stack.97.places_ref, bf16[1024,2176]{1,0:T(8,128)(2,1)} %get-tuple-element.163.refs_0_.refs_2_, bf16[2,256,2176]{2,1,0:T(8,128)(2,1)} %copy-done.4, bf16[2,256,2176]{2,1,0:T(8,128)(2,1)} %copy-done.6, bf16[2,256,2176]{2,1,0:T(8,128)(2,1)} %copy-done.4, ...), custom_call_target="tpu_custom_call" | custom-call | flops 1140850688 | bytes 2195456 | tf_op jit(solution)/shard_map/project_home/pallas_call | solution.py:571
  386.4 4.0 collective-permute-done.30
  390.4 3.7 add_convert_fusion.4
  394.1 4.4 all-to-all-start.3
  401.1 45.1 %all-to-all-done.3 = bf16[4,128,2048]{2,1,0:T(8,128)(2,1)S(1)} async-done(((bf16[4,128,2048]{2,1,0:T(8,128)(2,1)}), bf16[4,128,2048]{2,1,0:T(8,128)(2,1)S(1)}, u32[]{:S(2)}, u32[]{:S(2)}) %all-to-all-start.3) | async-done | bytes 2097184 | tf_op jit(solution)/shard_map/all_to_all | solution.py:46
  446.2 2.7 fusion.21
  449.2 50.1 %all_to_all.71 = bf16[4,128,2048]{2,1,0:T(8,128)(2,1)S(1)} all-to-all(bf16[4,128,2048]{2,1,0:T(8,128)(2,1)S(1)} %broadcast_in_dim.222), channel_id=1, replica_groups=mesh['dp'=4,'ctx'=2,'exp'=4] {'exp'}, dimensions={0} | all-to-all | bytes 4194304 | tf_op jit(solution)/shard_map/all_to_all | solution.py:46
  501.9 3.2 collective-permute-done.31.refs_1_
  505.1 18.2 %weight_grad.3 = (bf16[2,256,2176]{2,1,0:T(8,128)(2,1)}, bf16[2,256,2176]{2,1,0:T(8,128)(2,1)}, bf16[2,256,2176]{2,1,0:T(8,128)(2,1)}, bf16[2,256,2176]{2,1,0:T(8,128)(2,1)}) custom-call(s32[8]{0:T(128)} %stack.114.places_ref, bf16[512,2048]{1,0:T(8,128)(2,1)} %bitcast.270, bf16[512,2048]{1,0:T(8,128)(2,1)} %collective-permute-done.31.refs_1_, ...), custom_call_target="tpu_custom_call" | custom-call | flops 1140850688 | bytes 2195456 | tf_op jit(solution)/shard_map/weight_grad/pallas_call | solution.py:650
  524.5 22.5 %down_back.1 = (bf16[1024,2176]{1,0:T(8,128)(2,1)}, bf16[1024,2176]{1,0:T(8,128)(2,1)}, f32[1024,128]{1,0:T(8,128)}) custom-call(s32[10]{0:T(128)} %concatenate.152.info_ref, bf16[512,2048]{1,0:T(8,128)(2,1)} %bitcast.271, bf16[512,2048]{1,0:T(8,128)(2,1)} %collective-permute-done.31.refs_1_, bf16[2,256,2176]{2,1,0:T(8,128)(2,1)} %copy-done.4, ...), custom_call_target="tpu_custom_call" | custom-call | flops 1140850688 | bytes 4423680 | tf_op jit(solution)/shard_map/down_back/pallas_call | solution.py:445
  547.0 29.1 %project_home.6 = (bf16[512,2048]{1,0:T(8,128)(2,1)}, bf16[512,2048]{1,0:T(8,128)(2,1)}) custom-call(s32[8]{0:T(128)} %stack.97.places_ref, bf16[1024,2176]{1,0:T(8,128)(2,1)} %get-tuple-element.184.refs_0_.refs_4_, bf16[1024,2176]{1,0:T(8,128)(2,1)} %get-tuple-element.185.refs_1_.refs_5_, bf16[2,256,2176]{2,1,0:T(8,128)(2,1)} %copy-done.5, ...), custom_call_target="tpu_custom_call" | custom-call | flops 2281701376 | bytes 3866624 | tf_op jit(solution)/shard_map/project_home/pallas_call | solution.py:571
  583.7 3.8 all-to-all-start.5
  589.0 2.8 fusion.8
  591.9 2.5 fusion.7
  596.9 24.1 %collective-permute-done.37 = f32[1,9,128]{2,1,0:T(8,128)S(1)} collective-permute-done((f32[1,9,128]{2,1,0:T(8,128)S(1)}, f32[1,9,128]{2,1,0:T(8,128)S(1)}, u32[]{:S(2)}, u32[]{:S(2)}) %collective-permute-start.37) | collective-permute-done | bytes 4640 | tf_op jit(solution)/shard_map/ppermute | solution.py:113
  621.0 33.7 %weight_grad.4 = (bf16[2,256,4352]{2,1,0:T(8,128)(2,1)}, bf16[2,256,4352]{2,1,0:T(8,128)(2,1)}, bf16[2,256,4352]{2,1,0:T(8,128)(2,1)}, bf16[2,256,4352]{2,1,0:T(8,128)(2,1)}) custom-call(s32[8]{0:T(128)} %stack.114.places_ref, bf16[512,2048]{1,0:T(8,128)(2,1)} %bitcast.56.refs_0_.refs_2_, bf16[512,2048]{1,0:T(8,128)(2,1)} %copy-done.7, ...), custom_call_target="tpu_custom_call" | custom-call | flops 2281701376 | bytes 3866624 | tf_op jit(solution)/shard_map/weight_grad/pallas_call | solution.py:650
  661.5 5.3 all-to-all-start.6
  671.3 2.6 collective-permute-start.40
  677.8 38.5 %all-to-all-done.6 = bf16[4,128,2048]{2,1,0:T(8,128)(2,1)} async-done(((bf16[4,128,2048]{2,1,0:T(8,128)(2,1)}), bf16[4,128,2048]{2,1,0:T(8,128)(2,1)}, u32[]{:S(2)}, u32[]{:S(2)}) %all-to-all-start.6) | async-done | bytes 2097184 | tf_op jit(solution)/shard_map/all_to_all | solution.py:46
  718.4 2.6 collective-permute-done.41.refs_1_
  721.0 6.8 out_back.1
  727.8 12.4 %attend_back.1 = (bf16[1024,256]{1,0:T(8,128)(2,1)}, f32[1024,512]{1,0:T(8,128)}, bf16[1024,512]{1,0:T(8,128)(2,1)}) custom-call(s32[9]{0:T(128)} %pad_add_fusion.info_ref, bf16[1024,256]{1,0:T(8,128)(2,1)} %get-tuple-element.134.q_ref, bf16[1024,256]{1,0:T(8,128)(2,1)} %get-tuple-element.208.da_ref, bf16[1024,512]{1,0:T(8,128)(2,1)} %get-tuple-element.139.refs_0_, ...), custom_call_target="tpu_custom_call" | custom-call | flops 83886080 | bytes 851968 | tf_op jit(solution)/shard_map/attend_back/pallas_call | solution.py:768
  740.2 11.0 %collective-permute-done.43 = bf16[2,256,4352]{2,1,0:T(8,128)(2,1)} collective-permute-done((bf16[2,256,4352]{2,1,0:T(8,128)(2,1)}, bf16[2,256,4352]{2,1,0:T(8,128)(2,1)}, u32[]{:S(2)}, u32[]{:S(2)}) %collective-permute-start.43) | collective-permute-done | bytes 4456480 | tf_op jit(solution)/shard_map/ppermute | solution.py:29
  752.6 4.2 fusion.4
  756.8 4.3 fusion.3
  761.1 14.5 %collective-permute-done.42 = bf16[1024,512]{1,0:T(8,128)(2,1)S(1)} collective-permute-done((bf16[1024,512]{1,0:T(8,128)(2,1)}, bf16[1024,512]{1,0:T(8,128)(2,1)S(1)}, u32[]{:S(2)}, u32[]{:S(2)}) %collective-permute-start.42) | collective-permute-done | bytes 1048608 | tf_op jit(solution)/shard_map/ppermute | solution.py:1029
  777.2 10.1 %project_home.7 = (bf16[512,2048]{1,0:T(8,128)(2,1)}, bf16[512,2048]{1,0:T(8,128)(2,1)}) custom-call(s32[8]{0:T(128)} %stack.97.places_ref, bf16[1024,768]{1,0:T(8,128)(2,1)} %pad_maximum_fusion.8.refs_0_.refs_2_, bf16[2,256,1024]{2,1,0:T(8,128)(2,1)} %copy-done.1, bf16[2,256,1024]{2,1,0:T(8,128)(2,1)} %copy-done.2, bf16[2,256,1024]{2,1,0:T(8,128)(2,1)} %copy-done.1, ...), custom_call_target="tpu_custom_call" | custom-call | flops 402653184 | bytes 1114112 | tf_op jit(solution)/shard_map/project_home/pallas_call | solution.py:571
  787.3 3.5 collective-permute-start.45
  798.9 4.5 add_convert_fusion.2
  803.4 14.4 %weight_grad.5 = (bf16[2,256,1024]{2,1,0:T(8,128)(2,1)}, bf16[2,256,1024]{2,1,0:T(8,128)(2,1)}, bf16[2,256,1024]{2,1,0:T(8,128)(2,1)}, bf16[2,256,1024]{2,1,0:T(8,128)(2,1)}) custom-call(s32[8]{0:T(128)} %stack.114.places_ref, bf16[1024,2048]{1,0:T(8,128)(2,1)} %get-tuple-element.219.refs_0_, bf16[1024,2048]{1,0:T(8,128)(2,1)} %get-tuple-element.220.refs_1_, ...), custom_call_target="tpu_custom_call" | custom-call | flops 536870912 | bytes 1310720 | tf_op jit(solution)/shard_map/weight_grad/pallas_call | solution.py:650
  818.2 5.2 all-to-all-start.7
  824.9 16.2 %collective-permute-done.58 = bf16[256,4352]{1,0:T(8,128)(2,1)} collective-permute-done((bf16[256,4352]{1,0:T(8,128)(2,1)}, bf16[256,4352]{1,0:T(8,128)(2,1)}, u32[]{:S(2)}, u32[]{:S(2)}) %collective-permute-start.58) | collective-permute-done | bytes 2228256 | tf_op jit(solution)/shard_map/ppermute | solution.py:29
  841.1 3.8 fusion
  846.7 3.3 bitcast_add_fusion.1
  853.5 3.8 copy.89
  859.7 7.2 copy.88
  866.9 3.8 copy.87
  882.8 2.7 collective-permute-start.48
  886.4 3.1 collective-permute-start.49
  (379 shorter events, 176.1 us)
Async XLA Ops:
  2.3 15.6 %collective-permute-start.6 = (bf16[4,32,128]{1,2,0:T(8,128)(2,1)S(1)}, bf16[4,32,128]{1,2,0:T(8,128)(2,1)S(1)}, u32[]{:S(2)}, u32[]{:S(2)}) collective-permute-start(bf16[4,32,128]{1,2,0:T(8,128)(2,1)S(1)} %broadcast_select_fusion.9), channel_id=1, source_target_pairs={{0,1},{1,2},{2,3},{3,0},{4,5},{5,6},{6,7},{7,4},{8,9},{9,10},{10,1... | collective-permute-start | bytes 98312 | tf_op jit(solution)/shard_map/ppermute | solution.py:34
  4.5 13.5 %collective-permute-start.7 = (bf16[4,32,128]{1,2,0:T(8,128)(2,1)S(1)}, bf16[4,32,128]{1,2,0:T(8,128)(2,1)S(1)}, u32[]{:S(2)}, u32[]{:S(2)}) collective-permute-start(bf16[4,32,128]{1,2,0:T(8,128)(2,1)S(1)} %broadcast_select_fusion.9), channel_id=1, source_target_pairs={{0,2},{1,3},{2,0},{3,1},{4,6},{5,7},{6,4},{7,5},{8,10},{9,11},{10,... | collective-permute-start | bytes 98312 | tf_op jit(solution)/shard_map/ppermute | solution.py:34
  6.8 11.2 %collective-permute-start.8 = (bf16[4,32,128]{1,2,0:T(8,128)(2,1)S(1)}, bf16[4,32,128]{1,2,0:T(8,128)(2,1)S(1)}, u32[]{:S(2)}, u32[]{:S(2)}) collective-permute-start(bf16[4,32,128]{1,2,0:T(8,128)(2,1)S(1)} %broadcast_select_fusion.9), channel_id=1, source_target_pairs={{0,3},{1,0},{2,1},{3,2},{4,7},{5,4},{6,5},{7,6},{8,11},{9,8},{10,9... | collective-permute-start | bytes 98312 | tf_op jit(solution)/shard_map/ppermute | solution.py:34
  10.2 11.9 %collective-permute-start = (bf16[256,1024]{1,0:T(8,128)(2,1)S(1)}, bf16[256,1024]{1,0:T(8,128)(2,1)S(1)}, u32[]{:S(2)}, u32[]{:S(2)}) collective-permute-start(bf16[256,1024]{1,0:T(8,128)(2,1)S(1)} %pad_maximum_fusion.14), channel_id=1, source_target_pairs={{0,8},{8,0},{16,24},{24,16},{1,9},{9,1},{17,25},{25,17},{2,10},{10... | collective-permute-start | bytes 1572872 | tf_op jit(solution)/shard_map/ppermute | solution.py:24
  13.4 52.9 %all-to-all-start = ((bf16[4,128,2048]{2,1,0:T(8,128)(2,1)}), bf16[4,128,2048]{2,1,0:T(8,128)(2,1)}, u32[]{:S(2)}, u32[]{:S(2)}) async-start(bf16[4,128,2048]{2,1,0:T(8,128)(2,1)} %broadcast_in_dim.195), calls=%async_computation | async-start | bytes 4194304 | tf_op jit(solution)/shard_map/all_to_all | solution.py:46
  20.8 11.8 %collective-permute-start.10 = (bf16[2,2,4,11,64]{4,2,1,0,3:T(4,128)(2,1)S(1)}, bf16[2,2,4,11,64]{4,2,1,0,3:T(4,128)(2,1)S(1)}, u32[]{:S(2)}, u32[]{:S(2)}) collective-permute-start(bf16[2,2,4,11,64]{4,2,1,0,3:T(4,128)(2,1)S(1)} %broadcast_select_fusion.13), channel_id=1, source_target_pairs={{0,16},{8,24},{16,0},{24,8},{1,17},{9,25},{17,1},{25,9},{2,18},{10... | collective-permute-start | bytes 67592 | tf_op jit(solution)/shard_map/ppermute | solution.py:29
  22.3 24.5 %collective-permute-start.1 = (bf16[2,256,1024]{2,1,0:T(8,128)(2,1)S(1)}, bf16[2,256,1024]{2,1,0:T(8,128)(2,1)S(1)}, u32[]{:S(2)}, u32[]{:S(2)}) collective-permute-start(bf16[2,256,1024]{2,1,0:T(8,128)(2,1)S(1)} %pad_maximum_fusion.13.refs_2_.refs_4_.refs_1_.refs_3_), channel_id=1, source_target_pairs={{0,4},{4,0},{1,5},{5,1},{2,6},{6,2},{3,7},{7,3},{8,12},{12,8},{9,1... | collective-permute-start | bytes 3145736 | tf_op jit(solution)/shard_map/ppermute | solution.py:34
  23.6 24.3 %collective-permute-start.2 = (bf16[2,256,1024]{2,1,0:T(8,128)(2,1)S(1)}, bf16[2,256,1024]{2,1,0:T(8,128)(2,1)S(1)}, u32[]{:S(2)}, u32[]{:S(2)}) collective-permute-start(bf16[2,256,1024]{2,1,0:T(8,128)(2,1)S(1)} %pad_maximum_fusion.13.refs_2_.refs_4_.refs_1_.refs_3_), channel_id=1, source_target_pairs={{0,16},{8,24},{16,0},{24,8},{1,17},{9,25},{17,1},{25,9},{2,18},{10... | collective-permute-start | bytes 3145736 | tf_op jit(solution)/shard_map/ppermute | solution.py:29
  31.7 22.3 %collective-permute-start.5 = (bf16[256,2176]{1,0:T(8,128)(2,1)}, bf16[256,2176]{1,0:T(8,128)(2,1)}, u32[]{:S(2)}, u32[]{:S(2)}) collective-permute-start(bf16[256,2176]{1,0:T(8,128)(2,1)} %concatenate.142), channel_id=1, source_target_pairs={{0,8},{8,0},{16,24},{24,16},{1,9},{9,1},{17,25},{25,17},{2,10},{10... | collective-permute-start | bytes 3342344 | tf_op jit(solution)/shard_map/ppermute | solution.py:24
  32.9 17.1 %collective-permute-start.11 = (bf16[2,2,2,4,11,64]{5,3,0,2,1,4:T(4,128)(2,1)S(1)}, bf16[2,2,2,4,11,64]{5,3,0,2,1,4:T(4,128)(2,1)S(1)}, u32[]{:S(2)}, u32[]{:S(2)}) collective-permute-start(bf16[2,2,2,4,11,64]{5,3,0,2,1,4:T(4,128)(2,1)S(1)} %broadcast_select_fusion.12), channel_id=1, source_target_pairs={{0,4},{4,0},{1,5},{5,1},{2,6},{6,2},{3,7},{7,3},{8,12},{12,8},{9,1... | collective-permute-start | bytes 135176 | tf_op jit(solution)/shard_map/ppermute | solution.py:34
  47.7 11.7 %collective-permute-start.3 = (bf16[256,1024]{1,0:T(8,128)(2,1)}, bf16[256,1024]{1,0:T(8,128)(2,1)}, u32[]{:S(2)}, u32[]{:S(2)}) collective-permute-start(bf16[256,1024]{1,0:T(8,128)(2,1)} %slice_bitcast_fusion.33), channel_id=1, source_target_pairs={{0,16},{8,24},{16,0},{24,8},{1,17},{9,25},{17,1},{25,9},{2,18},{10... | collective-permute-start | bytes 1572872 | tf_op jit(solution)/shard_map/ppermute | solution.py:29
  48.8 11.4 %collective-permute-start.4 = (bf16[256,1024]{1,0:T(8,128)(2,1)}, bf16[256,1024]{1,0:T(8,128)(2,1)}, u32[]{:S(2)}, u32[]{:S(2)}) collective-permute-start(bf16[256,1024]{1,0:T(8,128)(2,1)} %slice_bitcast_fusion.32), channel_id=1, source_target_pairs={{0,4},{4,0},{1,5},{5,1},{2,6},{6,2},{3,7},{7,3},{8,12},{12,8},{9,1... | collective-permute-start | bytes 1572872 | tf_op jit(solution)/shard_map/ppermute | solution.py:34
  66.3 7.9 collective-permute-start.12
  70.3 50.2 %collective-permute-start.14 = (bf16[2,256,2176]{2,1,0:T(8,128)(2,1)S(1)}, bf16[2,256,2176]{2,1,0:T(8,128)(2,1)}, u32[]{:S(2)}, u32[]{:S(2)}) collective-permute-start(bf16[2,256,2176]{2,1,0:T(8,128)(2,1)S(1)} %pad_maximum_fusion.5.refs_2_.refs_4_), channel_id=1, source_target_pairs={{0,4},{4,0},{1,5},{5,1},{2,6},{6,2},{3,7},{7,3},{8,12},{12,8},{9,1... | collective-permute-start | bytes 6684680 | tf_op jit(solution)/shard_map/ppermute | solution.py:34
  71.5 49.9 %collective-permute-start.15 = (bf16[2,256,2176]{2,1,0:T(8,128)(2,1)S(1)}, bf16[2,256,2176]{2,1,0:T(8,128)(2,1)}, u32[]{:S(2)}, u32[]{:S(2)}) collective-permute-start(bf16[2,256,2176]{2,1,0:T(8,128)(2,1)S(1)} %pad_maximum_fusion.5.refs_2_.refs_4_), channel_id=1, source_target_pairs={{0,16},{8,24},{16,0},{24,8},{1,17},{9,25},{17,1},{25,9},{2,18},{10... | collective-permute-start | bytes 6684680 | tf_op jit(solution)/shard_map/ppermute | solution.py:29
  95.7 6.7 collective-permute-start.16
  96.0 45.8 %collective-permute-start.13 = (bf16[1024,512]{1,0:T(8,128)(2,1)S(1)}, bf16[1024,512]{1,0:T(8,128)(2,1)}, u32[]{:S(2)}, u32[]{:S(2)}) collective-permute-start(bf16[1024,512]{1,0:T(8,128)(2,1)S(1)} %copy-done.23), channel_id=1, source_target_pairs={{0,4},{1,5},{2,6},{3,7},{8,12},{9,13},{10,14},{11,15},{16,20},{17,... | collective-permute-start | bytes 3145736 | tf_op jit(solution)/shard_map/ppermute | solution.py:947
  144.2 25.5 %collective-permute-start.17 = (bf16[256,2176]{1,0:T(8,128)(2,1)}, bf16[256,2176]{1,0:T(8,128)(2,1)S(1)}, u32[]{:S(2)}, u32[]{:S(2)}) collective-permute-start(bf16[256,2176]{1,0:T(8,128)(2,1)} %slice_bitcast_fusion.13), channel_id=1, source_target_pairs={{0,16},{8,24},{16,0},{24,8},{1,17},{9,25},{17,1},{25,9},{2,18},{10... | collective-permute-start | bytes 3342344 | tf_op jit(solution)/shard_map/ppermute | solution.py:29
  147.7 26.4 %collective-permute-start.18 = (bf16[256,2176]{1,0:T(8,128)(2,1)}, bf16[256,2176]{1,0:T(8,128)(2,1)S(1)}, u32[]{:S(2)}, u32[]{:S(2)}) collective-permute-start(bf16[256,2176]{1,0:T(8,128)(2,1)} %slice_bitcast_fusion.12), channel_id=1, source_target_pairs={{0,4},{4,0},{1,5},{5,1},{2,6},{6,2},{3,7},{7,3},{8,12},{12,8},{9,1... | collective-permute-start | bytes 3342344 | tf_op jit(solution)/shard_map/ppermute | solution.py:34
  174.1 5.7 collective-permute-start.19
  183.4 52.8 %all-to-all-start.1 = ((bf16[4,128,2048]{2,1,0:T(8,128)(2,1)}), bf16[4,128,2048]{2,1,0:T(8,128)(2,1)}, u32[]{:S(2)}, u32[]{:S(2)}) async-start(bf16[4,128,2048]{2,1,0:T(8,128)(2,1)} %bitcast.46), calls=%async_computation.1 | async-start | bytes 4194304 | tf_op jit(solution)/shard_map/all_to_all | solution.py:46
  188.3 50.0 %collective-permute-start.20 = (bf16[2,256,2176]{2,1,0:T(8,128)(2,1)}, bf16[2,256,2176]{2,1,0:T(8,128)(2,1)}, u32[]{:S(2)}, u32[]{:S(2)}) collective-permute-start(bf16[2,256,2176]{2,1,0:T(8,128)(2,1)} %pad_maximum_fusion.6.refs_10_.refs_12_), channel_id=1, source_target_pairs={{0,4},{4,0},{1,5},{5,1},{2,6},{6,2},{3,7},{7,3},{8,12},{12,8},{9,1... | collective-permute-start | bytes 6684680 | tf_op jit(solution)/shard_map/ppermute | solution.py:34
  189.8 49.6 %collective-permute-start.21 = (bf16[2,256,2176]{2,1,0:T(8,128)(2,1)}, bf16[2,256,2176]{2,1,0:T(8,128)(2,1)}, u32[]{:S(2)}, u32[]{:S(2)}) collective-permute-start(bf16[2,256,2176]{2,1,0:T(8,128)(2,1)} %pad_maximum_fusion.6.refs_10_.refs_12_), channel_id=1, source_target_pairs={{0,16},{8,24},{16,0},{24,8},{1,17},{9,25},{17,1},{25,9},{2,18},{10... | collective-permute-start | bytes 6684680 | tf_op jit(solution)/shard_map/ppermute | solution.py:29
  192.4 3.5 collective-permute-start.22
  243.6 79.6 %all-to-all-start.2 = ((bf16[4,128,2048]{2,1,0:T(8,128)(2,1)}), bf16[4,128,2048]{2,1,0:T(8,128)(2,1)}, u32[]{:S(2)}, u32[]{:S(2)}) async-start(bf16[4,128,2048]{2,1,0:T(8,128)(2,1)} %broadcast_in_dim.216), calls=%async_computation.2 | async-start | bytes 4194304 | tf_op jit(solution)/shard_map/all_to_all | solution.py:46
  248.0 72.4 %collective-permute-start.25 = (bf16[2,256,2176]{2,1,0:T(8,128)(2,1)S(1)}, bf16[2,256,2176]{2,1,0:T(8,128)(2,1)S(1)}, u32[]{:S(2)}, u32[]{:S(2)}) collective-permute-start(bf16[2,256,2176]{2,1,0:T(8,128)(2,1)S(1)} %pad_maximum_fusion.7.refs_1_.refs_3_.refs_2_.refs_4_), channel_id=1, source_target_pairs={{0,4},{4,0},{1,5},{5,1},{2,6},{6,2},{3,7},{7,3},{8,12},{12,8},{9,1... | collective-permute-start | bytes 6684680 | tf_op jit(solution)/shard_map/ppermute | solution.py:34
  248.4 74.8 %collective-permute-start.26 = (bf16[2,256,2176]{2,1,0:T(8,128)(2,1)S(1)}, bf16[2,256,2176]{2,1,0:T(8,128)(2,1)}, u32[]{:S(2)}, u32[]{:S(2)}) collective-permute-start(bf16[2,256,2176]{2,1,0:T(8,128)(2,1)S(1)} %pad_maximum_fusion.7.refs_1_.refs_3_.refs_2_.refs_4_), channel_id=1, source_target_pairs={{0,16},{8,24},{16,0},{24,8},{1,17},{9,25},{17,1},{25,9},{2,18},{10... | collective-permute-start | bytes 6684680 | tf_op jit(solution)/shard_map/ppermute | solution.py:29
  250.0 70.4 %collective-permute-start.23 = (bf16[256,2176]{1,0:T(8,128)(2,1)S(1)}, bf16[256,2176]{1,0:T(8,128)(2,1)S(1)}, u32[]{:S(2)}, u32[]{:S(2)}) collective-permute-start(bf16[256,2176]{1,0:T(8,128)(2,1)S(1)} %slice_bitcast_fusion.11), channel_id=1, source_target_pairs={{0,16},{8,24},{16,0},{24,8},{1,17},{9,25},{17,1},{25,9},{2,18},{10... | collective-permute-start | bytes 3342344 | tf_op jit(solution)/shard_map/ppermute | solution.py:29
  252.6 67.8 %collective-permute-start.24 = (bf16[256,2176]{1,0:T(8,128)(2,1)S(1)}, bf16[256,2176]{1,0:T(8,128)(2,1)S(1)}, u32[]{:S(2)}, u32[]{:S(2)}) collective-permute-start(bf16[256,2176]{1,0:T(8,128)(2,1)S(1)} %slice_bitcast_fusion.10), channel_id=1, source_target_pairs={{0,4},{4,0},{1,5},{5,1},{2,6},{6,2},{3,7},{7,3},{8,12},{12,8},{9,1... | collective-permute-start | bytes 3342344 | tf_op jit(solution)/shard_map/ppermute | solution.py:34
  323.2 12.0 %collective-permute-start.27 = (bf16[512,2048]{1,0:T(8,128)(2,1)}, bf16[512,2048]{1,0:T(8,128)(2,1)S(1)}, u32[]{:S(2)}, u32[]{:S(2)}) collective-permute-start(bf16[512,2048]{1,0:T(8,128)(2,1)} %bitcast.56.refs_0_.refs_2_), channel_id=1, source_target_pairs={{0,8},{8,0},{16,24},{24,16},{1,9},{9,1},{17,25},{25,17},{2,10},{10... | collective-permute-start | bytes 6291464 | tf_op jit(solution)/shard_map/ppermute | solution.py:24
  328.3 39.5 %collective-permute-start.28 = (bf16[256,2176]{1,0:T(8,128)(2,1)}, bf16[256,2176]{1,0:T(8,128)(2,1)}, u32[]{:S(2)}, u32[]{:S(2)}) collective-permute-start(bf16[256,2176]{1,0:T(8,128)(2,1)} %slice_bitcast_fusion.9), channel_id=1, source_target_pairs={{0,16},{8,24},{16,0},{24,8},{1,17},{9,25},{17,1},{25,9},{2,18},{10... | collective-permute-start | bytes 3342344 | tf_op jit(solution)/shard_map/ppermute | solution.py:29
  330.8 36.9 %collective-permute-start.29 = (bf16[256,2176]{1,0:T(8,128)(2,1)}, bf16[256,2176]{1,0:T(8,128)(2,1)}, u32[]{:S(2)}, u32[]{:S(2)}) collective-permute-start(bf16[256,2176]{1,0:T(8,128)(2,1)} %slice_bitcast_fusion.8), channel_id=1, source_target_pairs={{0,4},{4,0},{1,5},{5,1},{2,6},{6,2},{3,7},{7,3},{8,12},{12,8},{9,1... | collective-permute-start | bytes 3342344 | tf_op jit(solution)/shard_map/ppermute | solution.py:34
  385.3 5.1 collective-permute-start.30
  394.1 52.2 %all-to-all-start.3 = ((bf16[4,128,2048]{2,1,0:T(8,128)(2,1)}), bf16[4,128,2048]{2,1,0:T(8,128)(2,1)S(1)}, u32[]{:S(2)}, u32[]{:S(2)}) async-start(bf16[4,128,2048]{2,1,0:T(8,128)(2,1)} %bitcast.273), calls=%async_computation.3 | async-start | bytes 4194304 | tf_op jit(solution)/shard_map/all_to_all | solution.py:46
  499.3 5.8 collective-permute-start.31
  523.3 58.2 %collective-permute-start.33 = (bf16[2,256,2176]{2,1,0:T(8,128)(2,1)}, bf16[2,256,2176]{2,1,0:T(8,128)(2,1)}, u32[]{:S(2)}, u32[]{:S(2)}) collective-permute-start(bf16[2,256,2176]{2,1,0:T(8,128)(2,1)} %get-tuple-element.169), channel_id=1, source_target_pairs={{0,16},{8,24},{16,0},{24,8},{1,17},{9,25},{17,1},{25,9},{2,18},{10... | collective-permute-start | bytes 6684680 | tf_op jit(solution)/shard_map/ppermute | solution.py:29
  524.1 57.4 %collective-permute-start.34 = (bf16[2,256,2176]{2,1,0:T(8,128)(2,1)}, bf16[2,256,2176]{2,1,0:T(8,128)(2,1)}, u32[]{:S(2)}, u32[]{:S(2)}) collective-permute-start(bf16[2,256,2176]{2,1,0:T(8,128)(2,1)} %get-tuple-element.171), channel_id=1, source_target_pairs={{0,4},{4,0},{1,5},{5,1},{2,6},{6,2},{3,7},{7,3},{8,12},{12,8},{9,1... | collective-permute-start | bytes 6684680 | tf_op jit(solution)/shard_map/ppermute | solution.py:34
  576.2 5.4 collective-permute-start.32
  581.4 6.1 collective-permute-start.36
  583.7 72.6 %all-to-all-start.5 = ((bf16[4,128,2048]{2,1,0:T(8,128)(2,1)}), bf16[4,128,2048]{2,1,0:T(8,128)(2,1)S(1)}, u32[]{:S(2)}, u32[]{:S(2)}) async-start(bf16[4,128,2048]{2,1,0:T(8,128)(2,1)} %bitcast.73), calls=%async_computation.5 | async-start | bytes 4194304 | tf_op jit(solution)/shard_map/all_to_all | solution.py:46
  587.5 33.5 %collective-permute-start.37 = (f32[1,9,128]{2,1,0:T(8,128)S(1)}, f32[1,9,128]{2,1,0:T(8,128)S(1)}, u32[]{:S(2)}, u32[]{:S(2)}) collective-permute-start(f32[1,9,128]{2,1,0:T(8,128)S(1)} %slice_select_fusion.7), channel_id=1, source_target_pairs={{0,1},{1,0},{2,3},{3,2},{4,5},{5,4},{6,7},{7,6},{8,9},{9,8},{10,11... | collective-permute-start | bytes 13832 | tf_op jit(solution)/shard_map/ppermute | solution.py:113
  591.9 64.7 %collective-permute-start.39 = (bf16[256,2176]{1,0:T(8,128)(2,1)}, bf16[256,2176]{1,0:T(8,128)(2,1)}, u32[]{:S(2)}, u32[]{:S(2)}) collective-permute-start(bf16[256,2176]{1,0:T(8,128)(2,1)} %fusion.8), channel_id=1, source_target_pairs={{0,16},{8,24},{16,0},{24,8},{1,17},{9,25},{17,1},{25,9},{2,18},{10... | collective-permute-start | bytes 3342344 | tf_op jit(solution)/shard_map/ppermute | solution.py:29
  594.4 62.2 %collective-permute-start.38 = (bf16[256,2176]{1,0:T(8,128)(2,1)}, bf16[256,2176]{1,0:T(8,128)(2,1)}, u32[]{:S(2)}, u32[]{:S(2)}) collective-permute-start(bf16[256,2176]{1,0:T(8,128)(2,1)} %fusion.7), channel_id=1, source_target_pairs={{0,4},{4,0},{1,5},{5,1},{2,6},{6,2},{3,7},{7,3},{8,12},{12,8},{9,1... | collective-permute-start | bytes 3342344 | tf_op jit(solution)/shard_map/ppermute | solution.py:34
  654.8 96.5 %collective-permute-start.43 = (bf16[2,256,4352]{2,1,0:T(8,128)(2,1)}, bf16[2,256,4352]{2,1,0:T(8,128)(2,1)}, u32[]{:S(2)}, u32[]{:S(2)}) collective-permute-start(bf16[2,256,4352]{2,1,0:T(8,128)(2,1)} %get-tuple-element.187), channel_id=1, source_target_pairs={{0,16},{8,24},{16,0},{24,8},{1,17},{9,25},{17,1},{25,9},{2,18},{10... | collective-permute-start | bytes 13369352 | tf_op jit(solution)/shard_map/ppermute | solution.py:29
  654.8 96.5 %collective-permute-start.44 = (bf16[2,256,4352]{2,1,0:T(8,128)(2,1)}, bf16[2,256,4352]{2,1,0:T(8,128)(2,1)}, u32[]{:S(2)}, u32[]{:S(2)}) collective-permute-start(bf16[2,256,4352]{2,1,0:T(8,128)(2,1)} %get-tuple-element.189), channel_id=1, source_target_pairs={{0,4},{4,0},{1,5},{5,1},{2,6},{6,2},{3,7},{7,3},{8,12},{12,8},{9,1... | collective-permute-start | bytes 13369352 | tf_op jit(solution)/shard_map/ppermute | solution.py:34
  661.5 54.7 %all-to-all-start.6 = ((bf16[4,128,2048]{2,1,0:T(8,128)(2,1)}), bf16[4,128,2048]{2,1,0:T(8,128)(2,1)}, u32[]{:S(2)}, u32[]{:S(2)}) async-start(bf16[4,128,2048]{2,1,0:T(8,128)(2,1)} %broadcast_in_dim.223), calls=%async_computation.6 | async-start | bytes 4194304 | tf_op jit(solution)/shard_map/all_to_all | solution.py:46
  671.3 5.0 collective-permute-start.40
  716.2 4.7 collective-permute-start.41
  751.3 24.3 %collective-permute-start.42 = (bf16[1024,512]{1,0:T(8,128)(2,1)}, bf16[1024,512]{1,0:T(8,128)(2,1)S(1)}, u32[]{:S(2)}, u32[]{:S(2)}) collective-permute-start(bf16[1024,512]{1,0:T(8,128)(2,1)} %get-tuple-element.211), channel_id=1, source_target_pairs={{4,0},{5,1},{6,2},{7,3},{12,8},{13,9},{14,10},{15,11},{20,16},{21,... | collective-permute-start | bytes 3145736 | tf_op jit(solution)/shard_map/ppermute | solution.py:1029
  787.3 11.5 %collective-permute-start.45 = (bf16[512,2048]{1,0:T(8,128)(2,1)}, bf16[512,2048]{1,0:T(8,128)(2,1)}, u32[]{:S(2)}, u32[]{:S(2)}) collective-permute-start(bf16[512,2048]{1,0:T(8,128)(2,1)} %get-tuple-element.218), channel_id=1, source_target_pairs={{0,8},{8,0},{16,24},{24,16},{1,9},{9,1},{17,25},{25,17},{2,10},{10... | collective-permute-start | bytes 6291464 | tf_op jit(solution)/shard_map/ppermute | solution.py:24
  790.8 50.3 %collective-permute-start.58 = (bf16[256,4352]{1,0:T(8,128)(2,1)}, bf16[256,4352]{1,0:T(8,128)(2,1)}, u32[]{:S(2)}, u32[]{:S(2)}) collective-permute-start(bf16[256,4352]{1,0:T(8,128)(2,1)} %fusion.4), channel_id=1, source_target_pairs={{0,16},{8,24},{16,0},{24,8},{1,17},{9,25},{17,1},{25,9},{2,18},{10... | collective-permute-start | bytes 6684680 | tf_op jit(solution)/shard_map/ppermute | solution.py:29
  796.7 50.0 %collective-permute-start.57 = (bf16[256,4352]{1,0:T(8,128)(2,1)}, bf16[256,4352]{1,0:T(8,128)(2,1)}, u32[]{:S(2)}, u32[]{:S(2)}) collective-permute-start(bf16[256,4352]{1,0:T(8,128)(2,1)} %fusion.3), channel_id=1, source_target_pairs={{0,4},{4,0},{1,5},{5,1},{2,6},{6,2},{3,7},{7,3},{8,12},{12,8},{9,1... | collective-permute-start | bytes 6684680 | tf_op jit(solution)/shard_map/ppermute | solution.py:34
  817.8 58.8 %collective-permute-start.52 = (bf16[2,256,1024]{2,1,0:T(8,128)(2,1)}, bf16[2,256,1024]{2,1,0:T(8,128)(2,1)}, u32[]{:S(2)}, u32[]{:S(2)}) collective-permute-start(bf16[2,256,1024]{2,1,0:T(8,128)(2,1)} %get-tuple-element.223), channel_id=1, source_target_pairs={{0,16},{8,24},{16,0},{24,8},{1,17},{9,25},{17,1},{25,9},{2,18},{10... | collective-permute-start | bytes 3145736 | tf_op jit(solution)/shard_map/ppermute | solution.py:29
  818.2 54.5 %all-to-all-start.7 = ((bf16[4,128,2048]{2,1,0:T(8,128)(2,1)}), bf16[4,128,2048]{2,1,0:T(8,128)(2,1)}, u32[]{:S(2)}, u32[]{:S(2)}) async-start(bf16[4,128,2048]{2,1,0:T(8,128)(2,1)} %bitcast.272), calls=%async_computation.7 | async-start | bytes 4194304 | tf_op jit(solution)/shard_map/all_to_all | solution.py:46
  823.4 57.2 %collective-permute-start.54 = (bf16[2,256,1024]{2,1,0:T(8,128)(2,1)}, bf16[2,256,1024]{2,1,0:T(8,128)(2,1)}, u32[]{:S(2)}, u32[]{:S(2)}) collective-permute-start(bf16[2,256,1024]{2,1,0:T(8,128)(2,1)} %get-tuple-element.225), channel_id=1, source_target_pairs={{0,4},{4,0},{1,5},{5,1},{2,6},{6,2},{3,7},{7,3},{8,12},{12,8},{9,1... | collective-permute-start | bytes 3145736 | tf_op jit(solution)/shard_map/ppermute | solution.py:34
  844.9 12.6 %collective-permute-start.59 = (bf16[256,4352]{1,0:T(8,128)(2,1)S(1)}, bf16[256,4352]{1,0:T(8,128)(2,1)S(1)}, u32[]{:S(2)}, u32[]{:S(2)}) collective-permute-start(bf16[256,4352]{1,0:T(8,128)(2,1)S(1)} %fusion), channel_id=1, source_target_pairs={{0,8},{8,0},{16,24},{24,16},{1,9},{9,1},{17,25},{25,17},{2,10},{10... | collective-permute-start | bytes 6684680 | tf_op jit(solution)/shard_map/ppermute | solution.py:24
  875.2 4.2 collective-permute-start.46
  878.0 21.2 %collective-permute-start.53 = (bf16[256,1024]{1,0:T(8,128)(2,1)S(1)}, bf16[256,1024]{1,0:T(8,128)(2,1)S(1)}, u32[]{:S(2)}, u32[]{:S(2)}) collective-permute-start(bf16[256,1024]{1,0:T(8,128)(2,1)S(1)} %fusion.19), channel_id=1, source_target_pairs={{0,4},{4,0},{1,5},{5,1},{2,6},{6,2},{3,7},{7,3},{8,12},{12,8},{9,1... | collective-permute-start | bytes 1572872 | tf_op jit(solution)/shard_map/ppermute | solution.py:34
  881.8 13.7 %collective-permute-start.55 = (bf16[256,1024]{1,0:T(8,128)(2,1)S(1)}, bf16[256,1024]{1,0:T(8,128)(2,1)S(1)}, u32[]{:S(2)}, u32[]{:S(2)}) collective-permute-start(bf16[256,1024]{1,0:T(8,128)(2,1)S(1)} %fusion.20), channel_id=1, source_target_pairs={{0,16},{8,24},{16,0},{24,8},{1,17},{9,25},{17,1},{25,9},{2,18},{10... | collective-permute-start | bytes 1572872 | tf_op jit(solution)/shard_map/ppermute | solution.py:29
  882.8 3.6 collective-permute-start.48
  886.4 8.5 collective-permute-start.49
  889.6 5.4 collective-permute-start.50
  891.1 3.8 collective-permute-start.51
  896.8 3.7 collective-permute-start.56
  (55 other events, 552.5 us)
